TPU v7x, 32 devices: a whole 2x2x4 slice. The times are simulated.
32 devices in a mesh: shot: 2 (over x), gx: 16 (over z, y, core).
Axes of the slice: x: 2, y: 2, z: 4, core: 2. Of those that a mesh axis runs over, the one named last changes fastest.
Arguments:
- source_field: float32 [512, 16, 128], P(('shot', 'gx')), parts along dimension 0, may hold values from -6 to 6
- source_prior: float32 [512, 16, 128], P(('shot', 'gx')), parts along dimension 0, may hold values from -6 to 6
- receiver_field: float32 [512, 16, 128], P(('shot', 'gx')), parts along dimension 0, may hold values from -6 to 6
- receiver_prior: float32 [512, 16, 128], P(('shot', 'gx')), parts along dimension 0, may hold values from -6 to 6
- stiffness: float32 [256, 16, 128], P('gx'), may hold values from 0.02 to 0.085
- buoyancy: float32 [256, 16, 128], P('gx'), may hold values from 0.5 to 2
- wavelet: float32 [32, 8], P('shot'), parts along dimension 0, may hold values from -6 to 6
- fire_step: int32 [32], P('shot'), parts along dimension 0, may hold values from 0 to 7
- shot_cell: int32 [32], P('shot'), parts along dimension 0, may hold values from 0 to 4095
- receiver_cell: int32 [4096], P('shot'), parts along dimension 0, may hold values from 0 to 4095
- traces: float32 [16, 2048], P('shot', 'gx'), parts along dimension 0, may hold values from -6 to 6
Outputs:
- image_sum: float32 [66, 256, 16, 128], P('shot', 'gx'), parts along dimension 0
There are 2 independent parts, one for each index of `shot`. A program takes and returns all parts, laid end to end along the dimension named above; an argument that names none is the same for every part. Nothing has to cross between parts.
All inputs are finite; a program needn't handle non-finite values.
Results may differ from a plain program's by a relative error of at most 0.0003.
Values sent between devices are 32-bit elements; how exact they have to be, the bound alone decides.
No kernel may reach another device: no remote copies, remote signals or barrier semaphores. Data moves between devices by JAX's collectives and lax.ppermute only.
A program may use at most 64 MiB of HBM per device.

v0:
```python
import jax
import jax.numpy as jnp
from jax import lax
from jax.sharding import PartitionSpec as P

STEPS = 8
IMG_EVERY = 4
NOFF = 33
SURFACE = 4
HALF = 16


stencil_weights = (1.6, -0.2, 8.0 / 315.0, -1.0 / 560.0)


def with_halo(cells, sides, width):
    for axis, dim in sides:
        count = lax.axis_size(axis)
        ends = count - 1
        head = lax.slice_in_dim(cells, 0, width, axis=dim)
        tail = lax.slice_in_dim(cells, cells.shape[dim] - width, cells.shape[dim], axis=dim)
        cells = jnp.concatenate(
            [
                lax.ppermute(tail, axis, [(i, (i + 1) % count) for i in range(ends)]),
                cells,
                lax.ppermute(head, axis, [((i + 1) % count, i) for i in range(ends)]),
            ],
            axis=dim,
        )
    return cells


def window(padded, direction, offset, extent):
    starts = [4, 4, 4]
    starts[direction] = starts[direction] + offset
    return padded[
        starts[0] : starts[0] + extent[0],
        starts[1] : starts[1] + extent[1],
        starts[2] : starts[2] + extent[2],
    ]


def laplace(wavefield, buoyant):
    extent = (wavefield.shape[0] - 8, wavefield.shape[1], wavefield.shape[2])
    padded_field = jnp.pad(wavefield, ((0, 0), (4, 4), (4, 4)))
    padded_buoyant = jnp.pad(buoyant, ((0, 0), (4, 4), (4, 4)))
    centre_field = window(padded_field, 0, 0, extent)
    centre_buoyant = window(padded_buoyant, 0, 0, extent)
    accumulated = jnp.zeros(extent, jnp.float32)
    for direction in range(3):
        for distance in range(4):
            for orientation in (1, -1):
                other_field = window(padded_field, direction, orientation * (distance + 1), extent)
                other_buoyant = window(
                    padded_buoyant, direction, orientation * (distance + 1), extent
                )
                accumulated = accumulated + stencil_weights[distance] * (
                    0.5 * (centre_buoyant + other_buoyant)
                ) * (other_field - centre_field)
    return accumulated


def plane_terms(cell_index, amounts, first_row, span_rows, lateral):
    inline = cell_index // lateral
    crossline = cell_index % lateral
    row_hot = (
        (inline - first_row)[:, None] == jnp.arange(span_rows, dtype=jnp.int32)[None, :]
    ).astype(jnp.float32)
    cross_hot = (crossline[:, None] == jnp.arange(lateral, dtype=jnp.int32)[None, :]).astype(
        jnp.float32
    )
    weighted = amounts[:, :, None] * cross_hot[None, :, :]
    return jnp.einsum("tnc,nr->trc", weighted, row_hot, precision=lax.Precision.HIGHEST)


def advance(current, prior_field, buoyant, stiff_cells, source_term):
    centre_cells = current[4 : current.shape[0] - 4]
    updated = 2.0 * centre_cells - prior_field + stiff_cells * laplace(current, buoyant)
    return updated.at[:, :, SURFACE].add(source_term)


def correlate(lag_source, lag_receiver, span_rows):
    pieces = []
    for offset_index in range(NOFF):
        lag_shift = offset_index - HALF
        pieces.append(
            lag_source[HALF - lag_shift : HALF - lag_shift + span_rows]
            * lag_receiver[HALF + lag_shift : HALF + lag_shift + span_rows]
        )
    return jnp.stack(pieces, 0)


def local(
    source_field,
    source_prior,
    receiver_field,
    receiver_prior,
    stiffness,
    buoyancy,
    wavelet,
    fire_step,
    shot_cell,
    receiver_cell,
    traces,
):
    brick_width = source_field.shape[0]
    lateral = source_field.shape[1]
    anchor = lax.axis_index("gx") * brick_width
    all_traces = lax.all_gather(traces, "gx", axis=1, tiled=True)
    wide_rows = brick_width + 2 * HALF
    reversed_traces = all_traces[::-1]
    moments = jnp.arange(STEPS, dtype=jnp.int32)
    delays = moments[:, None] - fire_step[None, :]
    choose = delays[:, :, None] == jnp.arange(wavelet.shape[1], dtype=jnp.int32)[None, None, :]
    shot_amounts = jnp.sum(jnp.where(choose, wavelet[None, :, :], 0.0), axis=2)
    shot_planes = plane_terms(shot_cell, shot_amounts, anchor - HALF, wide_rows, lateral)
    receiver_planes = plane_terms(receiver_cell, reversed_traces, anchor - HALF, wide_rows, lateral)
    wide_buoyant = with_halo(buoyancy, (("gx", 0),), HALF)
    wide_stiff = with_halo(stiffness, (("gx", 0),), HALF - 4)
    source_now, source_before = (source_field, source_prior)
    receiver_now, receiver_before = (receiver_field, receiver_prior)
    rounds = STEPS // IMG_EVERY
    image_sum = None
    for imaging_round in range(rounds + 1):
        lag_source, lag_receiver = (
            with_halo(source_now, (("gx", 0),), HALF),
            with_halo(receiver_now, (("gx", 0),), HALF),
        )
        product = correlate(lag_source, lag_receiver, brick_width)
        image_sum = product if imaging_round == 0 else image_sum + product
        if imaging_round < rounds:
            block_start = imaging_round * IMG_EVERY
            older_source, older_receiver = (
                with_halo(source_before, (("gx", 0),), HALF - 4),
                with_halo(receiver_before, (("gx", 0),), HALF - 4),
            )
            wide_source, wide_receiver = (lag_source, lag_receiver)
            for substep in range(IMG_EVERY):
                moment = block_start + substep
                margin = HALF - 4 * (substep + 1)
                extent = brick_width + 2 * margin
                cut_rows = 4 * substep
                first = HALF - margin
                buoyant_now = wide_buoyant[cut_rows : cut_rows + extent + 8]
                stiff_now = wide_stiff[cut_rows : cut_rows + extent]
                source_term = shot_planes[moment, first : first + extent]
                receiver_term = receiver_planes[moment, first : first + extent]
                source_next = advance(
                    wide_source, older_source, buoyant_now, stiff_now, source_term
                )
                receiver_next = advance(
                    wide_receiver, older_receiver, buoyant_now, stiff_now, receiver_term
                )
                previous_source, previous_receiver = (wide_source, wide_receiver)
                if substep < IMG_EVERY - 1:
                    older_source = previous_source[8 : previous_source.shape[0] - 8]
                    older_receiver = previous_receiver[8 : previous_receiver.shape[0] - 8]
                wide_source, wide_receiver = (source_next, receiver_next)
            source_before = previous_source[4 : previous_source.shape[0] - 4]
            receiver_before = previous_receiver[4 : previous_receiver.shape[0] - 4]
            source_now, receiver_now = (wide_source, wide_receiver)
    return image_sum


def solution(mesh):
    placed = (
        P(("shot", "gx"), None, None),
        P(("shot", "gx"), None, None),
        P(("shot", "gx"), None, None),
        P(("shot", "gx"), None, None),
        P("gx", None, None),
        P("gx", None, None),
        P("shot", None),
        P("shot"),
        P("shot"),
        P("shot"),
        P("shot", "gx"),
    )
    return jax.shard_map(
        local, mesh=mesh, in_specs=placed, out_specs=P("shot", "gx", None, None), check_vma=False
    )
```

profile of v0, /device:TPU:14, one launch (start us, length us, event | category | flops | bytes accessed | tf_op | source)
XLA Modules:
  0.0 241.1 jit_solution(14067689098078118635)
XLA Ops:
  0.0 2.0 collective-permute-start.1
  2.1 3.6 %collective-permute-start.3 = (f32[16,16,128]{2,1,0:T(8,128)}, f32[16,16,128]{2,1,0:T(8,128)S(1)}, u32[]{:S(2)}, u32[]{:S(2)}) collective-permute-start(f32[16,16,128]{2,1,0:T(8,128)} %param.45), channel_id=1, source_target_pairs={{1,0},{2,1},{3,2},{4,3},{5,4},{6,5},{7,6},{8,7},{9,8},{10,9},{11,1... | collective-permute-start | bytes 393224 | tf_op jit(solution)/shard_map/ppermute | solution.py:26
  5.7 1.9 collective-permute-start.8
  7.6 3.6 %collective-permute-start.9 = (f32[16,16,128]{2,1,0:T(8,128)}, f32[16,16,128]{2,1,0:T(8,128)S(1)}, u32[]{:S(2)}, u32[]{:S(2)}) collective-permute-start(f32[16,16,128]{2,1,0:T(8,128)} %param.48), channel_id=1, source_target_pairs={{1,0},{2,1},{3,2},{4,3},{5,4},{6,5},{7,6},{8,7},{9,8},{10,9},{11,1... | collective-permute-start | bytes 393224 | tf_op jit(solution)/shard_map/ppermute | solution.py:26
  12.3 2.7 %collective-permute-start.6 = (f32[12,16,128]{2,1,0:T(8,128)S(1)}, f32[12,16,128]{2,1,0:T(8,128)S(1)}, u32[]{:S(2)}, u32[]{:S(2)}) collective-permute-start(f32[12,16,128]{2,1,0:T(8,128)S(1)} %get-tuple-element.327), channel_id=1, source_target_pairs={{0,1},{1,2},{2,3},{3,4},{4,5},{5,6},{6,7},{7,8},{8,9},{9,10},{10,1... | collective-permute-start | bytes 294920 | tf_op jit(solution)/shard_map/ppermute | solution.py:24
  15.7 16.5 %all_gather.3 = f32[8,2048]{1,0:T(8,128)S(1)} all-gather(f32[8,128]{1,0:T(8,128)} %param.53), channel_id=1, replica_groups=mesh['shot'=2,'gx'=16] {'gx'}, dimensions={1}, use_global_device_ids=true | all-gather | bytes 69632 | tf_op jit(solution)/shard_map/all_gather | solution.py:109
  37.1 1.7 fusion.1570
  52.8 4.3 %collective-permute-start.7 = (f32[12,16,128]{2,1,0:T(8,128)S(1)}, f32[12,16,128]{2,1,0:T(8,128)S(1)}, u32[]{:S(2)}, u32[]{:S(2)}) collective-permute-start(f32[12,16,128]{2,1,0:T(8,128)S(1)} %get-tuple-element.326), channel_id=1, source_target_pairs={{1,0},{2,1},{3,2},{4,3},{5,4},{6,5},{7,6},{8,7},{9,8},{10,9},{11,1... | collective-permute-start | bytes 294920 | tf_op jit(solution)/shard_map/ppermute | solution.py:26
  57.2 2.1 collective-permute-done.7
  59.3 2.6 %collective-permute-start.2 = (f32[16,16,128]{2,1,0:T(8,128)}, f32[16,16,128]{2,1,0:T(8,128)}, u32[]{:S(2)}, u32[]{:S(2)}) collective-permute-start(f32[16,16,128]{2,1,0:T(8,128)} %param.43), channel_id=1, source_target_pairs={{0,1},{1,2},{2,3},{3,4},{4,5},{5,6},{6,7},{7,8},{8,9},{9,10},{10,1... | collective-permute-start | bytes 393224 | tf_op jit(solution)/shard_map/ppermute | solution.py:24
  61.9 3.1 %collective-permute-start = (f32[16,16,128]{2,1,0:T(8,128)}, f32[16,16,128]{2,1,0:T(8,128)}, u32[]{:S(2)}, u32[]{:S(2)}) collective-permute-start(f32[16,16,128]{2,1,0:T(8,128)} %param.43), channel_id=1, source_target_pairs={{1,0},{2,1},{3,2},{4,3},{5,4},{6,5},{7,6},{8,7},{9,8},{10,9},{11,1... | collective-permute-start | bytes 393224 | tf_op jit(solution)/shard_map/ppermute | solution.py:26
  65.0 2.5 %collective-permute-start.12 = (f32[12,16,128]{2,1,0:T(8,128)S(1)}, f32[12,16,128]{2,1,0:T(8,128)S(1)}, u32[]{:S(2)}, u32[]{:S(2)}) collective-permute-start(f32[12,16,128]{2,1,0:T(8,128)S(1)} %get-tuple-element.325), channel_id=1, source_target_pairs={{1,0},{2,1},{3,2},{4,3},{5,4},{6,5},{7,6},{8,7},{9,8},{10,9},{11,1... | collective-permute-start | bytes 294920 | tf_op jit(solution)/shard_map/ppermute | solution.py:26
  67.6 1.9 collective-permute-start.11
  70.4 4.6 %collective-permute-start.5 = (f32[12,16,128]{2,1,0:T(8,128)}, f32[12,16,128]{2,1,0:T(8,128)}, u32[]{:S(2)}, u32[]{:S(2)}) collective-permute-start(f32[12,16,128]{2,1,0:T(8,128)} %get-tuple-element.316), channel_id=1, source_target_pairs={{1,0},{2,1},{3,2},{4,3},{5,4},{6,5},{7,6},{8,7},{9,8},{10,9},{11,1... | collective-permute-start | bytes 294920 | tf_op jit(solution)/shard_map/ppermute | solution.py:26
  75.1 1.9 collective-permute-start.4
  77.1 4.3 %fusion.102 = (f32[40,16,128]{2,1,0:T(8,128)S(1)}, f32[40,16,128]{2,1,0:T(8,128)S(1)}, f32[40,16,128]{2,1,0:T(8,128)}, f32[40,16,128]{2,1,0:T(8,128)}, f32[40,16...) fusion(f32[40,16,128]{2,1,0:T(8,128)S(1)} %constant_dynamic-upd, ...), kind=kLoop, calls=%fused_computation.651 | loop fusion | flops 10240000 | bytes 15532032 | tf_op jit(solution)/shard_map/add | solution.py:78
  82.3 5.5 %scatter-add.60 = f32[40,16,128]{2,1,0:T(8,128)S(1)} dynamic-update-slice(f32[40,16,128]{2,1,0:T(8,128)S(1)} %get-tuple-element.272, f32[40,16,1]{2,1,0:T(8,128)} %slice_add_fusion.2, s32[]{:T(128)} %constant.500.clone.1, s32[]{:T(128)} %constant.500.clone.1, s32[]{:T(128)} %constant.502.clone.1) | dynamic-update-slice | bytes 5124 | tf_op jit(solution)/shard_map/scatter-add | solution.py:79
  87.8 3.6 %fusion.402 = (f32[32,16,128]{2,1,0:T(8,128)S(1)}, f32[32,16,128]{2,1,0:T(8,128)}, f32[32,16,128]{2,1,0:T(8,128)}, f32[32,16,128]{2,1,0:T(8,128)}, f32[32,16,128...) fusion(f32[40,16,128]{2,1,0:T(8,128)S(1)} %scatter-add.60, ...), kind=kLoop, calls=%fused_computation.999 | loop fusion | flops 8060928 | bytes 12451840 | tf_op jit(solution)/shard_map/add | solution.py:78
  91.5 2.4 scatter-add.61
  93.9 6.3 %fusion.702 = (f32[24,16,128]{2,1,0:T(8,128)S(1)}, f32[24,16,128]{2,1,0:T(8,128)}, f32[24,16,128]{2,1,0:T(8,128)}, f32[24,16,128]{2,1,0:T(8,128)}, f32[24,16,128...) fusion(f32[32,16,128]{2,1,0:T(8,128)S(1)} %scatter-add.61, ...), kind=kLoop, calls=%fused_computation.1470 | loop fusion | flops 6045696 | bytes 9371648 | tf_op jit(solution)/shard_map/add | solution.py:78
  102.0 2.0 scatter-add.64
  105.9 4.3 %fusion.52 = f32[40,16,128]{2,1,0:T(8,128)S(1)} fusion(f32[40,16,128]{2,1,0:T(8,128)S(1)} %constant_dynamic-update-slice_fusion.44, f32[40,16,128]{2,1,0:T(8,128)} %get-tuple-element.296, f32[48,16,128]{2,1,0:T(8,128)S(1)} %get-tuple-element.312, f32[40,16,128]{2,1,0:T(8,128)} %get-tuple-element.295, f32[40,16,128]{2,1,0:T(8,128)} %get-tuple-element.294, ...), kind=kLoop, calls=%fused_computation.601 | loop fusion | flops 6307840 | bytes 12189696 | tf_op jit(solution)/shard_map/add | solution.py:78
  110.4 5.3 %scatter-add.54 = f32[40,16,128]{2,1,0:T(8,128)S(1)} dynamic-update-slice(f32[40,16,128]{2,1,0:T(8,128)S(1)} %fusion.52, f32[40,16,1]{2,1,0:T(8,128)S(1)} %slice_add_fusion.3, s32[]{:T(128)} %constant.500.clone.1, s32[]{:T(128)} %constant.500.clone.1, s32[]{:T(128)} %constant.502.clone.1) | dynamic-update-slice | bytes 5124 | tf_op jit(solution)/shard_map/scatter-add | solution.py:79
  115.7 3.7 %fusion.352 = f32[32,16,128]{2,1,0:T(8,128)S(1)} fusion(f32[32,16,128]{2,1,0:T(8,128)} %get-tuple-element.271, f32[40,16,128]{2,1,0:T(8,128)S(1)} %scatter-add.54, f32[32,16,128]{2,1,0:T(8,128)} %get-tuple-element.270, f32[32,16,128]{2,1,0:T(8,128)} %get-tuple-element.269, f32[32,16,128]{2,1,0:T(8,128)} %get-tuple-element.268, ...), kind=kLoop, calls=%fused_computation.949 | loop fusion | flops 4915200 | bytes 9764864 | tf_op jit(solution)/shard_map/add | solution.py:78
  120.3 3.3 %scatter-add.55 = f32[32,16,128]{2,1,0:T(8,128)S(1)} dynamic-update-slice(f32[32,16,128]{2,1,0:T(8,128)S(1)} %fusion.352, f32[32,16,1]{2,1,0:T(8,128)} %slice_add_fusion.15, s32[]{:T(128)} %constant.500.clone.1, s32[]{:T(128)} %constant.500.clone.1, s32[]{:T(128)} %constant.502.clone.1) | dynamic-update-slice | bytes 4100 | tf_op jit(solution)/shard_map/scatter-add | solution.py:79
  123.6 3.0 %fusion.652 = f32[24,16,128]{2,1,0:T(8,128)S(1)} fusion(f32[24,16,128]{2,1,0:T(8,128)} %get-tuple-element.246, f32[32,16,128]{2,1,0:T(8,128)S(1)} %scatter-add.55, f32[24,16,128]{2,1,0:T(8,128)} %get-tuple-element.245, f32[24,16,128]{2,1,0:T(8,128)} %get-tuple-element.244, f32[24,16,128]{2,1,0:T(8,128)} %get-tuple-element.243, ...), kind=kLoop, calls=%fused_computation.1420 | loop fusion | flops 3686400 | bytes 7340032 | tf_op jit(solution)/shard_map/add | solution.py:78
  127.7 1.8 scatter-add.56
  129.5 3.8 %fusion.1227 = (f32[16,16,128]{2,1,0:T(8,128)S(1)}, f32[16,16,128]{2,1,0:T(8,128)S(1)}, f32[16,16,128]{2,1,0:T(8,128)S(1)}, f32[16,16,128]{2,1,0:T(8,128)S(1)}, ...) fusion(f32[16,16,128]{2,1,0:T(8,128)S(1)} %copy-done, ...), kind=kLoop, calls=%fused_computation.2043 | loop fusion | flops 4030464 | bytes 6291456 | tf_op jit(solution)/shard_map/add | solution.py:78
  135.0 1.2 scatter-add.59
  136.2 3.6 %collective-permute-start.10 = (f32[16,16,128]{2,1,0:T(8,128)S(1)}, f32[16,16,128]{2,1,0:T(8,128)S(1)}, u32[]{:S(2)}, u32[]{:S(2)}) collective-permute-start(f32[16,16,128]{2,1,0:T(8,128)S(1)} %scatter-add.59), channel_id=1, source_target_pairs={{1,0},{2,1},{3,2},{4,3},{5,4},{6,5},{7,6},{8,7},{9,8},{10,9},{11,1... | collective-permute-start | bytes 393224 | tf_op jit(solution)/shard_map/ppermute | solution.py:26
  139.9 1.9 collective-permute-start.14
  143.3 1.2 scatter-add.65
  144.6 3.6 %collective-permute-start.15 = (f32[16,16,128]{2,1,0:T(8,128)S(1)}, f32[16,16,128]{2,1,0:T(8,128)S(1)}, u32[]{:S(2)}, u32[]{:S(2)}) collective-permute-start(f32[16,16,128]{2,1,0:T(8,128)S(1)} %scatter-add.65), channel_id=1, source_target_pairs={{1,0},{2,1},{3,2},{4,3},{5,4},{6,5},{7,6},{8,7},{9,8},{10,9},{11,1... | collective-permute-start | bytes 393224 | tf_op jit(solution)/shard_map/ppermute | solution.py:26
  148.2 2.4 collective-permute-start.13
  150.6 3.7 %collective-permute-start.17 = (f32[12,16,128]{2,1,0:T(8,128)}, f32[12,16,128]{2,1,0:T(8,128)}, u32[]{:S(2)}, u32[]{:S(2)}) collective-permute-start(f32[12,16,128]{2,1,0:T(8,128)} %get-tuple-element.300), channel_id=1, source_target_pairs={{1,0},{2,1},{3,2},{4,3},{5,4},{6,5},{7,6},{8,7},{9,8},{10,9},{11,1... | collective-permute-start | bytes 294920 | tf_op jit(solution)/shard_map/ppermute | solution.py:26
  157.4 1.5 constant_dynamic-update-slice_fusion.8
  159.0 4.5 %collective-permute-start.20 = (f32[12,16,128]{2,1,0:T(8,128)S(1)}, f32[12,16,128]{2,1,0:T(8,128)S(1)}, u32[]{:S(2)}, u32[]{:S(2)}) collective-permute-start(f32[12,16,128]{2,1,0:T(8,128)S(1)} %get-tuple-element.298), channel_id=1, source_target_pairs={{1,0},{2,1},{3,2},{4,3},{5,4},{6,5},{7,6},{8,7},{9,8},{10,9},{11,1... | collective-permute-start | bytes 294920 | tf_op jit(solution)/shard_map/ppermute | solution.py:26
  163.6 1.9 collective-permute-start.19
  165.8 3.2 %collective-permute-start.16 = (f32[12,16,128]{2,1,0:T(8,128)}, f32[12,16,128]{2,1,0:T(8,128)}, u32[]{:S(2)}, u32[]{:S(2)}) collective-permute-start(f32[12,16,128]{2,1,0:T(8,128)} %get-tuple-element.299), channel_id=1, source_target_pairs={{0,1},{1,2},{2,3},{3,4},{4,5},{5,6},{6,7},{7,8},{8,9},{9,10},{10,1... | collective-permute-start | bytes 294920 | tf_op jit(solution)/shard_map/ppermute | solution.py:24
  169.0 1.4 collective-permute-done.19
  170.6 1.2 fusion.202
  172.7 5.5 %scatter-add.74 = f32[40,16,128]{2,1,0:T(8,128)S(1)} dynamic-update-slice(f32[40,16,128]{2,1,0:T(8,128)S(1)} %fusion.202, f32[40,16,1]{2,1,0:T(8,128)} %slice_add_fusion, s32[]{:T(128)} %constant.500.clone.1, s32[]{:T(128)} %constant.500.clone.1, s32[]{:T(128)} %constant.502.clone.1) | dynamic-update-slice | bytes 5124 | tf_op jit(solution)/shard_map/scatter-add | solution.py:79
  178.3 3.3 %fusion.502 = f32[32,16,128]{2,1,0:T(8,128)S(1)} fusion(f32[32,16,128]{2,1,0:T(8,128)} %get-tuple-element.271, f32[40,16,128]{2,1,0:T(8,128)S(1)} %scatter-add.74, f32[32,16,128]{2,1,0:T(8,128)} %get-tuple-element.270, f32[32,16,128]{2,1,0:T(8,128)} %get-tuple-element.269, f32[32,16,128]{2,1,0:T(8,128)} %get-tuple-element.268, ...), kind=kLoop, calls=%fused_computation.1099 | loop fusion | flops 4915200 | bytes 9764864 | tf_op jit(solution)/shard_map/add | solution.py:78
  181.7 2.4 scatter-add.75
  184.1 3.1 %fusion.802 = f32[24,16,128]{2,1,0:T(8,128)S(1)} fusion(f32[24,16,128]{2,1,0:T(8,128)} %get-tuple-element.246, f32[32,16,128]{2,1,0:T(8,128)S(1)} %scatter-add.75, f32[24,16,128]{2,1,0:T(8,128)} %get-tuple-element.245, f32[24,16,128]{2,1,0:T(8,128)} %get-tuple-element.244, f32[24,16,128]{2,1,0:T(8,128)} %get-tuple-element.243, ...), kind=kLoop, calls=%fused_computation.1570 | loop fusion | flops 3686400 | bytes 7340032 | tf_op jit(solution)/shard_map/add | solution.py:78
  187.3 1.1 slice_add_fusion.24
  188.4 1.8 scatter-add.76
  190.3 2.3 fusion.1327
  192.7 1.2 scatter-add.79
  193.9 1.9 collective-permute-start.21
  195.9 3.6 %collective-permute-start.23 = (f32[16,16,128]{2,1,0:T(8,128)S(1)}, f32[16,16,128]{2,1,0:T(8,128)S(1)}, u32[]{:S(2)}, u32[]{:S(2)}) collective-permute-start(f32[16,16,128]{2,1,0:T(8,128)S(1)} %scatter-add.79), channel_id=1, source_target_pairs={{1,0},{2,1},{3,2},{4,3},{5,4},{6,5},{7,6},{8,7},{9,8},{10,9},{11,1... | collective-permute-start | bytes 393224 | tf_op jit(solution)/shard_map/ppermute | solution.py:26
  199.6 4.2 %fusion.152 = f32[40,16,128]{2,1,0:T(8,128)S(1)} fusion(f32[40,16,128]{2,1,0:T(8,128)S(1)} %constant_dynamic-update-slice_fusion.44, f32[40,16,128]{2,1,0:T(8,128)} %get-tuple-element.296, f32[48,16,128]{2,1,0:T(8,128)S(1)} %pad_maximum_fusion, f32[40,16,128]{2,1,0:T(8,128)} %get-tuple-element.295, f32[40,16,128]{2,1,0:T(8,128)} %get-tuple-element.294, ...), kind=kLoop, calls=%fused_computation.701 | loop fusion | flops 6307840 | bytes 12189696 | tf_op jit(solution)/shard_map/add | solution.py:78
  203.9 5.3 %scatter-add.66 = f32[40,16,128]{2,1,0:T(8,128)S(1)} dynamic-update-slice(f32[40,16,128]{2,1,0:T(8,128)S(1)} %fusion.152, f32[40,16,1]{2,1,0:T(8,128)S(1)} %slice_add_fusion.1, s32[]{:T(128)} %constant.500.clone.1, s32[]{:T(128)} %constant.500.clone.1, s32[]{:T(128)} %constant.502.clone.1) | dynamic-update-slice | bytes 5124 | tf_op jit(solution)/shard_map/scatter-add | solution.py:79
  209.3 3.7 %fusion.452 = f32[32,16,128]{2,1,0:T(8,128)S(1)} fusion(f32[32,16,128]{2,1,0:T(8,128)} %get-tuple-element.271, f32[40,16,128]{2,1,0:T(8,128)S(1)} %scatter-add.66, f32[32,16,128]{2,1,0:T(8,128)} %get-tuple-element.270, f32[32,16,128]{2,1,0:T(8,128)} %get-tuple-element.269, f32[32,16,128]{2,1,0:T(8,128)} %get-tuple-element.268, ...), kind=kLoop, calls=%fused_computation.1049 | loop fusion | flops 4915200 | bytes 9764864 | tf_op jit(solution)/shard_map/add | solution.py:78
  213.9 3.3 %scatter-add.69 = f32[32,16,128]{2,1,0:T(8,128)S(1)} dynamic-update-slice(f32[32,16,128]{2,1,0:T(8,128)S(1)} %fusion.452, f32[32,16,1]{2,1,0:T(8,128)} %slice_add_fusion.13, s32[]{:T(128)} %constant.500.clone.1, s32[]{:T(128)} %constant.500.clone.1, s32[]{:T(128)} %constant.502.clone.1) | dynamic-update-slice | bytes 4100 | tf_op jit(solution)/shard_map/scatter-add | solution.py:79
  217.3 2.8 %fusion.752 = f32[24,16,128]{2,1,0:T(8,128)S(1)} fusion(f32[24,16,128]{2,1,0:T(8,128)} %get-tuple-element.246, f32[32,16,128]{2,1,0:T(8,128)S(1)} %scatter-add.69, f32[24,16,128]{2,1,0:T(8,128)} %get-tuple-element.245, f32[24,16,128]{2,1,0:T(8,128)} %get-tuple-element.244, f32[24,16,128]{2,1,0:T(8,128)} %get-tuple-element.243, ...), kind=kLoop, calls=%fused_computation.1520 | loop fusion | flops 3686400 | bytes 7340032 | tf_op jit(solution)/shard_map/add | solution.py:78
  220.1 1.1 slice_add_fusion.25
  221.2 2.1 scatter-add.70
  223.3 2.3 fusion.1277
  225.8 1.2 scatter-add.71
  227.0 2.8 %collective-permute-start.18 = (f32[16,16,128]{2,1,0:T(8,128)S(1)}, f32[16,16,128]{2,1,0:T(8,128)S(1)}, u32[]{:S(2)}, u32[]{:S(2)}) collective-permute-start(f32[16,16,128]{2,1,0:T(8,128)S(1)} %scatter-add.71), channel_id=1, source_target_pairs={{1,0},{2,1},{3,2},{4,3},{5,4},{6,5},{7,6},{8,7},{9,8},{10,9},{11,1... | collective-permute-start | bytes 393224 | tf_op jit(solution)/shard_map/ppermute | solution.py:26
  229.8 1.9 collective-permute-start.22
  233.1 3.9 %collective-permute-done.22 = f32[16,16,128]{2,1,0:T(8,128)S(1)} collective-permute-done((f32[16,16,128]{2,1,0:T(8,128)S(1)}, f32[16,16,128]{2,1,0:T(8,128)S(1)}, u32[]{:S(2)}, u32[]{:S(2)}) %collective-permute-start.22) | collective-permute-done | bytes 131104 | tf_op jit(solution)/shard_map/ppermute | solution.py:24
  238.0 3.1 %add_add_fusion = f32[33,16,16,128]{3,2,1,0:T(8,128)} fusion(f32[33,16,16,128]{3,2,1,0:T(8,128)S(1)} %constant_dynamic-update-slice_fusion.90, f32[33,16,16,128]{3,2,1,0:T(8,128)S(1)} %bitcast.425, f32[33,16,16,128]{3,2,1,0:T(8,128)S(1)} %constant_dynamic-update-slice_fusion.57), kind=kLoop, calls=%fused_computation.160 | loop fusion | flops 2162688 | bytes 17301504 | tf_op jit(solution)/shard_map/add | solution.py:130
  (383 shorter events, 38.2 us)
Async XLA Ops:
  0.0 57.1 %copy-start = (f32[16,16,128]{2,1,0:T(8,128)S(1)}, f32[16,16,128]{2,1,0:T(8,128)}, u32[]{:S(2)}) copy-start(f32[16,16,128]{2,1,0:T(8,128)} %param.47) | copy-start | bytes 393220
  0.0 61.9 %collective-permute-start.1 = (f32[16,16,128]{2,1,0:T(8,128)}, f32[16,16,128]{2,1,0:T(8,128)S(1)}, u32[]{:S(2)}, u32[]{:S(2)}) collective-permute-start(f32[16,16,128]{2,1,0:T(8,128)} %param.45), channel_id=1, source_target_pairs={{0,1},{1,2},{2,3},{3,4},{4,5},{5,6},{6,7},{7,8},{8,9},{9,10},{10,1... | collective-permute-start | bytes 393224 | tf_op jit(solution)/shard_map/ppermute | solution.py:24
  2.1 68.4 %collective-permute-start.3 = (f32[16,16,128]{2,1,0:T(8,128)}, f32[16,16,128]{2,1,0:T(8,128)S(1)}, u32[]{:S(2)}, u32[]{:S(2)}) collective-permute-start(f32[16,16,128]{2,1,0:T(8,128)} %param.45), channel_id=1, source_target_pairs={{1,0},{2,1},{3,2},{4,3},{5,4},{6,5},{7,6},{8,7},{9,8},{10,9},{11,1... | collective-permute-start | bytes 393224 | tf_op jit(solution)/shard_map/ppermute | solution.py:26
  5.7 59.3 %collective-permute-start.8 = (f32[16,16,128]{2,1,0:T(8,128)}, f32[16,16,128]{2,1,0:T(8,128)S(1)}, u32[]{:S(2)}, u32[]{:S(2)}) collective-permute-start(f32[16,16,128]{2,1,0:T(8,128)} %param.48), channel_id=1, source_target_pairs={{0,1},{1,2},{2,3},{3,4},{4,5},{5,6},{6,7},{7,8},{8,9},{9,10},{10,1... | collective-permute-start | bytes 393224 | tf_op jit(solution)/shard_map/ppermute | solution.py:24
  7.6 60.0 %collective-permute-start.9 = (f32[16,16,128]{2,1,0:T(8,128)}, f32[16,16,128]{2,1,0:T(8,128)S(1)}, u32[]{:S(2)}, u32[]{:S(2)}) collective-permute-start(f32[16,16,128]{2,1,0:T(8,128)} %param.48), channel_id=1, source_target_pairs={{1,0},{2,1},{3,2},{4,3},{5,4},{6,5},{7,6},{8,7},{9,8},{10,9},{11,1... | collective-permute-start | bytes 393224 | tf_op jit(solution)/shard_map/ppermute | solution.py:26
  12.3 40.5 %collective-permute-start.6 = (f32[12,16,128]{2,1,0:T(8,128)S(1)}, f32[12,16,128]{2,1,0:T(8,128)S(1)}, u32[]{:S(2)}, u32[]{:S(2)}) collective-permute-start(f32[12,16,128]{2,1,0:T(8,128)S(1)} %get-tuple-element.327), channel_id=1, source_target_pairs={{0,1},{1,2},{2,3},{3,4},{4,5},{5,6},{6,7},{7,8},{8,9},{9,10},{10,1... | collective-permute-start | bytes 294920 | tf_op jit(solution)/shard_map/ppermute | solution.py:24
  32.5 35.1 %copy-start.90 = (f32[16,16,128]{2,1,0:T(8,128)S(1)}, f32[16,16,128]{2,1,0:T(8,128)}, u32[]{:S(2)}) copy-start(f32[16,16,128]{2,1,0:T(8,128)} %param.48) | copy-start | bytes 393220
  33.3 37.1 %copy-start.91 = (f32[16,16,128]{2,1,0:T(8,128)S(1)}, f32[16,16,128]{2,1,0:T(8,128)}, u32[]{:S(2)}) copy-start(f32[16,16,128]{2,1,0:T(8,128)} %param.45) | copy-start | bytes 393220
  37.0 40.1 %copy-start.80 = (f32[16,16,128]{2,1,0:T(8,128)S(1)}, f32[16,16,128]{2,1,0:T(8,128)}, u32[]{:S(2)}) copy-start(f32[16,16,128]{2,1,0:T(8,128)} %param.46) | copy-start | bytes 393220
  52.8 6.5 %collective-permute-start.7 = (f32[12,16,128]{2,1,0:T(8,128)S(1)}, f32[12,16,128]{2,1,0:T(8,128)S(1)}, u32[]{:S(2)}, u32[]{:S(2)}) collective-permute-start(f32[12,16,128]{2,1,0:T(8,128)S(1)} %get-tuple-element.326), channel_id=1, source_target_pairs={{1,0},{2,1},{3,2},{4,3},{5,4},{6,5},{7,6},{8,7},{9,8},{10,9},{11,1... | collective-permute-start | bytes 294920 | tf_op jit(solution)/shard_map/ppermute | solution.py:26
  59.3 41.1 %collective-permute-start.2 = (f32[16,16,128]{2,1,0:T(8,128)}, f32[16,16,128]{2,1,0:T(8,128)}, u32[]{:S(2)}, u32[]{:S(2)}) collective-permute-start(f32[16,16,128]{2,1,0:T(8,128)} %param.43), channel_id=1, source_target_pairs={{0,1},{1,2},{2,3},{3,4},{4,5},{5,6},{6,7},{7,8},{8,9},{9,10},{10,1... | collective-permute-start | bytes 393224 | tf_op jit(solution)/shard_map/ppermute | solution.py:24
  61.9 15.2 %copy-start.84 = (f32[16,16,128]{2,1,0:T(8,128)}, f32[16,16,128]{2,1,0:T(8,128)S(1)}, u32[]{:S(2)}) copy-start(f32[16,16,128]{2,1,0:T(8,128)S(1)} %collective-permute-done.1) | copy-start | bytes 393220
  61.9 43.0 %collective-permute-start = (f32[16,16,128]{2,1,0:T(8,128)}, f32[16,16,128]{2,1,0:T(8,128)}, u32[]{:S(2)}, u32[]{:S(2)}) collective-permute-start(f32[16,16,128]{2,1,0:T(8,128)} %param.43), channel_id=1, source_target_pairs={{1,0},{2,1},{3,2},{4,3},{5,4},{6,5},{7,6},{8,7},{9,8},{10,9},{11,1... | collective-permute-start | bytes 393224 | tf_op jit(solution)/shard_map/ppermute | solution.py:26
  65.0 10.1 %collective-permute-start.12 = (f32[12,16,128]{2,1,0:T(8,128)S(1)}, f32[12,16,128]{2,1,0:T(8,128)S(1)}, u32[]{:S(2)}, u32[]{:S(2)}) collective-permute-start(f32[12,16,128]{2,1,0:T(8,128)S(1)} %get-tuple-element.325), channel_id=1, source_target_pairs={{1,0},{2,1},{3,2},{4,3},{5,4},{6,5},{7,6},{8,7},{9,8},{10,9},{11,1... | collective-permute-start | bytes 294920 | tf_op jit(solution)/shard_map/ppermute | solution.py:26
  67.6 26.3 %copy-start.42 = (f32[32,16,128]{2,1,0:T(8,128)}, f32[32,16,128]{2,1,0:T(8,128)S(1)}, u32[]{:S(2)}) copy-start(f32[32,16,128]{2,1,0:T(8,128)S(1)} %get-tuple-element.317) | copy-start | bytes 786436
  67.6 9.5 %collective-permute-start.11 = (f32[12,16,128]{2,1,0:T(8,128)S(1)}, f32[12,16,128]{2,1,0:T(8,128)S(1)}, u32[]{:S(2)}, u32[]{:S(2)}) collective-permute-start(f32[12,16,128]{2,1,0:T(8,128)S(1)} %get-tuple-element.324), channel_id=1, source_target_pairs={{0,1},{1,2},{2,3},{3,4},{4,5},{5,6},{6,7},{7,8},{8,9},{9,10},{10,1... | collective-permute-start | bytes 294920 | tf_op jit(solution)/shard_map/ppermute | solution.py:24
  69.6 24.3 %copy-start.44 = (f32[32,16,128]{2,1,0:T(8,128)}, f32[32,16,128]{2,1,0:T(8,128)S(1)}, u32[]{:S(2)}) copy-start(f32[32,16,128]{2,1,0:T(8,128)S(1)} %get-tuple-element.322) | copy-start | bytes 786436
  70.4 35.4 %collective-permute-start.5 = (f32[12,16,128]{2,1,0:T(8,128)}, f32[12,16,128]{2,1,0:T(8,128)}, u32[]{:S(2)}, u32[]{:S(2)}) collective-permute-start(f32[12,16,128]{2,1,0:T(8,128)} %get-tuple-element.316), channel_id=1, source_target_pairs={{1,0},{2,1},{3,2},{4,3},{5,4},{6,5},{7,6},{8,7},{9,8},{10,9},{11,1... | collective-permute-start | bytes 294920 | tf_op jit(solution)/shard_map/ppermute | solution.py:26
  75.1 30.7 %collective-permute-start.4 = (f32[12,16,128]{2,1,0:T(8,128)}, f32[12,16,128]{2,1,0:T(8,128)}, u32[]{:S(2)}, u32[]{:S(2)}) collective-permute-start(f32[12,16,128]{2,1,0:T(8,128)} %get-tuple-element.315), channel_id=1, source_target_pairs={{0,1},{1,2},{2,3},{3,4},{4,5},{5,6},{6,7},{7,8},{8,9},{9,10},{10,1... | collective-permute-start | bytes 294920 | tf_op jit(solution)/shard_map/ppermute | solution.py:24
  81.4 24.5 %copy-start.1 = (f32[40,16,128]{2,1,0:T(8,128)}, f32[40,16,128]{2,1,0:T(8,128)S(1)}, u32[]{:S(2)}) copy-start(f32[40,16,128]{2,1,0:T(8,128)S(1)} %get-tuple-element.273) | copy-start | bytes 983044
  133.6 20.8 %copy-start.85 = (f32[16,16,128]{2,1,0:T(8,128)S(1)}, f32[16,16,128]{2,1,0:T(8,128)}, u32[]{:S(2)}) copy-start(f32[16,16,128]{2,1,0:T(8,128)} %copy-done.84) | copy-start | bytes 393220
  134.9 21.1 %copy-start.92 = (f32[16,16,128]{2,1,0:T(8,128)S(1)}, f32[16,16,128]{2,1,0:T(8,128)}, u32[]{:S(2)}) copy-start(f32[16,16,128]{2,1,0:T(8,128)} %param.45) | copy-start | bytes 393220
  136.2 59.6 %collective-permute-start.10 = (f32[16,16,128]{2,1,0:T(8,128)S(1)}, f32[16,16,128]{2,1,0:T(8,128)S(1)}, u32[]{:S(2)}, u32[]{:S(2)}) collective-permute-start(f32[16,16,128]{2,1,0:T(8,128)S(1)} %scatter-add.59), channel_id=1, source_target_pairs={{1,0},{2,1},{3,2},{4,3},{5,4},{6,5},{7,6},{8,7},{9,8},{10,9},{11,1... | collective-permute-start | bytes 393224 | tf_op jit(solution)/shard_map/ppermute | solution.py:26
  139.9 59.6 %collective-permute-start.14 = (f32[16,16,128]{2,1,0:T(8,128)S(1)}, f32[16,16,128]{2,1,0:T(8,128)S(1)}, u32[]{:S(2)}, u32[]{:S(2)}) collective-permute-start(f32[16,16,128]{2,1,0:T(8,128)S(1)} %scatter-add.59), channel_id=1, source_target_pairs={{0,1},{1,2},{2,3},{3,4},{4,5},{5,6},{6,7},{7,8},{8,9},{9,10},{10,1... | collective-permute-start | bytes 393224 | tf_op jit(solution)/shard_map/ppermute | solution.py:24
  144.6 14.4 %collective-permute-start.15 = (f32[16,16,128]{2,1,0:T(8,128)S(1)}, f32[16,16,128]{2,1,0:T(8,128)S(1)}, u32[]{:S(2)}, u32[]{:S(2)}) collective-permute-start(f32[16,16,128]{2,1,0:T(8,128)S(1)} %scatter-add.65), channel_id=1, source_target_pairs={{1,0},{2,1},{3,2},{4,3},{5,4},{6,5},{7,6},{8,7},{9,8},{10,9},{11,1... | collective-permute-start | bytes 393224 | tf_op jit(solution)/shard_map/ppermute | solution.py:26
  148.2 15.3 %collective-permute-start.13 = (f32[16,16,128]{2,1,0:T(8,128)S(1)}, f32[16,16,128]{2,1,0:T(8,128)S(1)}, u32[]{:S(2)}, u32[]{:S(2)}) collective-permute-start(f32[16,16,128]{2,1,0:T(8,128)S(1)} %scatter-add.65), channel_id=1, source_target_pairs={{0,1},{1,2},{2,3},{3,4},{4,5},{5,6},{6,7},{7,8},{8,9},{9,10},{10,1... | collective-permute-start | bytes 393224 | tf_op jit(solution)/shard_map/ppermute | solution.py:24
  150.6 48.9 %collective-permute-start.17 = (f32[12,16,128]{2,1,0:T(8,128)}, f32[12,16,128]{2,1,0:T(8,128)}, u32[]{:S(2)}, u32[]{:S(2)}) collective-permute-start(f32[12,16,128]{2,1,0:T(8,128)} %get-tuple-element.300), channel_id=1, source_target_pairs={{1,0},{2,1},{3,2},{4,3},{5,4},{6,5},{7,6},{8,7},{9,8},{10,9},{11,1... | collective-permute-start | bytes 294920 | tf_op jit(solution)/shard_map/ppermute | solution.py:26
  155.6 14.8 %copy-start.2 = (f32[40,16,128]{2,1,0:T(8,128)S(1)}, f32[40,16,128]{2,1,0:T(8,128)}, u32[]{:S(2)}) copy-start(f32[40,16,128]{2,1,0:T(8,128)} %copy-done.1) | copy-start | bytes 983044
  155.7 14.7 %copy-start.5 = (f32[40,16,128]{2,1,0:T(8,128)S(1)}, f32[40,16,128]{2,1,0:T(8,128)}, u32[]{:S(2)}) copy-start(f32[40,16,128]{2,1,0:T(8,128)} %get-tuple-element.274) | copy-start | bytes 983044
  155.7 14.7 %copy-start.7 = (f32[40,16,128]{2,1,0:T(8,128)S(1)}, f32[40,16,128]{2,1,0:T(8,128)}, u32[]{:S(2)}) copy-start(f32[40,16,128]{2,1,0:T(8,128)} %get-tuple-element.275) | copy-start | bytes 983044
  155.7 14.7 %copy-start.9 = (f32[40,16,128]{2,1,0:T(8,128)S(1)}, f32[40,16,128]{2,1,0:T(8,128)}, u32[]{:S(2)}) copy-start(f32[40,16,128]{2,1,0:T(8,128)} %get-tuple-element.276) | copy-start | bytes 983044
  155.7 14.7 %copy-start.10 = (f32[40,16,128]{2,1,0:T(8,128)S(1)}, f32[40,16,128]{2,1,0:T(8,128)}, u32[]{:S(2)}) copy-start(f32[40,16,128]{2,1,0:T(8,128)} %get-tuple-element.277) | copy-start | bytes 983044
  155.7 14.7 %copy-start.11 = (f32[40,16,128]{2,1,0:T(8,128)S(1)}, f32[40,16,128]{2,1,0:T(8,128)}, u32[]{:S(2)}) copy-start(f32[40,16,128]{2,1,0:T(8,128)} %get-tuple-element.278) | copy-start | bytes 983044
  155.7 14.7 %copy-start.12 = (f32[40,16,128]{2,1,0:T(8,128)S(1)}, f32[40,16,128]{2,1,0:T(8,128)}, u32[]{:S(2)}) copy-start(f32[40,16,128]{2,1,0:T(8,128)} %get-tuple-element.279) | copy-start | bytes 983044
  155.7 14.7 %copy-start.13 = (f32[40,16,128]{2,1,0:T(8,128)S(1)}, f32[40,16,128]{2,1,0:T(8,128)}, u32[]{:S(2)}) copy-start(f32[40,16,128]{2,1,0:T(8,128)} %get-tuple-element.280) | copy-start | bytes 983044
  155.7 14.7 %copy-start.14 = (f32[40,16,128]{2,1,0:T(8,128)S(1)}, f32[40,16,128]{2,1,0:T(8,128)}, u32[]{:S(2)}) copy-start(f32[40,16,128]{2,1,0:T(8,128)} %get-tuple-element.281) | copy-start | bytes 983044
  155.7 14.7 %copy-start.15 = (f32[40,16,128]{2,1,0:T(8,128)S(1)}, f32[40,16,128]{2,1,0:T(8,128)}, u32[]{:S(2)}) copy-start(f32[40,16,128]{2,1,0:T(8,128)} %get-tuple-element.282) | copy-start | bytes 983044
  155.7 14.7 %copy-start.16 = (f32[40,16,128]{2,1,0:T(8,128)S(1)}, f32[40,16,128]{2,1,0:T(8,128)}, u32[]{:S(2)}) copy-start(f32[40,16,128]{2,1,0:T(8,128)} %get-tuple-element.283) | copy-start | bytes 983044
  155.8 14.7 %copy-start.17 = (f32[40,16,128]{2,1,0:T(8,128)S(1)}, f32[40,16,128]{2,1,0:T(8,128)}, u32[]{:S(2)}) copy-start(f32[40,16,128]{2,1,0:T(8,128)} %get-tuple-element.284) | copy-start | bytes 983044
  155.8 14.7 %copy-start.18 = (f32[40,16,128]{2,1,0:T(8,128)S(1)}, f32[40,16,128]{2,1,0:T(8,128)}, u32[]{:S(2)}) copy-start(f32[40,16,128]{2,1,0:T(8,128)} %get-tuple-element.285) | copy-start | bytes 983044
  155.8 14.7 %copy-start.19 = (f32[40,16,128]{2,1,0:T(8,128)S(1)}, f32[40,16,128]{2,1,0:T(8,128)}, u32[]{:S(2)}) copy-start(f32[40,16,128]{2,1,0:T(8,128)} %get-tuple-element.286) | copy-start | bytes 983044
  155.8 14.7 %copy-start.20 = (f32[40,16,128]{2,1,0:T(8,128)S(1)}, f32[40,16,128]{2,1,0:T(8,128)}, u32[]{:S(2)}) copy-start(f32[40,16,128]{2,1,0:T(8,128)} %get-tuple-element.287) | copy-start | bytes 983044
  155.8 14.7 %copy-start.21 = (f32[40,16,128]{2,1,0:T(8,128)S(1)}, f32[40,16,128]{2,1,0:T(8,128)}, u32[]{:S(2)}) copy-start(f32[40,16,128]{2,1,0:T(8,128)} %get-tuple-element.288) | copy-start | bytes 983044
  155.8 14.7 %copy-start.22 = (f32[40,16,128]{2,1,0:T(8,128)S(1)}, f32[40,16,128]{2,1,0:T(8,128)}, u32[]{:S(2)}) copy-start(f32[40,16,128]{2,1,0:T(8,128)} %get-tuple-element.289) | copy-start | bytes 983044
  155.8 14.7 %copy-start.23 = (f32[40,16,128]{2,1,0:T(8,128)S(1)}, f32[40,16,128]{2,1,0:T(8,128)}, u32[]{:S(2)}) copy-start(f32[40,16,128]{2,1,0:T(8,128)} %get-tuple-element.290) | copy-start | bytes 983044
  155.8 14.7 %copy-start.24 = (f32[40,16,128]{2,1,0:T(8,128)S(1)}, f32[40,16,128]{2,1,0:T(8,128)}, u32[]{:S(2)}) copy-start(f32[40,16,128]{2,1,0:T(8,128)} %get-tuple-element.291) | copy-start | bytes 983044
  155.8 14.7 %copy-start.25 = (f32[40,16,128]{2,1,0:T(8,128)S(1)}, f32[40,16,128]{2,1,0:T(8,128)}, u32[]{:S(2)}) copy-start(f32[40,16,128]{2,1,0:T(8,128)} %get-tuple-element.292) | copy-start | bytes 983044
  155.8 14.7 %copy-start.26 = (f32[40,16,128]{2,1,0:T(8,128)S(1)}, f32[40,16,128]{2,1,0:T(8,128)}, u32[]{:S(2)}) copy-start(f32[40,16,128]{2,1,0:T(8,128)} %get-tuple-element.293) | copy-start | bytes 983044
  155.9 14.7 %copy-start.27 = (f32[40,16,128]{2,1,0:T(8,128)S(1)}, f32[40,16,128]{2,1,0:T(8,128)}, u32[]{:S(2)}) copy-start(f32[40,16,128]{2,1,0:T(8,128)} %get-tuple-element.294) | copy-start | bytes 983044
  155.9 14.7 %copy-start.28 = (f32[40,16,128]{2,1,0:T(8,128)S(1)}, f32[40,16,128]{2,1,0:T(8,128)}, u32[]{:S(2)}) copy-start(f32[40,16,128]{2,1,0:T(8,128)} %get-tuple-element.295) | copy-start | bytes 983044
  155.9 14.7 %copy-start.29 = (f32[40,16,128]{2,1,0:T(8,128)S(1)}, f32[40,16,128]{2,1,0:T(8,128)}, u32[]{:S(2)}) copy-start(f32[40,16,128]{2,1,0:T(8,128)} %get-tuple-element.296) | copy-start | bytes 983044
  159.0 12.9 %copy-start.30 = (f32[33,16,16,128]{3,2,1,0:T(8,128)}, f32[33,16,16,128]{3,2,1,0:T(8,128)S(1)}, u32[]{:S(2)}) copy-start(f32[33,16,16,128]{3,2,1,0:T(8,128)S(1)} %constant_dynamic-update-slice_fusion.8) | copy-start | bytes 12976132
  159.0 6.7 %collective-permute-start.20 = (f32[12,16,128]{2,1,0:T(8,128)S(1)}, f32[12,16,128]{2,1,0:T(8,128)S(1)}, u32[]{:S(2)}, u32[]{:S(2)}) collective-permute-start(f32[12,16,128]{2,1,0:T(8,128)S(1)} %get-tuple-element.298), channel_id=1, source_target_pairs={{1,0},{2,1},{3,2},{4,3},{5,4},{6,5},{7,6},{8,7},{9,8},{10,9},{11,1... | collective-permute-start | bytes 294920 | tf_op jit(solution)/shard_map/ppermute | solution.py:26
  163.6 6.8 %collective-permute-start.19 = (f32[12,16,128]{2,1,0:T(8,128)S(1)}, f32[12,16,128]{2,1,0:T(8,128)S(1)}, u32[]{:S(2)}, u32[]{:S(2)}) collective-permute-start(f32[12,16,128]{2,1,0:T(8,128)S(1)} %get-tuple-element.297), channel_id=1, source_target_pairs={{0,1},{1,2},{2,3},{3,4},{4,5},{5,6},{6,7},{7,8},{8,9},{9,10},{10,1... | collective-permute-start | bytes 294920 | tf_op jit(solution)/shard_map/ppermute | solution.py:24
  165.7 12.5 %copy-start.31 = (f32[32,16,128]{2,1,0:T(8,128)S(1)}, f32[32,16,128]{2,1,0:T(8,128)}, u32[]{:S(2)}) copy-start(f32[32,16,128]{2,1,0:T(8,128)} %get-tuple-element.248) | copy-start | bytes 786436
  165.7 12.5 %copy-start.32 = (f32[32,16,128]{2,1,0:T(8,128)S(1)}, f32[32,16,128]{2,1,0:T(8,128)}, u32[]{:S(2)}) copy-start(f32[32,16,128]{2,1,0:T(8,128)} %get-tuple-element.249) | copy-start | bytes 786436
  165.7 12.5 %copy-start.33 = (f32[32,16,128]{2,1,0:T(8,128)S(1)}, f32[32,16,128]{2,1,0:T(8,128)}, u32[]{:S(2)}) copy-start(f32[32,16,128]{2,1,0:T(8,128)} %get-tuple-element.250) | copy-start | bytes 786436
  165.7 12.5 %copy-start.34 = (f32[32,16,128]{2,1,0:T(8,128)S(1)}, f32[32,16,128]{2,1,0:T(8,128)}, u32[]{:S(2)}) copy-start(f32[32,16,128]{2,1,0:T(8,128)} %get-tuple-element.251) | copy-start | bytes 786436
  165.8 12.5 %copy-start.35 = (f32[32,16,128]{2,1,0:T(8,128)S(1)}, f32[32,16,128]{2,1,0:T(8,128)}, u32[]{:S(2)}) copy-start(f32[32,16,128]{2,1,0:T(8,128)} %get-tuple-element.252) | copy-start | bytes 786436
  165.8 33.8 %collective-permute-start.16 = (f32[12,16,128]{2,1,0:T(8,128)}, f32[12,16,128]{2,1,0:T(8,128)}, u32[]{:S(2)}, u32[]{:S(2)}) collective-permute-start(f32[12,16,128]{2,1,0:T(8,128)} %get-tuple-element.299), channel_id=1, source_target_pairs={{0,1},{1,2},{2,3},{3,4},{4,5},{5,6},{6,7},{7,8},{8,9},{9,10},{10,1... | collective-permute-start | bytes 294920 | tf_op jit(solution)/shard_map/ppermute | solution.py:24
  193.9 38.7 %collective-permute-start.21 = (f32[16,16,128]{2,1,0:T(8,128)S(1)}, f32[16,16,128]{2,1,0:T(8,128)S(1)}, u32[]{:S(2)}, u32[]{:S(2)}) collective-permute-start(f32[16,16,128]{2,1,0:T(8,128)S(1)} %scatter-add.79), channel_id=1, source_target_pairs={{0,1},{1,2},{2,3},{3,4},{4,5},{5,6},{6,7},{7,8},{8,9},{9,10},{10,1... | collective-permute-start | bytes 393224 | tf_op jit(solution)/shard_map/ppermute | solution.py:24
  195.9 37.2 %collective-permute-start.23 = (f32[16,16,128]{2,1,0:T(8,128)S(1)}, f32[16,16,128]{2,1,0:T(8,128)S(1)}, u32[]{:S(2)}, u32[]{:S(2)}) collective-permute-start(f32[16,16,128]{2,1,0:T(8,128)S(1)} %scatter-add.79), channel_id=1, source_target_pairs={{1,0},{2,1},{3,2},{4,3},{5,4},{6,5},{7,6},{8,7},{9,8},{10,9},{11,1... | collective-permute-start | bytes 393224 | tf_op jit(solution)/shard_map/ppermute | solution.py:26
  227.0 5.6 %collective-permute-start.18 = (f32[16,16,128]{2,1,0:T(8,128)S(1)}, f32[16,16,128]{2,1,0:T(8,128)S(1)}, u32[]{:S(2)}, u32[]{:S(2)}) collective-permute-start(f32[16,16,128]{2,1,0:T(8,128)S(1)} %scatter-add.71), channel_id=1, source_target_pairs={{1,0},{2,1},{3,2},{4,3},{5,4},{6,5},{7,6},{8,7},{9,8},{10,9},{11,1... | collective-permute-start | bytes 393224 | tf_op jit(solution)/shard_map/ppermute | solution.py:26
  229.8 7.2 %collective-permute-start.22 = (f32[16,16,128]{2,1,0:T(8,128)S(1)}, f32[16,16,128]{2,1,0:T(8,128)S(1)}, u32[]{:S(2)}, u32[]{:S(2)}) collective-permute-start(f32[16,16,128]{2,1,0:T(8,128)S(1)} %scatter-add.71), channel_id=1, source_target_pairs={{0,1},{1,2},{2,3},{3,4},{4,5},{5,6},{6,7},{7,8},{8,9},{9,10},{10,1... | collective-permute-start | bytes 393224 | tf_op jit(solution)/shard_map/ppermute | solution.py:24
  (55 other events, 256.4 us)
where the time goes:
time: 245 us; the launch traced here: 241 us
  local copies, waits for them, and re-layouts  71.6 us (29%)
  other arithmetic  71.5 us (29%)
  starting transfers between devices  70.2 us (29%)
  blocking collectives  16.5 us (7%)
  waiting for transfers between devices  7.74 us (3%)
  between operations  2.78 us (1%)
    add x16, other arithmetic, advance(): 2.0 * centre_cells - prior_field + stiff_cells * laplace(current, buoyant)  52.4 us
    scatter-add x16, local copies, waits for them, and re-layouts, advance(): return updated.at[:, :, SURFACE].add(source_term)  45.7 us
    ppermute x12, starting transfers between devices, with_halo(): lax.ppermute(head, axis, [((i + 1) % count, i) for i in range(ends)])  43.8 us
    ppermute x12, starting transfers between devices, with_halo(): lax.ppermute(tail, axis, [(i, (i + 1) % count) for i in range(ends)])  26.4 us
    all_gather x1, blocking collectives, local(): all_traces = lax.all_gather(traces, 'gx', axis=1, tiled=True)  16.5 us
    another operation x24, local copies, waits for them, and re-layouts  14.6 us
    add x16, other arithmetic, advance(): return updated.at[:, :, SURFACE].add(source_term)  7.77 us
    ppermute x12, waiting for transfers between devices, with_halo(): lax.ppermute(tail, axis, [(i, (i + 1) % count) for i in range(ends)])  5.35 us
  transfers between devices with their start and end apart: 24, of which 4 were waited for; matrix products, arithmetic and copies ran while one was open for 46% of the time, Pallas kernels for 0%

commit v1 on v0

v1 whole, which is shorter than its diff:
```python
import functools

import jax
import jax.numpy as jnp
from jax import lax
from jax.experimental import pallas as pl
from jax.experimental.pallas import tpu as pltpu
from jax.sharding import PartitionSpec as P

STEPS = 8
IMG_EVERY = 4
NOFF = 33
SURFACE = 4
HALF = 16
REACH = 4
TRIM = HALF - REACH
PAD = 8

SCALE = 5040.0
WHOLE = (8064.0, -1008.0, 128.0, -9.0)
CENTRE = 6.0 * sum(WHOLE)

f32 = jnp.float32
bf16 = jnp.bfloat16


def vmem_specs(count):
    return [pl.BlockSpec(memory_space=pltpu.VMEM)] * count


def params(megabytes):
    return pltpu.CompilerParams(vmem_limit_bytes=megabytes * 1024 * 1024)


def shape(*dims):
    return jax.ShapeDtypeStruct(dims, f32)


def parity():
    return lax.rem(lax.axis_index("gx"), 2)


def split2(value):
    high = value.astype(bf16)
    low = (value - high.astype(f32)).astype(bf16)
    return high, low


def split3(value):
    high = value.astype(bf16)
    rest = value - high.astype(f32)
    mid = rest.astype(bf16)
    low = (rest - mid.astype(f32)).astype(bf16)
    return high, mid, low


def depth_matrix(nz):
    row = lax.broadcasted_iota(jnp.int32, (nz, nz), 0)
    col = lax.broadcasted_iota(jnp.int32, (nz, nz), 1)
    gap = jnp.abs(row - col)
    band = jnp.zeros((nz, nz), f32)
    for k, weight in enumerate(WHOLE):
        band = jnp.where(gap == k + 1, weight, band)
    band = band.astype(bf16)
    return jnp.concatenate([band, band], axis=0)


def weighted_sum(ref, r0, depth):
    ny = ref.shape[1] - 2 * PAD
    nz = ref.shape[2]
    tiles = ny // 8
    block = ref[pl.ds(r0, 8), PAD : PAD + ny, :].reshape(8 * ny, nz)
    high, low = split2(block)
    along = jnp.dot(jnp.concatenate([high, low], axis=1), depth, preferred_element_type=f32)
    out = {}
    for t in range(tiles):
        at = PAD + 8 * t
        column = [ref[r0 - REACH + m, at : at + 8, :] for m in range(8 + 2 * REACH)]
        for i in range(8):
            row = i * ny + 8 * t
            total = along[row : row + 8]
            for k in range(1, REACH + 1):
                four = (column[i + REACH + k] + column[i + REACH - k]) + (
                    ref[r0 + i, at + k : at + k + 8, :] + ref[r0 + i, at - k : at - k + 8, :]
                )
                total = total + WHOLE[k - 1] * four
            out[i, t] = total
    return out


def clear_pads(ref):
    zero = jnp.zeros((ref.shape[0], PAD, ref.shape[2]), f32)
    ref[:, 0:PAD, :] = zero
    ref[:, ref.shape[1] - PAD :, :] = zero


def pack_kernel(s0, sp, r0, rp, stiff, buoy, od1, od2, ev1, ev2):
    p = parity()
    n = s0.shape[0]
    for full, trimmed, first in ((od1, od2, p), (ev1, ev2, 1 - p)):
        cut = pl.ds(REACH * first, TRIM)
        full[0:n] = buoy[...]
        full[n : n + TRIM] = stiff[cut]
        full[n + TRIM : 2 * n + TRIM] = s0[...]
        full[2 * n + TRIM :] = sp[cut]
        trimmed[0:n] = r0[...]
        trimmed[n:] = rp[cut]


def planes_kernel(cells, traces, shots, fire, wavelet, ps, pr, lhs, acc):
    groups, width = cells.shape
    span, lateral, nz = ps.shape
    nt = traces.shape[1]
    ns = shots.shape[1]
    me = lax.axis_index("gx")
    first_cell = (me * HALF - TRIM) * lateral
    chunk = 8 * lateral
    spread = jnp.broadcast_to(fire[...], (ns, ns))
    same = lax.broadcasted_iota(jnp.int32, (ns, ns), 0) == lax.broadcasted_iota(jnp.int32, (ns, ns), 1)
    fire_col = jnp.sum(jnp.where(same, spread.astype(f32), 0.0), axis=1, keepdims=True)
    lane = lax.broadcasted_iota(jnp.int32, (ns, nz), 1).astype(f32)
    amounts = jnp.zeros((ns, nz), f32)
    for d in range(wavelet.shape[1]):
        amounts = amounts + jnp.where(lane == fire_col + float(d), wavelet[:, d : d + 1], 0.0)
    parts = split3(amounts)
    shot_row = shots[...] - first_cell
    for c in range(span // 8):
        spot = lax.broadcasted_iota(jnp.int32, (chunk, ns), 0) + c * chunk
        hot = jnp.where(spot == shot_row, 1.0, 0.0).astype(bf16)
        total = jnp.zeros((chunk, nz), f32)
        for part in parts:
            total = total + jnp.dot(hot, part, preferred_element_type=f32)
        ps[8 * c : 8 * c + 8] = total.reshape(8, lateral, nz)
    def stage(j, carry):
        for half in range(2):
            block = traces[2 * j + half]
            back = jnp.concatenate([block[nt - 1 - t : nt - t] for t in range(nt)], axis=0)
            for q, part in enumerate(split3(back)):
                lhs[j, q * nt : (q + 1) * nt, half * width : (half + 1) * width] = part.astype(f32)
        return carry

    lax.fori_loop(0, groups // 2, stage, 0)
    acc[...] = jnp.zeros(acc.shape, f32)

    def gather(j, carry):
        a = jnp.bitwise_xor(me, 2 * j)
        b = jnp.bitwise_xor(me, 2 * j + 1)
        row = jnp.concatenate([cells[pl.ds(a, 1), :], cells[pl.ds(b, 1), :]], axis=1) - first_cell
        amounts_j = lhs[j].astype(bf16)
        for c in range(span // 8):
            spot = lax.broadcasted_iota(jnp.int32, (chunk, 2 * width), 0) + c * chunk
            hot = jnp.where(spot == row, 1.0, 0.0).astype(bf16)
            acc[c * chunk : (c + 1) * chunk, 0 : 3 * nt] += lax.dot_general(
                hot, amounts_j, (((1,), (1,)), ((), ())), preferred_element_type=f32
            )
        return carry

    lax.fori_loop(0, groups // 2, gather, 0)
    for c in range(span // 8):
        part = acc[c * chunk : (c + 1) * chunk]
        part = part + pltpu.roll(part, nz - nt, axis=1) + pltpu.roll(part, nz - 2 * nt, axis=1)
        pr[8 * c : 8 * c + 8] = part.reshape(8, lateral, nz)


def load_field(dst, own, od, ev, lo, n, full, p):
    rows = own.shape[0]
    inner = slice(PAD, PAD + own.shape[1])
    dst[rows : 2 * rows, inner, :] = own[...]
    skip = 0 if full else REACH
    dst[pl.ds(2 * rows * p + skip * (1 - p), n), inner, :] = od[lo : lo + n]
    dst[pl.ds(2 * rows * (1 - p) + skip * p, n), inner, :] = ev[lo : lo + n]


def run_steps(field, product, coefs, planes, depth, base, ny):
    buoy, kb, kk, gg = coefs
    wide = field.shape[1]
    nz = field.shape[3]
    surface = lax.broadcasted_iota(jnp.int32, (8, nz), 1) == SURFACE
    for step in range(IMG_EVERY):
        now, new = step % 2, 1 - step % 2
        first = REACH * (step + 1)
        shift = (SURFACE - (base + step)) % nz

        def chunk(c, carry, now=now, new=new, first=first, shift=shift, step=step):
            r0 = first + 8 * c
            plain = weighted_sum(field.at[now], r0, depth)
            scaled = weighted_sum(product.at[now], r0, depth)
            for (i, t), value in plain.items():
                at = PAD + 8 * t
                tile = slice(8 * t, 8 * t + 8)
                r = r0 + i
                term = planes[r - REACH, tile, :]
                if shift:
                    term = pltpu.roll(term, shift, axis=1)
                term = jnp.where(surface, term, 0.0)
                fresh = (
                    (gg[r, tile, :] * field[now, r, at : at + 8, :] - field[new, r, at : at + 8, :])
                    + (kb[r, tile, :] * value + kk[r, tile, :] * scaled[i, t])
                    + term
                )
                field[new, r, at : at + 8, :] = fresh
                if step < IMG_EVERY - 1:
                    product[new, r, at : at + 8, :] = buoy[r, tile, :] * fresh
            return carry

        lax.fori_loop(0, (wide - 2 * first) // 8, chunk, 0)


def start_products(field, product, buoy, ny):
    inner = slice(PAD, PAD + ny)
    for which in range(2):
        clear_pads(field.at[which])
        clear_pads(product.at[which])
    product[0, :, inner, :] = buoy[...] * field[0, :, inner, :]


def first_kernel(own, prior, stiff, buoy_own, od, ev, planes, now_out, before_out, od_out, ev_out, buoy, kb, kk, gg, field, product, base):
    p = parity()
    n, ny, nz = own.shape
    inner = slice(PAD, PAD + ny)
    depth = depth_matrix(nz)
    pad_buoy = product.at[1]
    clear_pads(pad_buoy)
    load_field(pad_buoy, buoy_own, od, ev, 0, n, True, p)
    load_field(field.at[1], stiff, od, ev, n, TRIM, False, p)
    buoy[...] = pad_buoy[:, inner, :]

    def coefficients(c, carry):
        r0 = REACH + 8 * c
        total = weighted_sum(pad_buoy, r0, depth)
        for (i, t), value in total.items():
            tile = slice(8 * t, 8 * t + 8)
            r = r0 + i
            at = PAD + 8 * t
            b = pad_buoy[r, at : at + 8, :]
            k = field[1, r, at : at + 8, :] * (0.5 / SCALE)
            kk[r, tile, :] = k
            kb[r, tile, :] = k * b
            gg[r, tile, :] = 2.0 - k * (CENTRE * b + value)
        return carry

    lax.fori_loop(0, (3 * n - 2 * REACH) // 8, coefficients, 0)
    load_field(field.at[0], own, od, ev, n + TRIM, n, True, p)
    load_field(field.at[1], prior, od, ev, 2 * n + TRIM, TRIM, False, p)
    start_products(field, product, buoy, ny)
    run_steps(field, product, (buoy, kb, kk, gg), planes, depth, base, ny)
    finish(field, now_out, before_out, od_out, ev_out, p, n, inner)


def finish(field, now_out, before_out, od_out, ev_out, p, n, inner):
    last, earlier = IMG_EVERY % 2, 1 - IMG_EVERY % 2
    value = field[last, n : 2 * n, inner, :]
    now_out[...] = value
    before_out[...] = field[earlier, n : 2 * n, inner, :]
    od_out[0:n] = value
    ev_out[0:n] = value
    od_out[n:] = field[earlier, pl.ds(n + REACH * p, TRIM), inner, :]
    ev_out[n:] = field[earlier, pl.ds(n + REACH * (1 - p), TRIM), inner, :]


def block_kernel(own, prior, od, ev, planes, buoy, kb, kk, gg, now_out, before_out, od_out, ev_out, field, product, base):
    p = parity()
    n, ny, nz = own.shape
    inner = slice(PAD, PAD + ny)
    depth = depth_matrix(nz)
    load_field(field.at[0], own, od, ev, 0, n, True, p)
    load_field(field.at[1], prior, od, ev, n, TRIM, False, p)
    start_products(field, product, buoy, ny)
    run_steps(field, product, (buoy, kb, kk, gg), planes, depth, base, ny)
    finish(field, now_out, before_out, od_out, ev_out, p, n, inner)


def last_kernel(own, prior, od, ev, planes, buoy, kb, kk, gg, now_out, field, product, base):
    p = parity()
    n, ny, nz = own.shape
    inner = slice(PAD, PAD + ny)
    depth = depth_matrix(nz)
    load_field(field.at[0], own, od, ev, 0, n, True, p)
    load_field(field.at[1], prior, od, ev, n, TRIM, False, p)
    start_products(field, product, buoy, ny)
    run_steps(field, product, (buoy, kb, kk, gg), planes, depth, base, ny)
    now_out[...] = field[IMG_EVERY % 2, n : 2 * n, inner, :]


def image_kernel(s0, s4, s8, r0, r4, r8, od1, ev1, od2, ev2, ods, evs, odr, evr, ods8, evs8, odr8, evr8, out, lag_s, lag_r, block, sems):
    p = parity()
    n, ny, nz = s0.shape
    left, right = 2 * n * p, 2 * n * (1 - p)
    groups = (
        (lag_s, 0, s0, od1, ev1, n + TRIM),
        (lag_r, 0, r0, od2, ev2, 0),
        (lag_s, 1, s4, ods, evs, 0),
        (lag_r, 1, r4, odr, evr, 0),
        (lag_s, 2, s8, ods8, evs8, 0),
        (lag_r, 2, r8, odr8, evr8, 0),
    )
    for dst, level, own, od, ev, lo in groups:
        dst[level, n : 2 * n] = own[...]
        dst[level, pl.ds(left, n)] = od[lo : lo + n]
        dst[level, pl.ds(right, n)] = ev[lo : lo + n]

    def one(j, carry):
        lag = j - HALF
        for x in range(n):
            total = lag_s[0, HALF + x - lag] * lag_r[0, HALF + x + lag]
            for level in (1, 2):
                total = total + lag_s[level, HALF + x - lag] * lag_r[level, HALF + x + lag]
            block[j, x] = total
        pltpu.make_async_copy(block.at[j], out.at[j], sems.at[j]).start()
        return carry

    lax.fori_loop(0, NOFF, one, 0)

    def drain(j, carry):
        pltpu.make_async_copy(block.at[j], out.at[j], sems.at[j]).wait()
        return carry

    lax.fori_loop(0, NOFF, drain, 0)


def estimate(flops, nbytes):
    return pl.CostEstimate(flops=flops, bytes_accessed=nbytes, transcendentals=0)


def local(source_field, source_prior, receiver_field, receiver_prior, stiffness, buoyancy, wavelet, fire_step, shot_cell, receiver_cell, traces):
    n, ny, nz = source_field.shape
    count = lax.axis_size("gx")
    near = [(i, i ^ 1) for i in range(count)]
    far = [(i, i + 1) for i in range(1, count - 1, 2)] + [(i + 1, i) for i in range(1, count - 1, 2)]
    swap_near = lambda x: lax.ppermute(x, "gx", near)
    swap_far = lambda x: lax.ppermute(x, "gx", far)

    big, small = 2 * n + 2 * TRIM + 0, n + TRIM
    od1, od2, ev1, ev2 = pl.pallas_call(
        pack_kernel,
        out_shape=[shape(big, ny, nz), shape(small, ny, nz)] * 2,
        in_specs=vmem_specs(6),
        out_specs=vmem_specs(4),
        compiler_params=params(8),
        name="pack",
    )(source_field, source_prior, receiver_field, receiver_prior, stiffness, buoyancy)
    od1 = swap_far(od1)
    ev1 = swap_near(ev1)
    od2 = swap_far(od2)
    ev2 = swap_near(ev2)

    gathered = traces[None]
    hop = 1
    while hop < count:
        gathered = jnp.concatenate([gathered, lax.ppermute(gathered, "gx", [(i, i ^ hop) for i in range(count)])], axis=0)
        hop *= 2

    span = n + 2 * TRIM
    width = traces.shape[1]
    ns = shot_cell.shape[0]
    plane_s, plane_r = pl.pallas_call(
        planes_kernel,
        out_shape=[shape(span, ny, nz)] * 2,
        in_specs=vmem_specs(5),
        out_specs=vmem_specs(2),
        scratch_shapes=[
            pltpu.VMEM((count // 2, 3 * traces.shape[0], 2 * width), f32),
            pltpu.VMEM((span * ny, nz), f32),
        ],
        compiler_params=params(8),
        cost_estimate=estimate(2 * span * ny * 24 * 2048, 1000000),
        name="planes",
    )(receiver_cell.reshape(count, width), gathered, shot_cell.reshape(1, ns), fire_step.reshape(1, ns), wavelet)

    wide = 3 * n
    scratch = [pltpu.VMEM((2, wide, ny + 2 * PAD, nz), f32)] * 2
    cost = estimate(224 * 8 * 128 * 60, 6000000)
    own = shape(n, ny, nz)
    s4, s3, ods, evs, buoy, kb, kk, gg = pl.pallas_call(
        functools.partial(first_kernel, base=0),
        out_shape=[own, own, shape(small, ny, nz), shape(small, ny, nz)] + [shape(wide, ny, nz)] * 4,
        in_specs=vmem_specs(7),
        out_specs=vmem_specs(8),
        scratch_shapes=scratch,
        compiler_params=params(16),
        cost_estimate=cost,
        name="first_s",
    )(source_field, source_prior, stiffness, buoyancy, od1, ev1, plane_s)
    coefs = (buoy, kb, kk, gg)
    ods = swap_far(ods)
    evs = swap_near(evs)
    block = pl.pallas_call(
        functools.partial(block_kernel, base=0),
        out_shape=[own, own, shape(small, ny, nz), shape(small, ny, nz)],
        in_specs=vmem_specs(9),
        out_specs=vmem_specs(4),
        scratch_shapes=scratch,
        compiler_params=params(16),
        cost_estimate=cost,
        name="first_r",
    )
    r4, r3, odr, evr = block(receiver_field, receiver_prior, od2, ev2, plane_r, *coefs)
    odr = swap_far(odr)
    evr = swap_near(evr)

    def last(name):
        return pl.pallas_call(
            functools.partial(last_kernel, base=IMG_EVERY),
            out_shape=own,
            in_specs=vmem_specs(9),
            out_specs=pl.BlockSpec(memory_space=pltpu.VMEM),
            scratch_shapes=scratch,
            compiler_params=params(16),
            cost_estimate=cost,
            name=name,
        )

    s8 = last("last_s")(s4, s3, ods, evs, plane_s, *coefs)
    ods8 = swap_far(s8)
    evs8 = swap_near(s8)
    r8 = last("last_r")(r4, r3, odr, evr, plane_r, *coefs)
    odr8 = swap_far(r8)
    evr8 = swap_near(r8)
    return pl.pallas_call(
        image_kernel,
        out_shape=shape(NOFF, n, ny, nz),
        in_specs=vmem_specs(18),
        out_specs=pl.BlockSpec(memory_space=pl.ANY),
        scratch_shapes=[
            pltpu.VMEM((3, wide, ny, nz), f32),
            pltpu.VMEM((3, wide, ny, nz), f32),
            pltpu.VMEM((NOFF, n, ny, nz), f32),
            pltpu.SemaphoreType.DMA((NOFF,)),
        ],
        compiler_params=params(24),
        cost_estimate=estimate(NOFF * n * ny * nz * 5, 4400000),
        name="image",
    )(source_field, s4, s8, receiver_field, r4, r8, od1, ev1, od2, ev2, ods, evs, odr, evr, ods8, evs8, odr8, evr8)


def solution(mesh):
    placed = (
        P(("shot", "gx"), None, None),
        P(("shot", "gx"), None, None),
        P(("shot", "gx"), None, None),
        P(("shot", "gx"), None, None),
        P("gx", None, None),
        P("gx", None, None),
        P("shot", None),
        P("shot"),
        P("shot"),
        P("shot"),
        P("shot", "gx"),
    )
    return jax.shard_map(local, mesh=mesh, in_specs=placed, out_specs=P("shot", "gx", None, None), check_vma=False)
```

time: 245 us -> 84 us (0.34); the launches traced: 241 us -> 83.3 us
  other arithmetic: 71.5 us -> 2.07 us
  local copies, waits for them, and re-layouts: 71.6 us -> 14.3 us
  starting transfers between devices: 70.2 us -> 25.4 us
  Pallas kernels: 0 us -> 20.9 us
  blocking collectives: 16.5 us -> 0 us
  waiting for transfers between devices: 7.74 us -> 20.4 us
  between operations: 2.78 us -> 0.2 us
    add x33 -> x0, other arithmetic: 63.3 us -> none  [the longest x16 52.4 us: advance(): 2.0 * centre_cells - prior_field + stiff_cells * laplace(current, buoyant)]
    scatter-add x16 -> x0, local copies, waits for them, and re-layouts: 45.7 us -> none  [advance(): return updated.at[:, :, SURFACE].add(source_term)]
    ppermute x24 -> x16, starting transfers between devices: 70.2 us -> 25.4 us  [the longest x6 14.4 us: local(): swap_far = lambda x: lax.ppermute(x, 'gx', far)]
    pallas_call x0 -> x7, Pallas kernels: none -> 20.9 us  [the longest x1 4.59 us: local(): pl.pallas_call(functools.partial(first_kernel, base=0), out_shape=[own, o...]
    all_gather x1 -> x0, blocking collectives: 16.5 us -> none  [local(): all_traces = lax.all_gather(traces, 'gx', axis=1, tiled=True)]
    another operation x24 -> x0, local copies, waits for them, and re-layouts: 14.6 us -> none
    ppermute x24 -> x16, waiting for transfers between devices: 7.74 us -> 20.4 us  [the longest x4 14.6 us: local(): lax.ppermute(gathered, 'gx', [(i, i ^ hop) for i in range(count)])]
    unnamed x196 -> x39, local copies, waits for them, and re-layouts: 2.62 us -> 14.3 us
  transfers between devices with their start and end apart: 24 -> 16, of which waited for: 4 -> 4; matrix products, arithmetic and copies ran while one was open for 46% -> 4% of each run, Pallas kernels for 0% -> 22%
where the time goes in v1:
time: 84 us; the launch traced here: 83.3 us
  starting transfers between devices  25.4 us (30%)
  Pallas kernels  20.9 us (25%)
  waiting for transfers between devices  20.4 us (24%)
  local copies, waits for them, and re-layouts  14.3 us (17%)
  other arithmetic  2.07 us (2%)
    ppermute x4, waiting for transfers between devices, local(): lax.ppermute(gathered, 'gx', [(i, i ^ hop) for i in range(count)])  14.6 us
    ppermute x6, starting transfers between devices, local(): swap_far = lambda x: lax.ppermute(x, 'gx', far)  14.4 us
    unnamed x39, local copies, waits for them, and re-layouts  14.3 us
    ppermute x6, starting transfers between devices, local(): swap_near = lambda x: lax.ppermute(x, 'gx', near)  7.89 us
    ppermute x6, waiting for transfers between devices, local(): swap_far = lambda x: lax.ppermute(x, 'gx', far)  5.74 us
    pallas_call x1, Pallas kernels, local(): pl.pallas_call(functools.partial(first_kernel, base=0), out_shape=[own, o...  4.59 us
    pallas_call x1, Pallas kernels, local(): s8 = last('last_s')(s4, s3, ods, evs, plane_s, *coefs)  3.62 us
    pallas_call x1, Pallas kernels, local(): block(receiver_field, receiver_prior, od2, ev2, plane_r, *coefs)  3.62 us
  transfers between devices with their start and end apart: 16, of which 4 were waited for; matrix products, arithmetic and copies ran while one was open for 4% of the time, Pallas kernels for 22%

profile of v1, /device:TPU:14, one launch (start us, length us, event | category | flops | bytes accessed | tf_op | source)
XLA Modules:
  0.0 83.3 jit_solution(11137309660195612792)
XLA Ops:
  0.0 0.0 collective-permute-start.2
  0.0 0.0 copy-start
  0.0 0.9 %copy-done = f32[16,16,128]{2,1,0:T(8,128)S(1)} copy-done((f32[16,16,128]{2,1,0:T(8,128)S(1)}, f32[16,16,128]{2,1,0:T(8,128)}, u32[]{:S(2)}) %copy-start) | copy-done | bytes 131096
  0.9 0.9 %copy-done.3 = f32[16,16,128]{2,1,0:T(8,128)S(1)} copy-done((f32[16,16,128]{2,1,0:T(8,128)S(1)}, f32[16,16,128]{2,1,0:T(8,128)}, u32[]{:S(2)}) %copy-start.3) | copy-done | bytes 131096
  1.8 0.9 %copy-done.6 = f32[16,16,128]{2,1,0:T(8,128)S(1)} copy-done((f32[16,16,128]{2,1,0:T(8,128)S(1)}, f32[16,16,128]{2,1,0:T(8,128)}, u32[]{:S(2)}) %copy-start.6) | copy-done | bytes 131096
  2.7 0.9 %copy-done.8 = f32[16,16,128]{2,1,0:T(8,128)S(1)} copy-done((f32[16,16,128]{2,1,0:T(8,128)S(1)}, f32[16,16,128]{2,1,0:T(8,128)}, u32[]{:S(2)}) %copy-start.8) | copy-done | bytes 131096
  3.6 0.9 %copy-done.10 = f32[16,16,128]{2,1,0:T(8,128)S(1)} copy-done((f32[16,16,128]{2,1,0:T(8,128)S(1)}, f32[16,16,128]{2,1,0:T(8,128)}, u32[]{:S(2)}) %copy-start.10) | copy-done | bytes 131096
  4.5 0.9 %copy-done.12 = f32[16,16,128]{2,1,0:T(8,128)S(1)} copy-done((f32[16,16,128]{2,1,0:T(8,128)S(1)}, f32[16,16,128]{2,1,0:T(8,128)}, u32[]{:S(2)}) %copy-start.12) | copy-done | bytes 131096
  5.4 0.1 pack.1
  5.5 2.5 %collective-permute-start.8 = (f32[28,16,128]{2,1,0:T(8,128)S(1)}, f32[28,16,128]{2,1,0:T(8,128)S(1)}, u32[]{:S(2)}, u32[]{:S(2)}) collective-permute-start(f32[28,16,128]{2,1,0:T(8,128)S(1)} %get-tuple-element.34), channel_id=1, source_target_pairs={{1,2},{3,4},{5,6},{7,8},{9,10},{11,12},{13,14},{2,1},{4,3},{6,5},{... | collective-permute-start | bytes 688136 | tf_op jit(solution)/shard_map/ppermute | solution.py:331
  8.1 1.1 %collective-permute-start.9 = (f32[28,16,128]{2,1,0:T(8,128)S(1)}, f32[28,16,128]{2,1,0:T(8,128)S(1)}, u32[]{:S(2)}, u32[]{:S(2)}) collective-permute-start(f32[28,16,128]{2,1,0:T(8,128)S(1)} %get-tuple-element.35), channel_id=1, source_target_pairs={{0,1},{1,0},{2,3},{3,2},{4,5},{5,4},{6,7},{7,6},{8,9},{9,8},{10,11... | collective-permute-start | bytes 688136 | tf_op jit(solution)/shard_map/ppermute | solution.py:330
  9.1 2.4 %collective-permute-start = (f32[56,16,128]{2,1,0:T(8,128)S(1)}, f32[56,16,128]{2,1,0:T(8,128)S(1)}, u32[]{:S(2)}, u32[]{:S(2)}) collective-permute-start(f32[56,16,128]{2,1,0:T(8,128)S(1)} %get-tuple-element.23), channel_id=1, source_target_pairs={{1,2},{3,4},{5,6},{7,8},{9,10},{11,12},{13,14},{2,1},{4,3},{6,5},{... | collective-permute-start | bytes 1376264 | tf_op jit(solution)/shard_map/ppermute | solution.py:331
  11.5 1.2 %collective-permute-start.1 = (f32[56,16,128]{2,1,0:T(8,128)S(1)}, f32[56,16,128]{2,1,0:T(8,128)S(1)}, u32[]{:S(2)}, u32[]{:S(2)}) collective-permute-start(f32[56,16,128]{2,1,0:T(8,128)S(1)} %get-tuple-element.24), channel_id=1, source_target_pairs={{0,1},{1,0},{2,3},{3,2},{4,5},{5,4},{6,7},{7,6},{8,9},{9,8},{10,11... | collective-permute-start | bytes 1376264 | tf_op jit(solution)/shard_map/ppermute | solution.py:330
  12.7 0.7 constant_dynamic-update-slice_fusion.4
  13.4 0.8 copy.12.wavelet
  14.2 0.0 collective-permute-done.2
  14.2 0.7 pad_maximum_fusion.2
  14.9 0.5 collective-permute-start.3
  15.4 8.6 %collective-permute-done.3 = f32[2,8,128]{2,1,0:T(8,128)S(1)} collective-permute-done((f32[2,8,128]{2,1,0:T(8,128)S(1)}, f32[2,8,128]{2,1,0:T(8,128)S(1)}, u32[]{:S(2)}, u32[]{:S(2)}) %collective-permute-start.3) | collective-permute-done | bytes 8224 | tf_op jit(solution)/shard_map/ppermute | solution.py:350
  24.0 0.7 pad_maximum_fusion.1
  24.7 0.0 collective-permute-start.4
  24.7 3.7 %collective-permute-done.4 = f32[4,8,128]{2,1,0:T(8,128)S(1)} collective-permute-done((f32[4,8,128]{2,1,0:T(8,128)S(1)}, f32[4,8,128]{2,1,0:T(8,128)S(1)}, u32[]{:S(2)}, u32[]{:S(2)}) %collective-permute-start.4) | collective-permute-done | bytes 16416 | tf_op jit(solution)/shard_map/ppermute | solution.py:350
  28.5 0.7 pad_maximum_fusion
  29.2 2.6 %collective-permute-start.5 = (f32[8,8,128]{2,1,0:T(8,128)S(1)}, f32[8,8,128]{2,1,0:T(8,128)S(1)}, u32[]{:S(2)}, u32[]{:S(2)}) collective-permute-start(f32[8,8,128]{2,1,0:T(8,128)S(1)} %pad_maximum_fusion), channel_id=1, source_target_pairs={{0,8},{1,9},{2,10},{3,11},{4,12},{5,13},{6,14},{7,15},{8,0},{9,1},... | collective-permute-start | bytes 98312 | tf_op jit(solution)/shard_map/ppermute | solution.py:350
  31.8 2.2 %collective-permute-done.5 = f32[8,8,128]{2,1,0:T(8,128)S(1)} collective-permute-done((f32[8,8,128]{2,1,0:T(8,128)S(1)}, f32[8,8,128]{2,1,0:T(8,128)S(1)}, u32[]{:S(2)}, u32[]{:S(2)}) %collective-permute-start.5) | collective-permute-done | bytes 32800 | tf_op jit(solution)/shard_map/ppermute | solution.py:350
  34.0 0.7 copy-done.14
  34.7 0.7 copy-done.15
  35.3 0.7 copy-done.16
  36.0 2.6 %planes.1 = (f32[40,16,128]{2,1,0:T(8,128)S(1)}, f32[40,16,128]{2,1,0:T(8,128)S(1)}) custom-call(s32[16,128]{1,0:T(8,128)S(1)} %bitcast.5, f32[16,8,128]{2,1,0:T(8,128)S(1)} %constant_dynamic-update-slice_fusion.traces, s32[1,16]{1,0:T(1,128)S(1)} %bitcast.6, s32[1,16]{1,0:T(1,128)S(1)} %bitcast.7, f32[16,8]{1,0:T(8,128)S(1)} %copy.12.wavelet), custom_call_target="tpu_custom_call" | custom-call | flops 62914560 | bytes 1000000 | tf_op jit(solution)/shard_map/planes/pallas_call | solution.py:356
  38.6 0.0 collective-permute-done.od.od1
  38.6 0.0 collective-permute-done.1.ev.ev1
  38.6 0.0 copy-start.1
  38.6 0.9 %copy-done.1 = f32[16,16,128]{2,1,0:T(8,128)S(1)} copy-done((f32[16,16,128]{2,1,0:T(8,128)S(1)}, f32[16,16,128]{2,1,0:T(8,128)}, u32[]{:S(2)}) %copy-start.1) | copy-done | bytes 131096
  39.5 0.9 %copy-done.7 = f32[16,16,128]{2,1,0:T(8,128)S(1)} copy-done((f32[16,16,128]{2,1,0:T(8,128)S(1)}, f32[16,16,128]{2,1,0:T(8,128)}, u32[]{:S(2)}) %copy-start.7) | copy-done | bytes 131096
  40.4 0.9 %copy-done.9 = f32[16,16,128]{2,1,0:T(8,128)S(1)} copy-done((f32[16,16,128]{2,1,0:T(8,128)S(1)}, f32[16,16,128]{2,1,0:T(8,128)}, u32[]{:S(2)}) %copy-start.9) | copy-done | bytes 131096
  41.3 0.9 %copy-done.11 = f32[16,16,128]{2,1,0:T(8,128)S(1)} copy-done((f32[16,16,128]{2,1,0:T(8,128)S(1)}, f32[16,16,128]{2,1,0:T(8,128)}, u32[]{:S(2)}) %copy-start.11) | copy-done | bytes 131096
  42.2 4.6 %first_s.1 = (f32[16,16,128]{2,1,0:T(8,128)S(1)}, f32[16,16,128]{2,1,0:T(8,128)S(1)}, f32[28,16,128]{2,1,0:T(8,128)S(1)}, f32[28,16,128]{2,1,0:T(8,128)S(1)}, f3...) custom-call(f32[16,16,128]{2,1,0:T(8,128)S(1)} %copy-done.1, ...), custom_call_target="tpu_custom_call" | custom-call | flops 13762560 | bytes 6000000 | tf_op jit(solution)/shard_map/first_s/pallas_call | solution.py:374
  46.8 0.0 copy-start.2
  46.8 2.1 %collective-permute-start.6 = (f32[28,16,128]{2,1,0:T(8,128)S(1)}, f32[28,16,128]{2,1,0:T(8,128)S(1)}, u32[]{:S(2)}, u32[]{:S(2)}) collective-permute-start(f32[28,16,128]{2,1,0:T(8,128)S(1)} %get-tuple-element.28), channel_id=1, source_target_pairs={{1,2},{3,4},{5,6},{7,8},{9,10},{11,12},{13,14},{2,1},{4,3},{6,5},{... | collective-permute-start | bytes 688136 | tf_op jit(solution)/shard_map/ppermute | solution.py:331
  48.9 3.7 %collective-permute-start.7 = (f32[28,16,128]{2,1,0:T(8,128)S(1)}, f32[28,16,128]{2,1,0:T(8,128)S(1)}, u32[]{:S(2)}, u32[]{:S(2)}) collective-permute-start(f32[28,16,128]{2,1,0:T(8,128)S(1)} %get-tuple-element.29), channel_id=1, source_target_pairs={{0,1},{1,0},{2,3},{3,2},{4,5},{5,4},{6,7},{7,6},{8,9},{9,8},{10,11... | collective-permute-start | bytes 688136 | tf_op jit(solution)/shard_map/ppermute | solution.py:330
  52.5 0.0 collective-permute-done.8.od.od2
  52.5 0.0 collective-permute-done.9.ev.ev2
  52.6 0.9 %copy-done.4 = f32[16,16,128]{2,1,0:T(8,128)S(1)} copy-done((f32[16,16,128]{2,1,0:T(8,128)S(1)}, f32[16,16,128]{2,1,0:T(8,128)}, u32[]{:S(2)}) %copy-start.4) | copy-done | bytes 131096
  53.5 0.9 %copy-done.13 = f32[16,16,128]{2,1,0:T(8,128)S(1)} copy-done((f32[16,16,128]{2,1,0:T(8,128)S(1)}, f32[16,16,128]{2,1,0:T(8,128)}, u32[]{:S(2)}) %copy-start.13) | copy-done | bytes 131096
  54.4 3.6 %first_r.1 = (f32[16,16,128]{2,1,0:T(8,128)S(1)}, f32[16,16,128]{2,1,0:T(8,128)S(1)}, f32[28,16,128]{2,1,0:T(8,128)S(1)}, f32[28,16,128]{2,1,0:T(8,128)S(1)}) custom-call(f32[16,16,128]{2,1,0:T(8,128)S(1)} %copy-done.4, f32[16,16,128]{2,1,0:T(8,128)S(1)} %copy-done.13, f32[28,16,128]{2,1,0:T(8,128)S(1)} %collective-permute-done.8.od.od2, ...), custom_call_target="tpu_custom_call" | custom-call | flops 13762560 | bytes 6000000 | tf_op jit(solution)/shard_map/first_r/pallas_call | solution.py:397
  58.0 1.9 %collective-permute-start.10 = (f32[28,16,128]{2,1,0:T(8,128)S(1)}, f32[28,16,128]{2,1,0:T(8,128)S(1)}, u32[]{:S(2)}, u32[]{:S(2)}) collective-permute-start(f32[28,16,128]{2,1,0:T(8,128)S(1)} %get-tuple-element.39), channel_id=1, source_target_pairs={{1,2},{3,4},{5,6},{7,8},{9,10},{11,12},{13,14},{2,1},{4,3},{6,5},{... | collective-permute-start | bytes 688136 | tf_op jit(solution)/shard_map/ppermute | solution.py:331
  59.9 0.1 collective-permute-start.11
  60.0 0.0 collective-permute-done.6.od.ods
  60.0 0.0 collective-permute-done.7.ev.evs
  60.0 3.6 %last_s.1.s8 = f32[16,16,128]{2,1,0:T(8,128)S(1)} custom-call(f32[16,16,128]{2,1,0:T(8,128)S(1)} %get-tuple-element.26.own.s4, f32[16,16,128]{2,1,0:T(8,128)S(1)} %get-tuple-element.27.prior, f32[28,16,128]{2,1,0:T(8,128)S(1)} %collective-permute-done.6.od.ods, f32[28,16,128]{2,1,0:T(8,128)S(1)} %collective-permute-done.7.ev.evs, ...), custom_call_target="tpu_custom_call" | custom-call | flops 13762560 | bytes 6000000 | tf_op jit(solution)/shard_map/last_s/pallas_call | solution.py:413
  63.6 0.5 collective-permute-start.13
  64.2 3.6 %collective-permute-start.12 = (f32[16,16,128]{2,1,0:T(8,128)S(1)}, f32[16,16,128]{2,1,0:T(8,128)S(1)}, u32[]{:S(2)}, u32[]{:S(2)}) collective-permute-start(f32[16,16,128]{2,1,0:T(8,128)S(1)} %last_s.1.s8), channel_id=1, source_target_pairs={{1,2},{3,4},{5,6},{7,8},{9,10},{11,12},{13,14},{2,1},{4,3},{6,5},{... | collective-permute-start | bytes 393224 | tf_op jit(solution)/shard_map/ppermute | solution.py:331
  67.8 0.0 collective-permute-done.10.od.odr
  67.8 0.0 collective-permute-done.11.ev.evr
  67.8 3.6 %last_r.1.r8 = f32[16,16,128]{2,1,0:T(8,128)S(1)} custom-call(f32[16,16,128]{2,1,0:T(8,128)S(1)} %get-tuple-element.37.own.r4, f32[16,16,128]{2,1,0:T(8,128)S(1)} %get-tuple-element.38.prior, f32[28,16,128]{2,1,0:T(8,128)S(1)} %collective-permute-done.10.od.odr, f32[28,16,128]{2,1,0:T(8,128)S(1)} %collective-permute-done.11.ev.evr, ...), custom_call_target="tpu_custom_call" | custom-call | flops 13762560 | bytes 6000000 | tf_op jit(solution)/shard_map/last_r/pallas_call | solution.py:416
  71.4 1.3 %collective-permute-start.15 = (f32[16,16,128]{2,1,0:T(8,128)S(1)}, f32[16,16,128]{2,1,0:T(8,128)S(1)}, u32[]{:S(2)}, u32[]{:S(2)}) collective-permute-start(f32[16,16,128]{2,1,0:T(8,128)S(1)} %last_r.1.r8), channel_id=1, source_target_pairs={{0,1},{1,0},{2,3},{3,2},{4,5},{5,4},{6,7},{7,6},{8,9},{9,8},{10,11... | collective-permute-start | bytes 393224 | tf_op jit(solution)/shard_map/ppermute | solution.py:330
  72.8 1.9 %collective-permute-start.14 = (f32[16,16,128]{2,1,0:T(8,128)S(1)}, f32[16,16,128]{2,1,0:T(8,128)S(1)}, u32[]{:S(2)}, u32[]{:S(2)}) collective-permute-start(f32[16,16,128]{2,1,0:T(8,128)S(1)} %last_r.1.r8), channel_id=1, source_target_pairs={{1,2},{3,4},{5,6},{7,8},{9,10},{11,12},{13,14},{2,1},{4,3},{6,5},{... | collective-permute-start | bytes 393224 | tf_op jit(solution)/shard_map/ppermute | solution.py:331
  74.7 0.0 collective-permute-done.13.evs8
  74.7 0.0 collective-permute-done.12.ods8
  74.7 0.0 collective-permute-done.15.evr8
  74.7 5.7 %collective-permute-done.14.odr8 = f32[16,16,128]{2,1,0:T(8,128)S(1)} collective-permute-done((f32[16,16,128]{2,1,0:T(8,128)S(1)}, f32[16,16,128]{2,1,0:T(8,128)S(1)}, u32[]{:S(2)}, u32[]{:S(2)}) %collective-permute-start.14) | collective-permute-done | bytes 131104 | tf_op jit(solution)/shard_map/ppermute | solution.py:331
  80.4 0.0 copy-done.5
  80.5 0.0 copy-done.2
  80.5 2.8 %image.1 = f32[33,16,16,128]{3,2,1,0:T(8,128)} custom-call(f32[16,16,128]{2,1,0:T(8,128)S(1)} %copy-done.2, f32[16,16,128]{2,1,0:T(8,128)S(1)} %get-tuple-element.26.own.s4, f32[16,16,128]{2,1,0:T(8,128)S(1)} %last_s.1.s8, f32[16,16,128]{2,1,0:T(8,128)S(1)} %copy-done.5, f32[16,16,128]{2,1,0:T(8,128)S(1)} %get-tuple-element.37.own.r4, ...), custom_call_target="tpu_custom_call" | custom-call | flops 5406720 | bytes 4400000 | tf_op jit(solution)/shard_map/image/pallas_call | solution.py:419
  (18 shorter events, 0.0 us)
Async XLA Ops:
  0.0 14.2 %collective-permute-start.2 = (f32[1,8,128]{2,1,0:T(8,128)}, f32[1,8,128]{2,1,0:T(8,128)S(1)}, u32[]{:S(2)}, u32[]{:S(2)}) collective-permute-start(f32[1,8,128]{2,1,0:T(8,128)} %bitcast.8), channel_id=1, source_target_pairs={{0,1},{1,0},{2,3},{3,2},{4,5},{5,4},{6,7},{7,6},{8,9},{9,8},{10,11... | collective-permute-start | bytes 12296 | tf_op jit(solution)/shard_map/ppermute | solution.py:350
  0.0 0.9 %copy-start = (f32[16,16,128]{2,1,0:T(8,128)S(1)}, f32[16,16,128]{2,1,0:T(8,128)}, u32[]{:S(2)}) copy-start(f32[16,16,128]{2,1,0:T(8,128)} %s0.3) | copy-start | bytes 393220
  0.9 0.9 %copy-start.3 = (f32[16,16,128]{2,1,0:T(8,128)S(1)}, f32[16,16,128]{2,1,0:T(8,128)}, u32[]{:S(2)}) copy-start(f32[16,16,128]{2,1,0:T(8,128)} %r0.3) | copy-start | bytes 393220
  1.8 0.9 %copy-start.6 = (f32[16,16,128]{2,1,0:T(8,128)S(1)}, f32[16,16,128]{2,1,0:T(8,128)}, u32[]{:S(2)}) copy-start(f32[16,16,128]{2,1,0:T(8,128)} %prior.2) | copy-start | bytes 393220
  2.7 0.9 %copy-start.8 = (f32[16,16,128]{2,1,0:T(8,128)S(1)}, f32[16,16,128]{2,1,0:T(8,128)}, u32[]{:S(2)}) copy-start(f32[16,16,128]{2,1,0:T(8,128)} %stiff.3) | copy-start | bytes 393220
  3.6 0.9 %copy-start.10 = (f32[16,16,128]{2,1,0:T(8,128)S(1)}, f32[16,16,128]{2,1,0:T(8,128)}, u32[]{:S(2)}) copy-start(f32[16,16,128]{2,1,0:T(8,128)} %buoy_own.1) | copy-start | bytes 393220
  4.5 0.9 %copy-start.12 = (f32[16,16,128]{2,1,0:T(8,128)S(1)}, f32[16,16,128]{2,1,0:T(8,128)}, u32[]{:S(2)}) copy-start(f32[16,16,128]{2,1,0:T(8,128)} %prior.3) | copy-start | bytes 393220
  5.5 47.0 %collective-permute-start.8 = (f32[28,16,128]{2,1,0:T(8,128)S(1)}, f32[28,16,128]{2,1,0:T(8,128)S(1)}, u32[]{:S(2)}, u32[]{:S(2)}) collective-permute-start(f32[28,16,128]{2,1,0:T(8,128)S(1)} %get-tuple-element.34), channel_id=1, source_target_pairs={{1,2},{3,4},{5,6},{7,8},{9,10},{11,12},{13,14},{2,1},{4,3},{6,5},{... | collective-permute-start | bytes 688136 | tf_op jit(solution)/shard_map/ppermute | solution.py:331
  8.1 44.5 %collective-permute-start.9 = (f32[28,16,128]{2,1,0:T(8,128)S(1)}, f32[28,16,128]{2,1,0:T(8,128)S(1)}, u32[]{:S(2)}, u32[]{:S(2)}) collective-permute-start(f32[28,16,128]{2,1,0:T(8,128)S(1)} %get-tuple-element.35), channel_id=1, source_target_pairs={{0,1},{1,0},{2,3},{3,2},{4,5},{5,4},{6,7},{7,6},{8,9},{9,8},{10,11... | collective-permute-start | bytes 688136 | tf_op jit(solution)/shard_map/ppermute | solution.py:330
  9.1 29.4 %collective-permute-start = (f32[56,16,128]{2,1,0:T(8,128)S(1)}, f32[56,16,128]{2,1,0:T(8,128)S(1)}, u32[]{:S(2)}, u32[]{:S(2)}) collective-permute-start(f32[56,16,128]{2,1,0:T(8,128)S(1)} %get-tuple-element.23), channel_id=1, source_target_pairs={{1,2},{3,4},{5,6},{7,8},{9,10},{11,12},{13,14},{2,1},{4,3},{6,5},{... | collective-permute-start | bytes 1376264 | tf_op jit(solution)/shard_map/ppermute | solution.py:331
  11.5 27.0 %collective-permute-start.1 = (f32[56,16,128]{2,1,0:T(8,128)S(1)}, f32[56,16,128]{2,1,0:T(8,128)S(1)}, u32[]{:S(2)}, u32[]{:S(2)}) collective-permute-start(f32[56,16,128]{2,1,0:T(8,128)S(1)} %get-tuple-element.24), channel_id=1, source_target_pairs={{0,1},{1,0},{2,3},{3,2},{4,5},{5,4},{6,7},{7,6},{8,9},{9,8},{10,11... | collective-permute-start | bytes 1376264 | tf_op jit(solution)/shard_map/ppermute | solution.py:330
  14.9 9.2 %collective-permute-start.3 = (f32[2,8,128]{2,1,0:T(8,128)S(1)}, f32[2,8,128]{2,1,0:T(8,128)S(1)}, u32[]{:S(2)}, u32[]{:S(2)}) collective-permute-start(f32[2,8,128]{2,1,0:T(8,128)S(1)} %pad_maximum_fusion.2), channel_id=1, source_target_pairs={{0,2},{1,3},{2,0},{3,1},{4,6},{5,7},{6,4},{7,5},{8,10},{9,11},{10,... | collective-permute-start | bytes 24584 | tf_op jit(solution)/shard_map/ppermute | solution.py:350
  24.7 3.7 %collective-permute-start.4 = (f32[4,8,128]{2,1,0:T(8,128)S(1)}, f32[4,8,128]{2,1,0:T(8,128)S(1)}, u32[]{:S(2)}, u32[]{:S(2)}) collective-permute-start(f32[4,8,128]{2,1,0:T(8,128)S(1)} %pad_maximum_fusion.1), channel_id=1, source_target_pairs={{0,4},{1,5},{2,6},{3,7},{4,0},{5,1},{6,2},{7,3},{8,12},{9,13},{10,... | collective-permute-start | bytes 49160 | tf_op jit(solution)/shard_map/ppermute | solution.py:350
  29.2 4.8 %collective-permute-start.5 = (f32[8,8,128]{2,1,0:T(8,128)S(1)}, f32[8,8,128]{2,1,0:T(8,128)S(1)}, u32[]{:S(2)}, u32[]{:S(2)}) collective-permute-start(f32[8,8,128]{2,1,0:T(8,128)S(1)} %pad_maximum_fusion), channel_id=1, source_target_pairs={{0,8},{1,9},{2,10},{3,11},{4,12},{5,13},{6,14},{7,15},{8,0},{9,1},... | collective-permute-start | bytes 98312 | tf_op jit(solution)/shard_map/ppermute | solution.py:350
  34.0 0.7 copy-start.14
  34.7 0.7 copy-start.15
  35.3 0.7 copy-start.16
  38.6 0.9 %copy-start.1 = (f32[16,16,128]{2,1,0:T(8,128)S(1)}, f32[16,16,128]{2,1,0:T(8,128)}, u32[]{:S(2)}) copy-start(f32[16,16,128]{2,1,0:T(8,128)} %s0.3) | copy-start | bytes 393220
  39.5 0.9 %copy-start.7 = (f32[16,16,128]{2,1,0:T(8,128)S(1)}, f32[16,16,128]{2,1,0:T(8,128)}, u32[]{:S(2)}) copy-start(f32[16,16,128]{2,1,0:T(8,128)} %prior.2) | copy-start | bytes 393220
  40.4 0.9 %copy-start.9 = (f32[16,16,128]{2,1,0:T(8,128)S(1)}, f32[16,16,128]{2,1,0:T(8,128)}, u32[]{:S(2)}) copy-start(f32[16,16,128]{2,1,0:T(8,128)} %stiff.3) | copy-start | bytes 393220
  41.3 0.9 %copy-start.11 = (f32[16,16,128]{2,1,0:T(8,128)S(1)}, f32[16,16,128]{2,1,0:T(8,128)}, u32[]{:S(2)}) copy-start(f32[16,16,128]{2,1,0:T(8,128)} %buoy_own.1) | copy-start | bytes 393220
  42.2 38.2 %copy-start.5 = (f32[16,16,128]{2,1,0:T(8,128)S(1)}, f32[16,16,128]{2,1,0:T(8,128)}, u32[]{:S(2)}) copy-start(f32[16,16,128]{2,1,0:T(8,128)} %r0.3) | copy-start | bytes 393220
  46.8 33.6 %copy-start.2 = (f32[16,16,128]{2,1,0:T(8,128)S(1)}, f32[16,16,128]{2,1,0:T(8,128)}, u32[]{:S(2)}) copy-start(f32[16,16,128]{2,1,0:T(8,128)} %s0.3) | copy-start | bytes 393220
  46.8 13.2 %collective-permute-start.6 = (f32[28,16,128]{2,1,0:T(8,128)S(1)}, f32[28,16,128]{2,1,0:T(8,128)S(1)}, u32[]{:S(2)}, u32[]{:S(2)}) collective-permute-start(f32[28,16,128]{2,1,0:T(8,128)S(1)} %get-tuple-element.28), channel_id=1, source_target_pairs={{1,2},{3,4},{5,6},{7,8},{9,10},{11,12},{13,14},{2,1},{4,3},{6,5},{... | collective-permute-start | bytes 688136 | tf_op jit(solution)/shard_map/ppermute | solution.py:331
  48.9 11.1 %collective-permute-start.7 = (f32[28,16,128]{2,1,0:T(8,128)S(1)}, f32[28,16,128]{2,1,0:T(8,128)S(1)}, u32[]{:S(2)}, u32[]{:S(2)}) collective-permute-start(f32[28,16,128]{2,1,0:T(8,128)S(1)} %get-tuple-element.29), channel_id=1, source_target_pairs={{0,1},{1,0},{2,3},{3,2},{4,5},{5,4},{6,7},{7,6},{8,9},{9,8},{10,11... | collective-permute-start | bytes 688136 | tf_op jit(solution)/shard_map/ppermute | solution.py:330
  52.5 0.9 %copy-start.4 = (f32[16,16,128]{2,1,0:T(8,128)S(1)}, f32[16,16,128]{2,1,0:T(8,128)}, u32[]{:S(2)}) copy-start(f32[16,16,128]{2,1,0:T(8,128)} %r0.3) | copy-start | bytes 393220
  53.5 0.9 %copy-start.13 = (f32[16,16,128]{2,1,0:T(8,128)S(1)}, f32[16,16,128]{2,1,0:T(8,128)}, u32[]{:S(2)}) copy-start(f32[16,16,128]{2,1,0:T(8,128)} %prior.3) | copy-start | bytes 393220
  58.0 9.8 %collective-permute-start.10 = (f32[28,16,128]{2,1,0:T(8,128)S(1)}, f32[28,16,128]{2,1,0:T(8,128)S(1)}, u32[]{:S(2)}, u32[]{:S(2)}) collective-permute-start(f32[28,16,128]{2,1,0:T(8,128)S(1)} %get-tuple-element.39), channel_id=1, source_target_pairs={{1,2},{3,4},{5,6},{7,8},{9,10},{11,12},{13,14},{2,1},{4,3},{6,5},{... | collective-permute-start | bytes 688136 | tf_op jit(solution)/shard_map/ppermute | solution.py:331
  59.9 7.9 %collective-permute-start.11 = (f32[28,16,128]{2,1,0:T(8,128)S(1)}, f32[28,16,128]{2,1,0:T(8,128)S(1)}, u32[]{:S(2)}, u32[]{:S(2)}) collective-permute-start(f32[28,16,128]{2,1,0:T(8,128)S(1)} %get-tuple-element.40), channel_id=1, source_target_pairs={{0,1},{1,0},{2,3},{3,2},{4,5},{5,4},{6,7},{7,6},{8,9},{9,8},{10,11... | collective-permute-start | bytes 688136 | tf_op jit(solution)/shard_map/ppermute | solution.py:330
  63.6 11.0 %collective-permute-start.13 = (f32[16,16,128]{2,1,0:T(8,128)S(1)}, f32[16,16,128]{2,1,0:T(8,128)S(1)}, u32[]{:S(2)}, u32[]{:S(2)}) collective-permute-start(f32[16,16,128]{2,1,0:T(8,128)S(1)} %last_s.1.s8), channel_id=1, source_target_pairs={{0,1},{1,0},{2,3},{3,2},{4,5},{5,4},{6,7},{7,6},{8,9},{9,8},{10,11... | collective-permute-start | bytes 393224 | tf_op jit(solution)/shard_map/ppermute | solution.py:330
  64.2 10.5 %collective-permute-start.12 = (f32[16,16,128]{2,1,0:T(8,128)S(1)}, f32[16,16,128]{2,1,0:T(8,128)S(1)}, u32[]{:S(2)}, u32[]{:S(2)}) collective-permute-start(f32[16,16,128]{2,1,0:T(8,128)S(1)} %last_s.1.s8), channel_id=1, source_target_pairs={{1,2},{3,4},{5,6},{7,8},{9,10},{11,12},{13,14},{2,1},{4,3},{6,5},{... | collective-permute-start | bytes 393224 | tf_op jit(solution)/shard_map/ppermute | solution.py:331
  71.4 3.3 %collective-permute-start.15 = (f32[16,16,128]{2,1,0:T(8,128)S(1)}, f32[16,16,128]{2,1,0:T(8,128)S(1)}, u32[]{:S(2)}, u32[]{:S(2)}) collective-permute-start(f32[16,16,128]{2,1,0:T(8,128)S(1)} %last_r.1.r8), channel_id=1, source_target_pairs={{0,1},{1,0},{2,3},{3,2},{4,5},{5,4},{6,7},{7,6},{8,9},{9,8},{10,11... | collective-permute-start | bytes 393224 | tf_op jit(solution)/shard_map/ppermute | solution.py:330
  72.8 7.7 %collective-permute-start.14 = (f32[16,16,128]{2,1,0:T(8,128)S(1)}, f32[16,16,128]{2,1,0:T(8,128)S(1)}, u32[]{:S(2)}, u32[]{:S(2)}) collective-permute-start(f32[16,16,128]{2,1,0:T(8,128)S(1)} %last_r.1.r8), channel_id=1, source_target_pairs={{1,2},{3,4},{5,6},{7,8},{9,10},{11,12},{13,14},{2,1},{4,3},{6,5},{... | collective-permute-start | bytes 393224 | tf_op jit(solution)/shard_map/ppermute | solution.py:331

commit v2 on v1

v2 whole, which is shorter than its diff:
```python
import functools

import jax
import jax.numpy as jnp
from jax import lax
from jax.experimental import pallas as pl
from jax.experimental.pallas import tpu as pltpu
from jax.sharding import PartitionSpec as P


STEPS = 8
IMG_EVERY = 4
NOFF = 33
SURFACE = 4
HALF = 16
REACH = 4
TRIM = HALF - REACH
PAD = 8

SCALE = 5040.0
WHOLE = (8064.0, -1008.0, 128.0, -9.0)
CENTRE = 6.0 * sum(WHOLE)

f32 = jnp.float32
bf16 = jnp.bfloat16


def vmem_specs(count):
    return [pl.BlockSpec(memory_space=pltpu.VMEM)] * count


def params(megabytes):
    return pltpu.CompilerParams(vmem_limit_bytes=megabytes * 1024 * 1024)


def shape(*dims):
    return jax.ShapeDtypeStruct(dims, f32)


def place():
    me = lax.axis_index("gx")
    return lax.rem(me, 2), (me > 0) & (me < lax.axis_size("gx") - 1)


def split2(value):
    high = value.astype(bf16)
    low = (value - high.astype(f32)).astype(bf16)
    return high, low


def split3(value):
    high = value.astype(bf16)
    rest = value - high.astype(f32)
    mid = rest.astype(bf16)
    low = (rest - mid.astype(f32)).astype(bf16)
    return high, mid, low


def depth_matrix(nz):
    row = lax.broadcasted_iota(jnp.int32, (nz, nz), 0)
    col = lax.broadcasted_iota(jnp.int32, (nz, nz), 1)
    gap = jnp.abs(row - col)
    band = jnp.zeros((nz, nz), f32)
    for k, weight in enumerate(WHOLE):
        band = jnp.where(gap == k + 1, weight, band)
    band = band.astype(bf16)
    return jnp.concatenate([band, band], axis=0)


def along_depth(refs, r0, at, depth):
    nz = refs[0].shape[2]
    high, low = split2(jnp.concatenate([ref[pl.ds(r0, 8), pl.ds(at, 8), :].reshape(64, nz) for ref in refs], axis=0))
    return jnp.dot(jnp.concatenate([high, low], axis=1), depth, preferred_element_type=f32)


def across(ref, r0, at, i):
    total = None
    for k in range(1, REACH + 1):
        four = (ref[r0 + i + k, pl.ds(at, 8), :] + ref[r0 + i - k, pl.ds(at, 8), :]) + (
            ref[r0 + i, pl.ds(at + k, 8), :] + ref[r0 + i, pl.ds(at - k, 8), :]
        )
        total = WHOLE[k - 1] * four if total is None else total + WHOLE[k - 1] * four
    return total


def clear_pads(ref):
    zero = jnp.zeros((ref.shape[0], PAD, ref.shape[2]), f32)
    ref[:, 0:PAD, :] = zero
    ref[:, ref.shape[1] - PAD :, :] = zero


def pack_kernel(*refs):
    count = (len(refs) - 5) // 2
    args, copies, (od1, od2, ev1, ev2), sems = refs[:count], refs[count : 2 * count], refs[2 * count : -1], refs[-1]
    moves = [pltpu.make_async_copy(a, b, sems.at[i]) for i, (a, b) in enumerate(zip(args, copies))]
    for move in moves:
        move.start()
    for move in moves:
        move.wait()
    s0, sp, r0, rp, stiff, buoy = copies[:6]
    p, _ = place()
    n = s0.shape[0]
    for full, trimmed, first in ((od1, od2, p), (ev1, ev2, 1 - p)):
        cut = pl.ds(REACH * first, TRIM)
        full[0:n] = buoy[...]
        full[n : n + TRIM] = stiff[cut]
        full[n + TRIM : 2 * n + TRIM] = s0[...]
        full[2 * n + TRIM :] = sp[cut]
        trimmed[0:n] = r0[...]
        trimmed[n:] = rp[cut]


def first_plane_cell(lateral):
    return (lax.axis_index("gx") * HALF - TRIM) * lateral


def collect(acc, nt):
    nz = acc.shape[1]
    return acc + pltpu.roll(acc, nz - nt, axis=1) + pltpu.roll(acc, nz - 2 * nt, axis=1)


def hot_cells(base, row, rows):
    spot = lax.broadcasted_iota(jnp.int32, (rows, row.shape[1]), 0) + base
    return jnp.where(spot == row, 1.0, 0.0).astype(bf16)


def shots_kernel(shots, fire, wavelet, planes, acc):
    span, lateral, nz = planes.shape
    taps, ns = wavelet.shape
    delay = lax.broadcasted_iota(jnp.int32, (STEPS, ns), 0) - fire[...]
    amounts = jnp.zeros((STEPS, ns), f32)
    for d in range(taps):
        amounts = amounts + jnp.where(delay == d, wavelet[d : d + 1, :], 0.0)
    parts = jnp.concatenate([x.astype(f32) for x in split3(amounts)], axis=0).astype(bf16)
    row = shots[...] - first_plane_cell(lateral)
    chunk = 8 * lateral
    for c in range(span // 8):
        acc[:, 0 : 3 * STEPS] = lax.dot_general(
            hot_cells(c * chunk, row, chunk), parts, (((1,), (1,)), ((), ())), preferred_element_type=f32
        )
        planes[8 * c : 8 * c + 8] = collect(acc[...], STEPS).reshape(8, lateral, nz)


def receivers_kernel(cells, traces, planes, amounts, acc, hops):
    groups, width = cells.shape
    span, lateral, nz = planes.shape
    nt = traces.shape[1]
    me = lax.axis_index("gx")
    chunk = 8 * lateral

    def owner(q):
        other = me
        for bit, hop in enumerate(hops):
            other = jnp.bitwise_xor(other, hop * jnp.bitwise_and(lax.shift_right_logical(q, bit), 1))
        return other

    def stage(j, carry):
        for half in range(2):
            block = traces[2 * j + half]
            back = jnp.concatenate([block[nt - 1 - t : nt - t] for t in range(nt)], axis=0)
            for q, part in enumerate(split3(back)):
                amounts[j, q * nt : (q + 1) * nt, half * width : (half + 1) * width] = part.astype(f32)
        return carry

    lax.fori_loop(0, groups // 2, stage, 0)
    acc[...] = jnp.zeros(acc.shape, f32)

    def gather(j, carry):
        pair = [cells[pl.ds(owner(2 * j + half), 1), :] for half in range(2)]
        row = jnp.concatenate(pair, axis=1) - first_plane_cell(lateral)
        amounts_j = amounts[j].astype(bf16)
        for c in range(span // 8):
            acc[c * chunk : (c + 1) * chunk, 0 : 3 * nt] += lax.dot_general(
                hot_cells(c * chunk, row, chunk), amounts_j, (((1,), (1,)), ((), ())), preferred_element_type=f32
            )
        return carry

    lax.fori_loop(0, groups // 2, gather, 0)
    for c in range(span // 8):
        planes[8 * c : 8 * c + 8] = collect(acc[c * chunk : (c + 1) * chunk], nt).reshape(8, lateral, nz)


def load_field(dst, own, od, ev, lo, n, full):
    p, there = place()
    rows = own.shape[0]
    inner = slice(PAD, PAD + own.shape[1])
    dst[rows : 2 * rows, inner, :] = own[...]
    skip = 0 if full else REACH
    dst[pl.ds(2 * rows * p + skip * (1 - p), n), inner, :] = jnp.where(there, od[lo : lo + n], 0.0)
    dst[pl.ds(2 * rows * (1 - p) + skip * p, n), inner, :] = ev[lo : lo + n]


def run_steps(field, product, along, coefs, planes, depth, base):
    buoy, kb, kk, gg = coefs
    wide, tall, nz = field[0].shape
    tiles = (tall - 2 * PAD) // 8
    surface = lax.broadcasted_iota(jnp.int32, (8, nz), 1) == SURFACE
    for step in range(IMG_EVERY):
        old, new = field[step % 2], field[1 - step % 2]
        flux, flux_new = product[step % 2], product[1 - step % 2]
        first = REACH * (step + 1)
        shift = (SURFACE - (base + step)) % nz
        count = tiles * (wide - 2 * first) // 8

        def spot(q, first=first):
            y0 = pl.multiple_of(8 * lax.rem(q, tiles), 8)
            return first + 8 * lax.div(q, tiles), y0, pl.multiple_of(PAD + y0, 8)

        def chunk(q, carry, old=old, new=new, flux=flux, flux_new=flux_new, shift=shift, step=step, count=count, spot=spot):
            r0, y0, at = spot(q)
            slot = lax.rem(q, 2)
            later = spot(jnp.minimum(q + 1, count - 1))
            following = along_depth((old, flux), later[0], later[2], depth)
            tile = pl.ds(y0, 8)
            for i in range(8):
                r = r0 + i
                term = planes[r - REACH, tile, :]
                if shift:
                    term = pltpu.roll(term, shift, axis=1)
                part = gg[r, tile, :] * old[r, pl.ds(at, 8), :] - new[r, pl.ds(at, 8), :] + jnp.where(surface, term, 0.0)
                part = part + kb[r, tile, :] * (across(old, r0, at, i) + along[slot, 8 * i : 8 * i + 8, :])
                part = part + kk[r, tile, :] * (across(flux, r0, at, i) + along[slot, 64 + 8 * i : 72 + 8 * i, :])
                new[r, pl.ds(at, 8), :] = part
                if step < IMG_EVERY - 1:
                    flux_new[r, pl.ds(at, 8), :] = buoy[r, tile, :] * part
            along[1 - slot] = following
            return carry

        begin = spot(0)
        along[0] = along_depth((old, flux), begin[0], begin[2], depth)
        lax.fori_loop(0, count, chunk, 0)


def start_products(field, product, buoy):
    for ref in (*field, *product):
        clear_pads(ref)
    inner = slice(PAD, field[0].shape[1] - PAD)
    product[0][:, inner, :] = buoy[...] * field[0][:, inner, :]


def finish(field, n, now_out, before_out, od_out, ev_out):
    p, _ = place()
    last, earlier = field[IMG_EVERY % 2], field[1 - IMG_EVERY % 2]
    inner = slice(PAD, last.shape[1] - PAD)
    value = last[n : 2 * n, inner, :]
    now_out[...] = value
    before_out[...] = earlier[n : 2 * n, inner, :]
    od_out[0:n] = value
    ev_out[0:n] = value
    od_out[n:] = earlier[pl.ds(n + REACH * p, TRIM), inner, :]
    ev_out[n:] = earlier[pl.ds(n + REACH * (1 - p), TRIM), inner, :]


def first_kernel(own, prior, stiff, buoy_own, od, ev, planes, now_out, before_out, od_out, ev_out, buoy, kb, kk, gg, f0, f1, p0, p1, along):
    n, ny, nz = own.shape
    tiles = ny // 8
    inner = slice(PAD, PAD + ny)
    depth = depth_matrix(nz)
    clear_pads(p1)
    load_field(p1, buoy_own, od, ev, 0, n, True)
    load_field(f1, stiff, od, ev, n, TRIM, False)
    buoy[...] = p1[:, inner, :]

    def coefficients(q, carry):
        r0 = REACH + 8 * lax.div(q, tiles)
        y0 = pl.multiple_of(8 * lax.rem(q, tiles), 8)
        at = pl.multiple_of(PAD + y0, 8)
        tile = pl.ds(y0, 8)
        deep = along_depth((p1,), r0, at, depth)
        for i in range(8):
            r = r0 + i
            b = p1[r, pl.ds(at, 8), :]
            k = f1[r, pl.ds(at, 8), :] * (0.5 / SCALE)
            kk[r, tile, :] = k
            kb[r, tile, :] = k * b
            gg[r, tile, :] = 2.0 - k * (CENTRE * b + (across(p1, r0, at, i) + deep[8 * i : 8 * i + 8]))
        return carry

    lax.fori_loop(0, tiles * (3 * n - 2 * REACH) // 8, coefficients, 0)
    load_field(f0, own, od, ev, n + TRIM, n, True)
    load_field(f1, prior, od, ev, 2 * n + TRIM, TRIM, False)
    start_products((f0, f1), (p0, p1), buoy)
    run_steps((f0, f1), (p0, p1), along, (buoy, kb, kk, gg), planes, depth, 0)
    finish((f0, f1), n, now_out, before_out, od_out, ev_out)


def block_steps(own, prior, od, ev, planes, coefs, field, product, along, base):
    n, _, nz = own.shape
    depth = depth_matrix(nz)
    load_field(field[0], own, od, ev, 0, n, True)
    load_field(field[1], prior, od, ev, n, TRIM, False)
    start_products(field, product, coefs[0])
    run_steps(field, product, along, coefs, planes, depth, base)


def block_kernel(own, prior, od, ev, planes, buoy, kb, kk, gg, now_out, before_out, od_out, ev_out, f0, f1, p0, p1, along, base):
    block_steps(own, prior, od, ev, planes, (buoy, kb, kk, gg), (f0, f1), (p0, p1), along, base)
    finish((f0, f1), own.shape[0], now_out, before_out, od_out, ev_out)


def last_kernel(own, prior, od, ev, planes, buoy, kb, kk, gg, now_out, f0, f1, p0, p1, along, base):
    block_steps(own, prior, od, ev, planes, (buoy, kb, kk, gg), (f0, f1), (p0, p1), along, base)
    n, ny, _ = own.shape
    now_out[...] = (f0, f1)[IMG_EVERY % 2][n : 2 * n, PAD : PAD + ny, :]


def image_kernel(s0, s4, s8, r0, r4, r8, od1, ev1, od2, ev2, ods, evs, odr, evr, ods8, evs8, odr8, evr8, out, lag_s, lag_r, block, sems):
    p, there = place()
    n, _, _ = s0.shape
    left, right = 2 * n * p, 2 * n * (1 - p)
    groups = (
        (lag_s, 0, s0, od1, ev1, n + TRIM),
        (lag_r, 0, r0, od2, ev2, 0),
        (lag_s, 1, s4, ods, evs, 0),
        (lag_r, 1, r4, odr, evr, 0),
        (lag_s, 2, s8, ods8, evs8, 0),
        (lag_r, 2, r8, odr8, evr8, 0),
    )
    for dst, level, own, od, ev, lo in groups:
        dst[level, n : 2 * n] = own[...]
        dst[level, pl.ds(left, n)] = jnp.where(there, od[lo : lo + n], 0.0)
        dst[level, pl.ds(right, n)] = ev[lo : lo + n]

    def one(j, carry):
        lag = j - HALF
        for x in range(n):
            total = lag_s[0, HALF + x - lag] * lag_r[0, HALF + x + lag]
            for level in (1, 2):
                total = total + lag_s[level, HALF + x - lag] * lag_r[level, HALF + x + lag]
            block[j, x] = total
        pltpu.make_async_copy(block.at[j], out.at[j], sems.at[j]).start()
        return carry

    lax.fori_loop(0, NOFF, one, 0)

    def drain(j, carry):
        pltpu.make_async_copy(block.at[j], out.at[j], sems.at[j]).wait()
        return carry

    lax.fori_loop(0, NOFF, drain, 0)


def estimate(flops, nbytes):
    return pl.CostEstimate(flops=flops, bytes_accessed=nbytes, transcendentals=0)


def local(source_field, source_prior, receiver_field, receiver_prior, stiffness, buoyancy, wavelet, fire_step, shot_cell, receiver_cell, traces):
    n, ny, nz = source_field.shape
    shots, count = lax.axis_size("shot"), lax.axis_size("gx")
    near = [(i, i ^ 1) for i in range(count)]
    far = [(s * count + i, s * count + i + 1) for s in range(shots) for i in range(1, count - 1, 2)]
    far = far + [(b, a) for a, b in far]
    if shots % 2 == 0:
        far += [(s * count + e, (s ^ 1) * count + e) for s in range(shots) for e in (0, count - 1)]

    def swap_near(x):
        return lax.ppermute(x, "gx", near)

    def swap_far(x):
        return lax.ppermute(x, ("shot", "gx"), far)

    hops = []
    hop = 2
    while hop < count:
        hops.append(hop)
        hop *= 2
    hops.append(1)

    def exchange(x, which):
        return lax.ppermute(x, "gx", [(i, i ^ hops[which]) for i in range(count)])

    received = exchange(traces[None], 0)

    big, small = 2 * n + 2 * TRIM, n + TRIM
    width = traces.shape[1]
    ns = shot_cell.shape[0]
    args = (
        source_field,
        source_prior,
        receiver_field,
        receiver_prior,
        stiffness,
        buoyancy,
        traces[None],
        receiver_cell.reshape(count, width),
        shot_cell.reshape(1, ns),
        fire_step.reshape(1, ns),
        wavelet.T,
    )
    packed = pl.pallas_call(
        pack_kernel,
        out_shape=[jax.ShapeDtypeStruct(a.shape, a.dtype) for a in args] + [shape(big, ny, nz), shape(small, ny, nz)] * 2,
        in_specs=[pl.BlockSpec(memory_space=pltpu.MemorySpace.HBM)] * len(args),
        out_specs=vmem_specs(len(args) + 4),
        scratch_shapes=[pltpu.SemaphoreType.DMA((len(args),))],
        compiler_params=params(8),
        name="pack",
    )(*(pltpu.with_memory_space_constraint(a, pltpu.MemorySpace.HBM) for a in args))
    source_field, source_prior, receiver_field, receiver_prior, stiffness, buoyancy, gathered, cells, shot_row, fire_row, wave = packed[: len(args)]
    od1, od2, ev1, ev2 = packed[len(args) :]
    od1 = swap_far(od1)
    ev1 = swap_near(ev1)
    od2 = swap_far(od2)
    ev2 = swap_near(ev2)

    gathered = jnp.concatenate([gathered, received], axis=0)
    for which in range(1, len(hops)):
        gathered = jnp.concatenate([gathered, exchange(gathered, which)], axis=0)

    span = n + 2 * TRIM
    chunk = pltpu.VMEM((8 * ny, nz), f32)
    plane_s = pl.pallas_call(
        shots_kernel,
        out_shape=shape(span, ny, nz),
        in_specs=vmem_specs(3),
        out_specs=pl.BlockSpec(memory_space=pltpu.VMEM),
        scratch_shapes=[chunk],
        compiler_params=params(8),
        cost_estimate=estimate(1000000, 100000),
        name="shots",
    )(shot_row, fire_row, wave)
    plane_r = pl.pallas_call(
        functools.partial(receivers_kernel, hops=tuple(hops)),
        out_shape=shape(span, ny, nz),
        in_specs=vmem_specs(2),
        out_specs=pl.BlockSpec(memory_space=pltpu.VMEM),
        scratch_shapes=[pltpu.VMEM((count // 2, 3 * traces.shape[0], 2 * width), f32), pltpu.VMEM((span * ny, nz), f32)],
        compiler_params=params(8),
        cost_estimate=estimate(2 * span * ny * 24 * 2048, 1000000),
        name="receivers",
    )(cells, gathered)

    wide = 3 * n
    scratch = [pltpu.VMEM((wide, ny + 2 * PAD, nz), f32)] * 4 + [pltpu.VMEM((2, 128, nz), f32)]
    cost = estimate(224 * 8 * 128 * 60, 6000000)
    own = shape(n, ny, nz)
    s4, s3, ods, evs, buoy, kb, kk, gg = pl.pallas_call(
        first_kernel,
        out_shape=[own, own, shape(small, ny, nz), shape(small, ny, nz)] + [shape(wide, ny, nz)] * 4,
        in_specs=vmem_specs(7),
        out_specs=vmem_specs(8),
        scratch_shapes=scratch,
        compiler_params=params(16),
        cost_estimate=cost,
        name="first_s",
    )(source_field, source_prior, stiffness, buoyancy, od1, ev1, plane_s)
    coefs = (buoy, kb, kk, gg)
    ods = swap_far(ods)
    evs = swap_near(evs)
    r4, r3, odr, evr = pl.pallas_call(
        functools.partial(block_kernel, base=0),
        out_shape=[own, own, shape(small, ny, nz), shape(small, ny, nz)],
        in_specs=vmem_specs(9),
        out_specs=vmem_specs(4),
        scratch_shapes=scratch,
        compiler_params=params(16),
        cost_estimate=cost,
        name="first_r",
    )(receiver_field, receiver_prior, od2, ev2, plane_r, *coefs)
    odr = swap_far(odr)
    evr = swap_near(evr)

    def last():
        return pl.pallas_call(
            functools.partial(last_kernel, base=IMG_EVERY),
            out_shape=own,
            in_specs=vmem_specs(9),
            out_specs=pl.BlockSpec(memory_space=pltpu.VMEM),
            scratch_shapes=scratch,
            compiler_params=params(16),
            cost_estimate=cost,
        )

    s8 = last()(s4, s3, ods, evs, plane_s, *coefs)
    ods8 = swap_far(s8)
    evs8 = swap_near(s8)
    r8 = last()(r4, r3, odr, evr, plane_r, *coefs)
    odr8 = swap_far(r8)
    evr8 = swap_near(r8)
    return pl.pallas_call(
        image_kernel,
        out_shape=shape(NOFF, n, ny, nz),
        in_specs=vmem_specs(18),
        out_specs=pl.BlockSpec(memory_space=pl.ANY),
        scratch_shapes=[
            pltpu.VMEM((3, wide, ny, nz), f32),
            pltpu.VMEM((3, wide, ny, nz), f32),
            pltpu.VMEM((NOFF, n, ny, nz), f32),
            pltpu.SemaphoreType.DMA((NOFF,)),
        ],
        compiler_params=params(24),
        cost_estimate=estimate(NOFF * n * ny * nz * 5, 4400000),
        name="image",
    )(source_field, s4, s8, receiver_field, r4, r8, od1, ev1, od2, ev2, ods, evs, odr, evr, ods8, evs8, odr8, evr8)


def solution(mesh):
    placed = (
        P(("shot", "gx"), None, None),
        P(("shot", "gx"), None, None),
        P(("shot", "gx"), None, None),
        P(("shot", "gx"), None, None),
        P("gx", None, None),
        P("gx", None, None),
        P("shot", None),
        P("shot"),
        P("shot"),
        P("shot"),
        P("shot", "gx"),
    )
    return jax.shard_map(local, mesh=mesh, in_specs=placed, out_specs=P("shot", "gx", None, None), check_vma=False)
```

time: 84 us -> 59.5 us (0.71)
  local copies, waits for them, and re-layouts: 14.3 us -> 0.01 us
  starting transfers between devices: 25.4 us -> 15.2 us
  Pallas kernels: 20.9 us -> 30.2 us
  waiting for transfers between devices: 20.4 us -> 13.7 us
  other arithmetic: 2.07 us -> 0.01 us
    unnamed x39 -> x4, local copies, waits for them, and re-layouts: 14.3 us -> 0.01 us
    ppermute x16, starting transfers between devices: 25.4 us -> 15.2 us  [the longest x6 7.35 us: swap_near(): return lax.ppermute(x, 'gx', near)]
    pallas_call x6 -> x7, Pallas kernels: 18.1 us -> 27.3 us  [the longest x1 7.02 us: local(): pl.pallas_call(first_kernel, out_shape=[own, own, shape(small, ny, nz), s...]
    ppermute x16, waiting for transfers between devices: 20.4 us -> 13.7 us  [the longest x4 7.71 us: exchange(): return lax.ppermute(x, 'gx', [(i, i ^ hops[which]) for i in range(count)])]
    concatenate x3, other arithmetic: 2.07 us -> 0.01 us  [the longest x2 0.01 us: local(): gathered = jnp.concatenate([gathered, exchange(gathered, which)], axis=0)]
  transfers between devices with their start and end apart: 16 -> 16, of which waited for: 4 -> 6; matrix products, arithmetic and copies ran while one was open for 4% -> 0% of each run, Pallas kernels for 22% -> 46%
where the time goes in v2:
time: 59.5 us; the launch traced here: 59.2 us
  Pallas kernels  30.2 us (51%)
  starting transfers between devices  15.2 us (26%)
  waiting for transfers between devices  13.7 us (23%)
    ppermute x4, waiting for transfers between devices, exchange(): return lax.ppermute(x, 'gx', [(i, i ^ hops[which]) for i in range(count)])  7.71 us
    ppermute x6, starting transfers between devices, swap_near(): return lax.ppermute(x, 'gx', near)  7.35 us
    pallas_call x1, Pallas kernels, local(): pl.pallas_call(first_kernel, out_shape=[own, own, shape(small, ny, nz), s...  7.02 us
    pallas_call x1, Pallas kernels, local(): pl.pallas_call(functools.partial(block_kernel, base=0), out_shape=[own, o...  5.42 us
    pallas_call x1, Pallas kernels, local(): s8 = last()(s4, s3, ods, evs, plane_s, *coefs)  5.39 us
    pallas_call x1, Pallas kernels, local(): r8 = last()(r4, r3, odr, evr, plane_r, *coefs)  5.39 us
    ppermute x4, starting transfers between devices, exchange(): return lax.ppermute(x, 'gx', [(i, i ^ hops[which]) for i in range(count)])  5.1 us
    ppermute x6, waiting for transfers between devices, swap_far(): return lax.ppermute(x, ('shot', 'gx'), far)  5.01 us
  transfers between devices with their start and end apart: 16, of which 6 were waited for; matrix products, arithmetic and copies ran while one was open for 0% of the time, Pallas kernels for 46%

profile of v2, /device:TPU:14, one launch (start us, length us, event | category | flops | bytes accessed | tf_op | source)
XLA Modules:
  0.0 59.2 jit_solution(3011156546714967809)
XLA Ops:
  0.0 0.5 collective-permute-start.6
  0.5 1.4 %pack.1 = (f32[16,16,128]{2,1,0:T(8,128)S(1)}, f32[16,16,128]{2,1,0:T(8,128)S(1)}, f32[16,16,128]{2,1,0:T(8,128)S(1)}, f32[16,16,128]{2,1,0:T(8,128)S(1)}, f32[1...) custom-call(f32[16,16,128]{2,1,0:T(8,128)} %refs_0_.1, ...), custom_call_target="tpu_custom_call" | custom-call | tf_op jit(solution)/shard_map/pack/pallas_call | solution.py:390
  1.9 0.7 %collective-permute-start.4 = (f32[28,16,128]{2,1,0:T(8,128)S(1)}, f32[28,16,128]{2,1,0:T(8,128)S(1)}, u32[]{:S(2)}, u32[]{:S(2)}) collective-permute-start(f32[28,16,128]{2,1,0:T(8,128)S(1)} %get-tuple-element.51), channel_id=1, source_target_pairs={{1,2},{3,4},{5,6},{7,8},{9,10},{11,12},{13,14},{17,18},{19,20},{21... | collective-permute-start | bytes 688136 | tf_op jit(solution)/shard_map/ppermute | solution.py:360
  2.7 2.0 %collective-permute-start.5 = (f32[28,16,128]{2,1,0:T(8,128)S(1)}, f32[28,16,128]{2,1,0:T(8,128)S(1)}, u32[]{:S(2)}, u32[]{:S(2)}) collective-permute-start(f32[28,16,128]{2,1,0:T(8,128)S(1)} %get-tuple-element.52), channel_id=1, source_target_pairs={{0,1},{1,0},{2,3},{3,2},{4,5},{5,4},{6,7},{7,6},{8,9},{9,8},{10,11... | collective-permute-start | bytes 688136 | tf_op jit(solution)/shard_map/ppermute | solution.py:357
  4.6 0.0 collective-permute-start
  4.6 0.6 %collective-permute-start.1 = (f32[56,16,128]{2,1,0:T(8,128)S(1)}, f32[56,16,128]{2,1,0:T(8,128)S(1)}, u32[]{:S(2)}, u32[]{:S(2)}) collective-permute-start(f32[56,16,128]{2,1,0:T(8,128)S(1)} %get-tuple-element.37), channel_id=1, source_target_pairs={{0,1},{1,0},{2,3},{3,2},{4,5},{5,4},{6,7},{7,6},{8,9},{9,8},{10,11... | collective-permute-start | bytes 1376264 | tf_op jit(solution)/shard_map/ppermute | solution.py:357
  5.2 0.4 shots.1.planes
  5.7 0.0 collective-permute-done.6
  5.7 0.5 collective-permute-start.7
  6.2 3.3 %collective-permute-done.7 = f32[2,8,128]{2,1,0:T(8,128)S(1)} collective-permute-done((f32[2,8,128]{2,1,0:T(8,128)S(1)}, f32[2,8,128]{2,1,0:T(8,128)S(1)}, u32[]{:S(2)}, u32[]{:S(2)}) %collective-permute-start.7) | collective-permute-done | bytes 8224 | tf_op jit(solution)/shard_map/ppermute | solution.py:370
  9.5 1.1 %collective-permute-start.8 = (f32[4,8,128]{2,1,0:T(8,128)S(1)}, f32[4,8,128]{2,1,0:T(8,128)S(1)}, u32[]{:S(2)}, u32[]{:S(2)}) collective-permute-start(f32[4,8,128]{2,1,0:T(8,128)S(1)} %pad_maximum_fusion.1), channel_id=1, source_target_pairs={{0,8},{1,9},{2,10},{3,11},{4,12},{5,13},{6,14},{7,15},{8,0},{9,1},... | collective-permute-start | bytes 49160 | tf_op jit(solution)/shard_map/ppermute | solution.py:370
  10.5 3.6 %collective-permute-done.8 = f32[4,8,128]{2,1,0:T(8,128)S(1)} collective-permute-done((f32[4,8,128]{2,1,0:T(8,128)S(1)}, f32[4,8,128]{2,1,0:T(8,128)S(1)}, u32[]{:S(2)}, u32[]{:S(2)}) %collective-permute-start.8) | collective-permute-done | bytes 16416 | tf_op jit(solution)/shard_map/ppermute | solution.py:370
  14.1 3.0 %collective-permute-start.9 = (f32[8,8,128]{2,1,0:T(8,128)S(1)}, f32[8,8,128]{2,1,0:T(8,128)S(1)}, u32[]{:S(2)}, u32[]{:S(2)}) collective-permute-start(f32[8,8,128]{2,1,0:T(8,128)S(1)} %pad_maximum_fusion), channel_id=1, source_target_pairs={{0,1},{1,0},{2,3},{3,2},{4,5},{5,4},{6,7},{7,6},{8,9},{9,8},{10,11... | collective-permute-start | bytes 98312 | tf_op jit(solution)/shard_map/ppermute | solution.py:370
  17.1 0.9 %collective-permute-done.9 = f32[8,8,128]{2,1,0:T(8,128)S(1)} collective-permute-done((f32[8,8,128]{2,1,0:T(8,128)S(1)}, f32[8,8,128]{2,1,0:T(8,128)S(1)}, u32[]{:S(2)}, u32[]{:S(2)}) %collective-permute-start.9) | collective-permute-done | bytes 32800 | tf_op jit(solution)/shard_map/ppermute | solution.py:370
  18.0 2.3 %receivers.1.planes = f32[40,16,128]{2,1,0:T(8,128)S(1)} custom-call(s32[16,128]{1,0:T(8,128)S(1)} %get-tuple-element.53.cells, f32[16,8,128]{2,1,0:T(8,128)S(1)} %constant_dynamic-update-slice_fusion.traces), custom_call_target="tpu_custom_call" | custom-call | flops 62914560 | bytes 1000000 | tf_op jit(solution)/shard_map/receivers/pallas_call | solution.py:422
  20.3 0.0 collective-permute-done.od.od1
  20.3 0.0 collective-permute-done.1.ev.ev1
  20.4 7.0 %first_s.1 = (f32[16,16,128]{2,1,0:T(8,128)S(1)}, f32[16,16,128]{2,1,0:T(8,128)S(1)}, f32[28,16,128]{2,1,0:T(8,128)S(1)}, f32[28,16,128]{2,1,0:T(8,128)S(1)}, f3...) custom-call(f32[16,16,128]{2,1,0:T(8,128)S(1)} %get-tuple-element.32, ...), custom_call_target="tpu_custom_call" | custom-call | flops 13762560 | bytes 6000000 | tf_op jit(solution)/shard_map/first_s/pallas_call | solution.py:437
  27.4 0.2 collective-permute-start.2
  27.6 3.4 %collective-permute-start.3 = (f32[28,16,128]{2,1,0:T(8,128)S(1)}, f32[28,16,128]{2,1,0:T(8,128)S(1)}, u32[]{:S(2)}, u32[]{:S(2)}) collective-permute-start(f32[28,16,128]{2,1,0:T(8,128)S(1)} %get-tuple-element.44), channel_id=1, source_target_pairs={{0,1},{1,0},{2,3},{3,2},{4,5},{5,4},{6,7},{7,6},{8,9},{9,8},{10,11... | collective-permute-start | bytes 688136 | tf_op jit(solution)/shard_map/ppermute | solution.py:357
  31.0 0.0 collective-permute-done.4.od.od2
  31.0 0.0 collective-permute-done.5.ev.ev2
  31.0 5.4 %first_r.1 = (f32[16,16,128]{2,1,0:T(8,128)S(1)}, f32[16,16,128]{2,1,0:T(8,128)S(1)}, f32[28,16,128]{2,1,0:T(8,128)S(1)}, f32[28,16,128]{2,1,0:T(8,128)S(1)}) custom-call(f32[16,16,128]{2,1,0:T(8,128)S(1)} %get-tuple-element.49.own.r0, f32[16,16,128]{2,1,0:T(8,128)S(1)} %get-tuple-element.50.prior, f32[28,16,128]{2,1,0:T(8,128)S(1)} %collective-permute-done.4.od.od2, ...), custom_call_target="tpu_custom_call" | custom-call | flops 13762560 | bytes 6000000 | tf_op jit(solution)/shard_map/first_r/pallas_call | solution.py:450
  36.4 0.1 collective-permute-start.10
  36.5 0.2 collective-permute-start.11
  36.7 0.0 collective-permute-done.2.od.ods
  36.7 0.0 collective-permute-done.3.ev.evs
  36.7 5.4 %shard_map.109.s8 = f32[16,16,128]{2,1,0:T(8,128)S(1)} custom-call(f32[16,16,128]{2,1,0:T(8,128)S(1)} %get-tuple-element.41.own.s4, f32[16,16,128]{2,1,0:T(8,128)S(1)} %get-tuple-element.42.prior, f32[28,16,128]{2,1,0:T(8,128)S(1)} %collective-permute-done.2.od.ods, f32[28,16,128]{2,1,0:T(8,128)S(1)} %collective-permute-done.3.ev.evs, ...), custom_call_target="tpu_custom_call" | custom-call | flops 13762560 | bytes 6000000 | tf_op jit(solution)/shard_map/pallas_call | solution.py:474
  42.1 0.4 collective-permute-start.13
  42.5 1.7 %collective-permute-start.12 = (f32[16,16,128]{2,1,0:T(8,128)S(1)}, f32[16,16,128]{2,1,0:T(8,128)S(1)}, u32[]{:S(2)}, u32[]{:S(2)}) collective-permute-start(f32[16,16,128]{2,1,0:T(8,128)S(1)} %shard_map.109.s8), channel_id=1, source_target_pairs={{1,2},{3,4},{5,6},{7,8},{9,10},{11,12},{13,14},{17,18},{19,20},{21... | collective-permute-start | bytes 393224 | tf_op jit(solution)/shard_map/ppermute | solution.py:360
  44.2 0.2 collective-permute-done.10.od.odr
  44.4 0.0 collective-permute-done.11.ev.evr
  44.4 5.4 %shard_map.110.r8 = f32[16,16,128]{2,1,0:T(8,128)S(1)} custom-call(f32[16,16,128]{2,1,0:T(8,128)S(1)} %get-tuple-element.55.own.r4, f32[16,16,128]{2,1,0:T(8,128)S(1)} %get-tuple-element.56.prior, f32[28,16,128]{2,1,0:T(8,128)S(1)} %collective-permute-done.10.od.odr, f32[28,16,128]{2,1,0:T(8,128)S(1)} %collective-permute-done.11.ev.evr, ...), custom_call_target="tpu_custom_call" | custom-call | flops 13762560 | bytes 6000000 | tf_op jit(solution)/shard_map/pallas_call | solution.py:477
  49.7 0.8 %collective-permute-start.15 = (f32[16,16,128]{2,1,0:T(8,128)S(1)}, f32[16,16,128]{2,1,0:T(8,128)S(1)}, u32[]{:S(2)}, u32[]{:S(2)}) collective-permute-start(f32[16,16,128]{2,1,0:T(8,128)S(1)} %shard_map.110.r8), channel_id=1, source_target_pairs={{0,1},{1,0},{2,3},{3,2},{4,5},{5,4},{6,7},{7,6},{8,9},{9,8},{10,11... | collective-permute-start | bytes 393224 | tf_op jit(solution)/shard_map/ppermute | solution.py:357
  50.5 0.0 collective-permute-start.14
  50.5 0.0 collective-permute-done.13.evs8
  50.5 0.0 collective-permute-done.12.ods8
  50.5 1.0 %collective-permute-done.15.evr8 = f32[16,16,128]{2,1,0:T(8,128)S(1)} collective-permute-done((f32[16,16,128]{2,1,0:T(8,128)S(1)}, f32[16,16,128]{2,1,0:T(8,128)S(1)}, u32[]{:S(2)}, u32[]{:S(2)}) %collective-permute-start.15) | collective-permute-done | bytes 131104 | tf_op jit(solution)/shard_map/ppermute | solution.py:357
  51.5 4.8 %collective-permute-done.14.odr8 = f32[16,16,128]{2,1,0:T(8,128)S(1)} collective-permute-done((f32[16,16,128]{2,1,0:T(8,128)S(1)}, f32[16,16,128]{2,1,0:T(8,128)S(1)}, u32[]{:S(2)}, u32[]{:S(2)}) %collective-permute-start.14) | collective-permute-done | bytes 131104 | tf_op jit(solution)/shard_map/ppermute | solution.py:360
  56.3 2.9 %image.1 = f32[33,16,16,128]{3,2,1,0:T(8,128)} custom-call(f32[16,16,128]{2,1,0:T(8,128)S(1)} %get-tuple-element.32.own.s0, f32[16,16,128]{2,1,0:T(8,128)S(1)} %get-tuple-element.41.own.s4, f32[16,16,128]{2,1,0:T(8,128)S(1)} %shard_map.109.s8, f32[16,16,128]{2,1,0:T(8,128)S(1)} %get-tuple-element.49.own.r0, f32[16,16,128]{2,1,0:T(8,128)S(1)} %get-tuple-element.55.own.r4, ...), custom_call_target="tpu_custom_call" | custom-call | flops 5406720 | bytes 4400000 | tf_op jit(solution)/shard_map/image/pallas_call | solution.py:480
  (8 shorter events, 0.0 us)
Async XLA Ops:
  0.0 5.7 %collective-permute-start.6 = (f32[1,8,128]{2,1,0:T(8,128)}, f32[1,8,128]{2,1,0:T(8,128)S(1)}, u32[]{:S(2)}, u32[]{:S(2)}) collective-permute-start(f32[1,8,128]{2,1,0:T(8,128)} %bitcast.7), channel_id=1, source_target_pairs={{0,2},{1,3},{2,0},{3,1},{4,6},{5,7},{6,4},{7,5},{8,10},{9,11},{10,... | collective-permute-start | bytes 12296 | tf_op jit(solution)/shard_map/ppermute | solution.py:370
  1.9 29.0 %collective-permute-start.4 = (f32[28,16,128]{2,1,0:T(8,128)S(1)}, f32[28,16,128]{2,1,0:T(8,128)S(1)}, u32[]{:S(2)}, u32[]{:S(2)}) collective-permute-start(f32[28,16,128]{2,1,0:T(8,128)S(1)} %get-tuple-element.51), channel_id=1, source_target_pairs={{1,2},{3,4},{5,6},{7,8},{9,10},{11,12},{13,14},{17,18},{19,20},{21... | collective-permute-start | bytes 688136 | tf_op jit(solution)/shard_map/ppermute | solution.py:360
  2.7 28.3 %collective-permute-start.5 = (f32[28,16,128]{2,1,0:T(8,128)S(1)}, f32[28,16,128]{2,1,0:T(8,128)S(1)}, u32[]{:S(2)}, u32[]{:S(2)}) collective-permute-start(f32[28,16,128]{2,1,0:T(8,128)S(1)} %get-tuple-element.52), channel_id=1, source_target_pairs={{0,1},{1,0},{2,3},{3,2},{4,5},{5,4},{6,7},{7,6},{8,9},{9,8},{10,11... | collective-permute-start | bytes 688136 | tf_op jit(solution)/shard_map/ppermute | solution.py:357
  4.6 15.7 %collective-permute-start = (f32[56,16,128]{2,1,0:T(8,128)S(1)}, f32[56,16,128]{2,1,0:T(8,128)S(1)}, u32[]{:S(2)}, u32[]{:S(2)}) collective-permute-start(f32[56,16,128]{2,1,0:T(8,128)S(1)} %get-tuple-element.36), channel_id=1, source_target_pairs={{1,2},{3,4},{5,6},{7,8},{9,10},{11,12},{13,14},{17,18},{19,20},{21... | collective-permute-start | bytes 1376264 | tf_op jit(solution)/shard_map/ppermute | solution.py:360
  4.6 15.7 %collective-permute-start.1 = (f32[56,16,128]{2,1,0:T(8,128)S(1)}, f32[56,16,128]{2,1,0:T(8,128)S(1)}, u32[]{:S(2)}, u32[]{:S(2)}) collective-permute-start(f32[56,16,128]{2,1,0:T(8,128)S(1)} %get-tuple-element.37), channel_id=1, source_target_pairs={{0,1},{1,0},{2,3},{3,2},{4,5},{5,4},{6,7},{7,6},{8,9},{9,8},{10,11... | collective-permute-start | bytes 1376264 | tf_op jit(solution)/shard_map/ppermute | solution.py:357
  5.7 3.8 %collective-permute-start.7 = (f32[2,8,128]{2,1,0:T(8,128)S(1)}, f32[2,8,128]{2,1,0:T(8,128)S(1)}, u32[]{:S(2)}, u32[]{:S(2)}) collective-permute-start(f32[2,8,128]{2,1,0:T(8,128)S(1)} %pad_maximum_fusion.2), channel_id=1, source_target_pairs={{0,4},{1,5},{2,6},{3,7},{4,0},{5,1},{6,2},{7,3},{8,12},{9,13},{10,... | collective-permute-start | bytes 24584 | tf_op jit(solution)/shard_map/ppermute | solution.py:370
  9.5 4.6 %collective-permute-start.8 = (f32[4,8,128]{2,1,0:T(8,128)S(1)}, f32[4,8,128]{2,1,0:T(8,128)S(1)}, u32[]{:S(2)}, u32[]{:S(2)}) collective-permute-start(f32[4,8,128]{2,1,0:T(8,128)S(1)} %pad_maximum_fusion.1), channel_id=1, source_target_pairs={{0,8},{1,9},{2,10},{3,11},{4,12},{5,13},{6,14},{7,15},{8,0},{9,1},... | collective-permute-start | bytes 49160 | tf_op jit(solution)/shard_map/ppermute | solution.py:370
  14.1 3.9 %collective-permute-start.9 = (f32[8,8,128]{2,1,0:T(8,128)S(1)}, f32[8,8,128]{2,1,0:T(8,128)S(1)}, u32[]{:S(2)}, u32[]{:S(2)}) collective-permute-start(f32[8,8,128]{2,1,0:T(8,128)S(1)} %pad_maximum_fusion), channel_id=1, source_target_pairs={{0,1},{1,0},{2,3},{3,2},{4,5},{5,4},{6,7},{7,6},{8,9},{9,8},{10,11... | collective-permute-start | bytes 98312 | tf_op jit(solution)/shard_map/ppermute | solution.py:370
  27.4 9.3 %collective-permute-start.2 = (f32[28,16,128]{2,1,0:T(8,128)S(1)}, f32[28,16,128]{2,1,0:T(8,128)S(1)}, u32[]{:S(2)}, u32[]{:S(2)}) collective-permute-start(f32[28,16,128]{2,1,0:T(8,128)S(1)} %get-tuple-element.43), channel_id=1, source_target_pairs={{1,2},{3,4},{5,6},{7,8},{9,10},{11,12},{13,14},{17,18},{19,20},{21... | collective-permute-start | bytes 688136 | tf_op jit(solution)/shard_map/ppermute | solution.py:360
  27.6 9.1 %collective-permute-start.3 = (f32[28,16,128]{2,1,0:T(8,128)S(1)}, f32[28,16,128]{2,1,0:T(8,128)S(1)}, u32[]{:S(2)}, u32[]{:S(2)}) collective-permute-start(f32[28,16,128]{2,1,0:T(8,128)S(1)} %get-tuple-element.44), channel_id=1, source_target_pairs={{0,1},{1,0},{2,3},{3,2},{4,5},{5,4},{6,7},{7,6},{8,9},{9,8},{10,11... | collective-permute-start | bytes 688136 | tf_op jit(solution)/shard_map/ppermute | solution.py:357
  36.4 8.0 %collective-permute-start.10 = (f32[28,16,128]{2,1,0:T(8,128)S(1)}, f32[28,16,128]{2,1,0:T(8,128)S(1)}, u32[]{:S(2)}, u32[]{:S(2)}) collective-permute-start(f32[28,16,128]{2,1,0:T(8,128)S(1)} %get-tuple-element.57), channel_id=1, source_target_pairs={{1,2},{3,4},{5,6},{7,8},{9,10},{11,12},{13,14},{17,18},{19,20},{21... | collective-permute-start | bytes 688136 | tf_op jit(solution)/shard_map/ppermute | solution.py:360
  36.5 7.9 %collective-permute-start.11 = (f32[28,16,128]{2,1,0:T(8,128)S(1)}, f32[28,16,128]{2,1,0:T(8,128)S(1)}, u32[]{:S(2)}, u32[]{:S(2)}) collective-permute-start(f32[28,16,128]{2,1,0:T(8,128)S(1)} %get-tuple-element.58), channel_id=1, source_target_pairs={{0,1},{1,0},{2,3},{3,2},{4,5},{5,4},{6,7},{7,6},{8,9},{9,8},{10,11... | collective-permute-start | bytes 688136 | tf_op jit(solution)/shard_map/ppermute | solution.py:357
  42.1 8.4 %collective-permute-start.13 = (f32[16,16,128]{2,1,0:T(8,128)S(1)}, f32[16,16,128]{2,1,0:T(8,128)S(1)}, u32[]{:S(2)}, u32[]{:S(2)}) collective-permute-start(f32[16,16,128]{2,1,0:T(8,128)S(1)} %shard_map.109.s8), channel_id=1, source_target_pairs={{0,1},{1,0},{2,3},{3,2},{4,5},{5,4},{6,7},{7,6},{8,9},{9,8},{10,11... | collective-permute-start | bytes 393224 | tf_op jit(solution)/shard_map/ppermute | solution.py:357
  42.5 8.0 %collective-permute-start.12 = (f32[16,16,128]{2,1,0:T(8,128)S(1)}, f32[16,16,128]{2,1,0:T(8,128)S(1)}, u32[]{:S(2)}, u32[]{:S(2)}) collective-permute-start(f32[16,16,128]{2,1,0:T(8,128)S(1)} %shard_map.109.s8), channel_id=1, source_target_pairs={{1,2},{3,4},{5,6},{7,8},{9,10},{11,12},{13,14},{17,18},{19,20},{21... | collective-permute-start | bytes 393224 | tf_op jit(solution)/shard_map/ppermute | solution.py:360
  49.7 1.8 %collective-permute-start.15 = (f32[16,16,128]{2,1,0:T(8,128)S(1)}, f32[16,16,128]{2,1,0:T(8,128)S(1)}, u32[]{:S(2)}, u32[]{:S(2)}) collective-permute-start(f32[16,16,128]{2,1,0:T(8,128)S(1)} %shard_map.110.r8), channel_id=1, source_target_pairs={{0,1},{1,0},{2,3},{3,2},{4,5},{5,4},{6,7},{7,6},{8,9},{9,8},{10,11... | collective-permute-start | bytes 393224 | tf_op jit(solution)/shard_map/ppermute | solution.py:357
  50.5 5.8 %collective-permute-start.14 = (f32[16,16,128]{2,1,0:T(8,128)S(1)}, f32[16,16,128]{2,1,0:T(8,128)S(1)}, u32[]{:S(2)}, u32[]{:S(2)}) collective-permute-start(f32[16,16,128]{2,1,0:T(8,128)S(1)} %shard_map.110.r8), channel_id=1, source_target_pairs={{1,2},{3,4},{5,6},{7,8},{9,10},{11,12},{13,14},{17,18},{19,20},{21... | collective-permute-start | bytes 393224 | tf_op jit(solution)/shard_map/ppermute | solution.py:360

commit v3 on v2

v3 whole, which is shorter than its diff:
```python
import functools

import jax
import jax.numpy as jnp
from jax import lax
from jax.experimental import pallas as pl
from jax.experimental.pallas import tpu as pltpu
from jax.sharding import PartitionSpec as P


STEPS = 8
IMG_EVERY = 4
NOFF = 33
SURFACE = 4
HALF = 16
REACH = 4
TRIM = HALF - REACH
LANES = 48
PAD = 8

SCALE = 5040.0
WHOLE = (8064.0, -1008.0, 128.0, -9.0)
CENTRE = 6.0 * sum(WHOLE)

f32 = jnp.float32
bf16 = jnp.bfloat16


def vmem_specs(count):
    return [pl.BlockSpec(memory_space=pltpu.VMEM)] * count


def params(megabytes):
    return pltpu.CompilerParams(vmem_limit_bytes=megabytes * 1024 * 1024)


def shape(*dims):
    return jax.ShapeDtypeStruct(dims, f32)


def place():
    me = lax.axis_index("gx")
    return lax.rem(me, 2), (me > 0) & (me < lax.axis_size("gx") - 1)


def split2(value):
    high = value.astype(bf16)
    low = (value - high.astype(f32)).astype(bf16)
    return high, low


def split3(value):
    high = value.astype(bf16)
    rest = value - high.astype(f32)
    mid = rest.astype(bf16)
    low = (rest - mid.astype(f32)).astype(bf16)
    return high, mid, low


def depth_matrix(nz):
    row = lax.broadcasted_iota(jnp.int32, (nz, nz), 0)
    col = lax.broadcasted_iota(jnp.int32, (nz, nz), 1)
    gap = jnp.abs(row - col)
    band = jnp.zeros((nz, nz), f32)
    for k, weight in enumerate(WHOLE):
        band = jnp.where(gap == k + 1, weight, band)
    band = band.astype(bf16)
    return jnp.concatenate([band, band], axis=0)


def along_depth(refs, r0, depth):
    _, tall, nz = refs[0].shape
    ny = tall - 2 * PAD
    rows = [ref[r0 : r0 + 8, PAD : PAD + ny, :].reshape(8 * ny, nz) for ref in refs]
    high, low = split2(jnp.concatenate(rows, axis=0))
    return jnp.dot(jnp.concatenate([high, low], axis=1), depth, preferred_element_type=f32)


def across(ref, r0, at, i):
    total = None
    for k in range(1, REACH + 1):
        four = (ref[r0 + i + k, pl.ds(at, 8), :] + ref[r0 + i - k, pl.ds(at, 8), :]) + (
            ref[r0 + i, pl.ds(at + k, 8), :] + ref[r0 + i, pl.ds(at - k, 8), :]
        )
        total = WHOLE[k - 1] * four if total is None else total + WHOLE[k - 1] * four
    return total


def clear_pads(ref):
    zero = jnp.zeros((ref.shape[0], PAD, ref.shape[2]), f32)
    ref[:, 0:PAD, :] = zero
    ref[:, ref.shape[1] - PAD :, :] = zero


def pack_kernel(*refs, count):
    args, copies, sems = refs[:count], refs[count : 2 * count], refs[-1]
    far_coef, far_prior, far_r, near_s, near_r = refs[2 * count : -1]
    moves = [pltpu.make_async_copy(a, b, sems.at[i]) for i, (a, b) in enumerate(zip(args, copies))]
    for move in moves:
        move.start()
    for move in moves:
        move.wait()
    s0, sp, r0, rp, stiff, buoy = copies[:6]
    p, _ = place()
    n = s0.shape[0]
    far_cut, near_cut = pl.ds(REACH * p, TRIM), pl.ds(REACH * (1 - p), TRIM)
    far_coef[0:n] = buoy[...]
    far_coef[n:] = stiff[far_cut]
    far_prior[...] = sp[far_cut]
    far_r[0:n] = r0[...]
    far_r[n:] = rp[far_cut]
    near_s[0:n] = buoy[...]
    near_s[n : n + TRIM] = stiff[near_cut]
    near_s[n + TRIM : 2 * n + TRIM] = s0[...]
    near_s[2 * n + TRIM :] = sp[near_cut]
    near_r[0:n] = r0[...]
    near_r[n:] = rp[near_cut]


def spread(cells, parts, lateral, steps):
    width = cells.shape[1]
    bits = lateral.bit_length() - 1
    crossline = jnp.bitwise_and(cells, lateral - 1)
    inline = lax.shift_right_arithmetic(cells, bits) - (lax.axis_index("gx") * HALF - TRIM)
    here = lax.broadcasted_iota(jnp.int32, (lateral, width), 0) == crossline
    hot = jnp.where(lax.broadcasted_iota(jnp.int32, (LANES, width), 0) == inline, 1.0, 0.0).astype(bf16)
    total = None
    for part in parts:
        part = part.astype(f32)
        rows = [jnp.where(here, part[t : t + 1], 0.0) for t in range(steps)]
        term = lax.dot_general(
            jnp.concatenate(rows, axis=0).astype(bf16), hot, (((1,), (1,)), ((), ())), preferred_element_type=f32
        )
        total = term if total is None else total + term
    return total


def shots_kernel(shots, fire, wavelet, planes):
    steps, lateral, _ = planes.shape
    taps, ns = wavelet.shape
    delay = lax.broadcasted_iota(jnp.int32, (steps, ns), 0) - fire[...]
    amounts = jnp.zeros((steps, ns), f32)
    for d in range(taps):
        amounts = amounts + jnp.where(delay == d, wavelet[d : d + 1, :], 0.0)
    total = spread(shots[...], split3(amounts), lateral, steps)
    planes[:, :, 0:LANES] = total.reshape(steps, lateral, LANES)


def receivers_kernel(cells, traces, planes, acc, hops):
    groups = cells.shape[0]
    steps, lateral, _ = planes.shape
    me = lax.axis_index("gx")

    def owner(q):
        other = me
        for bit, hop in enumerate(hops):
            other = jnp.bitwise_xor(other, hop * jnp.bitwise_and(lax.shift_right_logical(q, bit), 1))
        return other

    acc[...] = jnp.zeros(acc.shape, f32)

    def gather(j, carry):
        row = jnp.concatenate([cells[pl.ds(owner(2 * j + half), 1), :] for half in range(2)], axis=1)
        block = jnp.concatenate([traces[2 * j], traces[2 * j + 1]], axis=1)
        back = jnp.concatenate([block[steps - 1 - t : steps - t] for t in range(steps)], axis=0)
        acc[:, 0:LANES] += spread(row, split3(back), lateral, steps)
        return carry

    lax.fori_loop(0, groups // 2, gather, 0)
    planes[:, :, 0:LANES] = acc[:, 0:LANES].reshape(steps, lateral, LANES)


def load_field(dst, own, od, od_lo, ev, ev_lo, n, full):
    p, there = place()
    rows = own.shape[0]
    inner = slice(PAD, PAD + own.shape[1])
    dst[rows : 2 * rows, inner, :] = own[...]
    skip = 0 if full else REACH
    dst[pl.ds(2 * rows * p + skip * (1 - p), n), inner, :] = jnp.where(there, od[od_lo : od_lo + n], 0.0)
    dst[pl.ds(2 * rows * (1 - p) + skip * p, n), inner, :] = ev[ev_lo : ev_lo + n]


def tiles_of(q, first, tiles):
    y0 = pl.multiple_of(8 * lax.rem(q, tiles), 8)
    return first + 8 * lax.div(q, tiles), y0, pl.multiple_of(PAD + y0, 8)


def run_steps(field, product, coefs, planes, depth, base):
    buoy, kb, kk, gg = coefs
    wide, tall, nz = field[0].shape
    ny = tall - 2 * PAD
    tiles = ny // 8
    surface = lax.broadcasted_iota(jnp.int32, (8, nz), 1) == SURFACE
    for step in range(IMG_EVERY):
        old, new = field[step % 2], field[1 - step % 2]
        flux, flux_new = product[step % 2], product[1 - step % 2]
        first = REACH * (step + 1)
        for r0 in range(first, wide - first, 8):
            deep = along_depth((old, flux), r0, depth)
            for i in range(8):
                r = r0 + i
                for t in range(tiles):
                    tile = slice(8 * t, 8 * t + 8)
                    at = slice(PAD + 8 * t, PAD + 8 * t + 8)
                    row = ny * i + 8 * t
                    term = pltpu.roll(planes[base + step, tile, :], (SURFACE - (r - REACH)) % nz, axis=1)
                    part = gg[r, tile, :] * old[r, at, :] - new[r, at, :] + jnp.where(surface, term, 0.0)
                    part = part + kb[r, tile, :] * deep[row : row + 8]
                    new[r, at, :] = part + kk[r, tile, :] * deep[8 * ny + row : 8 * ny + row + 8]

        def chunk(q, carry, old=old, new=new, flux=flux, flux_new=flux_new, step=step, first=first):
            r0, y0, at = tiles_of(q, first, tiles)
            tile = pl.ds(y0, 8)
            for i in range(8):
                r = r0 + i
                part = new[r, pl.ds(at, 8), :] + kb[r, tile, :] * across(old, r0, at, i)
                part = part + kk[r, tile, :] * across(flux, r0, at, i)
                new[r, pl.ds(at, 8), :] = part
                if step < IMG_EVERY - 1:
                    flux_new[r, pl.ds(at, 8), :] = buoy[r, tile, :] * part
            return carry

        lax.fori_loop(0, tiles * (wide - 2 * first) // 8, chunk, 0)


def start_products(field, product, buoy):
    for ref in (*field, *product):
        clear_pads(ref)
    inner = slice(PAD, field[0].shape[1] - PAD)
    product[0][:, inner, :] = buoy[...] * field[0][:, inner, :]


def finish(field, n, now_out, before_out, od_out, ev_out):
    p, _ = place()
    last, earlier = field[IMG_EVERY % 2], field[1 - IMG_EVERY % 2]
    inner = slice(PAD, last.shape[1] - PAD)
    value = last[n : 2 * n, inner, :]
    now_out[...] = value
    before_out[...] = earlier[n : 2 * n, inner, :]
    od_out[0:n] = value
    ev_out[0:n] = value
    od_out[n:] = earlier[pl.ds(n + REACH * p, TRIM), inner, :]
    ev_out[n:] = earlier[pl.ds(n + REACH * (1 - p), TRIM), inner, :]


def first_kernel(own, prior, stiff, buoy_own, far_own, far_coef, far_prior, ev, planes, now_out, before_out, od_out, ev_out, buoy, kb, kk, gg, f0, f1, p0, p1):
    n, ny, nz = own.shape
    tiles = ny // 8
    inner = slice(PAD, PAD + ny)
    depth = depth_matrix(nz)
    clear_pads(p1)
    load_field(p1, buoy_own, far_coef, 0, ev, 0, n, True)
    load_field(f1, stiff, far_coef, n, ev, n, TRIM, False)
    buoy[...] = p1[:, inner, :]

    for r0 in range(REACH, 3 * n - REACH, 8):
        gg[r0 : r0 + 8] = along_depth((p1,), r0, depth).reshape(8, ny, nz)

    def coefficients(q, carry):
        r0, y0, at = tiles_of(q, REACH, tiles)
        tile = pl.ds(y0, 8)
        for i in range(8):
            r = r0 + i
            b = p1[r, pl.ds(at, 8), :]
            k = f1[r, pl.ds(at, 8), :] * (0.5 / SCALE)
            kk[r, tile, :] = k
            kb[r, tile, :] = k * b
            gg[r, tile, :] = 2.0 - k * (CENTRE * b + (across(p1, r0, at, i) + gg[r, tile, :]))
        return carry

    lax.fori_loop(0, tiles * (3 * n - 2 * REACH) // 8, coefficients, 0)
    load_field(f0, own, far_own, 0, ev, n + TRIM, n, True)
    load_field(f1, prior, far_prior, 0, ev, 2 * n + TRIM, TRIM, False)
    start_products((f0, f1), (p0, p1), buoy)
    run_steps((f0, f1), (p0, p1), (buoy, kb, kk, gg), planes, depth, 0)
    finish((f0, f1), n, now_out, before_out, od_out, ev_out)


def block_steps(own, prior, od, ev, planes, coefs, field, product, base):
    n, _, nz = own.shape
    depth = depth_matrix(nz)
    load_field(field[0], own, od, 0, ev, 0, n, True)
    load_field(field[1], prior, od, n, ev, n, TRIM, False)
    start_products(field, product, coefs[0])
    run_steps(field, product, coefs, planes, depth, base)


def block_kernel(own, prior, od, ev, planes, buoy, kb, kk, gg, now_out, before_out, od_out, ev_out, f0, f1, p0, p1, base):
    block_steps(own, prior, od, ev, planes, (buoy, kb, kk, gg), (f0, f1), (p0, p1), base)
    finish((f0, f1), own.shape[0], now_out, before_out, od_out, ev_out)


def last_kernel(own, prior, od, ev, planes, buoy, kb, kk, gg, now_out, f0, f1, p0, p1, base):
    block_steps(own, prior, od, ev, planes, (buoy, kb, kk, gg), (f0, f1), (p0, p1), base)
    n, ny, _ = own.shape
    now_out[...] = (f0, f1)[IMG_EVERY % 2][n : 2 * n, PAD : PAD + ny, :]


def lagged(lag_s, lag_r, levels, x, lag):
    total = None
    for level in levels:
        term = lag_s[level, HALF + x - lag] * lag_r[level, HALF + x + lag]
        total = term if total is None else total + term
    return total


def write_out(block, out, sems, count, target):
    def drain(j, carry):
        pltpu.make_async_copy(block.at[j], out.at[target(j)], sems.at[j]).wait()
        return carry

    lax.fori_loop(0, count, drain, 0)


def image_kernel(s0, s4, s8, r0, r4, r8, far_s0, ev1, far_r, ev2, ods, evs, odr, evr, ods8, evs8, evr8, out, rest, lag_s, lag_r, block, sems):
    p, there = place()
    n = s0.shape[0]
    left, right = pl.ds(2 * n * p, n), pl.ds(2 * n * (1 - p), n)
    groups = (
        (lag_s, 0, s0, far_s0, 0, ev1, n + TRIM),
        (lag_r, 0, r0, far_r, 0, ev2, 0),
        (lag_s, 1, s4, ods, 0, evs, 0),
        (lag_r, 1, r4, odr, 0, evr, 0),
        (lag_s, 2, s8, ods8, 0, evs8, 0),
        (lag_r, 2, r8, None, 0, evr8, 0),
    )
    for dst, level, own, od, od_lo, ev, ev_lo in groups:
        dst[level, n : 2 * n] = own[...]
        if od is not None:
            dst[level, left] = jnp.where(there, od[od_lo : od_lo + n], 0.0)
        dst[level, right] = ev[ev_lo : ev_lo + n]
    sign = 1 - 2 * p
    target = lambda j: HALF + sign * j

    def whole(j, carry):
        for x in range(n):
            block[j, x] = lagged(lag_s, lag_r, (0, 1, 2), x, sign * j)
        pltpu.make_async_copy(block.at[j], out.at[target(j)], sems.at[j]).start()
        return carry

    lax.fori_loop(0, HALF + 1, whole, 0)

    def partial(j, carry):
        for x in range(n):
            rest[j, x] = lagged(lag_s, lag_r, (0, 1), x, -sign * (j + 1))
        return carry

    lax.fori_loop(0, HALF, partial, 0)
    write_out(block, out, sems, HALF + 1, target)


def last_image_kernel(s8, r8, evs8, odr8, rest, before, out, lag_s, lag_r, block, sems):
    p, there = place()
    n = s8.shape[0]
    lag_s[0, n : 2 * n] = s8[...]
    lag_s[0, pl.ds(2 * n * (1 - p), n)] = evs8[...]
    lag_r[0, n : 2 * n] = r8[...]
    lag_r[0, pl.ds(2 * n * p, n)] = jnp.where(there, odr8[...], 0.0)
    sign = 1 - 2 * p
    target = lambda j: HALF - sign * (j + 1)

    def one(j, carry):
        for x in range(n):
            block[j, x] = rest[j, x] + lagged(lag_s, lag_r, (0,), x, -sign * (j + 1))
        pltpu.make_async_copy(block.at[j], out.at[target(j)], sems.at[j]).start()
        return carry

    lax.fori_loop(0, HALF, one, 0)
    write_out(block, out, sems, HALF, target)


def estimate(flops, nbytes):
    return pl.CostEstimate(flops=flops, bytes_accessed=nbytes, transcendentals=0)


def local(source_field, source_prior, receiver_field, receiver_prior, stiffness, buoyancy, wavelet, fire_step, shot_cell, receiver_cell, traces):
    n, ny, nz = source_field.shape
    shots, count = lax.axis_size("shot"), lax.axis_size("gx")
    near = [(i, i ^ 1) for i in range(count)]
    far = [(s * count + i, s * count + i + 1) for s in range(shots) for i in range(1, count - 1, 2)]
    far = far + [(b, a) for a, b in far]
    if shots % 2 == 0:
        far += [(s * count + e, (s ^ 1) * count + e) for s in range(shots) for e in (0, count - 1)]

    def swap_near(x):
        return lax.ppermute(x, "gx", near)

    def swap_far(x):
        return lax.ppermute(x, ("shot", "gx"), far)

    hops = []
    hop = 2
    while hop < count:
        hops.append(hop)
        hop *= 2
    hops.append(1)

    def exchange(x, which):
        return lax.ppermute(x, "gx", [(i, i ^ hops[which]) for i in range(count)])

    received = exchange(traces[None], 0)
    far_s0 = swap_far(source_field)

    small = n + TRIM
    width = traces.shape[1]
    ns = shot_cell.shape[0]
    args = (
        source_field,
        source_prior,
        receiver_field,
        receiver_prior,
        stiffness,
        buoyancy,
        traces[None],
        receiver_cell.reshape(count, width),
        shot_cell.reshape(1, ns),
        fire_step.reshape(1, ns),
        wavelet.T,
    )
    packed = pl.pallas_call(
        functools.partial(pack_kernel, count=len(args)),
        out_shape=[jax.ShapeDtypeStruct(a.shape, a.dtype) for a in args]
        + [shape(small, ny, nz), shape(TRIM, ny, nz), shape(small, ny, nz), shape(2 * small, ny, nz), shape(small, ny, nz)],
        in_specs=[pl.BlockSpec(memory_space=pltpu.MemorySpace.HBM)] * len(args),
        out_specs=vmem_specs(len(args) + 5),
        scratch_shapes=[pltpu.SemaphoreType.DMA((len(args),))],
        compiler_params=params(8),
        cost_estimate=estimate(1000, 3000000),
        name="pack",
    )(*(pltpu.with_memory_space_constraint(a, pltpu.MemorySpace.HBM) for a in args))
    source_field, source_prior, receiver_field, receiver_prior, stiffness, buoyancy, gathered, cells, shot_row, fire_row, wave = packed[: len(args)]
    far_coef, far_prior, far_r, ev1, ev2 = packed[len(args) :]
    far_coef = swap_far(far_coef)
    far_prior = swap_far(far_prior)
    far_r = swap_far(far_r)
    ev1 = swap_near(ev1)
    ev2 = swap_near(ev2)

    gathered = jnp.concatenate([gathered, received], axis=0)
    for which in range(1, len(hops)):
        gathered = jnp.concatenate([gathered, exchange(gathered, which)], axis=0)

    plane = shape(STEPS, ny, nz)
    plane_s = pl.pallas_call(
        shots_kernel,
        out_shape=plane,
        in_specs=vmem_specs(3),
        out_specs=pl.BlockSpec(memory_space=pltpu.VMEM),
        compiler_params=params(8),
        cost_estimate=estimate(1000000, 100000),
        name="shots",
    )(shot_row, fire_row, wave)
    plane_r = pl.pallas_call(
        functools.partial(receivers_kernel, hops=tuple(hops)),
        out_shape=plane,
        in_specs=vmem_specs(2),
        out_specs=pl.BlockSpec(memory_space=pltpu.VMEM),
        scratch_shapes=[pltpu.VMEM((STEPS * ny, nz), f32)],
        compiler_params=params(8),
        cost_estimate=estimate(2 * LANES * STEPS * ny * 2048, 1000000),
        name="receivers",
    )(cells, gathered)

    wide = 3 * n
    scratch = [pltpu.VMEM((wide, ny + 2 * PAD, nz), f32)] * 4
    cost = estimate(224 * 8 * 128 * 60, 6000000)
    own = shape(n, ny, nz)
    s4, s3, ods, evs, buoy, kb, kk, gg = pl.pallas_call(
        first_kernel,
        out_shape=[own, own, shape(small, ny, nz), shape(small, ny, nz)] + [shape(wide, ny, nz)] * 4,
        in_specs=vmem_specs(9),
        out_specs=vmem_specs(8),
        scratch_shapes=scratch,
        compiler_params=params(16),
        cost_estimate=cost,
        name="first_s",
    )(source_field, source_prior, stiffness, buoyancy, far_s0, far_coef, far_prior, ev1, plane_s)
    coefs = (buoy, kb, kk, gg)
    ods = swap_far(ods)
    evs = swap_near(evs)
    r4, r3, odr, evr = pl.pallas_call(
        functools.partial(block_kernel, base=0),
        out_shape=[own, own, shape(small, ny, nz), shape(small, ny, nz)],
        in_specs=vmem_specs(9),
        out_specs=vmem_specs(4),
        scratch_shapes=scratch,
        compiler_params=params(16),
        cost_estimate=cost,
        name="first_r",
    )(receiver_field, receiver_prior, far_r, ev2, plane_r, *coefs)
    odr = swap_far(odr)
    evr = swap_near(evr)

    def last():
        return pl.pallas_call(
            functools.partial(last_kernel, base=IMG_EVERY),
            out_shape=own,
            in_specs=vmem_specs(9),
            out_specs=pl.BlockSpec(memory_space=pltpu.VMEM),
            scratch_shapes=scratch,
            compiler_params=params(16),
            cost_estimate=cost,
        )

    s8 = last()(s4, s3, ods, evs, plane_s, *coefs)
    ods8 = swap_far(s8)
    evs8 = swap_near(s8)
    r8 = last()(r4, r3, odr, evr, plane_r, *coefs)
    odr8 = swap_far(r8)
    evr8 = swap_near(r8)
    lags = lambda levels, blocks: [
        pltpu.VMEM((levels, wide, ny, nz), f32),
        pltpu.VMEM((levels, wide, ny, nz), f32),
        pltpu.VMEM((blocks, n, ny, nz), f32),
        pltpu.SemaphoreType.DMA((blocks,)),
    ]
    hbm = pl.BlockSpec(memory_space=pltpu.MemorySpace.HBM)
    image, rest = pl.pallas_call(
        image_kernel,
        out_shape=[shape(NOFF, n, ny, nz), shape(HALF, n, ny, nz)],
        in_specs=vmem_specs(17),
        out_specs=[hbm, pl.BlockSpec(memory_space=pltpu.VMEM)],
        scratch_shapes=lags(3, HALF + 1),
        compiler_params=params(16),
        cost_estimate=estimate(NOFF * n * ny * nz * 4, 4400000),
        name="image",
    )(source_field, s4, s8, receiver_field, r4, r8, far_s0, ev1, far_r, ev2, ods, evs, odr, evr, ods8, evs8, evr8)
    return pl.pallas_call(
        last_image_kernel,
        out_shape=shape(NOFF, n, ny, nz),
        in_specs=vmem_specs(5) + [hbm],
        out_specs=hbm,
        scratch_shapes=lags(1, HALF),
        input_output_aliases={5: 0},
        compiler_params=params(16),
        cost_estimate=estimate(HALF * n * ny * nz * 2, 2200000),
        name="last_image",
    )(s8, r8, evs8, odr8, rest, image)


def solution(mesh):
    placed = (
        P(("shot", "gx"), None, None),
        P(("shot", "gx"), None, None),
        P(("shot", "gx"), None, None),
        P(("shot", "gx"), None, None),
        P("gx", None, None),
        P("gx", None, None),
        P("shot", None),
        P("shot"),
        P("shot"),
        P("shot"),
        P("shot", "gx"),
    )
    return jax.shard_map(local, mesh=mesh, in_specs=placed, out_specs=P("shot", "gx", None, None), check_vma=False)
```

time: 59.5 us -> 53.1 us (0.89)
  the two profiles are of different devices: /device:TPU:14 before, /device:TPU:9 now
where the time goes in v3:
time: 53.1 us; the launch traced here: 52.9 us
  Pallas kernels  24.2 us (46%)
  starting transfers between devices  20.9 us (39%)
  waiting for transfers between devices  7.74 us (15%)
    ppermute x8, starting transfers between devices, swap_far(): return lax.ppermute(x, ('shot', 'gx'), far)  11.3 us
    ppermute x4, starting transfers between devices, exchange(): return lax.ppermute(x, 'gx', [(i, i ^ hops[which]) for i in range(count)])  7.67 us
    pallas_call x1, Pallas kernels, local(): pl.pallas_call(first_kernel, out_shape=[own, own, shape(small, ny, nz), s...  5.14 us
    pallas_call x1, Pallas kernels, local(): pl.pallas_call(functools.partial(block_kernel, base=0), out_shape=[own, o...  4.18 us
    pallas_call x1, Pallas kernels, local(): s8 = last()(s4, s3, ods, evs, plane_s, *coefs)  4.15 us
    pallas_call x1, Pallas kernels, local(): r8 = last()(r4, r3, odr, evr, plane_r, *coefs)  4.14 us
    ppermute x4, waiting for transfers between devices, exchange(): return lax.ppermute(x, 'gx', [(i, i ^ hops[which]) for i in range(count)])  3.57 us
    ppermute x8, waiting for transfers between devices, swap_far(): return lax.ppermute(x, ('shot', 'gx'), far)  3.43 us
  transfers between devices with their start and end apart: 18, of which 6 were waited for; matrix products, arithmetic and copies ran while one was open for 0% of the time, Pallas kernels for 43%

profile of v3, /device:TPU:9, one launch (start us, length us, event | category | flops | bytes accessed | tf_op | source)
XLA Modules:
  0.0 52.9 jit_solution(811136707799277376)
XLA Ops:
  0.0 1.2 %collective-permute-start.8 = (f32[1,8,128]{2,1,0:T(8,128)}, f32[1,8,128]{2,1,0:T(8,128)S(1)}, u32[]{:S(2)}, u32[]{:S(2)}) collective-permute-start(f32[1,8,128]{2,1,0:T(8,128)} %bitcast.7), channel_id=1, source_target_pairs={{0,2},{1,3},{2,0},{3,1},{4,6},{5,7},{6,4},{7,5},{8,10},{9,11},{10,... | collective-permute-start | bytes 12296 | tf_op jit(solution)/shard_map/ppermute | solution.py:399
  1.2 1.1 %collective-permute-start = (f32[16,16,128]{2,1,0:T(8,128)}, f32[16,16,128]{2,1,0:T(8,128)S(1)}, u32[]{:S(2)}, u32[]{:S(2)}) collective-permute-start(f32[16,16,128]{2,1,0:T(8,128)} %refs_0_.1), channel_id=1, source_target_pairs={{1,2},{3,4},{5,6},{7,8},{9,10},{11,12},{13,14},{17,18},{19,20},{21... | collective-permute-start | bytes 393224 | tf_op jit(solution)/shard_map/ppermute | solution.py:389
  2.3 1.4 %pack.1 = (f32[16,16,128]{2,1,0:T(8,128)S(1)}, f32[16,16,128]{2,1,0:T(8,128)S(1)}, f32[16,16,128]{2,1,0:T(8,128)S(1)}, f32[16,16,128]{2,1,0:T(8,128)S(1)}, f32[1...) custom-call(f32[16,16,128]{2,1,0:T(8,128)} %refs_0_.1, ...), custom_call_target="tpu_custom_call" | custom-call | flops 1000 | bytes 3000000 | tf_op jit(solution)/shard_map/pack/pallas_call | solution.py:420
  3.7 0.7 %collective-permute-start.2 = (f32[12,16,128]{2,1,0:T(8,128)S(1)}, f32[12,16,128]{2,1,0:T(8,128)S(1)}, u32[]{:S(2)}, u32[]{:S(2)}) collective-permute-start(f32[12,16,128]{2,1,0:T(8,128)S(1)} %get-tuple-element.40), channel_id=1, source_target_pairs={{1,2},{3,4},{5,6},{7,8},{9,10},{11,12},{13,14},{17,18},{19,20},{21... | collective-permute-start | bytes 294920 | tf_op jit(solution)/shard_map/ppermute | solution.py:389
  4.4 1.1 %collective-permute-start.1 = (f32[28,16,128]{2,1,0:T(8,128)S(1)}, f32[28,16,128]{2,1,0:T(8,128)S(1)}, u32[]{:S(2)}, u32[]{:S(2)}) collective-permute-start(f32[28,16,128]{2,1,0:T(8,128)S(1)} %get-tuple-element.39), channel_id=1, source_target_pairs={{1,2},{3,4},{5,6},{7,8},{9,10},{11,12},{13,14},{17,18},{19,20},{21... | collective-permute-start | bytes 688136 | tf_op jit(solution)/shard_map/ppermute | solution.py:389
  5.5 0.9 %collective-permute-start.3 = (f32[56,16,128]{2,1,0:T(8,128)S(1)}, f32[56,16,128]{2,1,0:T(8,128)S(1)}, u32[]{:S(2)}, u32[]{:S(2)}) collective-permute-start(f32[56,16,128]{2,1,0:T(8,128)S(1)} %get-tuple-element.41), channel_id=1, source_target_pairs={{0,1},{1,0},{2,3},{3,2},{4,5},{5,4},{6,7},{7,6},{8,9},{9,8},{10,11... | collective-permute-start | bytes 1376264 | tf_op jit(solution)/shard_map/ppermute | solution.py:386
  6.4 0.0 collective-permute-done.8
  6.4 1.0 %collective-permute-start.9 = (f32[2,8,128]{2,1,0:T(8,128)S(1)}, f32[2,8,128]{2,1,0:T(8,128)S(1)}, u32[]{:S(2)}, u32[]{:S(2)}) collective-permute-start(f32[2,8,128]{2,1,0:T(8,128)S(1)} %pad_maximum_fusion.2), channel_id=1, source_target_pairs={{0,4},{1,5},{2,6},{3,7},{4,0},{5,1},{6,2},{7,3},{8,12},{9,13},{10,... | collective-permute-start | bytes 24584 | tf_op jit(solution)/shard_map/ppermute | solution.py:399
  7.3 0.2 shots.1.planes
  7.5 1.4 %collective-permute-done.9 = f32[2,8,128]{2,1,0:T(8,128)S(1)} collective-permute-done((f32[2,8,128]{2,1,0:T(8,128)S(1)}, f32[2,8,128]{2,1,0:T(8,128)S(1)}, u32[]{:S(2)}, u32[]{:S(2)}) %collective-permute-start.9) | collective-permute-done | bytes 8224 | tf_op jit(solution)/shard_map/ppermute | solution.py:399
  8.9 2.3 %collective-permute-start.10 = (f32[4,8,128]{2,1,0:T(8,128)S(1)}, f32[4,8,128]{2,1,0:T(8,128)S(1)}, u32[]{:S(2)}, u32[]{:S(2)}) collective-permute-start(f32[4,8,128]{2,1,0:T(8,128)S(1)} %pad_maximum_fusion.1), channel_id=1, source_target_pairs={{0,8},{1,9},{2,10},{3,11},{4,12},{5,13},{6,14},{7,15},{8,0},{9,1},... | collective-permute-start | bytes 49160 | tf_op jit(solution)/shard_map/ppermute | solution.py:399
  11.2 1.3 %collective-permute-done.10 = f32[4,8,128]{2,1,0:T(8,128)S(1)} collective-permute-done((f32[4,8,128]{2,1,0:T(8,128)S(1)}, f32[4,8,128]{2,1,0:T(8,128)S(1)}, u32[]{:S(2)}, u32[]{:S(2)}) %collective-permute-start.10) | collective-permute-done | bytes 16416 | tf_op jit(solution)/shard_map/ppermute | solution.py:399
  12.6 3.2 %collective-permute-start.11 = (f32[8,8,128]{2,1,0:T(8,128)S(1)}, f32[8,8,128]{2,1,0:T(8,128)S(1)}, u32[]{:S(2)}, u32[]{:S(2)}) collective-permute-start(f32[8,8,128]{2,1,0:T(8,128)S(1)} %pad_maximum_fusion), channel_id=1, source_target_pairs={{0,1},{1,0},{2,3},{3,2},{4,5},{5,4},{6,7},{7,6},{8,9},{9,8},{10,11... | collective-permute-start | bytes 98312 | tf_op jit(solution)/shard_map/ppermute | solution.py:399
  15.7 0.9 %collective-permute-done.11 = f32[8,8,128]{2,1,0:T(8,128)S(1)} collective-permute-done((f32[8,8,128]{2,1,0:T(8,128)S(1)}, f32[8,8,128]{2,1,0:T(8,128)S(1)}, u32[]{:S(2)}, u32[]{:S(2)}) %collective-permute-start.11) | collective-permute-done | bytes 32800 | tf_op jit(solution)/shard_map/ppermute | solution.py:399
  16.6 2.1 %collective-permute-start.6 = (f32[28,16,128]{2,1,0:T(8,128)S(1)}, f32[28,16,128]{2,1,0:T(8,128)S(1)}, u32[]{:S(2)}, u32[]{:S(2)}) collective-permute-start(f32[28,16,128]{2,1,0:T(8,128)S(1)} %get-tuple-element.55), channel_id=1, source_target_pairs={{1,2},{3,4},{5,6},{7,8},{9,10},{11,12},{13,14},{17,18},{19,20},{21... | collective-permute-start | bytes 688136 | tf_op jit(solution)/shard_map/ppermute | solution.py:389
  18.7 0.0 collective-permute-done.2.far_prior
  18.7 0.0 collective-permute-start.7
  18.7 1.6 %receivers.1.planes = f32[8,16,128]{2,1,0:T(8,128)S(1)} custom-call(s32[16,128]{1,0:T(8,128)S(1)} %get-tuple-element.57.cells, f32[16,8,128]{2,1,0:T(8,128)S(1)} %constant_dynamic-update-slice_fusion.traces), custom_call_target="tpu_custom_call" | custom-call | flops 25165824 | bytes 1000000 | tf_op jit(solution)/shard_map/receivers/pallas_call | solution.py:453
  20.3 0.0 collective-permute-done.far_own.far_s0
  20.3 0.0 collective-permute-done.1.far_coef
  20.3 0.0 collective-permute-done.3.ev.ev1
  20.4 5.1 %first_s.1 = (f32[16,16,128]{2,1,0:T(8,128)S(1)}, f32[16,16,128]{2,1,0:T(8,128)S(1)}, f32[28,16,128]{2,1,0:T(8,128)S(1)}, f32[28,16,128]{2,1,0:T(8,128)S(1)}, f3...) custom-call(f32[16,16,128]{2,1,0:T(8,128)S(1)} %get-tuple-element.35, ...), custom_call_target="tpu_custom_call" | custom-call | flops 13762560 | bytes 6000000 | tf_op jit(solution)/shard_map/first_s/pallas_call | solution.py:468
  25.5 3.3 %collective-permute-start.4 = (f32[28,16,128]{2,1,0:T(8,128)S(1)}, f32[28,16,128]{2,1,0:T(8,128)S(1)}, u32[]{:S(2)}, u32[]{:S(2)}) collective-permute-start(f32[28,16,128]{2,1,0:T(8,128)S(1)} %get-tuple-element.47), channel_id=1, source_target_pairs={{1,2},{3,4},{5,6},{7,8},{9,10},{11,12},{13,14},{17,18},{19,20},{21... | collective-permute-start | bytes 688136 | tf_op jit(solution)/shard_map/ppermute | solution.py:389
  28.8 0.0 collective-permute-start.5
  28.8 0.0 collective-permute-done.6.od.far_r
  28.8 0.0 collective-permute-done.7.ev.ev2
  28.8 4.2 %first_r.1 = (f32[16,16,128]{2,1,0:T(8,128)S(1)}, f32[16,16,128]{2,1,0:T(8,128)S(1)}, f32[28,16,128]{2,1,0:T(8,128)S(1)}, f32[28,16,128]{2,1,0:T(8,128)S(1)}) custom-call(f32[16,16,128]{2,1,0:T(8,128)S(1)} %get-tuple-element.53.own.r0, f32[16,16,128]{2,1,0:T(8,128)S(1)} %get-tuple-element.54.prior, f32[28,16,128]{2,1,0:T(8,128)S(1)} %collective-permute-done.6.od.far_r, ...), custom_call_target="tpu_custom_call" | custom-call | flops 13762560 | bytes 6000000 | tf_op jit(solution)/shard_map/first_r/pallas_call | solution.py:481
  33.0 0.2 collective-permute-start.12
  33.2 0.5 %collective-permute-start.13 = (f32[28,16,128]{2,1,0:T(8,128)S(1)}, f32[28,16,128]{2,1,0:T(8,128)S(1)}, u32[]{:S(2)}, u32[]{:S(2)}) collective-permute-start(f32[28,16,128]{2,1,0:T(8,128)S(1)} %get-tuple-element.62), channel_id=1, source_target_pairs={{0,1},{1,0},{2,3},{3,2},{4,5},{5,4},{6,7},{7,6},{8,9},{9,8},{10,11... | collective-permute-start | bytes 688136 | tf_op jit(solution)/shard_map/ppermute | solution.py:386
  33.7 0.5 collective-permute-done.4.od.ods
  34.2 0.0 collective-permute-done.5.ev.evs
  34.2 4.1 %shard_map.109.s8 = f32[16,16,128]{2,1,0:T(8,128)S(1)} custom-call(f32[16,16,128]{2,1,0:T(8,128)S(1)} %get-tuple-element.45.own.s4, f32[16,16,128]{2,1,0:T(8,128)S(1)} %get-tuple-element.46.prior, f32[28,16,128]{2,1,0:T(8,128)S(1)} %collective-permute-done.4.od.ods, f32[28,16,128]{2,1,0:T(8,128)S(1)} %collective-permute-done.5.ev.evs, ...), custom_call_target="tpu_custom_call" | custom-call | flops 13762560 | bytes 6000000 | tf_op jit(solution)/shard_map/pallas_call | solution.py:505
  38.4 2.5 %collective-permute-start.16 = (f32[16,16,128]{2,1,0:T(8,128)S(1)}, f32[16,16,128]{2,1,0:T(8,128)S(1)}, u32[]{:S(2)}, u32[]{:S(2)}) collective-permute-start(f32[16,16,128]{2,1,0:T(8,128)S(1)} %shard_map.109.s8), channel_id=1, source_target_pairs={{1,2},{3,4},{5,6},{7,8},{9,10},{11,12},{13,14},{17,18},{19,20},{21... | collective-permute-start | bytes 393224 | tf_op jit(solution)/shard_map/ppermute | solution.py:389
  40.9 0.0 collective-permute-start.14
  40.9 0.0 collective-permute-done.12.od.odr
  40.9 0.0 collective-permute-done.13.ev.evr
  41.0 4.1 %shard_map.110.r8 = f32[16,16,128]{2,1,0:T(8,128)S(1)} custom-call(f32[16,16,128]{2,1,0:T(8,128)S(1)} %get-tuple-element.59.own.r4, f32[16,16,128]{2,1,0:T(8,128)S(1)} %get-tuple-element.60.prior, f32[28,16,128]{2,1,0:T(8,128)S(1)} %collective-permute-done.12.od.odr, f32[28,16,128]{2,1,0:T(8,128)S(1)} %collective-permute-done.13.ev.evr, ...), custom_call_target="tpu_custom_call" | custom-call | flops 13762560 | bytes 6000000 | tf_op jit(solution)/shard_map/pallas_call | solution.py:508
  45.1 0.5 %collective-permute-start.17 = (f32[16,16,128]{2,1,0:T(8,128)S(1)}, f32[16,16,128]{2,1,0:T(8,128)S(1)}, u32[]{:S(2)}, u32[]{:S(2)}) collective-permute-start(f32[16,16,128]{2,1,0:T(8,128)S(1)} %shard_map.110.r8), channel_id=1, source_target_pairs={{0,1},{1,0},{2,3},{3,2},{4,5},{5,4},{6,7},{7,6},{8,9},{9,8},{10,11... | collective-permute-start | bytes 393224 | tf_op jit(solution)/shard_map/ppermute | solution.py:386
  45.6 0.3 collective-permute-start.15
  45.9 0.0 collective-permute-done.16.ods8
  45.9 0.0 collective-permute-done.14.evs8
  45.9 0.7 %collective-permute-done.17.evr8 = f32[16,16,128]{2,1,0:T(8,128)S(1)} collective-permute-done((f32[16,16,128]{2,1,0:T(8,128)S(1)}, f32[16,16,128]{2,1,0:T(8,128)S(1)}, u32[]{:S(2)}, u32[]{:S(2)}) %collective-permute-start.17) | collective-permute-done | bytes 131104 | tf_op jit(solution)/shard_map/ppermute | solution.py:386
  46.6 1.9 %image.1 = (f32[33,16,16,128]{3,2,1,0:T(8,128)}, f32[16,16,16,128]{3,2,1,0:T(8,128)S(1)}) custom-call(f32[16,16,128]{2,1,0:T(8,128)S(1)} %get-tuple-element.35.own.s0, f32[16,16,128]{2,1,0:T(8,128)S(1)} %get-tuple-element.45.own.s4, f32[16,16,128]{2,1,0:T(8,128)S(1)} %shard_map.109.s8, f32[16,16,128]{2,1,0:T(8,128)S(1)} %get-tuple-element.53.own.r0, ...), custom_call_target="tpu_custom_call" | custom-call | flops 4325376 | bytes 4400000 | tf_op jit(solution)/shard_map/image/pallas_call | solution.py:518
  48.5 2.9 %collective-permute-done.15.odr8 = f32[16,16,128]{2,1,0:T(8,128)S(1)} collective-permute-done((f32[16,16,128]{2,1,0:T(8,128)S(1)}, f32[16,16,128]{2,1,0:T(8,128)S(1)}, u32[]{:S(2)}, u32[]{:S(2)}) %collective-permute-start.15) | collective-permute-done | bytes 131104 | tf_op jit(solution)/shard_map/ppermute | solution.py:389
  51.4 1.5 %last_image.1 = f32[33,16,16,128]{3,2,1,0:T(8,128)} custom-call(f32[16,16,128]{2,1,0:T(8,128)S(1)} %shard_map.109.s8, f32[16,16,128]{2,1,0:T(8,128)S(1)} %shard_map.110.r8, f32[16,16,128]{2,1,0:T(8,128)S(1)} %collective-permute-done.14.evs8, f32[16,16,128]{2,1,0:T(8,128)S(1)} %collective-permute-done.15.odr8, ...), custom_call_target="tpu_custom_call", output_to_operand_aliasing={{}: (5, {})} | custom-call | flops 1048576 | bytes 2200000 | tf_op jit(solution)/shard_map/last_image/pallas_call | solution.py:528
  (8 shorter events, 0.0 us)
Async XLA Ops:
  0.0 6.4 %collective-permute-start.8 = (f32[1,8,128]{2,1,0:T(8,128)}, f32[1,8,128]{2,1,0:T(8,128)S(1)}, u32[]{:S(2)}, u32[]{:S(2)}) collective-permute-start(f32[1,8,128]{2,1,0:T(8,128)} %bitcast.7), channel_id=1, source_target_pairs={{0,2},{1,3},{2,0},{3,1},{4,6},{5,7},{6,4},{7,5},{8,10},{9,11},{10,... | collective-permute-start | bytes 12296 | tf_op jit(solution)/shard_map/ppermute | solution.py:399
  1.2 19.1 %collective-permute-start = (f32[16,16,128]{2,1,0:T(8,128)}, f32[16,16,128]{2,1,0:T(8,128)S(1)}, u32[]{:S(2)}, u32[]{:S(2)}) collective-permute-start(f32[16,16,128]{2,1,0:T(8,128)} %refs_0_.1), channel_id=1, source_target_pairs={{1,2},{3,4},{5,6},{7,8},{9,10},{11,12},{13,14},{17,18},{19,20},{21... | collective-permute-start | bytes 393224 | tf_op jit(solution)/shard_map/ppermute | solution.py:389
  3.7 15.0 %collective-permute-start.2 = (f32[12,16,128]{2,1,0:T(8,128)S(1)}, f32[12,16,128]{2,1,0:T(8,128)S(1)}, u32[]{:S(2)}, u32[]{:S(2)}) collective-permute-start(f32[12,16,128]{2,1,0:T(8,128)S(1)} %get-tuple-element.40), channel_id=1, source_target_pairs={{1,2},{3,4},{5,6},{7,8},{9,10},{11,12},{13,14},{17,18},{19,20},{21... | collective-permute-start | bytes 294920 | tf_op jit(solution)/shard_map/ppermute | solution.py:389
  4.4 15.9 %collective-permute-start.1 = (f32[28,16,128]{2,1,0:T(8,128)S(1)}, f32[28,16,128]{2,1,0:T(8,128)S(1)}, u32[]{:S(2)}, u32[]{:S(2)}) collective-permute-start(f32[28,16,128]{2,1,0:T(8,128)S(1)} %get-tuple-element.39), channel_id=1, source_target_pairs={{1,2},{3,4},{5,6},{7,8},{9,10},{11,12},{13,14},{17,18},{19,20},{21... | collective-permute-start | bytes 688136 | tf_op jit(solution)/shard_map/ppermute | solution.py:389
  5.5 14.8 %collective-permute-start.3 = (f32[56,16,128]{2,1,0:T(8,128)S(1)}, f32[56,16,128]{2,1,0:T(8,128)S(1)}, u32[]{:S(2)}, u32[]{:S(2)}) collective-permute-start(f32[56,16,128]{2,1,0:T(8,128)S(1)} %get-tuple-element.41), channel_id=1, source_target_pairs={{0,1},{1,0},{2,3},{3,2},{4,5},{5,4},{6,7},{7,6},{8,9},{9,8},{10,11... | collective-permute-start | bytes 1376264 | tf_op jit(solution)/shard_map/ppermute | solution.py:386
  6.4 2.5 %collective-permute-start.9 = (f32[2,8,128]{2,1,0:T(8,128)S(1)}, f32[2,8,128]{2,1,0:T(8,128)S(1)}, u32[]{:S(2)}, u32[]{:S(2)}) collective-permute-start(f32[2,8,128]{2,1,0:T(8,128)S(1)} %pad_maximum_fusion.2), channel_id=1, source_target_pairs={{0,4},{1,5},{2,6},{3,7},{4,0},{5,1},{6,2},{7,3},{8,12},{9,13},{10,... | collective-permute-start | bytes 24584 | tf_op jit(solution)/shard_map/ppermute | solution.py:399
  8.9 3.7 %collective-permute-start.10 = (f32[4,8,128]{2,1,0:T(8,128)S(1)}, f32[4,8,128]{2,1,0:T(8,128)S(1)}, u32[]{:S(2)}, u32[]{:S(2)}) collective-permute-start(f32[4,8,128]{2,1,0:T(8,128)S(1)} %pad_maximum_fusion.1), channel_id=1, source_target_pairs={{0,8},{1,9},{2,10},{3,11},{4,12},{5,13},{6,14},{7,15},{8,0},{9,1},... | collective-permute-start | bytes 49160 | tf_op jit(solution)/shard_map/ppermute | solution.py:399
  12.6 4.0 %collective-permute-start.11 = (f32[8,8,128]{2,1,0:T(8,128)S(1)}, f32[8,8,128]{2,1,0:T(8,128)S(1)}, u32[]{:S(2)}, u32[]{:S(2)}) collective-permute-start(f32[8,8,128]{2,1,0:T(8,128)S(1)} %pad_maximum_fusion), channel_id=1, source_target_pairs={{0,1},{1,0},{2,3},{3,2},{4,5},{5,4},{6,7},{7,6},{8,9},{9,8},{10,11... | collective-permute-start | bytes 98312 | tf_op jit(solution)/shard_map/ppermute | solution.py:399
  16.6 12.2 %collective-permute-start.6 = (f32[28,16,128]{2,1,0:T(8,128)S(1)}, f32[28,16,128]{2,1,0:T(8,128)S(1)}, u32[]{:S(2)}, u32[]{:S(2)}) collective-permute-start(f32[28,16,128]{2,1,0:T(8,128)S(1)} %get-tuple-element.55), channel_id=1, source_target_pairs={{1,2},{3,4},{5,6},{7,8},{9,10},{11,12},{13,14},{17,18},{19,20},{21... | collective-permute-start | bytes 688136 | tf_op jit(solution)/shard_map/ppermute | solution.py:389
  18.7 10.1 %collective-permute-start.7 = (f32[28,16,128]{2,1,0:T(8,128)S(1)}, f32[28,16,128]{2,1,0:T(8,128)S(1)}, u32[]{:S(2)}, u32[]{:S(2)}) collective-permute-start(f32[28,16,128]{2,1,0:T(8,128)S(1)} %get-tuple-element.56), channel_id=1, source_target_pairs={{0,1},{1,0},{2,3},{3,2},{4,5},{5,4},{6,7},{7,6},{8,9},{9,8},{10,11... | collective-permute-start | bytes 688136 | tf_op jit(solution)/shard_map/ppermute | solution.py:386
  25.5 8.7 %collective-permute-start.4 = (f32[28,16,128]{2,1,0:T(8,128)S(1)}, f32[28,16,128]{2,1,0:T(8,128)S(1)}, u32[]{:S(2)}, u32[]{:S(2)}) collective-permute-start(f32[28,16,128]{2,1,0:T(8,128)S(1)} %get-tuple-element.47), channel_id=1, source_target_pairs={{1,2},{3,4},{5,6},{7,8},{9,10},{11,12},{13,14},{17,18},{19,20},{21... | collective-permute-start | bytes 688136 | tf_op jit(solution)/shard_map/ppermute | solution.py:389
  28.8 5.4 %collective-permute-start.5 = (f32[28,16,128]{2,1,0:T(8,128)S(1)}, f32[28,16,128]{2,1,0:T(8,128)S(1)}, u32[]{:S(2)}, u32[]{:S(2)}) collective-permute-start(f32[28,16,128]{2,1,0:T(8,128)S(1)} %get-tuple-element.48), channel_id=1, source_target_pairs={{0,1},{1,0},{2,3},{3,2},{4,5},{5,4},{6,7},{7,6},{8,9},{9,8},{10,11... | collective-permute-start | bytes 688136 | tf_op jit(solution)/shard_map/ppermute | solution.py:386
  33.0 8.0 %collective-permute-start.12 = (f32[28,16,128]{2,1,0:T(8,128)S(1)}, f32[28,16,128]{2,1,0:T(8,128)S(1)}, u32[]{:S(2)}, u32[]{:S(2)}) collective-permute-start(f32[28,16,128]{2,1,0:T(8,128)S(1)} %get-tuple-element.61), channel_id=1, source_target_pairs={{1,2},{3,4},{5,6},{7,8},{9,10},{11,12},{13,14},{17,18},{19,20},{21... | collective-permute-start | bytes 688136 | tf_op jit(solution)/shard_map/ppermute | solution.py:389
  33.2 7.8 %collective-permute-start.13 = (f32[28,16,128]{2,1,0:T(8,128)S(1)}, f32[28,16,128]{2,1,0:T(8,128)S(1)}, u32[]{:S(2)}, u32[]{:S(2)}) collective-permute-start(f32[28,16,128]{2,1,0:T(8,128)S(1)} %get-tuple-element.62), channel_id=1, source_target_pairs={{0,1},{1,0},{2,3},{3,2},{4,5},{5,4},{6,7},{7,6},{8,9},{9,8},{10,11... | collective-permute-start | bytes 688136 | tf_op jit(solution)/shard_map/ppermute | solution.py:386
  38.4 7.5 %collective-permute-start.16 = (f32[16,16,128]{2,1,0:T(8,128)S(1)}, f32[16,16,128]{2,1,0:T(8,128)S(1)}, u32[]{:S(2)}, u32[]{:S(2)}) collective-permute-start(f32[16,16,128]{2,1,0:T(8,128)S(1)} %shard_map.109.s8), channel_id=1, source_target_pairs={{1,2},{3,4},{5,6},{7,8},{9,10},{11,12},{13,14},{17,18},{19,20},{21... | collective-permute-start | bytes 393224 | tf_op jit(solution)/shard_map/ppermute | solution.py:389
  40.9 5.0 %collective-permute-start.14 = (f32[16,16,128]{2,1,0:T(8,128)S(1)}, f32[16,16,128]{2,1,0:T(8,128)S(1)}, u32[]{:S(2)}, u32[]{:S(2)}) collective-permute-start(f32[16,16,128]{2,1,0:T(8,128)S(1)} %shard_map.109.s8), channel_id=1, source_target_pairs={{0,1},{1,0},{2,3},{3,2},{4,5},{5,4},{6,7},{7,6},{8,9},{9,8},{10,11... | collective-permute-start | bytes 393224 | tf_op jit(solution)/shard_map/ppermute | solution.py:386
  45.1 1.5 %collective-permute-start.17 = (f32[16,16,128]{2,1,0:T(8,128)S(1)}, f32[16,16,128]{2,1,0:T(8,128)S(1)}, u32[]{:S(2)}, u32[]{:S(2)}) collective-permute-start(f32[16,16,128]{2,1,0:T(8,128)S(1)} %shard_map.110.r8), channel_id=1, source_target_pairs={{0,1},{1,0},{2,3},{3,2},{4,5},{5,4},{6,7},{7,6},{8,9},{9,8},{10,11... | collective-permute-start | bytes 393224 | tf_op jit(solution)/shard_map/ppermute | solution.py:386
  45.6 5.8 %collective-permute-start.15 = (f32[16,16,128]{2,1,0:T(8,128)S(1)}, f32[16,16,128]{2,1,0:T(8,128)S(1)}, u32[]{:S(2)}, u32[]{:S(2)}) collective-permute-start(f32[16,16,128]{2,1,0:T(8,128)S(1)} %shard_map.110.r8), channel_id=1, source_target_pairs={{1,2},{3,4},{5,6},{7,8},{9,10},{11,12},{13,14},{17,18},{19,20},{21... | collective-permute-start | bytes 393224 | tf_op jit(solution)/shard_map/ppermute | solution.py:389

commit v4 on v3

--- a/solution.py
+++ b/solution.py
@@ -16,7 +16,6 @@
 REACH = 4
 TRIM = HALF - REACH
 LANES = 48
-PAD = 8
 
 SCALE = 5040.0
 WHOLE = (8064.0, -1008.0, 128.0, -9.0)
@@ -57,39 +56,48 @@
     return high, mid, low
 
 
+def weights_of(gap):
+    value = jnp.zeros(gap.shape, f32)
+    for k, weight in enumerate(WHOLE):
+        value = jnp.where(gap == k + 1, weight, value)
+    return value
+
+
 def depth_matrix(nz):
     row = lax.broadcasted_iota(jnp.int32, (nz, nz), 0)
     col = lax.broadcasted_iota(jnp.int32, (nz, nz), 1)
-    gap = jnp.abs(row - col)
-    band = jnp.zeros((nz, nz), f32)
-    for k, weight in enumerate(WHOLE):
-        band = jnp.where(gap == k + 1, weight, band)
+    band = weights_of(jnp.abs(row - col)).astype(bf16)
+    return jnp.concatenate([band, band], axis=0)
+
+
+def cross_matrix(ny):
+    bits = ny.bit_length() - 1
+    row = lax.broadcasted_iota(jnp.int32, (8 * ny, 16 * ny), 0)
+    col = lax.broadcasted_iota(jnp.int32, (8 * ny, 16 * ny), 1)
+    along = jnp.abs(lax.shift_right_logical(col, bits) - lax.shift_right_logical(row, bits) - REACH)
+    aside = jnp.abs(jnp.bitwise_and(col, ny - 1) - jnp.bitwise_and(row, ny - 1))
+    band = jnp.where(aside == 0, weights_of(along), 0.0) + jnp.where(along == 0, weights_of(aside), 0.0)
     band = band.astype(bf16)
-    return jnp.concatenate([band, band], axis=0)
-
-
-def along_depth(refs, r0, depth):
-    _, tall, nz = refs[0].shape
-    ny = tall - 2 * PAD
-    rows = [ref[r0 : r0 + 8, PAD : PAD + ny, :].reshape(8 * ny, nz) for ref in refs]
-    high, low = split2(jnp.concatenate(rows, axis=0))
-    return jnp.dot(jnp.concatenate([high, low], axis=1), depth, preferred_element_type=f32)
-
-
-def across(ref, r0, at, i):
-    total = None
-    for k in range(1, REACH + 1):
-        four = (ref[r0 + i + k, pl.ds(at, 8), :] + ref[r0 + i - k, pl.ds(at, 8), :]) + (
-            ref[r0 + i, pl.ds(at + k, 8), :] + ref[r0 + i, pl.ds(at - k, 8), :]
-        )
-        total = WHOLE[k - 1] * four if total is None else total + WHOLE[k - 1] * four
-    return total
-
-
-def clear_pads(ref):
-    zero = jnp.zeros((ref.shape[0], PAD, ref.shape[2]), f32)
-    ref[:, 0:PAD, :] = zero
-    ref[:, ref.shape[1] - PAD :, :] = zero
+    return jnp.concatenate([band, band], axis=1)
+
+
+def neighbours(high, low, r0, depth, cross):
+    _, ny, both = high.shape
+    nz = both // 2
+    h, l = high[r0 : r0 + 8].reshape(8 * ny, both), low[r0 : r0 + 8].reshape(8 * ny, both)
+    split = [jnp.concatenate([h[:, cut], l[:, cut]], axis=1) for cut in (slice(0, nz), slice(nz, both))]
+    deep = jnp.dot(jnp.concatenate(split, axis=0), depth, preferred_element_type=f32)
+    rows = slice(r0 - REACH, r0 + 8 + REACH)
+    around = jnp.concatenate([high[rows].reshape(16 * ny, both), low[rows].reshape(16 * ny, both)], axis=0)
+    wide = jnp.dot(cross, around, preferred_element_type=f32)
+    return wide[:, 0:nz] + deep[0 : 8 * ny], wide[:, nz:] + deep[8 * ny :]
+
+
+def keep(high, low, rows, plain, scaled):
+    pair = jnp.concatenate([plain, scaled], axis=plain.ndim - 1)
+    h, l = split2(pair)
+    high[rows] = h
+    low[rows] = l
 
 
 def pack_kernel(*refs, count):
@@ -135,13 +143,15 @@
     return total
 
 
-def shots_kernel(shots, fire, wavelet, planes):
+def shots_kernel(shots, fire, wavelet, planes, depth, cross):
     steps, lateral, _ = planes.shape
     taps, ns = wavelet.shape
     delay = lax.broadcasted_iota(jnp.int32, (steps, ns), 0) - fire[...]
     amounts = jnp.zeros((steps, ns), f32)
     for d in range(taps):
         amounts = amounts + jnp.where(delay == d, wavelet[d : d + 1, :], 0.0)
+    depth[...] = depth_matrix(depth.shape[1])
+    cross[...] = cross_matrix(lateral)
     total = spread(shots[...], split3(amounts), lateral, steps)
     planes[:, :, 0:LANES] = total.reshape(steps, lateral, LANES)
 
@@ -173,127 +183,88 @@
 def load_field(dst, own, od, od_lo, ev, ev_lo, n, full):
     p, there = place()
     rows = own.shape[0]
-    inner = slice(PAD, PAD + own.shape[1])
-    dst[rows : 2 * rows, inner, :] = own[...]
+    dst[rows : 2 * rows] = own[...]
     skip = 0 if full else REACH
-    dst[pl.ds(2 * rows * p + skip * (1 - p), n), inner, :] = jnp.where(there, od[od_lo : od_lo + n], 0.0)
-    dst[pl.ds(2 * rows * (1 - p) + skip * p, n), inner, :] = ev[ev_lo : ev_lo + n]
-
-
-def tiles_of(q, first, tiles):
-    y0 = pl.multiple_of(8 * lax.rem(q, tiles), 8)
-    return first + 8 * lax.div(q, tiles), y0, pl.multiple_of(PAD + y0, 8)
-
-
-def run_steps(field, product, coefs, planes, depth, base):
+    dst[pl.ds(2 * rows * p + skip * (1 - p), n)] = jnp.where(there, od[od_lo : od_lo + n], 0.0)
+    dst[pl.ds(2 * rows * (1 - p) + skip * p, n)] = ev[ev_lo : ev_lo + n]
+
+
+def run_steps(field, parts, coefs, planes, depth, cross, base):
     buoy, kb, kk, gg = coefs
-    wide, tall, nz = field[0].shape
-    ny = tall - 2 * PAD
-    tiles = ny // 8
+    wide, ny, nz = field[0].shape
     surface = lax.broadcasted_iota(jnp.int32, (8, nz), 1) == SURFACE
+    band = depth[...], cross[...]
+    for r0 in range(0, wide, 8):
+        rows = slice(r0, r0 + 8)
+        keep(*parts[0], rows, field[0][rows], buoy[rows] * field[0][rows])
     for step in range(IMG_EVERY):
         old, new = field[step % 2], field[1 - step % 2]
-        flux, flux_new = product[step % 2], product[1 - step % 2]
         first = REACH * (step + 1)
         for r0 in range(first, wide - first, 8):
-            deep = along_depth((old, flux), r0, depth)
+            rows = slice(r0, r0 + 8)
+            plain, scaled = neighbours(*parts[step % 2], r0, *band)
+            terms = []
             for i in range(8):
-                r = r0 + i
-                for t in range(tiles):
-                    tile = slice(8 * t, 8 * t + 8)
-                    at = slice(PAD + 8 * t, PAD + 8 * t + 8)
-                    row = ny * i + 8 * t
-                    term = pltpu.roll(planes[base + step, tile, :], (SURFACE - (r - REACH)) % nz, axis=1)
-                    part = gg[r, tile, :] * old[r, at, :] - new[r, at, :] + jnp.where(surface, term, 0.0)
-                    part = part + kb[r, tile, :] * deep[row : row + 8]
-                    new[r, at, :] = part + kk[r, tile, :] * deep[8 * ny + row : 8 * ny + row + 8]
-
-        def chunk(q, carry, old=old, new=new, flux=flux, flux_new=flux_new, step=step, first=first):
-            r0, y0, at = tiles_of(q, first, tiles)
-            tile = pl.ds(y0, 8)
-            for i in range(8):
-                r = r0 + i
-                part = new[r, pl.ds(at, 8), :] + kb[r, tile, :] * across(old, r0, at, i)
-                part = part + kk[r, tile, :] * across(flux, r0, at, i)
-                new[r, pl.ds(at, 8), :] = part
-                if step < IMG_EVERY - 1:
-                    flux_new[r, pl.ds(at, 8), :] = buoy[r, tile, :] * part
-            return carry
-
-        lax.fori_loop(0, tiles * (wide - 2 * first) // 8, chunk, 0)
-
-
-def start_products(field, product, buoy):
-    for ref in (*field, *product):
-        clear_pads(ref)
-    inner = slice(PAD, field[0].shape[1] - PAD)
-    product[0][:, inner, :] = buoy[...] * field[0][:, inner, :]
+                for t in range(ny // 8):
+                    term = pltpu.roll(planes[base + step, 8 * t : 8 * t + 8, :], (SURFACE - (r0 + i - REACH)) % nz, axis=1)
+                    terms.append(jnp.where(surface, term, 0.0))
+            fresh = gg[rows] * old[rows] - new[rows] + jnp.concatenate(terms, axis=0).reshape(8, ny, nz)
+            fresh = fresh + kb[rows] * plain.reshape(8, ny, nz) + kk[rows] * scaled.reshape(8, ny, nz)
+            new[rows] = fresh
+            if step < IMG_EVERY - 1:
+                keep(*parts[1 - step % 2], rows, fresh, buoy[rows] * fresh)
 
 
 def finish(field, n, now_out, before_out, od_out, ev_out):
     p, _ = place()
     last, earlier = field[IMG_EVERY % 2], field[1 - IMG_EVERY % 2]
-    inner = slice(PAD, last.shape[1] - PAD)
-    value = last[n : 2 * n, inner, :]
+    value = last[n : 2 * n]
     now_out[...] = value
-    before_out[...] = earlier[n : 2 * n, inner, :]
+    before_out[...] = earlier[n : 2 * n]
     od_out[0:n] = value
     ev_out[0:n] = value
-    od_out[n:] = earlier[pl.ds(n + REACH * p, TRIM), inner, :]
-    ev_out[n:] = earlier[pl.ds(n + REACH * (1 - p), TRIM), inner, :]
-
-
-def first_kernel(own, prior, stiff, buoy_own, far_own, far_coef, far_prior, ev, planes, now_out, before_out, od_out, ev_out, buoy, kb, kk, gg, f0, f1, p0, p1):
+    od_out[n:] = earlier[pl.ds(n + REACH * p, TRIM)]
+    ev_out[n:] = earlier[pl.ds(n + REACH * (1 - p), TRIM)]
+
+
+def first_kernel(own, prior, stiff, buoy_own, far_own, far_coef, far_prior, ev, planes, depth, cross, now_out, before_out, od_out, ev_out, buoy, kb, kk, gg, f0, f1, h0, l0, h1, l1):
     n, ny, nz = own.shape
-    tiles = ny // 8
-    inner = slice(PAD, PAD + ny)
-    depth = depth_matrix(nz)
-    clear_pads(p1)
-    load_field(p1, buoy_own, far_coef, 0, ev, 0, n, True)
+    band = depth[...], cross[...]
+    load_field(buoy, buoy_own, far_coef, 0, ev, 0, n, True)
     load_field(f1, stiff, far_coef, n, ev, n, TRIM, False)
-    buoy[...] = p1[:, inner, :]
-
+    load_field(f0, own, far_own, 0, ev, n + TRIM, n, True)
+    for r0 in range(0, 3 * n, 8):
+        rows = slice(r0, r0 + 8)
+        keep(h1, l1, rows, buoy[rows], f0[rows])
     for r0 in range(REACH, 3 * n - REACH, 8):
-        gg[r0 : r0 + 8] = along_depth((p1,), r0, depth).reshape(8, ny, nz)
-
-    def coefficients(q, carry):
-        r0, y0, at = tiles_of(q, REACH, tiles)
-        tile = pl.ds(y0, 8)
-        for i in range(8):
-            r = r0 + i
-            b = p1[r, pl.ds(at, 8), :]
-            k = f1[r, pl.ds(at, 8), :] * (0.5 / SCALE)
-            kk[r, tile, :] = k
-            kb[r, tile, :] = k * b
-            gg[r, tile, :] = 2.0 - k * (CENTRE * b + (across(p1, r0, at, i) + gg[r, tile, :]))
-        return carry
-
-    lax.fori_loop(0, tiles * (3 * n - 2 * REACH) // 8, coefficients, 0)
-    load_field(f0, own, far_own, 0, ev, n + TRIM, n, True)
+        rows = slice(r0, r0 + 8)
+        around, _ = neighbours(h1, l1, r0, *band)
+        b = buoy[rows]
+        k = f1[rows] * (0.5 / SCALE)
+        kk[rows] = k
+        kb[rows] = k * b
+        gg[rows] = 2.0 - k * (CENTRE * b + around.reshape(8, ny, nz))
     load_field(f1, prior, far_prior, 0, ev, 2 * n + TRIM, TRIM, False)
-    start_products((f0, f1), (p0, p1), buoy)
-    run_steps((f0, f1), (p0, p1), (buoy, kb, kk, gg), planes, depth, 0)
+    run_steps((f0, f1), ((h0, l0), (h1, l1)), (buoy, kb, kk, gg), planes, depth, cross, 0)
     finish((f0, f1), n, now_out, before_out, od_out, ev_out)
 
 
-def block_steps(own, prior, od, ev, planes, coefs, field, product, base):
-    n, _, nz = own.shape
-    depth = depth_matrix(nz)
+def block_steps(own, prior, od, ev, planes, depth, cross, coefs, field, parts, base):
+    n = own.shape[0]
     load_field(field[0], own, od, 0, ev, 0, n, True)
     load_field(field[1], prior, od, n, ev, n, TRIM, False)
-    start_products(field, product, coefs[0])
-    run_steps(field, product, coefs, planes, depth, base)
-
-
-def block_kernel(own, prior, od, ev, planes, buoy, kb, kk, gg, now_out, before_out, od_out, ev_out, f0, f1, p0, p1, base):
-    block_steps(own, prior, od, ev, planes, (buoy, kb, kk, gg), (f0, f1), (p0, p1), base)
+    run_steps(field, parts, coefs, planes, depth, cross, base)
+
+
+def block_kernel(own, prior, od, ev, planes, depth, cross, buoy, kb, kk, gg, now_out, before_out, od_out, ev_out, f0, f1, h0, l0, h1, l1, base):
+    block_steps(own, prior, od, ev, planes, depth, cross, (buoy, kb, kk, gg), (f0, f1), ((h0, l0), (h1, l1)), base)
     finish((f0, f1), own.shape[0], now_out, before_out, od_out, ev_out)
 
 
-def last_kernel(own, prior, od, ev, planes, buoy, kb, kk, gg, now_out, f0, f1, p0, p1, base):
-    block_steps(own, prior, od, ev, planes, (buoy, kb, kk, gg), (f0, f1), (p0, p1), base)
-    n, ny, _ = own.shape
-    now_out[...] = (f0, f1)[IMG_EVERY % 2][n : 2 * n, PAD : PAD + ny, :]
+def last_kernel(own, prior, od, ev, planes, depth, cross, buoy, kb, kk, gg, now_out, f0, f1, h0, l0, h1, l1, base):
+    block_steps(own, prior, od, ev, planes, depth, cross, (buoy, kb, kk, gg), (f0, f1), ((h0, l0), (h1, l1)), base)
+    n = own.shape[0]
+    now_out[...] = (f0, f1)[IMG_EVERY % 2][n : 2 * n]
 
 
 def lagged(lag_s, lag_r, levels, x, lag):
@@ -441,11 +412,11 @@
         gathered = jnp.concatenate([gathered, exchange(gathered, which)], axis=0)
 
     plane = shape(STEPS, ny, nz)
-    plane_s = pl.pallas_call(
+    plane_s, *band = pl.pallas_call(
         shots_kernel,
-        out_shape=plane,
+        out_shape=[plane, jax.ShapeDtypeStruct((2 * nz, nz), bf16), jax.ShapeDtypeStruct((8 * ny, 32 * ny), bf16)],
         in_specs=vmem_specs(3),
-        out_specs=pl.BlockSpec(memory_space=pltpu.VMEM),
+        out_specs=vmem_specs(3),
         compiler_params=params(8),
         cost_estimate=estimate(1000000, 100000),
         name="shots",
@@ -462,32 +433,32 @@
     )(cells, gathered)
 
     wide = 3 * n
-    scratch = [pltpu.VMEM((wide, ny + 2 * PAD, nz), f32)] * 4
+    scratch = [pltpu.VMEM((wide, ny, nz), f32)] * 2 + [pltpu.VMEM((wide, ny, 2 * nz), bf16)] * 4
     cost = estimate(224 * 8 * 128 * 60, 6000000)
     own = shape(n, ny, nz)
     s4, s3, ods, evs, buoy, kb, kk, gg = pl.pallas_call(
         first_kernel,
         out_shape=[own, own, shape(small, ny, nz), shape(small, ny, nz)] + [shape(wide, ny, nz)] * 4,
-        in_specs=vmem_specs(9),
+        in_specs=vmem_specs(11),
         out_specs=vmem_specs(8),
         scratch_shapes=scratch,
         compiler_params=params(16),
         cost_estimate=cost,
         name="first_s",
-    )(source_field, source_prior, stiffness, buoyancy, far_s0, far_coef, far_prior, ev1, plane_s)
+    )(source_field, source_prior, stiffness, buoyancy, far_s0, far_coef, far_prior, ev1, plane_s, *band)
     coefs = (buoy, kb, kk, gg)
     ods = swap_far(ods)
     evs = swap_near(evs)
     r4, r3, odr, evr = pl.pallas_call(
         functools.partial(block_kernel, base=0),
         out_shape=[own, own, shape(small, ny, nz), shape(small, ny, nz)],
-        in_specs=vmem_specs(9),
+        in_specs=vmem_specs(11),
         out_specs=vmem_specs(4),
         scratch_shapes=scratch,
         compiler_params=params(16),
         cost_estimate=cost,
         name="first_r",
-    )(receiver_field, receiver_prior, far_r, ev2, plane_r, *coefs)
+    )(receiver_field, receiver_prior, far_r, ev2, plane_r, *band, *coefs)
     odr = swap_far(odr)
     evr = swap_near(evr)
 
@@ -495,17 +466,17 @@
         return pl.pallas_call(
             functools.partial(last_kernel, base=IMG_EVERY),
             out_shape=own,
-            in_specs=vmem_specs(9),
+            in_specs=vmem_specs(11),
             out_specs=pl.BlockSpec(memory_space=pltpu.VMEM),
             scratch_shapes=scratch,
             compiler_params=params(16),
             cost_estimate=cost,
         )
 
-    s8 = last()(s4, s3, ods, evs, plane_s, *coefs)
+    s8 = last()(s4, s3, ods, evs, plane_s, *band, *coefs)
     ods8 = swap_far(s8)
     evs8 = swap_near(s8)
-    r8 = last()(r4, r3, odr, evr, plane_r, *coefs)
+    r8 = last()(r4, r3, odr, evr, plane_r, *band, *coefs)
     odr8 = swap_far(r8)
     evr8 = swap_near(r8)
     lags = lambda levels, blocks: [

time: 53.1 us -> 46.8 us (0.88)
  the two profiles are of different devices: /device:TPU:9 before, /device:TPU:19 now
where the time goes in v4:
time: 46.8 us; the launch traced here: 46.6 us
  waiting for transfers between devices  18.5 us (40%)
  starting transfers between devices  15.6 us (33%)
  Pallas kernels  12.4 us (26%)
    ppermute x8, waiting for transfers between devices, swap_far(): return lax.ppermute(x, ('shot', 'gx'), far)  12.5 us
    ppermute x4, starting transfers between devices, exchange(): return lax.ppermute(x, 'gx', [(i, i ^ hops[which]) for i in range(count)])  8.08 us
    ppermute x4, waiting for transfers between devices, exchange(): return lax.ppermute(x, 'gx', [(i, i ^ hops[which]) for i in range(count)])  5.21 us
    ppermute x8, starting transfers between devices, swap_far(): return lax.ppermute(x, ('shot', 'gx'), far)  4.92 us
    ppermute x6, starting transfers between devices, swap_near(): return lax.ppermute(x, 'gx', near)  2.61 us
    pallas_call x1, Pallas kernels, local(): pl.pallas_call(image_kernel, out_shape=[shape(NOFF, n, ny, nz), shape(HAL...  1.9 us
    pallas_call x1, Pallas kernels, local(): pl.pallas_call(first_kernel, out_shape=[own, own, shape(small, ny, nz), s...  1.75 us
    pallas_call x1, Pallas kernels, local(): pl.pallas_call(functools.partial(receivers_kernel, hops=tuple(hops)), out...  1.64 us
  transfers between devices with their start and end apart: 18, of which 9 were waited for; matrix products, arithmetic and copies ran while one was open for 0% of the time, Pallas kernels for 23%

profile of v4, /device:TPU:19, one launch (start us, length us, event | category | flops | bytes accessed | tf_op | source)
XLA Modules:
  0.0 46.6 jit_solution(3044349909176596685)
XLA Ops:
  0.0 1.2 %collective-permute-start.8 = (f32[1,8,128]{2,1,0:T(8,128)}, f32[1,8,128]{2,1,0:T(8,128)S(1)}, u32[]{:S(2)}, u32[]{:S(2)}) collective-permute-start(f32[1,8,128]{2,1,0:T(8,128)} %bitcast.7), channel_id=1, source_target_pairs={{0,2},{1,3},{2,0},{3,1},{4,6},{5,7},{6,4},{7,5},{8,10},{9,11},{10,... | collective-permute-start | bytes 12296 | tf_op jit(solution)/shard_map/ppermute | solution.py:370
  1.2 1.1 %collective-permute-start = (f32[16,16,128]{2,1,0:T(8,128)}, f32[16,16,128]{2,1,0:T(8,128)S(1)}, u32[]{:S(2)}, u32[]{:S(2)}) collective-permute-start(f32[16,16,128]{2,1,0:T(8,128)} %refs_0_.1), channel_id=1, source_target_pairs={{1,2},{3,4},{5,6},{7,8},{9,10},{11,12},{13,14},{17,18},{19,20},{21... | collective-permute-start | bytes 393224 | tf_op jit(solution)/shard_map/ppermute | solution.py:360
  2.3 1.4 %pack.1 = (f32[16,16,128]{2,1,0:T(8,128)S(1)}, f32[16,16,128]{2,1,0:T(8,128)S(1)}, f32[16,16,128]{2,1,0:T(8,128)S(1)}, f32[16,16,128]{2,1,0:T(8,128)S(1)}, f32[1...) custom-call(f32[16,16,128]{2,1,0:T(8,128)} %refs_0_.1, ...), custom_call_target="tpu_custom_call" | custom-call | flops 1000 | bytes 3000000 | tf_op jit(solution)/shard_map/pack/pallas_call | solution.py:391
  3.7 0.7 %collective-permute-start.2 = (f32[12,16,128]{2,1,0:T(8,128)S(1)}, f32[12,16,128]{2,1,0:T(8,128)S(1)}, u32[]{:S(2)}, u32[]{:S(2)}) collective-permute-start(f32[12,16,128]{2,1,0:T(8,128)S(1)} %get-tuple-element.43), channel_id=1, source_target_pairs={{1,2},{3,4},{5,6},{7,8},{9,10},{11,12},{13,14},{17,18},{19,20},{21... | collective-permute-start | bytes 294920 | tf_op jit(solution)/shard_map/ppermute | solution.py:360
  4.4 1.1 %collective-permute-start.1 = (f32[28,16,128]{2,1,0:T(8,128)S(1)}, f32[28,16,128]{2,1,0:T(8,128)S(1)}, u32[]{:S(2)}, u32[]{:S(2)}) collective-permute-start(f32[28,16,128]{2,1,0:T(8,128)S(1)} %get-tuple-element.42), channel_id=1, source_target_pairs={{1,2},{3,4},{5,6},{7,8},{9,10},{11,12},{13,14},{17,18},{19,20},{21... | collective-permute-start | bytes 688136 | tf_op jit(solution)/shard_map/ppermute | solution.py:360
  5.5 0.9 %collective-permute-start.3 = (f32[56,16,128]{2,1,0:T(8,128)S(1)}, f32[56,16,128]{2,1,0:T(8,128)S(1)}, u32[]{:S(2)}, u32[]{:S(2)}) collective-permute-start(f32[56,16,128]{2,1,0:T(8,128)S(1)} %get-tuple-element.44), channel_id=1, source_target_pairs={{0,1},{1,0},{2,3},{3,2},{4,5},{5,4},{6,7},{7,6},{8,9},{9,8},{10,11... | collective-permute-start | bytes 1376264 | tf_op jit(solution)/shard_map/ppermute | solution.py:357
  6.4 0.0 collective-permute-done.8
  6.4 1.3 %collective-permute-start.9 = (f32[2,8,128]{2,1,0:T(8,128)S(1)}, f32[2,8,128]{2,1,0:T(8,128)S(1)}, u32[]{:S(2)}, u32[]{:S(2)}) collective-permute-start(f32[2,8,128]{2,1,0:T(8,128)S(1)} %pad_maximum_fusion.2), channel_id=1, source_target_pairs={{0,4},{1,5},{2,6},{3,7},{4,0},{5,1},{6,2},{7,3},{8,12},{9,13},{10,... | collective-permute-start | bytes 24584 | tf_op jit(solution)/shard_map/ppermute | solution.py:370
  7.7 0.3 shots.1
  8.0 1.0 %collective-permute-done.9 = f32[2,8,128]{2,1,0:T(8,128)S(1)} collective-permute-done((f32[2,8,128]{2,1,0:T(8,128)S(1)}, f32[2,8,128]{2,1,0:T(8,128)S(1)}, u32[]{:S(2)}, u32[]{:S(2)}) %collective-permute-start.9) | collective-permute-done | bytes 8224 | tf_op jit(solution)/shard_map/ppermute | solution.py:370
  9.0 0.1 collective-permute-start.10
  9.1 3.4 %collective-permute-done.10 = f32[4,8,128]{2,1,0:T(8,128)S(1)} collective-permute-done((f32[4,8,128]{2,1,0:T(8,128)S(1)}, f32[4,8,128]{2,1,0:T(8,128)S(1)}, u32[]{:S(2)}, u32[]{:S(2)}) %collective-permute-start.10) | collective-permute-done | bytes 16416 | tf_op jit(solution)/shard_map/ppermute | solution.py:370
  12.5 5.4 %collective-permute-start.11 = (f32[8,8,128]{2,1,0:T(8,128)S(1)}, f32[8,8,128]{2,1,0:T(8,128)S(1)}, u32[]{:S(2)}, u32[]{:S(2)}) collective-permute-start(f32[8,8,128]{2,1,0:T(8,128)S(1)} %pad_maximum_fusion), channel_id=1, source_target_pairs={{0,1},{1,0},{2,3},{3,2},{4,5},{5,4},{6,7},{7,6},{8,9},{9,8},{10,11... | collective-permute-start | bytes 98312 | tf_op jit(solution)/shard_map/ppermute | solution.py:370
  17.9 0.9 %collective-permute-done.11 = f32[8,8,128]{2,1,0:T(8,128)S(1)} collective-permute-done((f32[8,8,128]{2,1,0:T(8,128)S(1)}, f32[8,8,128]{2,1,0:T(8,128)S(1)}, u32[]{:S(2)}, u32[]{:S(2)}) %collective-permute-start.11) | collective-permute-done | bytes 32800 | tf_op jit(solution)/shard_map/ppermute | solution.py:370
  18.8 0.0 collective-permute-start.6
  18.8 0.0 collective-permute-done.2.far_prior
  18.8 0.3 collective-permute-start.7
  19.1 1.6 %receivers.1.planes = f32[8,16,128]{2,1,0:T(8,128)S(1)} custom-call(s32[16,128]{1,0:T(8,128)S(1)} %get-tuple-element.63.cells, f32[16,8,128]{2,1,0:T(8,128)S(1)} %constant_dynamic-update-slice_fusion.traces), custom_call_target="tpu_custom_call" | custom-call | flops 25165824 | bytes 1000000 | tf_op jit(solution)/shard_map/receivers/pallas_call | solution.py:424
  20.8 0.0 collective-permute-done.far_own.far_s0
  20.8 0.0 collective-permute-done.1.far_coef
  20.8 0.0 collective-permute-done.3.ev.ev1
  20.8 1.7 %first_s.1 = (f32[16,16,128]{2,1,0:T(8,128)S(1)}, f32[16,16,128]{2,1,0:T(8,128)S(1)}, f32[28,16,128]{2,1,0:T(8,128)S(1)}, f32[28,16,128]{2,1,0:T(8,128)S(1)}, f3...) custom-call(f32[16,16,128]{2,1,0:T(8,128)S(1)} %get-tuple-element.38, ...), custom_call_target="tpu_custom_call" | custom-call | flops 13762560 | bytes 6000000 | tf_op jit(solution)/shard_map/first_s/pallas_call | solution.py:439
  22.6 1.5 %collective-permute-start.4 = (f32[28,16,128]{2,1,0:T(8,128)S(1)}, f32[28,16,128]{2,1,0:T(8,128)S(1)}, u32[]{:S(2)}, u32[]{:S(2)}) collective-permute-start(f32[28,16,128]{2,1,0:T(8,128)S(1)} %get-tuple-element.53), channel_id=1, source_target_pairs={{1,2},{3,4},{5,6},{7,8},{9,10},{11,12},{13,14},{17,18},{19,20},{21... | collective-permute-start | bytes 688136 | tf_op jit(solution)/shard_map/ppermute | solution.py:360
  24.1 1.3 %collective-permute-start.5 = (f32[28,16,128]{2,1,0:T(8,128)S(1)}, f32[28,16,128]{2,1,0:T(8,128)S(1)}, u32[]{:S(2)}, u32[]{:S(2)}) collective-permute-start(f32[28,16,128]{2,1,0:T(8,128)S(1)} %get-tuple-element.54), channel_id=1, source_target_pairs={{0,1},{1,0},{2,3},{3,2},{4,5},{5,4},{6,7},{7,6},{8,9},{9,8},{10,11... | collective-permute-start | bytes 688136 | tf_op jit(solution)/shard_map/ppermute | solution.py:357
  25.3 3.8 %collective-permute-done.6.od.far_r = f32[28,16,128]{2,1,0:T(8,128)S(1)} collective-permute-done((f32[28,16,128]{2,1,0:T(8,128)S(1)}, f32[28,16,128]{2,1,0:T(8,128)S(1)}, u32[]{:S(2)}, u32[]{:S(2)}) %collective-permute-start.6) | collective-permute-done | bytes 229408 | tf_op jit(solution)/shard_map/ppermute | solution.py:360
  29.1 0.0 collective-permute-done.7.ev.ev2
  29.1 1.3 %first_r.1 = (f32[16,16,128]{2,1,0:T(8,128)S(1)}, f32[16,16,128]{2,1,0:T(8,128)S(1)}, f32[28,16,128]{2,1,0:T(8,128)S(1)}, f32[28,16,128]{2,1,0:T(8,128)S(1)}) custom-call(f32[16,16,128]{2,1,0:T(8,128)S(1)} %get-tuple-element.59.own.r0, f32[16,16,128]{2,1,0:T(8,128)S(1)} %get-tuple-element.60.prior, f32[28,16,128]{2,1,0:T(8,128)S(1)} %collective-permute-done.6.od.far_r, ...), custom_call_target="tpu_custom_call" | custom-call | flops 13762560 | bytes 6000000 | tf_op jit(solution)/shard_map/first_r/pallas_call | solution.py:452
  30.5 0.1 collective-permute-start.12
  30.5 0.1 collective-permute-start.13
  30.6 3.4 %collective-permute-done.4.od.ods = f32[28,16,128]{2,1,0:T(8,128)S(1)} collective-permute-done((f32[28,16,128]{2,1,0:T(8,128)S(1)}, f32[28,16,128]{2,1,0:T(8,128)S(1)}, u32[]{:S(2)}, u32[]{:S(2)}) %collective-permute-start.4) | collective-permute-done | bytes 229408 | tf_op jit(solution)/shard_map/ppermute | solution.py:360
  34.1 0.0 collective-permute-done.5.ev.evs
  34.1 1.3 %shard_map.109.s8 = f32[16,16,128]{2,1,0:T(8,128)S(1)} custom-call(f32[16,16,128]{2,1,0:T(8,128)S(1)} %get-tuple-element.51.own.s4, f32[16,16,128]{2,1,0:T(8,128)S(1)} %get-tuple-element.52.prior, f32[28,16,128]{2,1,0:T(8,128)S(1)} %collective-permute-done.4.od.ods, f32[28,16,128]{2,1,0:T(8,128)S(1)} %collective-permute-done.5.ev.evs, ...), custom_call_target="tpu_custom_call" | custom-call | flops 13762560 | bytes 6000000 | tf_op jit(solution)/shard_map/pallas_call | solution.py:476
  35.3 0.4 collective-permute-start.16
  35.8 0.0 collective-permute-start.14
  35.8 2.2 %collective-permute-done.12.od.odr = f32[28,16,128]{2,1,0:T(8,128)S(1)} collective-permute-done((f32[28,16,128]{2,1,0:T(8,128)S(1)}, f32[28,16,128]{2,1,0:T(8,128)S(1)}, u32[]{:S(2)}, u32[]{:S(2)}) %collective-permute-start.12) | collective-permute-done | bytes 229408 | tf_op jit(solution)/shard_map/ppermute | solution.py:360
  37.9 0.0 collective-permute-done.13.ev.evr
  37.9 1.3 %shard_map.110.r8 = f32[16,16,128]{2,1,0:T(8,128)S(1)} custom-call(f32[16,16,128]{2,1,0:T(8,128)S(1)} %get-tuple-element.65.own.r4, f32[16,16,128]{2,1,0:T(8,128)S(1)} %get-tuple-element.66.prior, f32[28,16,128]{2,1,0:T(8,128)S(1)} %collective-permute-done.12.od.odr, f32[28,16,128]{2,1,0:T(8,128)S(1)} %collective-permute-done.13.ev.evr, ...), custom_call_target="tpu_custom_call" | custom-call | flops 13762560 | bytes 6000000 | tf_op jit(solution)/shard_map/pallas_call | solution.py:479
  39.2 0.1 collective-permute-start.17
  39.3 0.1 collective-permute-start.15
  39.4 0.4 collective-permute-done.16.ods8
  39.8 0.0 collective-permute-done.14.evs8
  39.8 0.8 %collective-permute-done.17.evr8 = f32[16,16,128]{2,1,0:T(8,128)S(1)} collective-permute-done((f32[16,16,128]{2,1,0:T(8,128)S(1)}, f32[16,16,128]{2,1,0:T(8,128)S(1)}, u32[]{:S(2)}, u32[]{:S(2)}) %collective-permute-start.17) | collective-permute-done | bytes 131104 | tf_op jit(solution)/shard_map/ppermute | solution.py:357
  40.6 1.9 %image.1 = (f32[33,16,16,128]{3,2,1,0:T(8,128)}, f32[16,16,16,128]{3,2,1,0:T(8,128)S(1)}) custom-call(f32[16,16,128]{2,1,0:T(8,128)S(1)} %get-tuple-element.38.own.s0, f32[16,16,128]{2,1,0:T(8,128)S(1)} %get-tuple-element.51.own.s4, f32[16,16,128]{2,1,0:T(8,128)S(1)} %shard_map.109.s8, f32[16,16,128]{2,1,0:T(8,128)S(1)} %get-tuple-element.59.own.r0, ...), custom_call_target="tpu_custom_call" | custom-call | flops 4325376 | bytes 4400000 | tf_op jit(solution)/shard_map/image/pallas_call | solution.py:489
  42.5 2.6 %collective-permute-done.15.odr8 = f32[16,16,128]{2,1,0:T(8,128)S(1)} collective-permute-done((f32[16,16,128]{2,1,0:T(8,128)S(1)}, f32[16,16,128]{2,1,0:T(8,128)S(1)}, u32[]{:S(2)}, u32[]{:S(2)}) %collective-permute-start.15) | collective-permute-done | bytes 131104 | tf_op jit(solution)/shard_map/ppermute | solution.py:360
  45.1 1.5 %last_image.1 = f32[33,16,16,128]{3,2,1,0:T(8,128)} custom-call(f32[16,16,128]{2,1,0:T(8,128)S(1)} %shard_map.109.s8, f32[16,16,128]{2,1,0:T(8,128)S(1)} %shard_map.110.r8, f32[16,16,128]{2,1,0:T(8,128)S(1)} %collective-permute-done.14.evs8, f32[16,16,128]{2,1,0:T(8,128)S(1)} %collective-permute-done.15.odr8, ...), custom_call_target="tpu_custom_call", output_to_operand_aliasing={{}: (5, {})} | custom-call | flops 1048576 | bytes 2200000 | tf_op jit(solution)/shard_map/last_image/pallas_call | solution.py:499
  (8 shorter events, 0.0 us)
Async XLA Ops:
  0.0 6.4 %collective-permute-start.8 = (f32[1,8,128]{2,1,0:T(8,128)}, f32[1,8,128]{2,1,0:T(8,128)S(1)}, u32[]{:S(2)}, u32[]{:S(2)}) collective-permute-start(f32[1,8,128]{2,1,0:T(8,128)} %bitcast.7), channel_id=1, source_target_pairs={{0,2},{1,3},{2,0},{3,1},{4,6},{5,7},{6,4},{7,5},{8,10},{9,11},{10,... | collective-permute-start | bytes 12296 | tf_op jit(solution)/shard_map/ppermute | solution.py:370
  1.2 19.6 %collective-permute-start = (f32[16,16,128]{2,1,0:T(8,128)}, f32[16,16,128]{2,1,0:T(8,128)S(1)}, u32[]{:S(2)}, u32[]{:S(2)}) collective-permute-start(f32[16,16,128]{2,1,0:T(8,128)} %refs_0_.1), channel_id=1, source_target_pairs={{1,2},{3,4},{5,6},{7,8},{9,10},{11,12},{13,14},{17,18},{19,20},{21... | collective-permute-start | bytes 393224 | tf_op jit(solution)/shard_map/ppermute | solution.py:360
  3.7 15.1 %collective-permute-start.2 = (f32[12,16,128]{2,1,0:T(8,128)S(1)}, f32[12,16,128]{2,1,0:T(8,128)S(1)}, u32[]{:S(2)}, u32[]{:S(2)}) collective-permute-start(f32[12,16,128]{2,1,0:T(8,128)S(1)} %get-tuple-element.43), channel_id=1, source_target_pairs={{1,2},{3,4},{5,6},{7,8},{9,10},{11,12},{13,14},{17,18},{19,20},{21... | collective-permute-start | bytes 294920 | tf_op jit(solution)/shard_map/ppermute | solution.py:360
  4.4 16.4 %collective-permute-start.1 = (f32[28,16,128]{2,1,0:T(8,128)S(1)}, f32[28,16,128]{2,1,0:T(8,128)S(1)}, u32[]{:S(2)}, u32[]{:S(2)}) collective-permute-start(f32[28,16,128]{2,1,0:T(8,128)S(1)} %get-tuple-element.42), channel_id=1, source_target_pairs={{1,2},{3,4},{5,6},{7,8},{9,10},{11,12},{13,14},{17,18},{19,20},{21... | collective-permute-start | bytes 688136 | tf_op jit(solution)/shard_map/ppermute | solution.py:360
  5.5 15.3 %collective-permute-start.3 = (f32[56,16,128]{2,1,0:T(8,128)S(1)}, f32[56,16,128]{2,1,0:T(8,128)S(1)}, u32[]{:S(2)}, u32[]{:S(2)}) collective-permute-start(f32[56,16,128]{2,1,0:T(8,128)S(1)} %get-tuple-element.44), channel_id=1, source_target_pairs={{0,1},{1,0},{2,3},{3,2},{4,5},{5,4},{6,7},{7,6},{8,9},{9,8},{10,11... | collective-permute-start | bytes 1376264 | tf_op jit(solution)/shard_map/ppermute | solution.py:357
  6.4 2.6 %collective-permute-start.9 = (f32[2,8,128]{2,1,0:T(8,128)S(1)}, f32[2,8,128]{2,1,0:T(8,128)S(1)}, u32[]{:S(2)}, u32[]{:S(2)}) collective-permute-start(f32[2,8,128]{2,1,0:T(8,128)S(1)} %pad_maximum_fusion.2), channel_id=1, source_target_pairs={{0,4},{1,5},{2,6},{3,7},{4,0},{5,1},{6,2},{7,3},{8,12},{9,13},{10,... | collective-permute-start | bytes 24584 | tf_op jit(solution)/shard_map/ppermute | solution.py:370
  9.0 3.5 %collective-permute-start.10 = (f32[4,8,128]{2,1,0:T(8,128)S(1)}, f32[4,8,128]{2,1,0:T(8,128)S(1)}, u32[]{:S(2)}, u32[]{:S(2)}) collective-permute-start(f32[4,8,128]{2,1,0:T(8,128)S(1)} %pad_maximum_fusion.1), channel_id=1, source_target_pairs={{0,8},{1,9},{2,10},{3,11},{4,12},{5,13},{6,14},{7,15},{8,0},{9,1},... | collective-permute-start | bytes 49160 | tf_op jit(solution)/shard_map/ppermute | solution.py:370
  12.5 6.3 %collective-permute-start.11 = (f32[8,8,128]{2,1,0:T(8,128)S(1)}, f32[8,8,128]{2,1,0:T(8,128)S(1)}, u32[]{:S(2)}, u32[]{:S(2)}) collective-permute-start(f32[8,8,128]{2,1,0:T(8,128)S(1)} %pad_maximum_fusion), channel_id=1, source_target_pairs={{0,1},{1,0},{2,3},{3,2},{4,5},{5,4},{6,7},{7,6},{8,9},{9,8},{10,11... | collective-permute-start | bytes 98312 | tf_op jit(solution)/shard_map/ppermute | solution.py:370
  18.8 10.4 %collective-permute-start.6 = (f32[28,16,128]{2,1,0:T(8,128)S(1)}, f32[28,16,128]{2,1,0:T(8,128)S(1)}, u32[]{:S(2)}, u32[]{:S(2)}) collective-permute-start(f32[28,16,128]{2,1,0:T(8,128)S(1)} %get-tuple-element.61), channel_id=1, source_target_pairs={{1,2},{3,4},{5,6},{7,8},{9,10},{11,12},{13,14},{17,18},{19,20},{21... | collective-permute-start | bytes 688136 | tf_op jit(solution)/shard_map/ppermute | solution.py:360
  18.8 10.4 %collective-permute-start.7 = (f32[28,16,128]{2,1,0:T(8,128)S(1)}, f32[28,16,128]{2,1,0:T(8,128)S(1)}, u32[]{:S(2)}, u32[]{:S(2)}) collective-permute-start(f32[28,16,128]{2,1,0:T(8,128)S(1)} %get-tuple-element.62), channel_id=1, source_target_pairs={{0,1},{1,0},{2,3},{3,2},{4,5},{5,4},{6,7},{7,6},{8,9},{9,8},{10,11... | collective-permute-start | bytes 688136 | tf_op jit(solution)/shard_map/ppermute | solution.py:357
  22.6 11.5 %collective-permute-start.4 = (f32[28,16,128]{2,1,0:T(8,128)S(1)}, f32[28,16,128]{2,1,0:T(8,128)S(1)}, u32[]{:S(2)}, u32[]{:S(2)}) collective-permute-start(f32[28,16,128]{2,1,0:T(8,128)S(1)} %get-tuple-element.53), channel_id=1, source_target_pairs={{1,2},{3,4},{5,6},{7,8},{9,10},{11,12},{13,14},{17,18},{19,20},{21... | collective-permute-start | bytes 688136 | tf_op jit(solution)/shard_map/ppermute | solution.py:360
  24.1 10.0 %collective-permute-start.5 = (f32[28,16,128]{2,1,0:T(8,128)S(1)}, f32[28,16,128]{2,1,0:T(8,128)S(1)}, u32[]{:S(2)}, u32[]{:S(2)}) collective-permute-start(f32[28,16,128]{2,1,0:T(8,128)S(1)} %get-tuple-element.54), channel_id=1, source_target_pairs={{0,1},{1,0},{2,3},{3,2},{4,5},{5,4},{6,7},{7,6},{8,9},{9,8},{10,11... | collective-permute-start | bytes 688136 | tf_op jit(solution)/shard_map/ppermute | solution.py:357
  30.5 7.5 %collective-permute-start.12 = (f32[28,16,128]{2,1,0:T(8,128)S(1)}, f32[28,16,128]{2,1,0:T(8,128)S(1)}, u32[]{:S(2)}, u32[]{:S(2)}) collective-permute-start(f32[28,16,128]{2,1,0:T(8,128)S(1)} %get-tuple-element.67), channel_id=1, source_target_pairs={{1,2},{3,4},{5,6},{7,8},{9,10},{11,12},{13,14},{17,18},{19,20},{21... | collective-permute-start | bytes 688136 | tf_op jit(solution)/shard_map/ppermute | solution.py:360
  30.5 7.4 %collective-permute-start.13 = (f32[28,16,128]{2,1,0:T(8,128)S(1)}, f32[28,16,128]{2,1,0:T(8,128)S(1)}, u32[]{:S(2)}, u32[]{:S(2)}) collective-permute-start(f32[28,16,128]{2,1,0:T(8,128)S(1)} %get-tuple-element.68), channel_id=1, source_target_pairs={{0,1},{1,0},{2,3},{3,2},{4,5},{5,4},{6,7},{7,6},{8,9},{9,8},{10,11... | collective-permute-start | bytes 688136 | tf_op jit(solution)/shard_map/ppermute | solution.py:357
  35.3 4.5 %collective-permute-start.16 = (f32[16,16,128]{2,1,0:T(8,128)S(1)}, f32[16,16,128]{2,1,0:T(8,128)S(1)}, u32[]{:S(2)}, u32[]{:S(2)}) collective-permute-start(f32[16,16,128]{2,1,0:T(8,128)S(1)} %shard_map.109.s8), channel_id=1, source_target_pairs={{1,2},{3,4},{5,6},{7,8},{9,10},{11,12},{13,14},{17,18},{19,20},{21... | collective-permute-start | bytes 393224 | tf_op jit(solution)/shard_map/ppermute | solution.py:360
  35.8 4.0 %collective-permute-start.14 = (f32[16,16,128]{2,1,0:T(8,128)S(1)}, f32[16,16,128]{2,1,0:T(8,128)S(1)}, u32[]{:S(2)}, u32[]{:S(2)}) collective-permute-start(f32[16,16,128]{2,1,0:T(8,128)S(1)} %shard_map.109.s8), channel_id=1, source_target_pairs={{0,1},{1,0},{2,3},{3,2},{4,5},{5,4},{6,7},{7,6},{8,9},{9,8},{10,11... | collective-permute-start | bytes 393224 | tf_op jit(solution)/shard_map/ppermute | solution.py:357
  39.2 1.4 %collective-permute-start.17 = (f32[16,16,128]{2,1,0:T(8,128)S(1)}, f32[16,16,128]{2,1,0:T(8,128)S(1)}, u32[]{:S(2)}, u32[]{:S(2)}) collective-permute-start(f32[16,16,128]{2,1,0:T(8,128)S(1)} %shard_map.110.r8), channel_id=1, source_target_pairs={{0,1},{1,0},{2,3},{3,2},{4,5},{5,4},{6,7},{7,6},{8,9},{9,8},{10,11... | collective-permute-start | bytes 393224 | tf_op jit(solution)/shard_map/ppermute | solution.py:357
  39.3 5.9 %collective-permute-start.15 = (f32[16,16,128]{2,1,0:T(8,128)S(1)}, f32[16,16,128]{2,1,0:T(8,128)S(1)}, u32[]{:S(2)}, u32[]{:S(2)}) collective-permute-start(f32[16,16,128]{2,1,0:T(8,128)S(1)} %shard_map.110.r8), channel_id=1, source_target_pairs={{1,2},{3,4},{5,6},{7,8},{9,10},{11,12},{13,14},{17,18},{19,20},{21... | collective-permute-start | bytes 393224 | tf_op jit(solution)/shard_map/ppermute | solution.py:360

commit v5 on v4

--- a/solution.py
+++ b/solution.py
@@ -275,16 +275,13 @@
     return total
 
 
-def write_out(block, out, sems, count, target):
-    def drain(j, carry):
-        pltpu.make_async_copy(block.at[j], out.at[target(j)], sems.at[j]).wait()
-        return carry
-
-    lax.fori_loop(0, count, drain, 0)
+def sides():
+    p, there = place()
+    return p, there, 1 - 2 * p, lambda reach: (HALF - reach) * p, lambda reach: reach * (1 - p)
 
 
 def image_kernel(s0, s4, s8, r0, r4, r8, far_s0, ev1, far_r, ev2, ods, evs, odr, evr, ods8, evs8, evr8, out, rest, lag_s, lag_r, block, sems):
-    p, there = place()
+    p, there, sign, far_start, own_start = sides()
     n = s0.shape[0]
     left, right = pl.ds(2 * n * p, n), pl.ds(2 * n * (1 - p), n)
     groups = (
@@ -300,44 +297,52 @@
         if od is not None:
             dst[level, left] = jnp.where(there, od[od_lo : od_lo + n], 0.0)
         dst[level, right] = ev[ev_lo : ev_lo + n]
-    sign = 1 - 2 * p
-    target = lambda j: HALF + sign * j
+    move = lambda j: pltpu.make_async_copy(block.at[j], out.at[HALF + sign * j], sems.at[j])
 
     def whole(j, carry):
         for x in range(n):
             block[j, x] = lagged(lag_s, lag_r, (0, 1, 2), x, sign * j)
-        pltpu.make_async_copy(block.at[j], out.at[target(j)], sems.at[j]).start()
+        move(j).start()
         return carry
 
     lax.fori_loop(0, HALF + 1, whole, 0)
-
-    def partial(j, carry):
-        for x in range(n):
-            rest[j, x] = lagged(lag_s, lag_r, (0, 1), x, -sign * (j + 1))
+    moves = []
+    for reach in range(1, HALF):
+        for i in range(n - reach):
+            block[HALF + reach, i] = lagged(lag_s, lag_r, (0, 1, 2), own_start(reach) + i, -sign * reach)
+        target = out.at[HALF - sign * reach, pl.ds(own_start(reach), n - reach)]
+        moves.append(pltpu.make_async_copy(block.at[HALF + reach, 0 : n - reach], target, sems.at[HALF + reach]))
+        moves[-1].start()
+    for reach in range(1, HALF + 1):
+        for i in range(reach):
+            rest[reach * (reach - 1) // 2 + i] = lagged(lag_s, lag_r, (0, 1), far_start(reach) + i, -sign * reach)
+
+    def drain(j, carry):
+        move(j).wait()
         return carry
 
-    lax.fori_loop(0, HALF, partial, 0)
-    write_out(block, out, sems, HALF + 1, target)
+    lax.fori_loop(0, HALF + 1, drain, 0)
+    for each in moves:
+        each.wait()
 
 
 def last_image_kernel(s8, r8, evs8, odr8, rest, before, out, lag_s, lag_r, block, sems):
-    p, there = place()
+    p, there, sign, far_start, _ = sides()
     n = s8.shape[0]
     lag_s[0, n : 2 * n] = s8[...]
     lag_s[0, pl.ds(2 * n * (1 - p), n)] = evs8[...]
     lag_r[0, n : 2 * n] = r8[...]
     lag_r[0, pl.ds(2 * n * p, n)] = jnp.where(there, odr8[...], 0.0)
-    sign = 1 - 2 * p
-    target = lambda j: HALF - sign * (j + 1)
-
-    def one(j, carry):
-        for x in range(n):
-            block[j, x] = rest[j, x] + lagged(lag_s, lag_r, (0,), x, -sign * (j + 1))
-        pltpu.make_async_copy(block.at[j], out.at[target(j)], sems.at[j]).start()
-        return carry
-
-    lax.fori_loop(0, HALF, one, 0)
-    write_out(block, out, sems, HALF, target)
+    moves = []
+    for reach in range(HALF, 0, -1):
+        base = reach * (reach - 1) // 2
+        for i in range(reach):
+            block[base + i] = rest[base + i] + lagged(lag_s, lag_r, (0,), far_start(reach) + i, -sign * reach)
+        target = out.at[HALF - sign * reach, pl.ds(far_start(reach), reach)]
+        moves.append(pltpu.make_async_copy(block.at[base : base + reach], target, sems.at[reach - 1]))
+        moves[-1].start()
+    for each in moves:
+        each.wait()
 
 
 def estimate(flops, nbytes):
@@ -369,8 +374,8 @@
     def exchange(x, which):
         return lax.ppermute(x, "gx", [(i, i ^ hops[which]) for i in range(count)])
 
+    far_s0 = swap_far(source_field)
     received = exchange(traces[None], 0)
-    far_s0 = swap_far(source_field)
 
     small = n + TRIM
     width = traces.shape[1]
@@ -479,19 +484,15 @@
     r8 = last()(r4, r3, odr, evr, plane_r, *band, *coefs)
     odr8 = swap_far(r8)
     evr8 = swap_near(r8)
-    lags = lambda levels, blocks: [
-        pltpu.VMEM((levels, wide, ny, nz), f32),
-        pltpu.VMEM((levels, wide, ny, nz), f32),
-        pltpu.VMEM((blocks, n, ny, nz), f32),
-        pltpu.SemaphoreType.DMA((blocks,)),
-    ]
+    lags = lambda levels: [pltpu.VMEM((levels, wide, ny, nz), f32)] * 2
+    corner = HALF * (HALF + 1) // 2
     hbm = pl.BlockSpec(memory_space=pltpu.MemorySpace.HBM)
     image, rest = pl.pallas_call(
         image_kernel,
-        out_shape=[shape(NOFF, n, ny, nz), shape(HALF, n, ny, nz)],
+        out_shape=[shape(NOFF, n, ny, nz), shape(corner, ny, nz)],
         in_specs=vmem_specs(17),
         out_specs=[hbm, pl.BlockSpec(memory_space=pltpu.VMEM)],
-        scratch_shapes=lags(3, HALF + 1),
+        scratch_shapes=lags(3) + [pltpu.VMEM((2 * HALF, n, ny, nz), f32), pltpu.SemaphoreType.DMA((2 * HALF,))],
         compiler_params=params(16),
         cost_estimate=estimate(NOFF * n * ny * nz * 4, 4400000),
         name="image",
@@ -501,7 +502,7 @@
         out_shape=shape(NOFF, n, ny, nz),
         in_specs=vmem_specs(5) + [hbm],
         out_specs=hbm,
-        scratch_shapes=lags(1, HALF),
+        scratch_shapes=lags(1) + [pltpu.VMEM((corner, ny, nz), f32), pltpu.SemaphoreType.DMA((HALF,))],
         input_output_aliases={5: 0},
         compiler_params=params(16),
         cost_estimate=estimate(HALF * n * ny * nz * 2, 2200000),

time: 46.8 us -> 46.4 us (level)
  waiting for transfers between devices: 18.5 us -> 18 us
    ppermute x8, waiting for transfers between devices: 12.5 us -> 12 us  [swap_far(): return lax.ppermute(x, ('shot', 'gx'), far)]
    pallas_call x1, Pallas kernels: 1.9 us -> 2.41 us  [local(): pl.pallas_call(image_kernel, out_shape=[shape(NOFF, n, ny, nz), shape(cor...]
  transfers between devices with their start and end apart: 18 -> 18, of which waited for: 9 -> 9; matrix products, arithmetic and copies ran while one was open for 0% -> 0% of each run, Pallas kernels for 23% -> 25%
where the time goes in v5:
time: 46.4 us; the launch traced here: 46.3 us
  waiting for transfers between devices  18 us (39%)
  starting transfers between devices  15.6 us (34%)
  Pallas kernels  12.5 us (27%)
    ppermute x8, waiting for transfers between devices, swap_far(): return lax.ppermute(x, ('shot', 'gx'), far)  12 us
    ppermute x4, starting transfers between devices, exchange(): return lax.ppermute(x, 'gx', [(i, i ^ hops[which]) for i in range(count)])  8.08 us
    ppermute x4, waiting for transfers between devices, exchange(): return lax.ppermute(x, 'gx', [(i, i ^ hops[which]) for i in range(count)])  5.21 us
    ppermute x8, starting transfers between devices, swap_far(): return lax.ppermute(x, ('shot', 'gx'), far)  4.92 us
    ppermute x6, starting transfers between devices, swap_near(): return lax.ppermute(x, 'gx', near)  2.61 us
    pallas_call x1, Pallas kernels, local(): pl.pallas_call(image_kernel, out_shape=[shape(NOFF, n, ny, nz), shape(cor...  2.41 us
    pallas_call x1, Pallas kernels, local(): pl.pallas_call(first_kernel, out_shape=[own, own, shape(small, ny, nz), s...  1.75 us
    pallas_call x1, Pallas kernels, local(): pl.pallas_call(functools.partial(receivers_kernel, hops=tuple(hops)), out...  1.64 us
  transfers between devices with their start and end apart: 18, of which 9 were waited for; matrix products, arithmetic and copies ran while one was open for 0% of the time, Pallas kernels for 25%

profile of v5, /device:TPU:19, one launch (start us, length us, event | category | flops | bytes accessed | tf_op | source)
XLA Modules:
  0.0 46.3 jit_solution(1818342746208878331)
XLA Ops:
  0.0 1.2 %collective-permute-start.8 = (f32[1,8,128]{2,1,0:T(8,128)}, f32[1,8,128]{2,1,0:T(8,128)S(1)}, u32[]{:S(2)}, u32[]{:S(2)}) collective-permute-start(f32[1,8,128]{2,1,0:T(8,128)} %bitcast.7), channel_id=1, source_target_pairs={{0,2},{1,3},{2,0},{3,1},{4,6},{5,7},{6,4},{7,5},{8,10},{9,11},{10,... | collective-permute-start | bytes 12296 | tf_op jit(solution)/shard_map/ppermute | solution.py:375
  1.2 1.1 %collective-permute-start = (f32[16,16,128]{2,1,0:T(8,128)}, f32[16,16,128]{2,1,0:T(8,128)S(1)}, u32[]{:S(2)}, u32[]{:S(2)}) collective-permute-start(f32[16,16,128]{2,1,0:T(8,128)} %refs_0_.1), channel_id=1, source_target_pairs={{1,2},{3,4},{5,6},{7,8},{9,10},{11,12},{13,14},{17,18},{19,20},{21... | collective-permute-start | bytes 393224 | tf_op jit(solution)/shard_map/ppermute | solution.py:365
  2.3 1.4 %pack.1 = (f32[16,16,128]{2,1,0:T(8,128)S(1)}, f32[16,16,128]{2,1,0:T(8,128)S(1)}, f32[16,16,128]{2,1,0:T(8,128)S(1)}, f32[16,16,128]{2,1,0:T(8,128)S(1)}, f32[1...) custom-call(f32[16,16,128]{2,1,0:T(8,128)} %refs_0_.1, ...), custom_call_target="tpu_custom_call" | custom-call | flops 1000 | bytes 3000000 | tf_op jit(solution)/shard_map/pack/pallas_call | solution.py:396
  3.7 0.7 %collective-permute-start.2 = (f32[12,16,128]{2,1,0:T(8,128)S(1)}, f32[12,16,128]{2,1,0:T(8,128)S(1)}, u32[]{:S(2)}, u32[]{:S(2)}) collective-permute-start(f32[12,16,128]{2,1,0:T(8,128)S(1)} %get-tuple-element.43), channel_id=1, source_target_pairs={{1,2},{3,4},{5,6},{7,8},{9,10},{11,12},{13,14},{17,18},{19,20},{21... | collective-permute-start | bytes 294920 | tf_op jit(solution)/shard_map/ppermute | solution.py:365
  4.4 1.1 %collective-permute-start.1 = (f32[28,16,128]{2,1,0:T(8,128)S(1)}, f32[28,16,128]{2,1,0:T(8,128)S(1)}, u32[]{:S(2)}, u32[]{:S(2)}) collective-permute-start(f32[28,16,128]{2,1,0:T(8,128)S(1)} %get-tuple-element.42), channel_id=1, source_target_pairs={{1,2},{3,4},{5,6},{7,8},{9,10},{11,12},{13,14},{17,18},{19,20},{21... | collective-permute-start | bytes 688136 | tf_op jit(solution)/shard_map/ppermute | solution.py:365
  5.5 0.9 %collective-permute-start.3 = (f32[56,16,128]{2,1,0:T(8,128)S(1)}, f32[56,16,128]{2,1,0:T(8,128)S(1)}, u32[]{:S(2)}, u32[]{:S(2)}) collective-permute-start(f32[56,16,128]{2,1,0:T(8,128)S(1)} %get-tuple-element.44), channel_id=1, source_target_pairs={{0,1},{1,0},{2,3},{3,2},{4,5},{5,4},{6,7},{7,6},{8,9},{9,8},{10,11... | collective-permute-start | bytes 1376264 | tf_op jit(solution)/shard_map/ppermute | solution.py:362
  6.4 0.0 collective-permute-done.8
  6.4 1.3 %collective-permute-start.9 = (f32[2,8,128]{2,1,0:T(8,128)S(1)}, f32[2,8,128]{2,1,0:T(8,128)S(1)}, u32[]{:S(2)}, u32[]{:S(2)}) collective-permute-start(f32[2,8,128]{2,1,0:T(8,128)S(1)} %pad_maximum_fusion.2), channel_id=1, source_target_pairs={{0,4},{1,5},{2,6},{3,7},{4,0},{5,1},{6,2},{7,3},{8,12},{9,13},{10,... | collective-permute-start | bytes 24584 | tf_op jit(solution)/shard_map/ppermute | solution.py:375
  7.7 0.3 shots.1
  8.0 1.0 %collective-permute-done.9 = f32[2,8,128]{2,1,0:T(8,128)S(1)} collective-permute-done((f32[2,8,128]{2,1,0:T(8,128)S(1)}, f32[2,8,128]{2,1,0:T(8,128)S(1)}, u32[]{:S(2)}, u32[]{:S(2)}) %collective-permute-start.9) | collective-permute-done | bytes 8224 | tf_op jit(solution)/shard_map/ppermute | solution.py:375
  9.0 0.1 collective-permute-start.10
  9.1 3.4 %collective-permute-done.10 = f32[4,8,128]{2,1,0:T(8,128)S(1)} collective-permute-done((f32[4,8,128]{2,1,0:T(8,128)S(1)}, f32[4,8,128]{2,1,0:T(8,128)S(1)}, u32[]{:S(2)}, u32[]{:S(2)}) %collective-permute-start.10) | collective-permute-done | bytes 16416 | tf_op jit(solution)/shard_map/ppermute | solution.py:375
  12.5 5.4 %collective-permute-start.11 = (f32[8,8,128]{2,1,0:T(8,128)S(1)}, f32[8,8,128]{2,1,0:T(8,128)S(1)}, u32[]{:S(2)}, u32[]{:S(2)}) collective-permute-start(f32[8,8,128]{2,1,0:T(8,128)S(1)} %pad_maximum_fusion), channel_id=1, source_target_pairs={{0,1},{1,0},{2,3},{3,2},{4,5},{5,4},{6,7},{7,6},{8,9},{9,8},{10,11... | collective-permute-start | bytes 98312 | tf_op jit(solution)/shard_map/ppermute | solution.py:375
  17.9 0.9 %collective-permute-done.11 = f32[8,8,128]{2,1,0:T(8,128)S(1)} collective-permute-done((f32[8,8,128]{2,1,0:T(8,128)S(1)}, f32[8,8,128]{2,1,0:T(8,128)S(1)}, u32[]{:S(2)}, u32[]{:S(2)}) %collective-permute-start.11) | collective-permute-done | bytes 32800 | tf_op jit(solution)/shard_map/ppermute | solution.py:375
  18.8 0.0 collective-permute-start.6
  18.8 0.0 collective-permute-done.2.far_prior
  18.8 0.3 collective-permute-start.7
  19.1 1.6 %receivers.1.planes = f32[8,16,128]{2,1,0:T(8,128)S(1)} custom-call(s32[16,128]{1,0:T(8,128)S(1)} %get-tuple-element.63.cells, f32[16,8,128]{2,1,0:T(8,128)S(1)} %constant_dynamic-update-slice_fusion.traces), custom_call_target="tpu_custom_call" | custom-call | flops 25165824 | bytes 1000000 | tf_op jit(solution)/shard_map/receivers/pallas_call | solution.py:429
  20.8 0.0 collective-permute-done.far_own.far_s0
  20.8 0.0 collective-permute-done.1.far_coef
  20.8 0.0 collective-permute-done.3.ev.ev1
  20.8 1.7 %first_s.1 = (f32[16,16,128]{2,1,0:T(8,128)S(1)}, f32[16,16,128]{2,1,0:T(8,128)S(1)}, f32[28,16,128]{2,1,0:T(8,128)S(1)}, f32[28,16,128]{2,1,0:T(8,128)S(1)}, f3...) custom-call(f32[16,16,128]{2,1,0:T(8,128)S(1)} %get-tuple-element.38, ...), custom_call_target="tpu_custom_call" | custom-call | flops 13762560 | bytes 6000000 | tf_op jit(solution)/shard_map/first_s/pallas_call | solution.py:444
  22.6 1.5 %collective-permute-start.4 = (f32[28,16,128]{2,1,0:T(8,128)S(1)}, f32[28,16,128]{2,1,0:T(8,128)S(1)}, u32[]{:S(2)}, u32[]{:S(2)}) collective-permute-start(f32[28,16,128]{2,1,0:T(8,128)S(1)} %get-tuple-element.53), channel_id=1, source_target_pairs={{1,2},{3,4},{5,6},{7,8},{9,10},{11,12},{13,14},{17,18},{19,20},{21... | collective-permute-start | bytes 688136 | tf_op jit(solution)/shard_map/ppermute | solution.py:365
  24.1 1.2 %collective-permute-start.5 = (f32[28,16,128]{2,1,0:T(8,128)S(1)}, f32[28,16,128]{2,1,0:T(8,128)S(1)}, u32[]{:S(2)}, u32[]{:S(2)}) collective-permute-start(f32[28,16,128]{2,1,0:T(8,128)S(1)} %get-tuple-element.54), channel_id=1, source_target_pairs={{0,1},{1,0},{2,3},{3,2},{4,5},{5,4},{6,7},{7,6},{8,9},{9,8},{10,11... | collective-permute-start | bytes 688136 | tf_op jit(solution)/shard_map/ppermute | solution.py:362
  25.3 3.8 %collective-permute-done.6.od.far_r = f32[28,16,128]{2,1,0:T(8,128)S(1)} collective-permute-done((f32[28,16,128]{2,1,0:T(8,128)S(1)}, f32[28,16,128]{2,1,0:T(8,128)S(1)}, u32[]{:S(2)}, u32[]{:S(2)}) %collective-permute-start.6) | collective-permute-done | bytes 229408 | tf_op jit(solution)/shard_map/ppermute | solution.py:365
  29.1 0.0 collective-permute-done.7.ev.ev2
  29.1 1.3 %first_r.1 = (f32[16,16,128]{2,1,0:T(8,128)S(1)}, f32[16,16,128]{2,1,0:T(8,128)S(1)}, f32[28,16,128]{2,1,0:T(8,128)S(1)}, f32[28,16,128]{2,1,0:T(8,128)S(1)}) custom-call(f32[16,16,128]{2,1,0:T(8,128)S(1)} %get-tuple-element.59.own.r0, f32[16,16,128]{2,1,0:T(8,128)S(1)} %get-tuple-element.60.prior, f32[28,16,128]{2,1,0:T(8,128)S(1)} %collective-permute-done.6.od.far_r, ...), custom_call_target="tpu_custom_call" | custom-call | flops 13762560 | bytes 6000000 | tf_op jit(solution)/shard_map/first_r/pallas_call | solution.py:457
  30.5 0.1 collective-permute-start.12
  30.5 0.1 collective-permute-start.13
  30.6 3.4 %collective-permute-done.4.od.ods = f32[28,16,128]{2,1,0:T(8,128)S(1)} collective-permute-done((f32[28,16,128]{2,1,0:T(8,128)S(1)}, f32[28,16,128]{2,1,0:T(8,128)S(1)}, u32[]{:S(2)}, u32[]{:S(2)}) %collective-permute-start.4) | collective-permute-done | bytes 229408 | tf_op jit(solution)/shard_map/ppermute | solution.py:365
  34.1 0.0 collective-permute-done.5.ev.evs
  34.1 1.3 %shard_map.109.s8 = f32[16,16,128]{2,1,0:T(8,128)S(1)} custom-call(f32[16,16,128]{2,1,0:T(8,128)S(1)} %get-tuple-element.51.own.s4, f32[16,16,128]{2,1,0:T(8,128)S(1)} %get-tuple-element.52.prior, f32[28,16,128]{2,1,0:T(8,128)S(1)} %collective-permute-done.4.od.ods, f32[28,16,128]{2,1,0:T(8,128)S(1)} %collective-permute-done.5.ev.evs, ...), custom_call_target="tpu_custom_call" | custom-call | flops 13762560 | bytes 6000000 | tf_op jit(solution)/shard_map/pallas_call | solution.py:481
  35.3 0.4 collective-permute-start.16
  35.8 0.0 collective-permute-start.14
  35.8 2.2 %collective-permute-done.12.od.odr = f32[28,16,128]{2,1,0:T(8,128)S(1)} collective-permute-done((f32[28,16,128]{2,1,0:T(8,128)S(1)}, f32[28,16,128]{2,1,0:T(8,128)S(1)}, u32[]{:S(2)}, u32[]{:S(2)}) %collective-permute-start.12) | collective-permute-done | bytes 229408 | tf_op jit(solution)/shard_map/ppermute | solution.py:365
  37.9 0.0 collective-permute-done.13.ev.evr
  37.9 1.3 %shard_map.110.r8 = f32[16,16,128]{2,1,0:T(8,128)S(1)} custom-call(f32[16,16,128]{2,1,0:T(8,128)S(1)} %get-tuple-element.65.own.r4, f32[16,16,128]{2,1,0:T(8,128)S(1)} %get-tuple-element.66.prior, f32[28,16,128]{2,1,0:T(8,128)S(1)} %collective-permute-done.12.od.odr, f32[28,16,128]{2,1,0:T(8,128)S(1)} %collective-permute-done.13.ev.evr, ...), custom_call_target="tpu_custom_call" | custom-call | flops 13762560 | bytes 6000000 | tf_op jit(solution)/shard_map/pallas_call | solution.py:484
  39.2 0.1 collective-permute-start.17
  39.3 0.1 collective-permute-start.15
  39.4 0.4 collective-permute-done.16.ods8
  39.8 0.0 collective-permute-done.14.evs8
  39.8 0.8 %collective-permute-done.17.evr8 = f32[16,16,128]{2,1,0:T(8,128)S(1)} collective-permute-done((f32[16,16,128]{2,1,0:T(8,128)S(1)}, f32[16,16,128]{2,1,0:T(8,128)S(1)}, u32[]{:S(2)}, u32[]{:S(2)}) %collective-permute-start.17) | collective-permute-done | bytes 131104 | tf_op jit(solution)/shard_map/ppermute | solution.py:362
  40.6 2.4 %image.1 = (f32[33,16,16,128]{3,2,1,0:T(8,128)}, f32[136,16,128]{2,1,0:T(8,128)S(1)}) custom-call(f32[16,16,128]{2,1,0:T(8,128)S(1)} %get-tuple-element.38.own.s0, f32[16,16,128]{2,1,0:T(8,128)S(1)} %get-tuple-element.51.own.s4, f32[16,16,128]{2,1,0:T(8,128)S(1)} %shard_map.109.s8, f32[16,16,128]{2,1,0:T(8,128)S(1)} %get-tuple-element.59.own.r0, ...), custom_call_target="tpu_custom_call" | custom-call | flops 4325376 | bytes 4400000 | tf_op jit(solution)/shard_map/image/pallas_call | solution.py:490
  43.0 2.1 %collective-permute-done.15.odr8 = f32[16,16,128]{2,1,0:T(8,128)S(1)} collective-permute-done((f32[16,16,128]{2,1,0:T(8,128)S(1)}, f32[16,16,128]{2,1,0:T(8,128)S(1)}, u32[]{:S(2)}, u32[]{:S(2)}) %collective-permute-start.15) | collective-permute-done | bytes 131104 | tf_op jit(solution)/shard_map/ppermute | solution.py:365
  45.1 1.2 %last_image.1 = f32[33,16,16,128]{3,2,1,0:T(8,128)} custom-call(f32[16,16,128]{2,1,0:T(8,128)S(1)} %shard_map.109.s8, f32[16,16,128]{2,1,0:T(8,128)S(1)} %shard_map.110.r8, f32[16,16,128]{2,1,0:T(8,128)S(1)} %collective-permute-done.14.evs8, f32[16,16,128]{2,1,0:T(8,128)S(1)} %collective-permute-done.15.odr8, ...), custom_call_target="tpu_custom_call", output_to_operand_aliasing={{}: (5, {})} | custom-call | flops 1048576 | bytes 2200000 | tf_op jit(solution)/shard_map/last_image/pallas_call | solution.py:500
  (8 shorter events, 0.0 us)
Async XLA Ops:
  0.0 6.4 %collective-permute-start.8 = (f32[1,8,128]{2,1,0:T(8,128)}, f32[1,8,128]{2,1,0:T(8,128)S(1)}, u32[]{:S(2)}, u32[]{:S(2)}) collective-permute-start(f32[1,8,128]{2,1,0:T(8,128)} %bitcast.7), channel_id=1, source_target_pairs={{0,2},{1,3},{2,0},{3,1},{4,6},{5,7},{6,4},{7,5},{8,10},{9,11},{10,... | collective-permute-start | bytes 12296 | tf_op jit(solution)/shard_map/ppermute | solution.py:375
  1.2 19.6 %collective-permute-start = (f32[16,16,128]{2,1,0:T(8,128)}, f32[16,16,128]{2,1,0:T(8,128)S(1)}, u32[]{:S(2)}, u32[]{:S(2)}) collective-permute-start(f32[16,16,128]{2,1,0:T(8,128)} %refs_0_.1), channel_id=1, source_target_pairs={{1,2},{3,4},{5,6},{7,8},{9,10},{11,12},{13,14},{17,18},{19,20},{21... | collective-permute-start | bytes 393224 | tf_op jit(solution)/shard_map/ppermute | solution.py:365
  3.7 15.1 %collective-permute-start.2 = (f32[12,16,128]{2,1,0:T(8,128)S(1)}, f32[12,16,128]{2,1,0:T(8,128)S(1)}, u32[]{:S(2)}, u32[]{:S(2)}) collective-permute-start(f32[12,16,128]{2,1,0:T(8,128)S(1)} %get-tuple-element.43), channel_id=1, source_target_pairs={{1,2},{3,4},{5,6},{7,8},{9,10},{11,12},{13,14},{17,18},{19,20},{21... | collective-permute-start | bytes 294920 | tf_op jit(solution)/shard_map/ppermute | solution.py:365
  4.4 16.4 %collective-permute-start.1 = (f32[28,16,128]{2,1,0:T(8,128)S(1)}, f32[28,16,128]{2,1,0:T(8,128)S(1)}, u32[]{:S(2)}, u32[]{:S(2)}) collective-permute-start(f32[28,16,128]{2,1,0:T(8,128)S(1)} %get-tuple-element.42), channel_id=1, source_target_pairs={{1,2},{3,4},{5,6},{7,8},{9,10},{11,12},{13,14},{17,18},{19,20},{21... | collective-permute-start | bytes 688136 | tf_op jit(solution)/shard_map/ppermute | solution.py:365
  5.5 15.3 %collective-permute-start.3 = (f32[56,16,128]{2,1,0:T(8,128)S(1)}, f32[56,16,128]{2,1,0:T(8,128)S(1)}, u32[]{:S(2)}, u32[]{:S(2)}) collective-permute-start(f32[56,16,128]{2,1,0:T(8,128)S(1)} %get-tuple-element.44), channel_id=1, source_target_pairs={{0,1},{1,0},{2,3},{3,2},{4,5},{5,4},{6,7},{7,6},{8,9},{9,8},{10,11... | collective-permute-start | bytes 1376264 | tf_op jit(solution)/shard_map/ppermute | solution.py:362
  6.4 2.6 %collective-permute-start.9 = (f32[2,8,128]{2,1,0:T(8,128)S(1)}, f32[2,8,128]{2,1,0:T(8,128)S(1)}, u32[]{:S(2)}, u32[]{:S(2)}) collective-permute-start(f32[2,8,128]{2,1,0:T(8,128)S(1)} %pad_maximum_fusion.2), channel_id=1, source_target_pairs={{0,4},{1,5},{2,6},{3,7},{4,0},{5,1},{6,2},{7,3},{8,12},{9,13},{10,... | collective-permute-start | bytes 24584 | tf_op jit(solution)/shard_map/ppermute | solution.py:375
  9.0 3.5 %collective-permute-start.10 = (f32[4,8,128]{2,1,0:T(8,128)S(1)}, f32[4,8,128]{2,1,0:T(8,128)S(1)}, u32[]{:S(2)}, u32[]{:S(2)}) collective-permute-start(f32[4,8,128]{2,1,0:T(8,128)S(1)} %pad_maximum_fusion.1), channel_id=1, source_target_pairs={{0,8},{1,9},{2,10},{3,11},{4,12},{5,13},{6,14},{7,15},{8,0},{9,1},... | collective-permute-start | bytes 49160 | tf_op jit(solution)/shard_map/ppermute | solution.py:375
  12.5 6.3 %collective-permute-start.11 = (f32[8,8,128]{2,1,0:T(8,128)S(1)}, f32[8,8,128]{2,1,0:T(8,128)S(1)}, u32[]{:S(2)}, u32[]{:S(2)}) collective-permute-start(f32[8,8,128]{2,1,0:T(8,128)S(1)} %pad_maximum_fusion), channel_id=1, source_target_pairs={{0,1},{1,0},{2,3},{3,2},{4,5},{5,4},{6,7},{7,6},{8,9},{9,8},{10,11... | collective-permute-start | bytes 98312 | tf_op jit(solution)/shard_map/ppermute | solution.py:375
  18.8 10.4 %collective-permute-start.6 = (f32[28,16,128]{2,1,0:T(8,128)S(1)}, f32[28,16,128]{2,1,0:T(8,128)S(1)}, u32[]{:S(2)}, u32[]{:S(2)}) collective-permute-start(f32[28,16,128]{2,1,0:T(8,128)S(1)} %get-tuple-element.61), channel_id=1, source_target_pairs={{1,2},{3,4},{5,6},{7,8},{9,10},{11,12},{13,14},{17,18},{19,20},{21... | collective-permute-start | bytes 688136 | tf_op jit(solution)/shard_map/ppermute | solution.py:365
  18.8 10.4 %collective-permute-start.7 = (f32[28,16,128]{2,1,0:T(8,128)S(1)}, f32[28,16,128]{2,1,0:T(8,128)S(1)}, u32[]{:S(2)}, u32[]{:S(2)}) collective-permute-start(f32[28,16,128]{2,1,0:T(8,128)S(1)} %get-tuple-element.62), channel_id=1, source_target_pairs={{0,1},{1,0},{2,3},{3,2},{4,5},{5,4},{6,7},{7,6},{8,9},{9,8},{10,11... | collective-permute-start | bytes 688136 | tf_op jit(solution)/shard_map/ppermute | solution.py:362
  22.6 11.5 %collective-permute-start.4 = (f32[28,16,128]{2,1,0:T(8,128)S(1)}, f32[28,16,128]{2,1,0:T(8,128)S(1)}, u32[]{:S(2)}, u32[]{:S(2)}) collective-permute-start(f32[28,16,128]{2,1,0:T(8,128)S(1)} %get-tuple-element.53), channel_id=1, source_target_pairs={{1,2},{3,4},{5,6},{7,8},{9,10},{11,12},{13,14},{17,18},{19,20},{21... | collective-permute-start | bytes 688136 | tf_op jit(solution)/shard_map/ppermute | solution.py:365
  24.1 10.0 %collective-permute-start.5 = (f32[28,16,128]{2,1,0:T(8,128)S(1)}, f32[28,16,128]{2,1,0:T(8,128)S(1)}, u32[]{:S(2)}, u32[]{:S(2)}) collective-permute-start(f32[28,16,128]{2,1,0:T(8,128)S(1)} %get-tuple-element.54), channel_id=1, source_target_pairs={{0,1},{1,0},{2,3},{3,2},{4,5},{5,4},{6,7},{7,6},{8,9},{9,8},{10,11... | collective-permute-start | bytes 688136 | tf_op jit(solution)/shard_map/ppermute | solution.py:362
  30.5 7.5 %collective-permute-start.12 = (f32[28,16,128]{2,1,0:T(8,128)S(1)}, f32[28,16,128]{2,1,0:T(8,128)S(1)}, u32[]{:S(2)}, u32[]{:S(2)}) collective-permute-start(f32[28,16,128]{2,1,0:T(8,128)S(1)} %get-tuple-element.67), channel_id=1, source_target_pairs={{1,2},{3,4},{5,6},{7,8},{9,10},{11,12},{13,14},{17,18},{19,20},{21... | collective-permute-start | bytes 688136 | tf_op jit(solution)/shard_map/ppermute | solution.py:365
  30.5 7.4 %collective-permute-start.13 = (f32[28,16,128]{2,1,0:T(8,128)S(1)}, f32[28,16,128]{2,1,0:T(8,128)S(1)}, u32[]{:S(2)}, u32[]{:S(2)}) collective-permute-start(f32[28,16,128]{2,1,0:T(8,128)S(1)} %get-tuple-element.68), channel_id=1, source_target_pairs={{0,1},{1,0},{2,3},{3,2},{4,5},{5,4},{6,7},{7,6},{8,9},{9,8},{10,11... | collective-permute-start | bytes 688136 | tf_op jit(solution)/shard_map/ppermute | solution.py:362
  35.3 4.5 %collective-permute-start.16 = (f32[16,16,128]{2,1,0:T(8,128)S(1)}, f32[16,16,128]{2,1,0:T(8,128)S(1)}, u32[]{:S(2)}, u32[]{:S(2)}) collective-permute-start(f32[16,16,128]{2,1,0:T(8,128)S(1)} %shard_map.109.s8), channel_id=1, source_target_pairs={{1,2},{3,4},{5,6},{7,8},{9,10},{11,12},{13,14},{17,18},{19,20},{21... | collective-permute-start | bytes 393224 | tf_op jit(solution)/shard_map/ppermute | solution.py:365
  35.8 4.0 %collective-permute-start.14 = (f32[16,16,128]{2,1,0:T(8,128)S(1)}, f32[16,16,128]{2,1,0:T(8,128)S(1)}, u32[]{:S(2)}, u32[]{:S(2)}) collective-permute-start(f32[16,16,128]{2,1,0:T(8,128)S(1)} %shard_map.109.s8), channel_id=1, source_target_pairs={{0,1},{1,0},{2,3},{3,2},{4,5},{5,4},{6,7},{7,6},{8,9},{9,8},{10,11... | collective-permute-start | bytes 393224 | tf_op jit(solution)/shard_map/ppermute | solution.py:362
  39.2 1.4 %collective-permute-start.17 = (f32[16,16,128]{2,1,0:T(8,128)S(1)}, f32[16,16,128]{2,1,0:T(8,128)S(1)}, u32[]{:S(2)}, u32[]{:S(2)}) collective-permute-start(f32[16,16,128]{2,1,0:T(8,128)S(1)} %shard_map.110.r8), channel_id=1, source_target_pairs={{0,1},{1,0},{2,3},{3,2},{4,5},{5,4},{6,7},{7,6},{8,9},{9,8},{10,11... | collective-permute-start | bytes 393224 | tf_op jit(solution)/shard_map/ppermute | solution.py:362
  39.3 5.9 %collective-permute-start.15 = (f32[16,16,128]{2,1,0:T(8,128)S(1)}, f32[16,16,128]{2,1,0:T(8,128)S(1)}, u32[]{:S(2)}, u32[]{:S(2)}) collective-permute-start(f32[16,16,128]{2,1,0:T(8,128)S(1)} %shard_map.110.r8), channel_id=1, source_target_pairs={{1,2},{3,4},{5,6},{7,8},{9,10},{11,12},{13,14},{17,18},{19,20},{21... | collective-permute-start | bytes 393224 | tf_op jit(solution)/shard_map/ppermute | solution.py:365

commit v6 on v5

--- a/solution.py
+++ b/solution.py
@@ -15,6 +15,7 @@
 HALF = 16
 REACH = 4
 TRIM = HALF - REACH
+THIN = TRIM - REACH
 LANES = 48
 
 SCALE = 5040.0
@@ -102,7 +103,7 @@
 
 def pack_kernel(*refs, count):
     args, copies, sems = refs[:count], refs[count : 2 * count], refs[-1]
-    far_coef, far_prior, far_r, near_s, near_r = refs[2 * count : -1]
+    far_coef, far_r, near = refs[2 * count : -1]
     moves = [pltpu.make_async_copy(a, b, sems.at[i]) for i, (a, b) in enumerate(zip(args, copies))]
     for move in moves:
         move.start()
@@ -113,16 +114,16 @@
     n = s0.shape[0]
     far_cut, near_cut = pl.ds(REACH * p, TRIM), pl.ds(REACH * (1 - p), TRIM)
     far_coef[0:n] = buoy[...]
-    far_coef[n:] = stiff[far_cut]
-    far_prior[...] = sp[far_cut]
+    far_coef[n : n + TRIM] = stiff[far_cut]
+    far_coef[n + TRIM :] = sp[far_cut]
     far_r[0:n] = r0[...]
     far_r[n:] = rp[far_cut]
-    near_s[0:n] = buoy[...]
-    near_s[n : n + TRIM] = stiff[near_cut]
-    near_s[n + TRIM : 2 * n + TRIM] = s0[...]
-    near_s[2 * n + TRIM :] = sp[near_cut]
-    near_r[0:n] = r0[...]
-    near_r[n:] = rp[near_cut]
+    near[0:n] = buoy[...]
+    near[n : n + TRIM] = stiff[near_cut]
+    near[n + TRIM : 2 * n + TRIM] = s0[...]
+    near[2 * n + TRIM : 2 * (n + TRIM)] = sp[near_cut]
+    near[2 * (n + TRIM) : 3 * n + 2 * TRIM] = r0[...]
+    near[3 * n + 2 * TRIM :] = rp[near_cut]
 
 
 def spread(cells, parts, lateral, steps):
@@ -176,7 +177,7 @@
         acc[:, 0:LANES] += spread(row, split3(back), lateral, steps)
         return carry
 
-    lax.fori_loop(0, groups // 2, gather, 0)
+    lax.fori_loop(0, groups // 2, gather, 0, unroll=8)
     planes[:, :, 0:LANES] = acc[:, 0:LANES].reshape(steps, lateral, LANES)
 
 
@@ -216,18 +217,16 @@
 
 
 def finish(field, n, now_out, before_out, od_out, ev_out):
-    p, _ = place()
     last, earlier = field[IMG_EVERY % 2], field[1 - IMG_EVERY % 2]
-    value = last[n : 2 * n]
+    value, thin = last[n : 2 * n], earlier[n + REACH : n + REACH + THIN]
     now_out[...] = value
-    before_out[...] = earlier[n : 2 * n]
-    od_out[0:n] = value
-    ev_out[0:n] = value
-    od_out[n:] = earlier[pl.ds(n + REACH * p, TRIM)]
-    ev_out[n:] = earlier[pl.ds(n + REACH * (1 - p), TRIM)]
-
-
-def first_kernel(own, prior, stiff, buoy_own, far_own, far_coef, far_prior, ev, planes, depth, cross, now_out, before_out, od_out, ev_out, buoy, kb, kk, gg, f0, f1, h0, l0, h1, l1):
+    before_out[...] = earlier[n - REACH : 2 * n + REACH]
+    for out in (od_out, ev_out):
+        out[0:n] = value
+        out[n:] = thin
+
+
+def first_kernel(own, prior, stiff, buoy_own, far_own, far_coef, ev, planes, depth, cross, now_out, before_out, od_out, ev_out, buoy, kb, kk, gg, f0, f1, h0, l0, h1, l1):
     n, ny, nz = own.shape
     band = depth[...], cross[...]
     load_field(buoy, buoy_own, far_coef, 0, ev, 0, n, True)
@@ -244,20 +243,26 @@
         kk[rows] = k
         kb[rows] = k * b
         gg[rows] = 2.0 - k * (CENTRE * b + around.reshape(8, ny, nz))
-    load_field(f1, prior, far_prior, 0, ev, 2 * n + TRIM, TRIM, False)
+    load_field(f1, prior, far_coef, n + TRIM, ev, 2 * n + TRIM, TRIM, False)
     run_steps((f0, f1), ((h0, l0), (h1, l1)), (buoy, kb, kk, gg), planes, depth, cross, 0)
     finish((f0, f1), n, now_out, before_out, od_out, ev_out)
 
 
-def block_steps(own, prior, od, ev, planes, depth, cross, coefs, field, parts, base):
+def block_steps(own, prior, od, ev, planes, depth, cross, coefs, field, parts, base, near=0):
     n = own.shape[0]
-    load_field(field[0], own, od, 0, ev, 0, n, True)
-    load_field(field[1], prior, od, n, ev, n, TRIM, False)
+    load_field(field[0], own, od, 0, ev, near, n, True)
+    if prior.shape[0] == n:
+        load_field(field[1], prior, od, n, ev, near + n, TRIM, False)
+    else:
+        p, there = place()
+        field[1][n - REACH : 2 * n + REACH] = prior[...]
+        field[1][pl.ds(2 * n * p + REACH, THIN)] = jnp.where(there, od[n:], 0.0)
+        field[1][pl.ds(2 * n * (1 - p) + REACH, THIN)] = ev[n:]
     run_steps(field, parts, coefs, planes, depth, cross, base)
 
 
-def block_kernel(own, prior, od, ev, planes, depth, cross, buoy, kb, kk, gg, now_out, before_out, od_out, ev_out, f0, f1, h0, l0, h1, l1, base):
-    block_steps(own, prior, od, ev, planes, depth, cross, (buoy, kb, kk, gg), (f0, f1), ((h0, l0), (h1, l1)), base)
+def block_kernel(own, prior, od, ev, planes, depth, cross, buoy, kb, kk, gg, now_out, before_out, od_out, ev_out, f0, f1, h0, l0, h1, l1, base, near):
+    block_steps(own, prior, od, ev, planes, depth, cross, (buoy, kb, kk, gg), (f0, f1), ((h0, l0), (h1, l1)), base, near)
     finish((f0, f1), own.shape[0], now_out, before_out, od_out, ev_out)
 
 
@@ -280,28 +285,44 @@
     return p, there, 1 - 2 * p, lambda reach: (HALF - reach) * p, lambda reach: reach * (1 - p)
 
 
-def image_kernel(s0, s4, s8, r0, r4, r8, far_s0, ev1, far_r, ev2, ods, evs, odr, evr, ods8, evs8, evr8, out, rest, lag_s, lag_r, block, sems):
-    p, there, sign, far_start, own_start = sides()
+def place_rows(dst, level, own, od, od_lo, ev, ev_lo):
+    p, there = place()
+    n = own.shape[0]
+    dst[level, n : 2 * n] = own[...]
+    if od is not None:
+        dst[level, pl.ds(2 * n * p, n)] = jnp.where(there, od[od_lo : od_lo + n], 0.0)
+    dst[level, pl.ds(2 * n * (1 - p), n)] = ev[ev_lo : ev_lo + n]
+
+
+def early_image_kernel(s0, s4, r0, r4, far_s0, ev1, ods, evs, evr, block, lag_s, lag_r):
+    _, _, sign, _, own_start = sides()
     n = s0.shape[0]
-    left, right = pl.ds(2 * n * p, n), pl.ds(2 * n * (1 - p), n)
-    groups = (
-        (lag_s, 0, s0, far_s0, 0, ev1, n + TRIM),
-        (lag_r, 0, r0, far_r, 0, ev2, 0),
-        (lag_s, 1, s4, ods, 0, evs, 0),
-        (lag_r, 1, r4, odr, 0, evr, 0),
-        (lag_s, 2, s8, ods8, 0, evs8, 0),
-        (lag_r, 2, r8, None, 0, evr8, 0),
-    )
-    for dst, level, own, od, od_lo, ev, ev_lo in groups:
-        dst[level, n : 2 * n] = own[...]
-        if od is not None:
-            dst[level, left] = jnp.where(there, od[od_lo : od_lo + n], 0.0)
-        dst[level, right] = ev[ev_lo : ev_lo + n]
-    move = lambda j: pltpu.make_async_copy(block.at[j], out.at[HALF + sign * j], sems.at[j])
+    place_rows(lag_s, 0, s0, far_s0, 0, ev1, n + TRIM)
+    place_rows(lag_r, 0, r0, None, 0, ev1, 2 * (n + TRIM))
+    place_rows(lag_s, 1, s4, ods, 0, evs, 0)
+    place_rows(lag_r, 1, r4, None, 0, evr, 0)
 
     def whole(j, carry):
         for x in range(n):
-            block[j, x] = lagged(lag_s, lag_r, (0, 1, 2), x, sign * j)
+            block[j, x] = lagged(lag_s, lag_r, (0, 1), x, sign * j)
+        return carry
+
+    lax.fori_loop(0, HALF + 1, whole, 0)
+    for reach in range(1, HALF):
+        for i in range(n - reach):
+            block[HALF + reach, i] = lagged(lag_s, lag_r, (0, 1), own_start(reach) + i, -sign * reach)
+
+
+def image_kernel(s0, s4, s8, r0, r4, r8, ev1, far_r, evs, odr, evr, ods8, evs8, evr8, early, out, rest, lag_s, lag_r, block, sems):
+    _, _, sign, far_start, own_start = sides()
+    n = s0.shape[0]
+    place_rows(lag_s, 2, s8, ods8, 0, evs8, 0)
+    place_rows(lag_r, 2, r8, None, 0, evr8, 0)
+    move = lambda j: pltpu.make_async_copy(block.at[j], out.at[HALF + sign * j], sems.at[j])
+
+    def whole(j, carry):
+        for x in range(n):
+            block[j, x] = early[j, x] + lagged(lag_s, lag_r, (2,), x, sign * j)
         move(j).start()
         return carry
 
@@ -309,10 +330,14 @@
     moves = []
     for reach in range(1, HALF):
         for i in range(n - reach):
-            block[HALF + reach, i] = lagged(lag_s, lag_r, (0, 1, 2), own_start(reach) + i, -sign * reach)
+            block[HALF + reach, i] = early[HALF + reach, i] + lagged(lag_s, lag_r, (2,), own_start(reach) + i, -sign * reach)
         target = out.at[HALF - sign * reach, pl.ds(own_start(reach), n - reach)]
         moves.append(pltpu.make_async_copy(block.at[HALF + reach, 0 : n - reach], target, sems.at[HALF + reach]))
         moves[-1].start()
+    place_rows(lag_s, 0, s0, None, 0, ev1, n + TRIM)
+    place_rows(lag_r, 0, r0, far_r, 0, ev1, 2 * (n + TRIM))
+    place_rows(lag_s, 1, s4, None, 0, evs, 0)
+    place_rows(lag_r, 1, r4, odr, 0, evr, 0)
     for reach in range(1, HALF + 1):
         for i in range(reach):
             rest[reach * (reach - 1) // 2 + i] = lagged(lag_s, lag_r, (0, 1), far_start(reach) + i, -sign * reach)
@@ -364,12 +389,9 @@
     def swap_far(x):
         return lax.ppermute(x, ("shot", "gx"), far)
 
-    hops = []
-    hop = 2
-    while hop < count:
-        hops.append(hop)
-        hop *= 2
-    hops.append(1)
+    hops = [2, 1] if count > 2 else [1]
+    while 2 * max(hops) < count:
+        hops.append(2 * max(hops))
 
     def exchange(x, which):
         return lax.ppermute(x, "gx", [(i, i ^ hops[which]) for i in range(count)])
@@ -396,21 +418,19 @@
     packed = pl.pallas_call(
         functools.partial(pack_kernel, count=len(args)),
         out_shape=[jax.ShapeDtypeStruct(a.shape, a.dtype) for a in args]
-        + [shape(small, ny, nz), shape(TRIM, ny, nz), shape(small, ny, nz), shape(2 * small, ny, nz), shape(small, ny, nz)],
+        + [shape(n + 2 * TRIM, ny, nz), shape(small, ny, nz), shape(3 * small, ny, nz)],
         in_specs=[pl.BlockSpec(memory_space=pltpu.MemorySpace.HBM)] * len(args),
-        out_specs=vmem_specs(len(args) + 5),
+        out_specs=vmem_specs(len(args) + 3),
         scratch_shapes=[pltpu.SemaphoreType.DMA((len(args),))],
         compiler_params=params(8),
         cost_estimate=estimate(1000, 3000000),
         name="pack",
     )(*(pltpu.with_memory_space_constraint(a, pltpu.MemorySpace.HBM) for a in args))
     source_field, source_prior, receiver_field, receiver_prior, stiffness, buoyancy, gathered, cells, shot_row, fire_row, wave = packed[: len(args)]
-    far_coef, far_prior, far_r, ev1, ev2 = packed[len(args) :]
+    far_coef, far_r, ev1 = packed[len(args) :]
     far_coef = swap_far(far_coef)
-    far_prior = swap_far(far_prior)
     far_r = swap_far(far_r)
     ev1 = swap_near(ev1)
-    ev2 = swap_near(ev2)
 
     gathered = jnp.concatenate([gathered, received], axis=0)
     for which in range(1, len(hops)):
@@ -440,30 +460,30 @@
     wide = 3 * n
     scratch = [pltpu.VMEM((wide, ny, nz), f32)] * 2 + [pltpu.VMEM((wide, ny, 2 * nz), bf16)] * 4
     cost = estimate(224 * 8 * 128 * 60, 6000000)
-    own = shape(n, ny, nz)
+    own, prior = shape(n, ny, nz), shape(n + 2 * REACH, ny, nz)
     s4, s3, ods, evs, buoy, kb, kk, gg = pl.pallas_call(
         first_kernel,
-        out_shape=[own, own, shape(small, ny, nz), shape(small, ny, nz)] + [shape(wide, ny, nz)] * 4,
-        in_specs=vmem_specs(11),
+        out_shape=[own, prior, shape(n + THIN, ny, nz), shape(n + THIN, ny, nz)] + [shape(wide, ny, nz)] * 4,
+        in_specs=vmem_specs(10),
         out_specs=vmem_specs(8),
         scratch_shapes=scratch,
         compiler_params=params(16),
         cost_estimate=cost,
         name="first_s",
-    )(source_field, source_prior, stiffness, buoyancy, far_s0, far_coef, far_prior, ev1, plane_s, *band)
+    )(source_field, source_prior, stiffness, buoyancy, far_s0, far_coef, ev1, plane_s, *band)
     coefs = (buoy, kb, kk, gg)
     ods = swap_far(ods)
     evs = swap_near(evs)
     r4, r3, odr, evr = pl.pallas_call(
-        functools.partial(block_kernel, base=0),
-        out_shape=[own, own, shape(small, ny, nz), shape(small, ny, nz)],
+        functools.partial(block_kernel, base=0, near=2 * small),
+        out_shape=[own, prior, shape(n + THIN, ny, nz), shape(n + THIN, ny, nz)],
         in_specs=vmem_specs(11),
         out_specs=vmem_specs(4),
         scratch_shapes=scratch,
         compiler_params=params(16),
         cost_estimate=cost,
         name="first_r",
-    )(receiver_field, receiver_prior, far_r, ev2, plane_r, *band, *coefs)
+    )(receiver_field, receiver_prior, far_r, ev1, plane_r, *band, *coefs)
     odr = swap_far(odr)
     evr = swap_near(evr)
 
@@ -487,16 +507,26 @@
     lags = lambda levels: [pltpu.VMEM((levels, wide, ny, nz), f32)] * 2
     corner = HALF * (HALF + 1) // 2
     hbm = pl.BlockSpec(memory_space=pltpu.MemorySpace.HBM)
+    early = pl.pallas_call(
+        early_image_kernel,
+        out_shape=shape(2 * HALF, n, ny, nz),
+        in_specs=vmem_specs(9),
+        out_specs=pl.BlockSpec(memory_space=pltpu.VMEM),
+        scratch_shapes=lags(2),
+        compiler_params=params(8),
+        cost_estimate=estimate(NOFF * n * ny * nz * 3, 1000000),
+        name="early_image",
+    )(source_field, s4, receiver_field, r4, far_s0, ev1, ods, evs, evr)
     image, rest = pl.pallas_call(
         image_kernel,
         out_shape=[shape(NOFF, n, ny, nz), shape(corner, ny, nz)],
-        in_specs=vmem_specs(17),
+        in_specs=vmem_specs(15),
         out_specs=[hbm, pl.BlockSpec(memory_space=pltpu.VMEM)],
         scratch_shapes=lags(3) + [pltpu.VMEM((2 * HALF, n, ny, nz), f32), pltpu.SemaphoreType.DMA((2 * HALF,))],
         compiler_params=params(16),
         cost_estimate=estimate(NOFF * n * ny * nz * 4, 4400000),
         name="image",
-    )(source_field, s4, s8, receiver_field, r4, r8, far_s0, ev1, far_r, ev2, ods, evs, odr, evr, ods8, evs8, evr8)
+    )(source_field, s4, s8, receiver_field, r4, r8, ev1, far_r, evs, odr, evr, ods8, evs8, evr8, early)
     return pl.pallas_call(
         last_image_kernel,
         out_shape=shape(NOFF, n, ny, nz),

time: 46.4 us -> 48.1 us (1.037)
  the two profiles are of different devices: /device:TPU:19 before, /device:TPU:17 now
where the time goes in v6:
time: 48.1 us; the launch traced here: 47.9 us
  waiting for transfers between devices  19.9 us (41%)
  starting transfers between devices  15.9 us (33%)
  Pallas kernels  11.9 us (25%)
    ppermute x7, waiting for transfers between devices, swap_far(): return lax.ppermute(x, ('shot', 'gx'), far)  14 us
    ppermute x7, starting transfers between devices, swap_far(): return lax.ppermute(x, ('shot', 'gx'), far)  7.27 us
    ppermute x4, waiting for transfers between devices, exchange(): return lax.ppermute(x, 'gx', [(i, i ^ hops[which]) for i in range(count)])  5.97 us
    ppermute x5, starting transfers between devices, swap_near(): return lax.ppermute(x, 'gx', near)  5.19 us
    ppermute x4, starting transfers between devices, exchange(): return lax.ppermute(x, 'gx', [(i, i ^ hops[which]) for i in range(count)])  3.47 us
    pallas_call x1, Pallas kernels, local(): pl.pallas_call(image_kernel, out_shape=[shape(NOFF, n, ny, nz), shape(cor...  2.01 us
    pallas_call x1, Pallas kernels, local(): pl.pallas_call(first_kernel, out_shape=[own, prior, shape(n + THIN, ny, n...  1.69 us
    pallas_call x1, Pallas kernels, local(): pl.pallas_call(functools.partial(pack_kernel, count=len(args)), out_shape...  1.38 us
  transfers between devices with their start and end apart: 16, of which 8 were waited for; matrix products, arithmetic and copies ran while one was open for 0% of the time, Pallas kernels for 20%

profile of v6, /device:TPU:17, one launch (start us, length us, event | category | flops | bytes accessed | tf_op | source)
XLA Modules:
  0.0 47.9 jit_solution(2590297167247447688)
XLA Ops:
  0.0 1.2 %collective-permute-start.6 = (f32[1,8,128]{2,1,0:T(8,128)}, f32[1,8,128]{2,1,0:T(8,128)S(1)}, u32[]{:S(2)}, u32[]{:S(2)}) collective-permute-start(f32[1,8,128]{2,1,0:T(8,128)} %bitcast.7), channel_id=1, source_target_pairs={{0,2},{1,3},{2,0},{3,1},{4,6},{5,7},{6,4},{7,5},{8,10},{9,11},{10,... | collective-permute-start | bytes 12296 | tf_op jit(solution)/shard_map/ppermute | solution.py:397
  1.2 1.1 %collective-permute-start = (f32[16,16,128]{2,1,0:T(8,128)}, f32[16,16,128]{2,1,0:T(8,128)S(1)}, u32[]{:S(2)}, u32[]{:S(2)}) collective-permute-start(f32[16,16,128]{2,1,0:T(8,128)} %refs_0_.1), channel_id=1, source_target_pairs={{1,2},{3,4},{5,6},{7,8},{9,10},{11,12},{13,14},{17,18},{19,20},{21... | collective-permute-start | bytes 393224 | tf_op jit(solution)/shard_map/ppermute | solution.py:390
  2.3 1.4 %pack.1 = (f32[16,16,128]{2,1,0:T(8,128)S(1)}, f32[16,16,128]{2,1,0:T(8,128)S(1)}, f32[16,16,128]{2,1,0:T(8,128)S(1)}, f32[16,16,128]{2,1,0:T(8,128)S(1)}, f32[1...) custom-call(f32[16,16,128]{2,1,0:T(8,128)} %refs_0_.1, ...), custom_call_target="tpu_custom_call" | custom-call | flops 1000 | bytes 3000000 | tf_op jit(solution)/shard_map/pack/pallas_call | solution.py:418
  3.7 0.1 collective-permute-start.2
  3.8 2.6 %collective-permute-start.1 = (f32[40,16,128]{2,1,0:T(8,128)S(1)}, f32[40,16,128]{2,1,0:T(8,128)S(1)}, u32[]{:S(2)}, u32[]{:S(2)}) collective-permute-start(f32[40,16,128]{2,1,0:T(8,128)S(1)} %get-tuple-element.40), channel_id=1, source_target_pairs={{1,2},{3,4},{5,6},{7,8},{9,10},{11,12},{13,14},{17,18},{19,20},{21... | collective-permute-start | bytes 983048 | tf_op jit(solution)/shard_map/ppermute | solution.py:390
  6.4 0.0 collective-permute-start.5
  6.4 0.3 shots.1
  6.8 0.0 collective-permute-done.6
  6.8 0.6 %collective-permute-start.7 = (f32[2,8,128]{2,1,0:T(8,128)S(1)}, f32[2,8,128]{2,1,0:T(8,128)S(1)}, u32[]{:S(2)}, u32[]{:S(2)}) collective-permute-start(f32[2,8,128]{2,1,0:T(8,128)S(1)} %pad_maximum_fusion.2), channel_id=1, source_target_pairs={{0,1},{1,0},{2,3},{3,2},{4,5},{5,4},{6,7},{7,6},{8,9},{9,8},{10,11... | collective-permute-start | bytes 24584 | tf_op jit(solution)/shard_map/ppermute | solution.py:397
  7.3 0.8 %collective-permute-done.7 = f32[2,8,128]{2,1,0:T(8,128)S(1)} collective-permute-done((f32[2,8,128]{2,1,0:T(8,128)S(1)}, f32[2,8,128]{2,1,0:T(8,128)S(1)}, u32[]{:S(2)}, u32[]{:S(2)}) %collective-permute-start.7) | collective-permute-done | bytes 8224 | tf_op jit(solution)/shard_map/ppermute | solution.py:397
  8.2 1.3 %collective-permute-start.8 = (f32[4,8,128]{2,1,0:T(8,128)S(1)}, f32[4,8,128]{2,1,0:T(8,128)S(1)}, u32[]{:S(2)}, u32[]{:S(2)}) collective-permute-start(f32[4,8,128]{2,1,0:T(8,128)S(1)} %pad_maximum_fusion.1), channel_id=1, source_target_pairs={{0,4},{1,5},{2,6},{3,7},{4,0},{5,1},{6,2},{7,3},{8,12},{9,13},{10,... | collective-permute-start | bytes 49160 | tf_op jit(solution)/shard_map/ppermute | solution.py:397
  9.5 1.8 %collective-permute-done.8 = f32[4,8,128]{2,1,0:T(8,128)S(1)} collective-permute-done((f32[4,8,128]{2,1,0:T(8,128)S(1)}, f32[4,8,128]{2,1,0:T(8,128)S(1)}, u32[]{:S(2)}, u32[]{:S(2)}) %collective-permute-start.8) | collective-permute-done | bytes 16416 | tf_op jit(solution)/shard_map/ppermute | solution.py:397
  11.2 0.4 collective-permute-start.9
  11.6 3.4 %collective-permute-done.9 = f32[8,8,128]{2,1,0:T(8,128)S(1)} collective-permute-done((f32[8,8,128]{2,1,0:T(8,128)S(1)}, f32[8,8,128]{2,1,0:T(8,128)S(1)}, u32[]{:S(2)}, u32[]{:S(2)}) %collective-permute-start.9) | collective-permute-done | bytes 32800 | tf_op jit(solution)/shard_map/ppermute | solution.py:397
  15.0 0.6 %receivers.1.planes = f32[8,16,128]{2,1,0:T(8,128)S(1)} custom-call(s32[16,128]{1,0:T(8,128)S(1)} %get-tuple-element.59.cells, f32[16,8,128]{2,1,0:T(8,128)S(1)} %constant_dynamic-update-slice_fusion.traces), custom_call_target="tpu_custom_call" | custom-call | flops 25165824 | bytes 1000000 | tf_op jit(solution)/shard_map/receivers/pallas_call | solution.py:449
  15.6 0.0 collective-permute-done.far_own.far_s0
  15.6 1.4 %collective-permute-done.1.far_coef = f32[40,16,128]{2,1,0:T(8,128)S(1)} collective-permute-done((f32[40,16,128]{2,1,0:T(8,128)S(1)}, f32[40,16,128]{2,1,0:T(8,128)S(1)}, u32[]{:S(2)}, u32[]{:S(2)}) %collective-permute-start.1) | collective-permute-done | bytes 327712 | tf_op jit(solution)/shard_map/ppermute | solution.py:390
  17.0 0.0 collective-permute-done.2.ev.ev1
  17.0 1.7 %first_s.1 = (f32[16,16,128]{2,1,0:T(8,128)S(1)}, f32[24,16,128]{2,1,0:T(8,128)S(1)}, f32[24,16,128]{2,1,0:T(8,128)S(1)}, f32[24,16,128]{2,1,0:T(8,128)S(1)}, f3...) custom-call(f32[16,16,128]{2,1,0:T(8,128)S(1)} %get-tuple-element.36, ...), custom_call_target="tpu_custom_call" | custom-call | flops 13762560 | bytes 6000000 | tf_op jit(solution)/shard_map/first_s/pallas_call | solution.py:464
  18.7 0.8 %collective-permute-done.5.od.far_r = f32[28,16,128]{2,1,0:T(8,128)S(1)} collective-permute-done((f32[28,16,128]{2,1,0:T(8,128)S(1)}, f32[28,16,128]{2,1,0:T(8,128)S(1)}, u32[]{:S(2)}, u32[]{:S(2)}) %collective-permute-start.5) | collective-permute-done | bytes 229408 | tf_op jit(solution)/shard_map/ppermute | solution.py:390
  19.4 1.3 %first_r.1 = (f32[16,16,128]{2,1,0:T(8,128)S(1)}, f32[24,16,128]{2,1,0:T(8,128)S(1)}, f32[24,16,128]{2,1,0:T(8,128)S(1)}, f32[24,16,128]{2,1,0:T(8,128)S(1)}) custom-call(f32[16,16,128]{2,1,0:T(8,128)S(1)} %get-tuple-element.56.own.r0, f32[16,16,128]{2,1,0:T(8,128)S(1)} %get-tuple-element.57.prior, f32[28,16,128]{2,1,0:T(8,128)S(1)} %collective-permute-done.5.od.far_r, ...), custom_call_target="tpu_custom_call" | custom-call | flops 13762560 | bytes 6000000 | tf_op jit(solution)/shard_map/first_r/pallas_call | solution.py:477
  20.7 4.0 %collective-permute-start.11 = (f32[24,16,128]{2,1,0:T(8,128)S(1)}, f32[24,16,128]{2,1,0:T(8,128)S(1)}, u32[]{:S(2)}, u32[]{:S(2)}) collective-permute-start(f32[24,16,128]{2,1,0:T(8,128)S(1)} %get-tuple-element.64), channel_id=1, source_target_pairs={{0,1},{1,0},{2,3},{3,2},{4,5},{5,4},{6,7},{7,6},{8,9},{9,8},{10,11... | collective-permute-start | bytes 589832 | tf_op jit(solution)/shard_map/ppermute | solution.py:387
  24.7 0.0 collective-permute-start.10
  24.7 1.7 %collective-permute-start.3 = (f32[24,16,128]{2,1,0:T(8,128)S(1)}, f32[24,16,128]{2,1,0:T(8,128)S(1)}, u32[]{:S(2)}, u32[]{:S(2)}) collective-permute-start(f32[24,16,128]{2,1,0:T(8,128)S(1)} %get-tuple-element.50), channel_id=1, source_target_pairs={{1,2},{3,4},{5,6},{7,8},{9,10},{11,12},{13,14},{17,18},{19,20},{21... | collective-permute-start | bytes 589832 | tf_op jit(solution)/shard_map/ppermute | solution.py:390
  26.4 1.0 %collective-permute-start.4 = (f32[24,16,128]{2,1,0:T(8,128)S(1)}, f32[24,16,128]{2,1,0:T(8,128)S(1)}, u32[]{:S(2)}, u32[]{:S(2)}) collective-permute-start(f32[24,16,128]{2,1,0:T(8,128)S(1)} %get-tuple-element.51), channel_id=1, source_target_pairs={{0,1},{1,0},{2,3},{3,2},{4,5},{5,4},{6,7},{7,6},{8,9},{9,8},{10,11... | collective-permute-start | bytes 589832 | tf_op jit(solution)/shard_map/ppermute | solution.py:387
  27.4 0.0 collective-permute-done.11.ev.evr
  27.4 6.6 %collective-permute-done.10.od.odr = f32[24,16,128]{2,1,0:T(8,128)S(1)} collective-permute-done((f32[24,16,128]{2,1,0:T(8,128)S(1)}, f32[24,16,128]{2,1,0:T(8,128)S(1)}, u32[]{:S(2)}, u32[]{:S(2)}) %collective-permute-start.10) | collective-permute-done | bytes 196640 | tf_op jit(solution)/shard_map/ppermute | solution.py:390
  34.0 1.3 %shard_map.110.r8 = f32[16,16,128]{2,1,0:T(8,128)S(1)} custom-call(f32[16,16,128]{2,1,0:T(8,128)S(1)} %get-tuple-element.61.own.r4, f32[24,16,128]{2,1,0:T(8,128)S(1)} %get-tuple-element.62.prior, f32[24,16,128]{2,1,0:T(8,128)S(1)} %collective-permute-done.10.od.odr, f32[24,16,128]{2,1,0:T(8,128)S(1)} %collective-permute-done.11.ev.evr, ...), custom_call_target="tpu_custom_call" | custom-call | flops 13762560 | bytes 6000000 | tf_op jit(solution)/shard_map/pallas_call | solution.py:504
  35.3 0.1 collective-permute-start.15
  35.4 0.7 %collective-permute-done.3.od.ods = f32[24,16,128]{2,1,0:T(8,128)S(1)} collective-permute-done((f32[24,16,128]{2,1,0:T(8,128)S(1)}, f32[24,16,128]{2,1,0:T(8,128)S(1)}, u32[]{:S(2)}, u32[]{:S(2)}) %collective-permute-start.3) | collective-permute-done | bytes 196640 | tf_op jit(solution)/shard_map/ppermute | solution.py:390
  36.1 0.0 collective-permute-done.4.ev.evs
  36.1 1.3 %shard_map.109.s8 = f32[16,16,128]{2,1,0:T(8,128)S(1)} custom-call(f32[16,16,128]{2,1,0:T(8,128)S(1)} %get-tuple-element.48.own.s4, f32[24,16,128]{2,1,0:T(8,128)S(1)} %get-tuple-element.49.prior, f32[24,16,128]{2,1,0:T(8,128)S(1)} %collective-permute-done.3.od.ods, f32[24,16,128]{2,1,0:T(8,128)S(1)} %collective-permute-done.4.ev.evs, ...), custom_call_target="tpu_custom_call" | custom-call | flops 13762560 | bytes 6000000 | tf_op jit(solution)/shard_map/pallas_call | solution.py:501
  37.4 0.1 collective-permute-start.12
  37.5 0.1 collective-permute-start.14
  37.6 1.7 %collective-permute-start.13 = (f32[16,16,128]{2,1,0:T(8,128)S(1)}, f32[16,16,128]{2,1,0:T(8,128)S(1)}, u32[]{:S(2)}, u32[]{:S(2)}) collective-permute-start(f32[16,16,128]{2,1,0:T(8,128)S(1)} %shard_map.110.r8), channel_id=1, source_target_pairs={{1,2},{3,4},{5,6},{7,8},{9,10},{11,12},{13,14},{17,18},{19,20},{21... | collective-permute-start | bytes 393224 | tf_op jit(solution)/shard_map/ppermute | solution.py:390
  39.3 0.9 %early_image.1.early = f32[32,16,16,128]{3,2,1,0:T(8,128)S(1)} custom-call(f32[16,16,128]{2,1,0:T(8,128)S(1)} %get-tuple-element.36.own.s0, f32[16,16,128]{2,1,0:T(8,128)S(1)} %get-tuple-element.48.own.s4, f32[16,16,128]{2,1,0:T(8,128)S(1)} %get-tuple-element.56.own.r0, f32[16,16,128]{2,1,0:T(8,128)S(1)} %get-tuple-element.61.own.r4, ...), custom_call_target="tpu_custom_call" | custom-call | flops 3244032 | bytes 1000000 | tf_op jit(solution)/shard_map/early_image/pallas_call | solution.py:510
  40.2 0.0 collective-permute-done.15.evr8
  40.2 0.0 collective-permute-done.12.evs8
  40.2 4.5 %collective-permute-done.14.ods8 = f32[16,16,128]{2,1,0:T(8,128)S(1)} collective-permute-done((f32[16,16,128]{2,1,0:T(8,128)S(1)}, f32[16,16,128]{2,1,0:T(8,128)S(1)}, u32[]{:S(2)}, u32[]{:S(2)}) %collective-permute-start.14) | collective-permute-done | bytes 131104 | tf_op jit(solution)/shard_map/ppermute | solution.py:390
  44.8 2.0 %image.1 = (f32[33,16,16,128]{3,2,1,0:T(8,128)}, f32[136,16,128]{2,1,0:T(8,128)S(1)}) custom-call(f32[16,16,128]{2,1,0:T(8,128)S(1)} %get-tuple-element.36.own.s0, f32[16,16,128]{2,1,0:T(8,128)S(1)} %get-tuple-element.48.own.s4, f32[16,16,128]{2,1,0:T(8,128)S(1)} %shard_map.109.s8, f32[16,16,128]{2,1,0:T(8,128)S(1)} %get-tuple-element.56.own.r0, ...), custom_call_target="tpu_custom_call" | custom-call | flops 4325376 | bytes 4400000 | tf_op jit(solution)/shard_map/image/pallas_call | solution.py:520
  46.8 0.0 collective-permute-done.13.odr8
  46.8 1.2 %last_image.1 = f32[33,16,16,128]{3,2,1,0:T(8,128)} custom-call(f32[16,16,128]{2,1,0:T(8,128)S(1)} %shard_map.109.s8, f32[16,16,128]{2,1,0:T(8,128)S(1)} %shard_map.110.r8, f32[16,16,128]{2,1,0:T(8,128)S(1)} %collective-permute-done.12.evs8, f32[16,16,128]{2,1,0:T(8,128)S(1)} %collective-permute-done.13.odr8, ...), custom_call_target="tpu_custom_call", output_to_operand_aliasing={{}: (5, {})} | custom-call | flops 1048576 | bytes 2200000 | tf_op jit(solution)/shard_map/last_image/pallas_call | solution.py:530
  (8 shorter events, 0.0 us)
Async XLA Ops:
  0.0 6.8 %collective-permute-start.6 = (f32[1,8,128]{2,1,0:T(8,128)}, f32[1,8,128]{2,1,0:T(8,128)S(1)}, u32[]{:S(2)}, u32[]{:S(2)}) collective-permute-start(f32[1,8,128]{2,1,0:T(8,128)} %bitcast.7), channel_id=1, source_target_pairs={{0,2},{1,3},{2,0},{3,1},{4,6},{5,7},{6,4},{7,5},{8,10},{9,11},{10,... | collective-permute-start | bytes 12296 | tf_op jit(solution)/shard_map/ppermute | solution.py:397
  1.2 14.3 %collective-permute-start = (f32[16,16,128]{2,1,0:T(8,128)}, f32[16,16,128]{2,1,0:T(8,128)S(1)}, u32[]{:S(2)}, u32[]{:S(2)}) collective-permute-start(f32[16,16,128]{2,1,0:T(8,128)} %refs_0_.1), channel_id=1, source_target_pairs={{1,2},{3,4},{5,6},{7,8},{9,10},{11,12},{13,14},{17,18},{19,20},{21... | collective-permute-start | bytes 393224 | tf_op jit(solution)/shard_map/ppermute | solution.py:390
  3.7 13.3 %collective-permute-start.2 = (f32[84,16,128]{2,1,0:T(8,128)S(1)}, f32[84,16,128]{2,1,0:T(8,128)S(1)}, u32[]{:S(2)}, u32[]{:S(2)}) collective-permute-start(f32[84,16,128]{2,1,0:T(8,128)S(1)} %get-tuple-element.41), channel_id=1, source_target_pairs={{0,1},{1,0},{2,3},{3,2},{4,5},{5,4},{6,7},{7,6},{8,9},{9,8},{10,11... | collective-permute-start | bytes 2064392 | tf_op jit(solution)/shard_map/ppermute | solution.py:387
  3.8 13.2 %collective-permute-start.1 = (f32[40,16,128]{2,1,0:T(8,128)S(1)}, f32[40,16,128]{2,1,0:T(8,128)S(1)}, u32[]{:S(2)}, u32[]{:S(2)}) collective-permute-start(f32[40,16,128]{2,1,0:T(8,128)S(1)} %get-tuple-element.40), channel_id=1, source_target_pairs={{1,2},{3,4},{5,6},{7,8},{9,10},{11,12},{13,14},{17,18},{19,20},{21... | collective-permute-start | bytes 983048 | tf_op jit(solution)/shard_map/ppermute | solution.py:390
  6.4 13.0 %collective-permute-start.5 = (f32[28,16,128]{2,1,0:T(8,128)S(1)}, f32[28,16,128]{2,1,0:T(8,128)S(1)}, u32[]{:S(2)}, u32[]{:S(2)}) collective-permute-start(f32[28,16,128]{2,1,0:T(8,128)S(1)} %get-tuple-element.58), channel_id=1, source_target_pairs={{1,2},{3,4},{5,6},{7,8},{9,10},{11,12},{13,14},{17,18},{19,20},{21... | collective-permute-start | bytes 688136 | tf_op jit(solution)/shard_map/ppermute | solution.py:390
  6.8 1.4 %collective-permute-start.7 = (f32[2,8,128]{2,1,0:T(8,128)S(1)}, f32[2,8,128]{2,1,0:T(8,128)S(1)}, u32[]{:S(2)}, u32[]{:S(2)}) collective-permute-start(f32[2,8,128]{2,1,0:T(8,128)S(1)} %pad_maximum_fusion.2), channel_id=1, source_target_pairs={{0,1},{1,0},{2,3},{3,2},{4,5},{5,4},{6,7},{7,6},{8,9},{9,8},{10,11... | collective-permute-start | bytes 24584 | tf_op jit(solution)/shard_map/ppermute | solution.py:397
  8.2 3.1 %collective-permute-start.8 = (f32[4,8,128]{2,1,0:T(8,128)S(1)}, f32[4,8,128]{2,1,0:T(8,128)S(1)}, u32[]{:S(2)}, u32[]{:S(2)}) collective-permute-start(f32[4,8,128]{2,1,0:T(8,128)S(1)} %pad_maximum_fusion.1), channel_id=1, source_target_pairs={{0,4},{1,5},{2,6},{3,7},{4,0},{5,1},{6,2},{7,3},{8,12},{9,13},{10,... | collective-permute-start | bytes 49160 | tf_op jit(solution)/shard_map/ppermute | solution.py:397
  11.2 3.8 %collective-permute-start.9 = (f32[8,8,128]{2,1,0:T(8,128)S(1)}, f32[8,8,128]{2,1,0:T(8,128)S(1)}, u32[]{:S(2)}, u32[]{:S(2)}) collective-permute-start(f32[8,8,128]{2,1,0:T(8,128)S(1)} %pad_maximum_fusion), channel_id=1, source_target_pairs={{0,8},{1,9},{2,10},{3,11},{4,12},{5,13},{6,14},{7,15},{8,0},{9,1},... | collective-permute-start | bytes 98312 | tf_op jit(solution)/shard_map/ppermute | solution.py:397
  20.7 6.7 %collective-permute-start.11 = (f32[24,16,128]{2,1,0:T(8,128)S(1)}, f32[24,16,128]{2,1,0:T(8,128)S(1)}, u32[]{:S(2)}, u32[]{:S(2)}) collective-permute-start(f32[24,16,128]{2,1,0:T(8,128)S(1)} %get-tuple-element.64), channel_id=1, source_target_pairs={{0,1},{1,0},{2,3},{3,2},{4,5},{5,4},{6,7},{7,6},{8,9},{9,8},{10,11... | collective-permute-start | bytes 589832 | tf_op jit(solution)/shard_map/ppermute | solution.py:387
  24.7 9.3 %collective-permute-start.10 = (f32[24,16,128]{2,1,0:T(8,128)S(1)}, f32[24,16,128]{2,1,0:T(8,128)S(1)}, u32[]{:S(2)}, u32[]{:S(2)}) collective-permute-start(f32[24,16,128]{2,1,0:T(8,128)S(1)} %get-tuple-element.63), channel_id=1, source_target_pairs={{1,2},{3,4},{5,6},{7,8},{9,10},{11,12},{13,14},{17,18},{19,20},{21... | collective-permute-start | bytes 589832 | tf_op jit(solution)/shard_map/ppermute | solution.py:390
  24.7 11.4 %collective-permute-start.3 = (f32[24,16,128]{2,1,0:T(8,128)S(1)}, f32[24,16,128]{2,1,0:T(8,128)S(1)}, u32[]{:S(2)}, u32[]{:S(2)}) collective-permute-start(f32[24,16,128]{2,1,0:T(8,128)S(1)} %get-tuple-element.50), channel_id=1, source_target_pairs={{1,2},{3,4},{5,6},{7,8},{9,10},{11,12},{13,14},{17,18},{19,20},{21... | collective-permute-start | bytes 589832 | tf_op jit(solution)/shard_map/ppermute | solution.py:390
  26.4 9.7 %collective-permute-start.4 = (f32[24,16,128]{2,1,0:T(8,128)S(1)}, f32[24,16,128]{2,1,0:T(8,128)S(1)}, u32[]{:S(2)}, u32[]{:S(2)}) collective-permute-start(f32[24,16,128]{2,1,0:T(8,128)S(1)} %get-tuple-element.51), channel_id=1, source_target_pairs={{0,1},{1,0},{2,3},{3,2},{4,5},{5,4},{6,7},{7,6},{8,9},{9,8},{10,11... | collective-permute-start | bytes 589832 | tf_op jit(solution)/shard_map/ppermute | solution.py:387
  35.3 4.9 %collective-permute-start.15 = (f32[16,16,128]{2,1,0:T(8,128)S(1)}, f32[16,16,128]{2,1,0:T(8,128)S(1)}, u32[]{:S(2)}, u32[]{:S(2)}) collective-permute-start(f32[16,16,128]{2,1,0:T(8,128)S(1)} %shard_map.110.r8), channel_id=1, source_target_pairs={{0,1},{1,0},{2,3},{3,2},{4,5},{5,4},{6,7},{7,6},{8,9},{9,8},{10,11... | collective-permute-start | bytes 393224 | tf_op jit(solution)/shard_map/ppermute | solution.py:387
  37.4 2.8 %collective-permute-start.12 = (f32[16,16,128]{2,1,0:T(8,128)S(1)}, f32[16,16,128]{2,1,0:T(8,128)S(1)}, u32[]{:S(2)}, u32[]{:S(2)}) collective-permute-start(f32[16,16,128]{2,1,0:T(8,128)S(1)} %shard_map.109.s8), channel_id=1, source_target_pairs={{0,1},{1,0},{2,3},{3,2},{4,5},{5,4},{6,7},{7,6},{8,9},{9,8},{10,11... | collective-permute-start | bytes 393224 | tf_op jit(solution)/shard_map/ppermute | solution.py:387
  37.5 7.3 %collective-permute-start.14 = (f32[16,16,128]{2,1,0:T(8,128)S(1)}, f32[16,16,128]{2,1,0:T(8,128)S(1)}, u32[]{:S(2)}, u32[]{:S(2)}) collective-permute-start(f32[16,16,128]{2,1,0:T(8,128)S(1)} %shard_map.109.s8), channel_id=1, source_target_pairs={{1,2},{3,4},{5,6},{7,8},{9,10},{11,12},{13,14},{17,18},{19,20},{21... | collective-permute-start | bytes 393224 | tf_op jit(solution)/shard_map/ppermute | solution.py:390
  37.6 9.2 %collective-permute-start.13 = (f32[16,16,128]{2,1,0:T(8,128)S(1)}, f32[16,16,128]{2,1,0:T(8,128)S(1)}, u32[]{:S(2)}, u32[]{:S(2)}) collective-permute-start(f32[16,16,128]{2,1,0:T(8,128)S(1)} %shard_map.110.r8), channel_id=1, source_target_pairs={{1,2},{3,4},{5,6},{7,8},{9,10},{11,12},{13,14},{17,18},{19,20},{21... | collective-permute-start | bytes 393224 | tf_op jit(solution)/shard_map/ppermute | solution.py:390

commit v7 on v6

--- a/solution.py
+++ b/solution.py
@@ -294,23 +294,38 @@
     dst[level, pl.ds(2 * n * (1 - p), n)] = ev[ev_lo : ev_lo + n]
 
 
-def early_image_kernel(s0, s4, r0, r4, far_s0, ev1, ods, evs, evr, block, lag_s, lag_r):
+def first_image_kernel(s0, r0, far_s0, ev1, block, lag_s, lag_r):
     _, _, sign, _, own_start = sides()
     n = s0.shape[0]
     place_rows(lag_s, 0, s0, far_s0, 0, ev1, n + TRIM)
     place_rows(lag_r, 0, r0, None, 0, ev1, 2 * (n + TRIM))
-    place_rows(lag_s, 1, s4, ods, 0, evs, 0)
-    place_rows(lag_r, 1, r4, None, 0, evr, 0)
 
     def whole(j, carry):
         for x in range(n):
-            block[j, x] = lagged(lag_s, lag_r, (0, 1), x, sign * j)
+            block[j, x] = lagged(lag_s, lag_r, (0,), x, sign * j)
         return carry
 
     lax.fori_loop(0, HALF + 1, whole, 0)
     for reach in range(1, HALF):
         for i in range(n - reach):
-            block[HALF + reach, i] = lagged(lag_s, lag_r, (0, 1), own_start(reach) + i, -sign * reach)
+            block[HALF + reach, i] = lagged(lag_s, lag_r, (0,), own_start(reach) + i, -sign * reach)
+
+
+def early_image_kernel(s4, r4, ods, evs, evr, before, block, lag_s, lag_r):
+    _, _, sign, _, own_start = sides()
+    n = s4.shape[0]
+    place_rows(lag_s, 0, s4, ods, 0, evs, 0)
+    place_rows(lag_r, 0, r4, None, 0, evr, 0)
+
+    def whole(j, carry):
+        for x in range(n):
+            block[j, x] = before[j, x] + lagged(lag_s, lag_r, (0,), x, sign * j)
+        return carry
+
+    lax.fori_loop(0, HALF + 1, whole, 0)
+    for reach in range(1, HALF):
+        for i in range(n - reach):
+            block[HALF + reach, i] = before[HALF + reach, i] + lagged(lag_s, lag_r, (0,), own_start(reach) + i, -sign * reach)
 
 
 def image_kernel(s0, s4, s8, r0, r4, r8, ev1, far_r, evs, odr, evr, ods8, evs8, evr8, early, out, rest, lag_s, lag_r, block, sems):
@@ -390,8 +405,7 @@
         return lax.ppermute(x, ("shot", "gx"), far)
 
     hops = [2, 1] if count > 2 else [1]
-    while 2 * max(hops) < count:
-        hops.append(2 * max(hops))
+    hops += [1 << bit for bit in range(count.bit_length() - 2, 1, -1)]
 
     def exchange(x, which):
         return lax.ppermute(x, "gx", [(i, i ^ hops[which]) for i in range(count)])
@@ -507,16 +521,20 @@
     lags = lambda levels: [pltpu.VMEM((levels, wide, ny, nz), f32)] * 2
     corner = HALF * (HALF + 1) // 2
     hbm = pl.BlockSpec(memory_space=pltpu.MemorySpace.HBM)
-    early = pl.pallas_call(
-        early_image_kernel,
-        out_shape=shape(2 * HALF, n, ny, nz),
-        in_specs=vmem_specs(9),
-        out_specs=pl.BlockSpec(memory_space=pltpu.VMEM),
-        scratch_shapes=lags(2),
-        compiler_params=params(8),
-        cost_estimate=estimate(NOFF * n * ny * nz * 3, 1000000),
-        name="early_image",
-    )(source_field, s4, receiver_field, r4, far_s0, ev1, ods, evs, evr)
+
+    def products(kernel, *inputs):
+        return pl.pallas_call(
+            kernel,
+            out_shape=shape(2 * HALF, n, ny, nz),
+            in_specs=vmem_specs(len(inputs)),
+            out_specs=pl.BlockSpec(memory_space=pltpu.VMEM),
+            scratch_shapes=lags(1),
+            compiler_params=params(8),
+            cost_estimate=estimate(NOFF * n * ny * nz * 3, 1000000),
+        )(*inputs)
+
+    early = products(first_image_kernel, source_field, receiver_field, far_s0, ev1)
+    early = products(early_image_kernel, s4, r4, ods, evs, evr, early)
     image, rest = pl.pallas_call(
         image_kernel,
         out_shape=[shape(NOFF, n, ny, nz), shape(corner, ny, nz)],

time: 48.1 us -> 42 us (0.87)
  the two profiles are of different devices: /device:TPU:17 before, /device:TPU:27 now
where the time goes in v7:
time: 42 us; the launch traced here: 41.8 us
  waiting for transfers between devices  21.6 us (51%)
  Pallas kernels  12.2 us (29%)
  starting transfers between devices  7.77 us (18%)
    ppermute x7, waiting for transfers between devices, swap_far(): return lax.ppermute(x, ('shot', 'gx'), far)  13.8 us
    ppermute x4, waiting for transfers between devices, exchange(): return lax.ppermute(x, 'gx', [(i, i ^ hops[which]) for i in range(count)])  7.78 us
    ppermute x7, starting transfers between devices, swap_far(): return lax.ppermute(x, ('shot', 'gx'), far)  4.82 us
    pallas_call x1, Pallas kernels, local(): pl.pallas_call(image_kernel, out_shape=[shape(NOFF, n, ny, nz), shape(cor...  2.02 us
    pallas_call x1, Pallas kernels, local(): pl.pallas_call(first_kernel, out_shape=[own, prior, shape(n + THIN, ny, n...  1.69 us
    ppermute x5, starting transfers between devices, swap_near(): return lax.ppermute(x, 'gx', near)  1.48 us
    ppermute x4, starting transfers between devices, exchange(): return lax.ppermute(x, 'gx', [(i, i ^ hops[which]) for i in range(count)])  1.47 us
    pallas_call x1, Pallas kernels, local(): pl.pallas_call(functools.partial(pack_kernel, count=len(args)), out_shape...  1.38 us
  transfers between devices with their start and end apart: 16, of which 7 were waited for; matrix products, arithmetic and copies ran while one was open for 0% of the time, Pallas kernels for 27%

profile of v7, /device:TPU:27, one launch (start us, length us, event | category | flops | bytes accessed | tf_op | source)
XLA Modules:
  0.0 41.8 jit_solution(13815760068936179639)
XLA Ops:
  0.0 1.2 %collective-permute-start.6 = (f32[1,8,128]{2,1,0:T(8,128)}, f32[1,8,128]{2,1,0:T(8,128)S(1)}, u32[]{:S(2)}, u32[]{:S(2)}) collective-permute-start(f32[1,8,128]{2,1,0:T(8,128)} %bitcast.7), channel_id=1, source_target_pairs={{0,2},{1,3},{2,0},{3,1},{4,6},{5,7},{6,4},{7,5},{8,10},{9,11},{10,... | collective-permute-start | bytes 12296 | tf_op jit(solution)/shard_map/ppermute | solution.py:411
  1.2 1.1 %collective-permute-start = (f32[16,16,128]{2,1,0:T(8,128)}, f32[16,16,128]{2,1,0:T(8,128)S(1)}, u32[]{:S(2)}, u32[]{:S(2)}) collective-permute-start(f32[16,16,128]{2,1,0:T(8,128)} %refs_0_.1), channel_id=1, source_target_pairs={{1,2},{3,4},{5,6},{7,8},{9,10},{11,12},{13,14},{17,18},{19,20},{21... | collective-permute-start | bytes 393224 | tf_op jit(solution)/shard_map/ppermute | solution.py:405
  2.3 1.4 %pack.1 = (f32[16,16,128]{2,1,0:T(8,128)S(1)}, f32[16,16,128]{2,1,0:T(8,128)S(1)}, f32[16,16,128]{2,1,0:T(8,128)S(1)}, f32[16,16,128]{2,1,0:T(8,128)S(1)}, f32[1...) custom-call(f32[16,16,128]{2,1,0:T(8,128)} %refs_0_.1, ...), custom_call_target="tpu_custom_call" | custom-call | flops 1000 | bytes 3000000 | tf_op jit(solution)/shard_map/pack/pallas_call | solution.py:432
  3.7 0.7 %collective-permute-start.5 = (f32[28,16,128]{2,1,0:T(8,128)S(1)}, f32[28,16,128]{2,1,0:T(8,128)S(1)}, u32[]{:S(2)}, u32[]{:S(2)}) collective-permute-start(f32[28,16,128]{2,1,0:T(8,128)S(1)} %get-tuple-element.58), channel_id=1, source_target_pairs={{1,2},{3,4},{5,6},{7,8},{9,10},{11,12},{13,14},{17,18},{19,20},{21... | collective-permute-start | bytes 688136 | tf_op jit(solution)/shard_map/ppermute | solution.py:405
  4.4 1.1 %collective-permute-start.1 = (f32[40,16,128]{2,1,0:T(8,128)S(1)}, f32[40,16,128]{2,1,0:T(8,128)S(1)}, u32[]{:S(2)}, u32[]{:S(2)}) collective-permute-start(f32[40,16,128]{2,1,0:T(8,128)S(1)} %get-tuple-element.40), channel_id=1, source_target_pairs={{1,2},{3,4},{5,6},{7,8},{9,10},{11,12},{13,14},{17,18},{19,20},{21... | collective-permute-start | bytes 983048 | tf_op jit(solution)/shard_map/ppermute | solution.py:405
  5.5 0.9 %collective-permute-start.2 = (f32[84,16,128]{2,1,0:T(8,128)S(1)}, f32[84,16,128]{2,1,0:T(8,128)S(1)}, u32[]{:S(2)}, u32[]{:S(2)}) collective-permute-start(f32[84,16,128]{2,1,0:T(8,128)S(1)} %get-tuple-element.41), channel_id=1, source_target_pairs={{0,1},{1,0},{2,3},{3,2},{4,5},{5,4},{6,7},{7,6},{8,9},{9,8},{10,11... | collective-permute-start | bytes 2064392 | tf_op jit(solution)/shard_map/ppermute | solution.py:402
  6.4 0.3 shots.1
  6.7 0.0 collective-permute-done.6
  6.7 0.1 collective-permute-start.7
  6.8 1.3 %collective-permute-done.7 = f32[2,8,128]{2,1,0:T(8,128)S(1)} collective-permute-done((f32[2,8,128]{2,1,0:T(8,128)S(1)}, f32[2,8,128]{2,1,0:T(8,128)S(1)}, u32[]{:S(2)}, u32[]{:S(2)}) %collective-permute-start.7) | collective-permute-done | bytes 8224 | tf_op jit(solution)/shard_map/ppermute | solution.py:411
  8.2 0.1 collective-permute-start.8
  8.2 3.8 %collective-permute-done.8 = f32[4,8,128]{2,1,0:T(8,128)S(1)} collective-permute-done((f32[4,8,128]{2,1,0:T(8,128)S(1)}, f32[4,8,128]{2,1,0:T(8,128)S(1)}, u32[]{:S(2)}, u32[]{:S(2)}) %collective-permute-start.8) | collective-permute-done | bytes 16416 | tf_op jit(solution)/shard_map/ppermute | solution.py:411
  12.0 0.1 collective-permute-start.9
  12.1 2.7 %collective-permute-done.9 = f32[8,8,128]{2,1,0:T(8,128)S(1)} collective-permute-done((f32[8,8,128]{2,1,0:T(8,128)S(1)}, f32[8,8,128]{2,1,0:T(8,128)S(1)}, u32[]{:S(2)}, u32[]{:S(2)}) %collective-permute-start.9) | collective-permute-done | bytes 32800 | tf_op jit(solution)/shard_map/ppermute | solution.py:411
  14.8 0.6 %receivers.1.planes = f32[8,16,128]{2,1,0:T(8,128)S(1)} custom-call(s32[16,128]{1,0:T(8,128)S(1)} %get-tuple-element.59.cells, f32[16,8,128]{2,1,0:T(8,128)S(1)} %constant_dynamic-update-slice_fusion.traces), custom_call_target="tpu_custom_call" | custom-call | flops 25165824 | bytes 1000000 | tf_op jit(solution)/shard_map/receivers/pallas_call | solution.py:463
  15.4 0.0 collective-permute-done.far_own.far_s0
  15.4 3.8 %collective-permute-done.1.far_coef = f32[40,16,128]{2,1,0:T(8,128)S(1)} collective-permute-done((f32[40,16,128]{2,1,0:T(8,128)S(1)}, f32[40,16,128]{2,1,0:T(8,128)S(1)}, u32[]{:S(2)}, u32[]{:S(2)}) %collective-permute-start.1) | collective-permute-done | bytes 327712 | tf_op jit(solution)/shard_map/ppermute | solution.py:405
  19.2 0.0 collective-permute-done.2.ev.ev1
  19.2 1.7 %first_s.1 = (f32[16,16,128]{2,1,0:T(8,128)S(1)}, f32[24,16,128]{2,1,0:T(8,128)S(1)}, f32[24,16,128]{2,1,0:T(8,128)S(1)}, f32[24,16,128]{2,1,0:T(8,128)S(1)}, f3...) custom-call(f32[16,16,128]{2,1,0:T(8,128)S(1)} %get-tuple-element.36, ...), custom_call_target="tpu_custom_call" | custom-call | flops 13762560 | bytes 6000000 | tf_op jit(solution)/shard_map/first_s/pallas_call | solution.py:478
  20.9 0.1 collective-permute-start.3
  21.0 0.1 collective-permute-start.4
  21.0 0.0 collective-permute-done.5.od.far_r
  21.1 1.3 %first_r.1 = (f32[16,16,128]{2,1,0:T(8,128)S(1)}, f32[24,16,128]{2,1,0:T(8,128)S(1)}, f32[24,16,128]{2,1,0:T(8,128)S(1)}, f32[24,16,128]{2,1,0:T(8,128)S(1)}) custom-call(f32[16,16,128]{2,1,0:T(8,128)S(1)} %get-tuple-element.56.own.r0, f32[16,16,128]{2,1,0:T(8,128)S(1)} %get-tuple-element.57.prior, f32[28,16,128]{2,1,0:T(8,128)S(1)} %collective-permute-done.5.od.far_r, ...), custom_call_target="tpu_custom_call" | custom-call | flops 13762560 | bytes 6000000 | tf_op jit(solution)/shard_map/first_r/pallas_call | solution.py:491
  22.3 1.7 %collective-permute-start.10 = (f32[24,16,128]{2,1,0:T(8,128)S(1)}, f32[24,16,128]{2,1,0:T(8,128)S(1)}, u32[]{:S(2)}, u32[]{:S(2)}) collective-permute-start(f32[24,16,128]{2,1,0:T(8,128)S(1)} %get-tuple-element.63), channel_id=1, source_target_pairs={{1,2},{3,4},{5,6},{7,8},{9,10},{11,12},{13,14},{17,18},{19,20},{21... | collective-permute-start | bytes 589832 | tf_op jit(solution)/shard_map/ppermute | solution.py:405
  24.0 0.4 collective-permute-start.11
  24.4 5.5 %collective-permute-done.3.od.ods = f32[24,16,128]{2,1,0:T(8,128)S(1)} collective-permute-done((f32[24,16,128]{2,1,0:T(8,128)S(1)}, f32[24,16,128]{2,1,0:T(8,128)S(1)}, u32[]{:S(2)}, u32[]{:S(2)}) %collective-permute-start.3) | collective-permute-done | bytes 196640 | tf_op jit(solution)/shard_map/ppermute | solution.py:405
  29.9 0.0 collective-permute-done.4.ev.evs
  29.9 1.3 %shard_map.109.s8 = f32[16,16,128]{2,1,0:T(8,128)S(1)} custom-call(f32[16,16,128]{2,1,0:T(8,128)S(1)} %get-tuple-element.48.own.s4, f32[24,16,128]{2,1,0:T(8,128)S(1)} %get-tuple-element.49.prior, f32[24,16,128]{2,1,0:T(8,128)S(1)} %collective-permute-done.3.od.ods, f32[24,16,128]{2,1,0:T(8,128)S(1)} %collective-permute-done.4.ev.evs, ...), custom_call_target="tpu_custom_call" | custom-call | flops 13762560 | bytes 6000000 | tf_op jit(solution)/shard_map/pallas_call | solution.py:515
  31.2 0.1 collective-permute-start.14
  31.3 0.1 collective-permute-start.12
  31.4 2.1 %collective-permute-done.10.od.odr = f32[24,16,128]{2,1,0:T(8,128)S(1)} collective-permute-done((f32[24,16,128]{2,1,0:T(8,128)S(1)}, f32[24,16,128]{2,1,0:T(8,128)S(1)}, u32[]{:S(2)}, u32[]{:S(2)}) %collective-permute-start.10) | collective-permute-done | bytes 196640 | tf_op jit(solution)/shard_map/ppermute | solution.py:405
  33.4 0.0 collective-permute-done.11.ev.evr
  33.4 1.3 %shard_map.110.r8 = f32[16,16,128]{2,1,0:T(8,128)S(1)} custom-call(f32[16,16,128]{2,1,0:T(8,128)S(1)} %get-tuple-element.61.own.r4, f32[24,16,128]{2,1,0:T(8,128)S(1)} %get-tuple-element.62.prior, f32[24,16,128]{2,1,0:T(8,128)S(1)} %collective-permute-done.10.od.odr, f32[24,16,128]{2,1,0:T(8,128)S(1)} %collective-permute-done.11.ev.evr, ...), custom_call_target="tpu_custom_call" | custom-call | flops 13762560 | bytes 6000000 | tf_op jit(solution)/shard_map/pallas_call | solution.py:518
  34.7 0.1 collective-permute-start.15
  34.8 0.1 collective-permute-start.13
  34.9 0.6 %shard_map.111.before = f32[32,16,16,128]{3,2,1,0:T(8,128)S(1)} custom-call(f32[16,16,128]{2,1,0:T(8,128)S(1)} %get-tuple-element.36.own.s0, f32[16,16,128]{2,1,0:T(8,128)S(1)} %get-tuple-element.56.own.r0, f32[16,16,128]{2,1,0:T(8,128)S(1)} %collective-permute-done.far_own.far_s0, f32[84,16,128]{2,1,0:T(8,128)S(1)} %collective-permute-done.2.ev.ev1), custom_call_target="tpu_custom_call" | custom-call | flops 3244032 | bytes 1000000 | tf_op jit(solution)/shard_map/pallas_call | solution.py:526
  35.5 0.7 %shard_map.112.early = f32[32,16,16,128]{3,2,1,0:T(8,128)S(1)} custom-call(f32[16,16,128]{2,1,0:T(8,128)S(1)} %get-tuple-element.48.own.s4, f32[16,16,128]{2,1,0:T(8,128)S(1)} %get-tuple-element.61.own.r4, f32[24,16,128]{2,1,0:T(8,128)S(1)} %collective-permute-done.3.od.ods, f32[24,16,128]{2,1,0:T(8,128)S(1)} %collective-permute-done.4.ev.evs, ...), custom_call_target="tpu_custom_call" | custom-call | flops 3244032 | bytes 1000000 | tf_op jit(solution)/shard_map/pallas_call | solution.py:526
  36.2 0.0 collective-permute-done.14.ods8
  36.2 0.0 collective-permute-done.12.evs8
  36.2 0.0 collective-permute-done.15.evr8
  36.2 2.0 %image.1 = (f32[33,16,16,128]{3,2,1,0:T(8,128)}, f32[136,16,128]{2,1,0:T(8,128)S(1)}) custom-call(f32[16,16,128]{2,1,0:T(8,128)S(1)} %get-tuple-element.36.own.s0, f32[16,16,128]{2,1,0:T(8,128)S(1)} %get-tuple-element.48.own.s4, f32[16,16,128]{2,1,0:T(8,128)S(1)} %shard_map.109.s8, f32[16,16,128]{2,1,0:T(8,128)S(1)} %get-tuple-element.56.own.r0, ...), custom_call_target="tpu_custom_call" | custom-call | flops 4325376 | bytes 4400000 | tf_op jit(solution)/shard_map/image/pallas_call | solution.py:538
  38.2 2.5 %collective-permute-done.13.odr8 = f32[16,16,128]{2,1,0:T(8,128)S(1)} collective-permute-done((f32[16,16,128]{2,1,0:T(8,128)S(1)}, f32[16,16,128]{2,1,0:T(8,128)S(1)}, u32[]{:S(2)}, u32[]{:S(2)}) %collective-permute-start.13) | collective-permute-done | bytes 131104 | tf_op jit(solution)/shard_map/ppermute | solution.py:405
  40.7 1.2 %last_image.1 = f32[33,16,16,128]{3,2,1,0:T(8,128)} custom-call(f32[16,16,128]{2,1,0:T(8,128)S(1)} %shard_map.109.s8, f32[16,16,128]{2,1,0:T(8,128)S(1)} %shard_map.110.r8, f32[16,16,128]{2,1,0:T(8,128)S(1)} %collective-permute-done.12.evs8, f32[16,16,128]{2,1,0:T(8,128)S(1)} %collective-permute-done.13.odr8, ...), custom_call_target="tpu_custom_call", output_to_operand_aliasing={{}: (5, {})} | custom-call | flops 1048576 | bytes 2200000 | tf_op jit(solution)/shard_map/last_image/pallas_call | solution.py:548
  (8 shorter events, 0.0 us)
Async XLA Ops:
  0.0 6.7 %collective-permute-start.6 = (f32[1,8,128]{2,1,0:T(8,128)}, f32[1,8,128]{2,1,0:T(8,128)S(1)}, u32[]{:S(2)}, u32[]{:S(2)}) collective-permute-start(f32[1,8,128]{2,1,0:T(8,128)} %bitcast.7), channel_id=1, source_target_pairs={{0,2},{1,3},{2,0},{3,1},{4,6},{5,7},{6,4},{7,5},{8,10},{9,11},{10,... | collective-permute-start | bytes 12296 | tf_op jit(solution)/shard_map/ppermute | solution.py:411
  1.2 14.1 %collective-permute-start = (f32[16,16,128]{2,1,0:T(8,128)}, f32[16,16,128]{2,1,0:T(8,128)S(1)}, u32[]{:S(2)}, u32[]{:S(2)}) collective-permute-start(f32[16,16,128]{2,1,0:T(8,128)} %refs_0_.1), channel_id=1, source_target_pairs={{1,2},{3,4},{5,6},{7,8},{9,10},{11,12},{13,14},{17,18},{19,20},{21... | collective-permute-start | bytes 393224 | tf_op jit(solution)/shard_map/ppermute | solution.py:405
  3.7 17.4 %collective-permute-start.5 = (f32[28,16,128]{2,1,0:T(8,128)S(1)}, f32[28,16,128]{2,1,0:T(8,128)S(1)}, u32[]{:S(2)}, u32[]{:S(2)}) collective-permute-start(f32[28,16,128]{2,1,0:T(8,128)S(1)} %get-tuple-element.58), channel_id=1, source_target_pairs={{1,2},{3,4},{5,6},{7,8},{9,10},{11,12},{13,14},{17,18},{19,20},{21... | collective-permute-start | bytes 688136 | tf_op jit(solution)/shard_map/ppermute | solution.py:405
  4.4 14.7 %collective-permute-start.1 = (f32[40,16,128]{2,1,0:T(8,128)S(1)}, f32[40,16,128]{2,1,0:T(8,128)S(1)}, u32[]{:S(2)}, u32[]{:S(2)}) collective-permute-start(f32[40,16,128]{2,1,0:T(8,128)S(1)} %get-tuple-element.40), channel_id=1, source_target_pairs={{1,2},{3,4},{5,6},{7,8},{9,10},{11,12},{13,14},{17,18},{19,20},{21... | collective-permute-start | bytes 983048 | tf_op jit(solution)/shard_map/ppermute | solution.py:405
  5.5 13.7 %collective-permute-start.2 = (f32[84,16,128]{2,1,0:T(8,128)S(1)}, f32[84,16,128]{2,1,0:T(8,128)S(1)}, u32[]{:S(2)}, u32[]{:S(2)}) collective-permute-start(f32[84,16,128]{2,1,0:T(8,128)S(1)} %get-tuple-element.41), channel_id=1, source_target_pairs={{0,1},{1,0},{2,3},{3,2},{4,5},{5,4},{6,7},{7,6},{8,9},{9,8},{10,11... | collective-permute-start | bytes 2064392 | tf_op jit(solution)/shard_map/ppermute | solution.py:402
  6.7 1.4 %collective-permute-start.7 = (f32[2,8,128]{2,1,0:T(8,128)S(1)}, f32[2,8,128]{2,1,0:T(8,128)S(1)}, u32[]{:S(2)}, u32[]{:S(2)}) collective-permute-start(f32[2,8,128]{2,1,0:T(8,128)S(1)} %pad_maximum_fusion.2), channel_id=1, source_target_pairs={{0,1},{1,0},{2,3},{3,2},{4,5},{5,4},{6,7},{7,6},{8,9},{9,8},{10,11... | collective-permute-start | bytes 24584 | tf_op jit(solution)/shard_map/ppermute | solution.py:411
  8.2 3.8 %collective-permute-start.8 = (f32[4,8,128]{2,1,0:T(8,128)S(1)}, f32[4,8,128]{2,1,0:T(8,128)S(1)}, u32[]{:S(2)}, u32[]{:S(2)}) collective-permute-start(f32[4,8,128]{2,1,0:T(8,128)S(1)} %pad_maximum_fusion.1), channel_id=1, source_target_pairs={{0,8},{1,9},{2,10},{3,11},{4,12},{5,13},{6,14},{7,15},{8,0},{9,1},... | collective-permute-start | bytes 49160 | tf_op jit(solution)/shard_map/ppermute | solution.py:411
  12.0 2.8 %collective-permute-start.9 = (f32[8,8,128]{2,1,0:T(8,128)S(1)}, f32[8,8,128]{2,1,0:T(8,128)S(1)}, u32[]{:S(2)}, u32[]{:S(2)}) collective-permute-start(f32[8,8,128]{2,1,0:T(8,128)S(1)} %pad_maximum_fusion), channel_id=1, source_target_pairs={{0,4},{1,5},{2,6},{3,7},{4,0},{5,1},{6,2},{7,3},{8,12},{9,13},{10,... | collective-permute-start | bytes 98312 | tf_op jit(solution)/shard_map/ppermute | solution.py:411
  20.9 9.0 %collective-permute-start.3 = (f32[24,16,128]{2,1,0:T(8,128)S(1)}, f32[24,16,128]{2,1,0:T(8,128)S(1)}, u32[]{:S(2)}, u32[]{:S(2)}) collective-permute-start(f32[24,16,128]{2,1,0:T(8,128)S(1)} %get-tuple-element.50), channel_id=1, source_target_pairs={{1,2},{3,4},{5,6},{7,8},{9,10},{11,12},{13,14},{17,18},{19,20},{21... | collective-permute-start | bytes 589832 | tf_op jit(solution)/shard_map/ppermute | solution.py:405
  21.0 9.0 %collective-permute-start.4 = (f32[24,16,128]{2,1,0:T(8,128)S(1)}, f32[24,16,128]{2,1,0:T(8,128)S(1)}, u32[]{:S(2)}, u32[]{:S(2)}) collective-permute-start(f32[24,16,128]{2,1,0:T(8,128)S(1)} %get-tuple-element.51), channel_id=1, source_target_pairs={{0,1},{1,0},{2,3},{3,2},{4,5},{5,4},{6,7},{7,6},{8,9},{9,8},{10,11... | collective-permute-start | bytes 589832 | tf_op jit(solution)/shard_map/ppermute | solution.py:402
  22.3 11.1 %collective-permute-start.10 = (f32[24,16,128]{2,1,0:T(8,128)S(1)}, f32[24,16,128]{2,1,0:T(8,128)S(1)}, u32[]{:S(2)}, u32[]{:S(2)}) collective-permute-start(f32[24,16,128]{2,1,0:T(8,128)S(1)} %get-tuple-element.63), channel_id=1, source_target_pairs={{1,2},{3,4},{5,6},{7,8},{9,10},{11,12},{13,14},{17,18},{19,20},{21... | collective-permute-start | bytes 589832 | tf_op jit(solution)/shard_map/ppermute | solution.py:405
  24.0 9.4 %collective-permute-start.11 = (f32[24,16,128]{2,1,0:T(8,128)S(1)}, f32[24,16,128]{2,1,0:T(8,128)S(1)}, u32[]{:S(2)}, u32[]{:S(2)}) collective-permute-start(f32[24,16,128]{2,1,0:T(8,128)S(1)} %get-tuple-element.64), channel_id=1, source_target_pairs={{0,1},{1,0},{2,3},{3,2},{4,5},{5,4},{6,7},{7,6},{8,9},{9,8},{10,11... | collective-permute-start | bytes 589832 | tf_op jit(solution)/shard_map/ppermute | solution.py:402
  31.2 4.9 %collective-permute-start.14 = (f32[16,16,128]{2,1,0:T(8,128)S(1)}, f32[16,16,128]{2,1,0:T(8,128)S(1)}, u32[]{:S(2)}, u32[]{:S(2)}) collective-permute-start(f32[16,16,128]{2,1,0:T(8,128)S(1)} %shard_map.109.s8), channel_id=1, source_target_pairs={{1,2},{3,4},{5,6},{7,8},{9,10},{11,12},{13,14},{17,18},{19,20},{21... | collective-permute-start | bytes 393224 | tf_op jit(solution)/shard_map/ppermute | solution.py:405
  31.3 4.9 %collective-permute-start.12 = (f32[16,16,128]{2,1,0:T(8,128)S(1)}, f32[16,16,128]{2,1,0:T(8,128)S(1)}, u32[]{:S(2)}, u32[]{:S(2)}) collective-permute-start(f32[16,16,128]{2,1,0:T(8,128)S(1)} %shard_map.109.s8), channel_id=1, source_target_pairs={{0,1},{1,0},{2,3},{3,2},{4,5},{5,4},{6,7},{7,6},{8,9},{9,8},{10,11... | collective-permute-start | bytes 393224 | tf_op jit(solution)/shard_map/ppermute | solution.py:402
  34.7 1.5 %collective-permute-start.15 = (f32[16,16,128]{2,1,0:T(8,128)S(1)}, f32[16,16,128]{2,1,0:T(8,128)S(1)}, u32[]{:S(2)}, u32[]{:S(2)}) collective-permute-start(f32[16,16,128]{2,1,0:T(8,128)S(1)} %shard_map.110.r8), channel_id=1, source_target_pairs={{0,1},{1,0},{2,3},{3,2},{4,5},{5,4},{6,7},{7,6},{8,9},{9,8},{10,11... | collective-permute-start | bytes 393224 | tf_op jit(solution)/shard_map/ppermute | solution.py:402
  34.8 5.9 %collective-permute-start.13 = (f32[16,16,128]{2,1,0:T(8,128)S(1)}, f32[16,16,128]{2,1,0:T(8,128)S(1)}, u32[]{:S(2)}, u32[]{:S(2)}) collective-permute-start(f32[16,16,128]{2,1,0:T(8,128)S(1)} %shard_map.110.r8), channel_id=1, source_target_pairs={{1,2},{3,4},{5,6},{7,8},{9,10},{11,12},{13,14},{17,18},{19,20},{21... | collective-permute-start | bytes 393224 | tf_op jit(solution)/shard_map/ppermute | solution.py:405

commit v8 on v7

--- a/solution.py
+++ b/solution.py
@@ -157,8 +157,7 @@
     planes[:, :, 0:LANES] = total.reshape(steps, lateral, LANES)
 
 
-def receivers_kernel(cells, traces, planes, acc, hops):
-    groups = cells.shape[0]
+def receivers_kernel(cells, traces, received, planes, acc, hops):
     steps, lateral, _ = planes.shape
     me = lax.axis_index("gx")
 
@@ -169,15 +168,16 @@
         return other
 
     acc[...] = jnp.zeros(acc.shape, f32)
-
-    def gather(j, carry):
-        row = jnp.concatenate([cells[pl.ds(owner(2 * j + half), 1), :] for half in range(2)], axis=1)
-        block = jnp.concatenate([traces[2 * j], traces[2 * j + 1]], axis=1)
-        back = jnp.concatenate([block[steps - 1 - t : steps - t] for t in range(steps)], axis=0)
-        acc[:, 0:LANES] += spread(row, split3(back), lateral, steps)
-        return carry
-
-    lax.fori_loop(0, groups // 2, gather, 0, unroll=8)
+    for source, first in ((traces, 0), (received, traces.shape[0])):
+
+        def gather(j, carry, source=source, first=first):
+            row = jnp.concatenate([cells[pl.ds(owner(first + 2 * j + half), 1), :] for half in range(2)], axis=1)
+            block = jnp.concatenate([source[2 * j], source[2 * j + 1]], axis=1)
+            back = jnp.concatenate([block[steps - 1 - t : steps - t] for t in range(steps)], axis=0)
+            acc[:, 0:LANES] += spread(row, split3(back), lateral, steps)
+            return carry
+
+        lax.fori_loop(0, source.shape[0] // 2, gather, 0, unroll=4)
     planes[:, :, 0:LANES] = acc[:, 0:LANES].reshape(steps, lateral, LANES)
 
 
@@ -328,10 +328,11 @@
             block[HALF + reach, i] = before[HALF + reach, i] + lagged(lag_s, lag_r, (0,), own_start(reach) + i, -sign * reach)
 
 
-def image_kernel(s0, s4, s8, r0, r4, r8, ev1, far_r, evs, odr, evr, ods8, evs8, evr8, early, out, rest, lag_s, lag_r, block, sems):
+def image_kernel(s0, s4, s8, r0, r4, r8, ev1, far_r, evs, odr, evr, ods8, evs8, evr8, early, out, rest, wide_s, lag_s, lag_r, block, sems):
     _, _, sign, far_start, own_start = sides()
     n = s0.shape[0]
     place_rows(lag_s, 2, s8, ods8, 0, evs8, 0)
+    wide_s[...] = lag_s[2]
     place_rows(lag_r, 2, r8, None, 0, evr8, 0)
     move = lambda j: pltpu.make_async_copy(block.at[j], out.at[HALF + sign * j], sems.at[j])
 
@@ -366,18 +367,16 @@
         each.wait()
 
 
-def last_image_kernel(s8, r8, evs8, odr8, rest, before, out, lag_s, lag_r, block, sems):
+def last_image_kernel(wide_s, odr8, rest, before, out, block, sems):
     p, there, sign, far_start, _ = sides()
-    n = s8.shape[0]
-    lag_s[0, n : 2 * n] = s8[...]
-    lag_s[0, pl.ds(2 * n * (1 - p), n)] = evs8[...]
-    lag_r[0, n : 2 * n] = r8[...]
-    lag_r[0, pl.ds(2 * n * p, n)] = jnp.where(there, odr8[...], 0.0)
+    n = odr8.shape[0]
     moves = []
     for reach in range(HALF, 0, -1):
         base = reach * (reach - 1) // 2
         for i in range(reach):
-            block[base + i] = rest[base + i] + lagged(lag_s, lag_r, (0,), far_start(reach) + i, -sign * reach)
+            x = far_start(reach) + i
+            far = jnp.where(there, odr8[x - sign * reach + n * (1 - 2 * p)], 0.0)
+            block[base + i] = rest[base + i] + wide_s[HALF + x + sign * reach] * far
         target = out.at[HALF - sign * reach, pl.ds(far_start(reach), reach)]
         moves.append(pltpu.make_async_copy(block.at[base : base + reach], target, sems.at[reach - 1]))
         moves[-1].start()
@@ -447,8 +446,9 @@
     ev1 = swap_near(ev1)
 
     gathered = jnp.concatenate([gathered, received], axis=0)
-    for which in range(1, len(hops)):
+    for which in range(1, len(hops) - 1):
         gathered = jnp.concatenate([gathered, exchange(gathered, which)], axis=0)
+    received = exchange(gathered, len(hops) - 1)
 
     plane = shape(STEPS, ny, nz)
     plane_s, *band = pl.pallas_call(
@@ -463,13 +463,13 @@
     plane_r = pl.pallas_call(
         functools.partial(receivers_kernel, hops=tuple(hops)),
         out_shape=plane,
-        in_specs=vmem_specs(2),
+        in_specs=vmem_specs(3),
         out_specs=pl.BlockSpec(memory_space=pltpu.VMEM),
         scratch_shapes=[pltpu.VMEM((STEPS * ny, nz), f32)],
         compiler_params=params(8),
         cost_estimate=estimate(2 * LANES * STEPS * ny * 2048, 1000000),
         name="receivers",
-    )(cells, gathered)
+    )(cells, gathered, received)
 
     wide = 3 * n
     scratch = [pltpu.VMEM((wide, ny, nz), f32)] * 2 + [pltpu.VMEM((wide, ny, 2 * nz), bf16)] * 4
@@ -535,11 +535,11 @@
 
     early = products(first_image_kernel, source_field, receiver_field, far_s0, ev1)
     early = products(early_image_kernel, s4, r4, ods, evs, evr, early)
-    image, rest = pl.pallas_call(
+    image, rest, wide_s = pl.pallas_call(
         image_kernel,
-        out_shape=[shape(NOFF, n, ny, nz), shape(corner, ny, nz)],
+        out_shape=[shape(NOFF, n, ny, nz), shape(corner, ny, nz), shape(wide, ny, nz)],
         in_specs=vmem_specs(15),
-        out_specs=[hbm, pl.BlockSpec(memory_space=pltpu.VMEM)],
+        out_specs=[hbm] + vmem_specs(2),
         scratch_shapes=lags(3) + [pltpu.VMEM((2 * HALF, n, ny, nz), f32), pltpu.SemaphoreType.DMA((2 * HALF,))],
         compiler_params=params(16),
         cost_estimate=estimate(NOFF * n * ny * nz * 4, 4400000),
@@ -548,14 +548,14 @@
     return pl.pallas_call(
         last_image_kernel,
         out_shape=shape(NOFF, n, ny, nz),
-        in_specs=vmem_specs(5) + [hbm],
+        in_specs=vmem_specs(3) + [hbm],
         out_specs=hbm,
-        scratch_shapes=lags(1) + [pltpu.VMEM((corner, ny, nz), f32), pltpu.SemaphoreType.DMA((HALF,))],
-        input_output_aliases={5: 0},
+        scratch_shapes=[pltpu.VMEM((corner, ny, nz), f32), pltpu.SemaphoreType.DMA((HALF,))],
+        input_output_aliases={3: 0},
         compiler_params=params(16),
         cost_estimate=estimate(HALF * n * ny * nz * 2, 2200000),
         name="last_image",
-    )(s8, r8, evs8, odr8, rest, image)
+    )(wide_s, odr8, rest, image)
 
 
 def solution(mesh):

time: 42 us -> 40 us (0.952)
  the two profiles are of different devices: /device:TPU:27 before, /device:TPU:1 now
where the time goes in v8:
time: 40 us; the launch traced here: 39.8 us
  starting transfers between devices  23.5 us (59%)
  Pallas kernels  12.3 us (31%)
  waiting for transfers between devices  3.87 us (10%)
    ppermute x7, starting transfers between devices, swap_far(): return lax.ppermute(x, ('shot', 'gx'), far)  11.8 us
    ppermute x5, starting transfers between devices, swap_near(): return lax.ppermute(x, 'gx', near)  6.37 us
    ppermute x4, starting transfers between devices, exchange(): return lax.ppermute(x, 'gx', [(i, i ^ hops[which]) for i in range(count)])  5.38 us
    ppermute x4, waiting for transfers between devices, exchange(): return lax.ppermute(x, 'gx', [(i, i ^ hops[which]) for i in range(count)])  3.32 us
    pallas_call x1, Pallas kernels, local(): pl.pallas_call(image_kernel, out_shape=[shape(NOFF, n, ny, nz), shape(cor...  2.04 us
    pallas_call x1, Pallas kernels, local(): pl.pallas_call(first_kernel, out_shape=[own, prior, shape(n + THIN, ny, n...  1.69 us
    pallas_call x1, Pallas kernels, local(): pl.pallas_call(functools.partial(pack_kernel, count=len(args)), out_shape...  1.39 us
    pallas_call x1, Pallas kernels, local(): s8 = last()(s4, s3, ods, evs, plane_s, *band, *coefs)  1.29 us
  transfers between devices with their start and end apart: 16, of which 5 were waited for; matrix products, arithmetic and copies ran while one was open for 0% of the time, Pallas kernels for 28%

profile of v8, /device:TPU:1, one launch (start us, length us, event | category | flops | bytes accessed | tf_op | source)
XLA Modules:
  0.0 39.8 jit_solution(4043761863967521917)
XLA Ops:
  0.0 2.6 %collective-permute-start = (f32[16,16,128]{2,1,0:T(8,128)}, f32[16,16,128]{2,1,0:T(8,128)S(1)}, u32[]{:S(2)}, u32[]{:S(2)}) collective-permute-start(f32[16,16,128]{2,1,0:T(8,128)} %refs_0_.1), channel_id=1, source_target_pairs={{1,2},{3,4},{5,6},{7,8},{9,10},{11,12},{13,14},{17,18},{19,20},{21... | collective-permute-start | bytes 393224 | tf_op jit(solution)/shard_map/ppermute | solution.py:404
  2.6 1.2 %collective-permute-start.6 = (f32[1,8,128]{2,1,0:T(8,128)}, f32[1,8,128]{2,1,0:T(8,128)S(1)}, u32[]{:S(2)}, u32[]{:S(2)}) collective-permute-start(f32[1,8,128]{2,1,0:T(8,128)} %bitcast.7), channel_id=1, source_target_pairs={{0,2},{1,3},{2,0},{3,1},{4,6},{5,7},{6,4},{7,5},{8,10},{9,11},{10,... | collective-permute-start | bytes 12296 | tf_op jit(solution)/shard_map/ppermute | solution.py:410
  3.9 1.4 %pack.1 = (f32[16,16,128]{2,1,0:T(8,128)S(1)}, f32[16,16,128]{2,1,0:T(8,128)S(1)}, f32[16,16,128]{2,1,0:T(8,128)S(1)}, f32[16,16,128]{2,1,0:T(8,128)S(1)}, f32[1...) custom-call(f32[16,16,128]{2,1,0:T(8,128)} %refs_0_.1, ...), custom_call_target="tpu_custom_call" | custom-call | flops 1000 | bytes 3000000 | tf_op jit(solution)/shard_map/pack/pallas_call | solution.py:431
  5.3 0.8 %collective-permute-start.1 = (f32[40,16,128]{2,1,0:T(8,128)S(1)}, f32[40,16,128]{2,1,0:T(8,128)S(1)}, u32[]{:S(2)}, u32[]{:S(2)}) collective-permute-start(f32[40,16,128]{2,1,0:T(8,128)S(1)} %get-tuple-element.41), channel_id=1, source_target_pairs={{1,2},{3,4},{5,6},{7,8},{9,10},{11,12},{13,14},{17,18},{19,20},{21... | collective-permute-start | bytes 983048 | tf_op jit(solution)/shard_map/ppermute | solution.py:404
  6.1 0.0 collective-permute-start.2
  6.1 1.2 %collective-permute-start.5 = (f32[28,16,128]{2,1,0:T(8,128)S(1)}, f32[28,16,128]{2,1,0:T(8,128)S(1)}, u32[]{:S(2)}, u32[]{:S(2)}) collective-permute-start(f32[28,16,128]{2,1,0:T(8,128)S(1)} %get-tuple-element.59), channel_id=1, source_target_pairs={{1,2},{3,4},{5,6},{7,8},{9,10},{11,12},{13,14},{17,18},{19,20},{21... | collective-permute-start | bytes 688136 | tf_op jit(solution)/shard_map/ppermute | solution.py:404
  7.2 0.0 collective-permute-done.6
  7.2 0.2 collective-permute-start.7
  7.5 1.0 %collective-permute-done.7 = f32[2,8,128]{2,1,0:T(8,128)S(1)} collective-permute-done((f32[2,8,128]{2,1,0:T(8,128)S(1)}, f32[2,8,128]{2,1,0:T(8,128)S(1)}, u32[]{:S(2)}, u32[]{:S(2)}) %collective-permute-start.7) | collective-permute-done | bytes 8224 | tf_op jit(solution)/shard_map/ppermute | solution.py:410
  8.5 2.3 %collective-permute-start.8 = (f32[4,8,128]{2,1,0:T(8,128)S(1)}, f32[4,8,128]{2,1,0:T(8,128)S(1)}, u32[]{:S(2)}, u32[]{:S(2)}) collective-permute-start(f32[4,8,128]{2,1,0:T(8,128)S(1)} %pad_maximum_fusion), channel_id=1, source_target_pairs={{0,8},{1,9},{2,10},{3,11},{4,12},{5,13},{6,14},{7,15},{8,0},{9,1},... | collective-permute-start | bytes 49160 | tf_op jit(solution)/shard_map/ppermute | solution.py:410
  10.8 1.3 %collective-permute-done.8 = f32[4,8,128]{2,1,0:T(8,128)S(1)} collective-permute-done((f32[4,8,128]{2,1,0:T(8,128)S(1)}, f32[4,8,128]{2,1,0:T(8,128)S(1)}, u32[]{:S(2)}, u32[]{:S(2)}) %collective-permute-start.8) | collective-permute-done | bytes 16416 | tf_op jit(solution)/shard_map/ppermute | solution.py:410
  12.2 1.6 %collective-permute-start.9 = (f32[8,8,128]{2,1,0:T(8,128)S(1)}, f32[8,8,128]{2,1,0:T(8,128)S(1)}, u32[]{:S(2)}, u32[]{:S(2)}) collective-permute-start(f32[8,8,128]{2,1,0:T(8,128)S(1)} %constant_dynamic-update-slice_fusion.traces), channel_id=1, source_target_pairs={{0,4},{1,5},{2,6},{3,7},{4,0},{5,1},{6,2},{7,3},{8,12},{9,13},{10,... | collective-permute-start | bytes 98312 | tf_op jit(solution)/shard_map/ppermute | solution.py:410
  13.8 0.3 shots.1
  14.1 1.0 %collective-permute-done.9.received = f32[8,8,128]{2,1,0:T(8,128)S(1)} collective-permute-done((f32[8,8,128]{2,1,0:T(8,128)S(1)}, f32[8,8,128]{2,1,0:T(8,128)S(1)}, u32[]{:S(2)}, u32[]{:S(2)}) %collective-permute-start.9) | collective-permute-done | bytes 32800 | tf_op jit(solution)/shard_map/ppermute | solution.py:410
  15.1 0.6 %receivers.1.planes = f32[8,16,128]{2,1,0:T(8,128)S(1)} custom-call(s32[16,128]{1,0:T(8,128)S(1)} %get-tuple-element.60.cells, f32[8,8,128]{2,1,0:T(8,128)S(1)} %constant_dynamic-update-slice_fusion.traces, f32[8,8,128]{2,1,0:T(8,128)S(1)} %collective-permute-done.9.received), custom_call_target="tpu_custom_call" | custom-call | flops 25165824 | bytes 1000000 | tf_op jit(solution)/shard_map/receivers/pallas_call | solution.py:463
  15.7 0.0 collective-permute-done.far_own.far_s0
  15.7 0.4 %collective-permute-done.1.far_coef = f32[40,16,128]{2,1,0:T(8,128)S(1)} collective-permute-done((f32[40,16,128]{2,1,0:T(8,128)S(1)}, f32[40,16,128]{2,1,0:T(8,128)S(1)}, u32[]{:S(2)}, u32[]{:S(2)}) %collective-permute-start.1) | collective-permute-done | bytes 327712 | tf_op jit(solution)/shard_map/ppermute | solution.py:404
  16.1 0.0 collective-permute-done.2.ev.ev1
  16.1 1.7 %first_s.1 = (f32[16,16,128]{2,1,0:T(8,128)S(1)}, f32[24,16,128]{2,1,0:T(8,128)S(1)}, f32[24,16,128]{2,1,0:T(8,128)S(1)}, f32[24,16,128]{2,1,0:T(8,128)S(1)}, f3...) custom-call(f32[16,16,128]{2,1,0:T(8,128)S(1)} %get-tuple-element.37, ...), custom_call_target="tpu_custom_call" | custom-call | flops 13762560 | bytes 6000000 | tf_op jit(solution)/shard_map/first_s/pallas_call | solution.py:478
  17.8 2.8 %collective-permute-start.3 = (f32[24,16,128]{2,1,0:T(8,128)S(1)}, f32[24,16,128]{2,1,0:T(8,128)S(1)}, u32[]{:S(2)}, u32[]{:S(2)}) collective-permute-start(f32[24,16,128]{2,1,0:T(8,128)S(1)} %get-tuple-element.51), channel_id=1, source_target_pairs={{1,2},{3,4},{5,6},{7,8},{9,10},{11,12},{13,14},{17,18},{19,20},{21... | collective-permute-start | bytes 589832 | tf_op jit(solution)/shard_map/ppermute | solution.py:404
  20.6 3.7 %collective-permute-start.4 = (f32[24,16,128]{2,1,0:T(8,128)S(1)}, f32[24,16,128]{2,1,0:T(8,128)S(1)}, u32[]{:S(2)}, u32[]{:S(2)}) collective-permute-start(f32[24,16,128]{2,1,0:T(8,128)S(1)} %get-tuple-element.52), channel_id=1, source_target_pairs={{0,1},{1,0},{2,3},{3,2},{4,5},{5,4},{6,7},{7,6},{8,9},{9,8},{10,11... | collective-permute-start | bytes 589832 | tf_op jit(solution)/shard_map/ppermute | solution.py:401
  24.3 0.0 collective-permute-done.5.od.far_r
  24.3 1.3 %first_r.1 = (f32[16,16,128]{2,1,0:T(8,128)S(1)}, f32[24,16,128]{2,1,0:T(8,128)S(1)}, f32[24,16,128]{2,1,0:T(8,128)S(1)}, f32[24,16,128]{2,1,0:T(8,128)S(1)}) custom-call(f32[16,16,128]{2,1,0:T(8,128)S(1)} %get-tuple-element.57.own.r0, f32[16,16,128]{2,1,0:T(8,128)S(1)} %get-tuple-element.58.prior, f32[28,16,128]{2,1,0:T(8,128)S(1)} %collective-permute-done.5.od.far_r, ...), custom_call_target="tpu_custom_call" | custom-call | flops 13762560 | bytes 6000000 | tf_op jit(solution)/shard_map/first_r/pallas_call | solution.py:491
  25.6 1.2 %collective-permute-start.10 = (f32[24,16,128]{2,1,0:T(8,128)S(1)}, f32[24,16,128]{2,1,0:T(8,128)S(1)}, u32[]{:S(2)}, u32[]{:S(2)}) collective-permute-start(f32[24,16,128]{2,1,0:T(8,128)S(1)} %get-tuple-element.64), channel_id=1, source_target_pairs={{1,2},{3,4},{5,6},{7,8},{9,10},{11,12},{13,14},{17,18},{19,20},{21... | collective-permute-start | bytes 589832 | tf_op jit(solution)/shard_map/ppermute | solution.py:404
  26.7 0.0 collective-permute-start.11
  26.7 0.0 collective-permute-done.3.od.ods
  26.7 0.0 collective-permute-done.4.ev.evs
  26.7 1.3 %shard_map.109.s8 = f32[16,16,128]{2,1,0:T(8,128)S(1)} custom-call(f32[16,16,128]{2,1,0:T(8,128)S(1)} %get-tuple-element.49.own.s4, f32[24,16,128]{2,1,0:T(8,128)S(1)} %get-tuple-element.50.prior, f32[24,16,128]{2,1,0:T(8,128)S(1)} %collective-permute-done.3.od.ods, f32[24,16,128]{2,1,0:T(8,128)S(1)} %collective-permute-done.4.ev.evs, ...), custom_call_target="tpu_custom_call" | custom-call | flops 13762560 | bytes 6000000 | tf_op jit(solution)/shard_map/pallas_call | solution.py:515
  28.0 0.7 %collective-permute-start.12 = (f32[16,16,128]{2,1,0:T(8,128)S(1)}, f32[16,16,128]{2,1,0:T(8,128)S(1)}, u32[]{:S(2)}, u32[]{:S(2)}) collective-permute-start(f32[16,16,128]{2,1,0:T(8,128)S(1)} %shard_map.109.s8), channel_id=1, source_target_pairs={{1,2},{3,4},{5,6},{7,8},{9,10},{11,12},{13,14},{17,18},{19,20},{21... | collective-permute-start | bytes 393224 | tf_op jit(solution)/shard_map/ppermute | solution.py:404
  28.7 2.6 %collective-permute-start.13 = (f32[16,16,128]{2,1,0:T(8,128)S(1)}, f32[16,16,128]{2,1,0:T(8,128)S(1)}, u32[]{:S(2)}, u32[]{:S(2)}) collective-permute-start(f32[16,16,128]{2,1,0:T(8,128)S(1)} %shard_map.109.s8), channel_id=1, source_target_pairs={{0,1},{1,0},{2,3},{3,2},{4,5},{5,4},{6,7},{7,6},{8,9},{9,8},{10,11... | collective-permute-start | bytes 393224 | tf_op jit(solution)/shard_map/ppermute | solution.py:401
  31.3 0.1 collective-permute-done.10.od.odr
  31.4 0.0 collective-permute-done.11.ev.evr
  31.4 1.3 %shard_map.110.r8 = f32[16,16,128]{2,1,0:T(8,128)S(1)} custom-call(f32[16,16,128]{2,1,0:T(8,128)S(1)} %get-tuple-element.62.own.r4, f32[24,16,128]{2,1,0:T(8,128)S(1)} %get-tuple-element.63.prior, f32[24,16,128]{2,1,0:T(8,128)S(1)} %collective-permute-done.10.od.odr, f32[24,16,128]{2,1,0:T(8,128)S(1)} %collective-permute-done.11.ev.evr, ...), custom_call_target="tpu_custom_call" | custom-call | flops 13762560 | bytes 6000000 | tf_op jit(solution)/shard_map/pallas_call | solution.py:518
  32.7 0.1 collective-permute-start.14
  32.8 2.5 %collective-permute-start.15 = (f32[16,16,128]{2,1,0:T(8,128)S(1)}, f32[16,16,128]{2,1,0:T(8,128)S(1)}, u32[]{:S(2)}, u32[]{:S(2)}) collective-permute-start(f32[16,16,128]{2,1,0:T(8,128)S(1)} %shard_map.110.r8), channel_id=1, source_target_pairs={{1,2},{3,4},{5,6},{7,8},{9,10},{11,12},{13,14},{17,18},{19,20},{21... | collective-permute-start | bytes 393224 | tf_op jit(solution)/shard_map/ppermute | solution.py:404
  35.4 0.6 %shard_map.111.before = f32[32,16,16,128]{3,2,1,0:T(8,128)S(1)} custom-call(f32[16,16,128]{2,1,0:T(8,128)S(1)} %get-tuple-element.37.own.s0, f32[16,16,128]{2,1,0:T(8,128)S(1)} %get-tuple-element.57.own.r0, f32[16,16,128]{2,1,0:T(8,128)S(1)} %collective-permute-done.far_own.far_s0, f32[84,16,128]{2,1,0:T(8,128)S(1)} %collective-permute-done.2.ev.ev1), custom_call_target="tpu_custom_call" | custom-call | flops 3244032 | bytes 1000000 | tf_op jit(solution)/shard_map/pallas_call | solution.py:526
  35.9 0.7 %shard_map.112.early = f32[32,16,16,128]{3,2,1,0:T(8,128)S(1)} custom-call(f32[16,16,128]{2,1,0:T(8,128)S(1)} %get-tuple-element.49.own.s4, f32[16,16,128]{2,1,0:T(8,128)S(1)} %get-tuple-element.62.own.r4, f32[24,16,128]{2,1,0:T(8,128)S(1)} %collective-permute-done.3.od.ods, f32[24,16,128]{2,1,0:T(8,128)S(1)} %collective-permute-done.4.ev.evs, ...), custom_call_target="tpu_custom_call" | custom-call | flops 3244032 | bytes 1000000 | tf_op jit(solution)/shard_map/pallas_call | solution.py:526
  36.6 0.0 collective-permute-done.12.ods8
  36.6 0.0 collective-permute-done.13.evs8
  36.6 0.0 collective-permute-done.14.evr8
  36.6 2.0 %image.1 = (f32[33,16,16,128]{3,2,1,0:T(8,128)}, f32[136,16,128]{2,1,0:T(8,128)S(1)}, f32[48,16,128]{2,1,0:T(8,128)S(1)}) custom-call(f32[16,16,128]{2,1,0:T(8,128)S(1)} %get-tuple-element.37.own.s0, f32[16,16,128]{2,1,0:T(8,128)S(1)} %get-tuple-element.49.own.s4, f32[16,16,128]{2,1,0:T(8,128)S(1)} %shard_map.109.s8, ...), custom_call_target="tpu_custom_call" | custom-call | flops 4325376 | bytes 4400000 | tf_op jit(solution)/shard_map/image/pallas_call | solution.py:538
  38.7 0.0 collective-permute-done.15.odr8
  38.7 1.1 %last_image.1 = f32[33,16,16,128]{3,2,1,0:T(8,128)} custom-call(f32[48,16,128]{2,1,0:T(8,128)S(1)} %get-tuple-element.66.wide_s, f32[16,16,128]{2,1,0:T(8,128)S(1)} %collective-permute-done.15.odr8, f32[136,16,128]{2,1,0:T(8,128)S(1)} %get-tuple-element.67.rest, f32[33,16,16,128]{3,2,1,0:T(8,128)} %get-tuple-element.68.before), custom_call_target="tpu_custom_call", output_to_operand_aliasing={{}: (3, {})} | custom-call | flops 1048576 | bytes 2200000 | tf_op jit(solution)/shard_map/last_image/pallas_call | solution.py:548
  (6 shorter events, 0.0 us)
Async XLA Ops:
  0.0 15.7 %collective-permute-start = (f32[16,16,128]{2,1,0:T(8,128)}, f32[16,16,128]{2,1,0:T(8,128)S(1)}, u32[]{:S(2)}, u32[]{:S(2)}) collective-permute-start(f32[16,16,128]{2,1,0:T(8,128)} %refs_0_.1), channel_id=1, source_target_pairs={{1,2},{3,4},{5,6},{7,8},{9,10},{11,12},{13,14},{17,18},{19,20},{21... | collective-permute-start | bytes 393224 | tf_op jit(solution)/shard_map/ppermute | solution.py:404
  2.6 4.6 %collective-permute-start.6 = (f32[1,8,128]{2,1,0:T(8,128)}, f32[1,8,128]{2,1,0:T(8,128)S(1)}, u32[]{:S(2)}, u32[]{:S(2)}) collective-permute-start(f32[1,8,128]{2,1,0:T(8,128)} %bitcast.7), channel_id=1, source_target_pairs={{0,2},{1,3},{2,0},{3,1},{4,6},{5,7},{6,4},{7,5},{8,10},{9,11},{10,... | collective-permute-start | bytes 12296 | tf_op jit(solution)/shard_map/ppermute | solution.py:410
  5.3 10.8 %collective-permute-start.1 = (f32[40,16,128]{2,1,0:T(8,128)S(1)}, f32[40,16,128]{2,1,0:T(8,128)S(1)}, u32[]{:S(2)}, u32[]{:S(2)}) collective-permute-start(f32[40,16,128]{2,1,0:T(8,128)S(1)} %get-tuple-element.41), channel_id=1, source_target_pairs={{1,2},{3,4},{5,6},{7,8},{9,10},{11,12},{13,14},{17,18},{19,20},{21... | collective-permute-start | bytes 983048 | tf_op jit(solution)/shard_map/ppermute | solution.py:404
  6.1 10.0 %collective-permute-start.2 = (f32[84,16,128]{2,1,0:T(8,128)S(1)}, f32[84,16,128]{2,1,0:T(8,128)S(1)}, u32[]{:S(2)}, u32[]{:S(2)}) collective-permute-start(f32[84,16,128]{2,1,0:T(8,128)S(1)} %get-tuple-element.42), channel_id=1, source_target_pairs={{0,1},{1,0},{2,3},{3,2},{4,5},{5,4},{6,7},{7,6},{8,9},{9,8},{10,11... | collective-permute-start | bytes 2064392 | tf_op jit(solution)/shard_map/ppermute | solution.py:401
  6.1 18.2 %collective-permute-start.5 = (f32[28,16,128]{2,1,0:T(8,128)S(1)}, f32[28,16,128]{2,1,0:T(8,128)S(1)}, u32[]{:S(2)}, u32[]{:S(2)}) collective-permute-start(f32[28,16,128]{2,1,0:T(8,128)S(1)} %get-tuple-element.59), channel_id=1, source_target_pairs={{1,2},{3,4},{5,6},{7,8},{9,10},{11,12},{13,14},{17,18},{19,20},{21... | collective-permute-start | bytes 688136 | tf_op jit(solution)/shard_map/ppermute | solution.py:404
  7.2 1.2 %collective-permute-start.7 = (f32[2,8,128]{2,1,0:T(8,128)S(1)}, f32[2,8,128]{2,1,0:T(8,128)S(1)}, u32[]{:S(2)}, u32[]{:S(2)}) collective-permute-start(f32[2,8,128]{2,1,0:T(8,128)S(1)} %pad_maximum_fusion.1), channel_id=1, source_target_pairs={{0,1},{1,0},{2,3},{3,2},{4,5},{5,4},{6,7},{7,6},{8,9},{9,8},{10,11... | collective-permute-start | bytes 24584 | tf_op jit(solution)/shard_map/ppermute | solution.py:410
  8.5 3.7 %collective-permute-start.8 = (f32[4,8,128]{2,1,0:T(8,128)S(1)}, f32[4,8,128]{2,1,0:T(8,128)S(1)}, u32[]{:S(2)}, u32[]{:S(2)}) collective-permute-start(f32[4,8,128]{2,1,0:T(8,128)S(1)} %pad_maximum_fusion), channel_id=1, source_target_pairs={{0,8},{1,9},{2,10},{3,11},{4,12},{5,13},{6,14},{7,15},{8,0},{9,1},... | collective-permute-start | bytes 49160 | tf_op jit(solution)/shard_map/ppermute | solution.py:410
  12.2 2.9 %collective-permute-start.9 = (f32[8,8,128]{2,1,0:T(8,128)S(1)}, f32[8,8,128]{2,1,0:T(8,128)S(1)}, u32[]{:S(2)}, u32[]{:S(2)}) collective-permute-start(f32[8,8,128]{2,1,0:T(8,128)S(1)} %constant_dynamic-update-slice_fusion.traces), channel_id=1, source_target_pairs={{0,4},{1,5},{2,6},{3,7},{4,0},{5,1},{6,2},{7,3},{8,12},{9,13},{10,... | collective-permute-start | bytes 98312 | tf_op jit(solution)/shard_map/ppermute | solution.py:410
  17.8 8.9 %collective-permute-start.3 = (f32[24,16,128]{2,1,0:T(8,128)S(1)}, f32[24,16,128]{2,1,0:T(8,128)S(1)}, u32[]{:S(2)}, u32[]{:S(2)}) collective-permute-start(f32[24,16,128]{2,1,0:T(8,128)S(1)} %get-tuple-element.51), channel_id=1, source_target_pairs={{1,2},{3,4},{5,6},{7,8},{9,10},{11,12},{13,14},{17,18},{19,20},{21... | collective-permute-start | bytes 589832 | tf_op jit(solution)/shard_map/ppermute | solution.py:404
  20.6 6.2 %collective-permute-start.4 = (f32[24,16,128]{2,1,0:T(8,128)S(1)}, f32[24,16,128]{2,1,0:T(8,128)S(1)}, u32[]{:S(2)}, u32[]{:S(2)}) collective-permute-start(f32[24,16,128]{2,1,0:T(8,128)S(1)} %get-tuple-element.52), channel_id=1, source_target_pairs={{0,1},{1,0},{2,3},{3,2},{4,5},{5,4},{6,7},{7,6},{8,9},{9,8},{10,11... | collective-permute-start | bytes 589832 | tf_op jit(solution)/shard_map/ppermute | solution.py:401
  25.6 5.9 %collective-permute-start.10 = (f32[24,16,128]{2,1,0:T(8,128)S(1)}, f32[24,16,128]{2,1,0:T(8,128)S(1)}, u32[]{:S(2)}, u32[]{:S(2)}) collective-permute-start(f32[24,16,128]{2,1,0:T(8,128)S(1)} %get-tuple-element.64), channel_id=1, source_target_pairs={{1,2},{3,4},{5,6},{7,8},{9,10},{11,12},{13,14},{17,18},{19,20},{21... | collective-permute-start | bytes 589832 | tf_op jit(solution)/shard_map/ppermute | solution.py:404
  26.7 4.7 %collective-permute-start.11 = (f32[24,16,128]{2,1,0:T(8,128)S(1)}, f32[24,16,128]{2,1,0:T(8,128)S(1)}, u32[]{:S(2)}, u32[]{:S(2)}) collective-permute-start(f32[24,16,128]{2,1,0:T(8,128)S(1)} %get-tuple-element.65), channel_id=1, source_target_pairs={{0,1},{1,0},{2,3},{3,2},{4,5},{5,4},{6,7},{7,6},{8,9},{9,8},{10,11... | collective-permute-start | bytes 589832 | tf_op jit(solution)/shard_map/ppermute | solution.py:401
  28.0 8.6 %collective-permute-start.12 = (f32[16,16,128]{2,1,0:T(8,128)S(1)}, f32[16,16,128]{2,1,0:T(8,128)S(1)}, u32[]{:S(2)}, u32[]{:S(2)}) collective-permute-start(f32[16,16,128]{2,1,0:T(8,128)S(1)} %shard_map.109.s8), channel_id=1, source_target_pairs={{1,2},{3,4},{5,6},{7,8},{9,10},{11,12},{13,14},{17,18},{19,20},{21... | collective-permute-start | bytes 393224 | tf_op jit(solution)/shard_map/ppermute | solution.py:404
  28.7 7.9 %collective-permute-start.13 = (f32[16,16,128]{2,1,0:T(8,128)S(1)}, f32[16,16,128]{2,1,0:T(8,128)S(1)}, u32[]{:S(2)}, u32[]{:S(2)}) collective-permute-start(f32[16,16,128]{2,1,0:T(8,128)S(1)} %shard_map.109.s8), channel_id=1, source_target_pairs={{0,1},{1,0},{2,3},{3,2},{4,5},{5,4},{6,7},{7,6},{8,9},{9,8},{10,11... | collective-permute-start | bytes 393224 | tf_op jit(solution)/shard_map/ppermute | solution.py:401
  32.7 3.9 %collective-permute-start.14 = (f32[16,16,128]{2,1,0:T(8,128)S(1)}, f32[16,16,128]{2,1,0:T(8,128)S(1)}, u32[]{:S(2)}, u32[]{:S(2)}) collective-permute-start(f32[16,16,128]{2,1,0:T(8,128)S(1)} %shard_map.110.r8), channel_id=1, source_target_pairs={{0,1},{1,0},{2,3},{3,2},{4,5},{5,4},{6,7},{7,6},{8,9},{9,8},{10,11... | collective-permute-start | bytes 393224 | tf_op jit(solution)/shard_map/ppermute | solution.py:401
  32.8 5.9 %collective-permute-start.15 = (f32[16,16,128]{2,1,0:T(8,128)S(1)}, f32[16,16,128]{2,1,0:T(8,128)S(1)}, u32[]{:S(2)}, u32[]{:S(2)}) collective-permute-start(f32[16,16,128]{2,1,0:T(8,128)S(1)} %shard_map.110.r8), channel_id=1, source_target_pairs={{1,2},{3,4},{5,6},{7,8},{9,10},{11,12},{13,14},{17,18},{19,20},{21... | collective-permute-start | bytes 393224 | tf_op jit(solution)/shard_map/ppermute | solution.py:404

commit v9 on v8

--- a/solution.py
+++ b/solution.py
@@ -328,28 +328,9 @@
             block[HALF + reach, i] = before[HALF + reach, i] + lagged(lag_s, lag_r, (0,), own_start(reach) + i, -sign * reach)
 
 
-def image_kernel(s0, s4, s8, r0, r4, r8, ev1, far_r, evs, odr, evr, ods8, evs8, evr8, early, out, rest, wide_s, lag_s, lag_r, block, sems):
-    _, _, sign, far_start, own_start = sides()
+def rest_kernel(s0, s4, r0, r4, ev1, far_r, evs, odr, evr, rest, lag_s, lag_r):
+    _, _, sign, far_start, _ = sides()
     n = s0.shape[0]
-    place_rows(lag_s, 2, s8, ods8, 0, evs8, 0)
-    wide_s[...] = lag_s[2]
-    place_rows(lag_r, 2, r8, None, 0, evr8, 0)
-    move = lambda j: pltpu.make_async_copy(block.at[j], out.at[HALF + sign * j], sems.at[j])
-
-    def whole(j, carry):
-        for x in range(n):
-            block[j, x] = early[j, x] + lagged(lag_s, lag_r, (2,), x, sign * j)
-        move(j).start()
-        return carry
-
-    lax.fori_loop(0, HALF + 1, whole, 0)
-    moves = []
-    for reach in range(1, HALF):
-        for i in range(n - reach):
-            block[HALF + reach, i] = early[HALF + reach, i] + lagged(lag_s, lag_r, (2,), own_start(reach) + i, -sign * reach)
-        target = out.at[HALF - sign * reach, pl.ds(own_start(reach), n - reach)]
-        moves.append(pltpu.make_async_copy(block.at[HALF + reach, 0 : n - reach], target, sems.at[HALF + reach]))
-        moves[-1].start()
     place_rows(lag_s, 0, s0, None, 0, ev1, n + TRIM)
     place_rows(lag_r, 0, r0, far_r, 0, ev1, 2 * (n + TRIM))
     place_rows(lag_s, 1, s4, None, 0, evs, 0)
@@ -357,6 +338,30 @@
     for reach in range(1, HALF + 1):
         for i in range(reach):
             rest[reach * (reach - 1) // 2 + i] = lagged(lag_s, lag_r, (0, 1), far_start(reach) + i, -sign * reach)
+
+
+def image_kernel(s8, r8, ods8, evs8, evr8, early, out, wide_s, lag_s, lag_r, block, sems):
+    _, _, sign, _, own_start = sides()
+    n = s8.shape[0]
+    place_rows(lag_s, 0, s8, ods8, 0, evs8, 0)
+    wide_s[...] = lag_s[0]
+    place_rows(lag_r, 0, r8, None, 0, evr8, 0)
+    move = lambda j: pltpu.make_async_copy(block.at[j], out.at[HALF + sign * j], sems.at[j])
+
+    def whole(j, carry):
+        for x in range(n):
+            block[j, x] = early[j, x] + lagged(lag_s, lag_r, (0,), x, sign * j)
+        move(j).start()
+        return carry
+
+    lax.fori_loop(0, HALF + 1, whole, 0)
+    moves = []
+    for reach in range(1, HALF):
+        for i in range(n - reach):
+            block[HALF + reach, i] = early[HALF + reach, i] + lagged(lag_s, lag_r, (0,), own_start(reach) + i, -sign * reach)
+        target = out.at[HALF - sign * reach, pl.ds(own_start(reach), n - reach)]
+        moves.append(pltpu.make_async_copy(block.at[HALF + reach, 0 : n - reach], target, sems.at[HALF + reach]))
+        moves[-1].start()
 
     def drain(j, carry):
         move(j).wait()
@@ -535,16 +540,26 @@
 
     early = products(first_image_kernel, source_field, receiver_field, far_s0, ev1)
     early = products(early_image_kernel, s4, r4, ods, evs, evr, early)
-    image, rest, wide_s = pl.pallas_call(
+    rest = pl.pallas_call(
+        rest_kernel,
+        out_shape=shape(corner, ny, nz),
+        in_specs=vmem_specs(9),
+        out_specs=pl.BlockSpec(memory_space=pltpu.VMEM),
+        scratch_shapes=lags(2),
+        compiler_params=params(8),
+        cost_estimate=estimate(1000000, 1000000),
+        name="rest",
+    )(source_field, s4, receiver_field, r4, ev1, far_r, evs, odr, evr)
+    image, wide_s = pl.pallas_call(
         image_kernel,
-        out_shape=[shape(NOFF, n, ny, nz), shape(corner, ny, nz), shape(wide, ny, nz)],
-        in_specs=vmem_specs(15),
-        out_specs=[hbm] + vmem_specs(2),
-        scratch_shapes=lags(3) + [pltpu.VMEM((2 * HALF, n, ny, nz), f32), pltpu.SemaphoreType.DMA((2 * HALF,))],
+        out_shape=[shape(NOFF, n, ny, nz), shape(wide, ny, nz)],
+        in_specs=vmem_specs(6),
+        out_specs=[hbm, pl.BlockSpec(memory_space=pltpu.VMEM)],
+        scratch_shapes=lags(1) + [pltpu.VMEM((2 * HALF, n, ny, nz), f32), pltpu.SemaphoreType.DMA((2 * HALF,))],
         compiler_params=params(16),
         cost_estimate=estimate(NOFF * n * ny * nz * 4, 4400000),
         name="image",
-    )(source_field, s4, s8, receiver_field, r4, r8, ev1, far_r, evs, odr, evr, ods8, evs8, evr8, early)
+    )(s8, r8, ods8, evs8, evr8, early)
     return pl.pallas_call(
         last_image_kernel,
         out_shape=shape(NOFF, n, ny, nz),

time: 40 us -> 42 us (1.050)
  waiting for transfers between devices: 3.87 us -> 8.46 us
  starting transfers between devices: 23.5 us -> 20.6 us
    ppermute x4, waiting for transfers between devices: 3.32 us -> 5.74 us  [exchange(): return lax.ppermute(x, 'gx', [(i, i ^ hops[which]) for i in range(count)])]
    ppermute x7, waiting for transfers between devices: 0.54 us -> 2.7 us  [swap_far(): return lax.ppermute(x, ('shot', 'gx'), far)]
    ppermute x7, starting transfers between devices: 11.8 us -> 9.64 us  [swap_far(): return lax.ppermute(x, ('shot', 'gx'), far)]
    ppermute x4, starting transfers between devices: 5.38 us -> 4.32 us  [exchange(): return lax.ppermute(x, 'gx', [(i, i ^ hops[which]) for i in range(count)])]
    pallas_call x1 -> x2, Pallas kernels: 2.04 us -> 2.41 us  [the longest x1 2.03 us: local(): pl.pallas_call(image_kernel, out_shape=[shape(NOFF, n, ny, nz), shape(wid...]
  transfers between devices with their start and end apart: 16 -> 16, of which waited for: 5 -> 5; matrix products, arithmetic and copies ran while one was open for 0% -> 0% of each run, Pallas kernels for 28% -> 27%
where the time goes in v9:
time: 42 us; the launch traced here: 41.8 us
  starting transfers between devices  20.6 us (49%)
  Pallas kernels  12.6 us (30%)
  waiting for transfers between devices  8.46 us (20%)
    ppermute x7, starting transfers between devices, swap_far(): return lax.ppermute(x, ('shot', 'gx'), far)  9.64 us
    ppermute x5, starting transfers between devices, swap_near(): return lax.ppermute(x, 'gx', near)  6.67 us
    ppermute x4, waiting for transfers between devices, exchange(): return lax.ppermute(x, 'gx', [(i, i ^ hops[which]) for i in range(count)])  5.74 us
    ppermute x4, starting transfers between devices, exchange(): return lax.ppermute(x, 'gx', [(i, i ^ hops[which]) for i in range(count)])  4.32 us
    ppermute x7, waiting for transfers between devices, swap_far(): return lax.ppermute(x, ('shot', 'gx'), far)  2.7 us
    pallas_call x1, Pallas kernels, local(): pl.pallas_call(image_kernel, out_shape=[shape(NOFF, n, ny, nz), shape(wid...  2.03 us
    pallas_call x1, Pallas kernels, local(): pl.pallas_call(first_kernel, out_shape=[own, prior, shape(n + THIN, ny, n...  1.69 us
    pallas_call x1, Pallas kernels, local(): pl.pallas_call(functools.partial(pack_kernel, count=len(args)), out_shape...  1.38 us
  transfers between devices with their start and end apart: 16, of which 5 were waited for; matrix products, arithmetic and copies ran while one was open for 0% of the time, Pallas kernels for 27%

profile of v9, /device:TPU:1, one launch (start us, length us, event | category | flops | bytes accessed | tf_op | source)
XLA Modules:
  0.0 41.8 jit_solution(8253360351730852749)
XLA Ops:
  0.0 2.1 %collective-permute-start.6 = (f32[1,8,128]{2,1,0:T(8,128)}, f32[1,8,128]{2,1,0:T(8,128)S(1)}, u32[]{:S(2)}, u32[]{:S(2)}) collective-permute-start(f32[1,8,128]{2,1,0:T(8,128)} %bitcast.7), channel_id=1, source_target_pairs={{0,2},{1,3},{2,0},{3,1},{4,6},{5,7},{6,4},{7,5},{8,10},{9,11},{10,... | collective-permute-start | bytes 12296 | tf_op jit(solution)/shard_map/ppermute | solution.py:415
  2.1 0.6 %collective-permute-start = (f32[16,16,128]{2,1,0:T(8,128)}, f32[16,16,128]{2,1,0:T(8,128)S(1)}, u32[]{:S(2)}, u32[]{:S(2)}) collective-permute-start(f32[16,16,128]{2,1,0:T(8,128)} %refs_0_.1), channel_id=1, source_target_pairs={{1,2},{3,4},{5,6},{7,8},{9,10},{11,12},{13,14},{17,18},{19,20},{21... | collective-permute-start | bytes 393224 | tf_op jit(solution)/shard_map/ppermute | solution.py:409
  2.6 1.4 %pack.1 = (f32[16,16,128]{2,1,0:T(8,128)S(1)}, f32[16,16,128]{2,1,0:T(8,128)S(1)}, f32[16,16,128]{2,1,0:T(8,128)S(1)}, f32[16,16,128]{2,1,0:T(8,128)S(1)}, f32[1...) custom-call(f32[16,16,128]{2,1,0:T(8,128)} %refs_0_.1, ...), custom_call_target="tpu_custom_call" | custom-call | flops 1000 | bytes 3000000 | tf_op jit(solution)/shard_map/pack/pallas_call | solution.py:436
  4.0 1.2 %collective-permute-start.5 = (f32[28,16,128]{2,1,0:T(8,128)S(1)}, f32[28,16,128]{2,1,0:T(8,128)S(1)}, u32[]{:S(2)}, u32[]{:S(2)}) collective-permute-start(f32[28,16,128]{2,1,0:T(8,128)S(1)} %get-tuple-element.58), channel_id=1, source_target_pairs={{1,2},{3,4},{5,6},{7,8},{9,10},{11,12},{13,14},{17,18},{19,20},{21... | collective-permute-start | bytes 688136 | tf_op jit(solution)/shard_map/ppermute | solution.py:409
  5.3 0.6 %collective-permute-start.1 = (f32[40,16,128]{2,1,0:T(8,128)S(1)}, f32[40,16,128]{2,1,0:T(8,128)S(1)}, u32[]{:S(2)}, u32[]{:S(2)}) collective-permute-start(f32[40,16,128]{2,1,0:T(8,128)S(1)} %get-tuple-element.40), channel_id=1, source_target_pairs={{1,2},{3,4},{5,6},{7,8},{9,10},{11,12},{13,14},{17,18},{19,20},{21... | collective-permute-start | bytes 983048 | tf_op jit(solution)/shard_map/ppermute | solution.py:409
  5.8 2.2 %collective-permute-start.2 = (f32[84,16,128]{2,1,0:T(8,128)S(1)}, f32[84,16,128]{2,1,0:T(8,128)S(1)}, u32[]{:S(2)}, u32[]{:S(2)}) collective-permute-start(f32[84,16,128]{2,1,0:T(8,128)S(1)} %get-tuple-element.41), channel_id=1, source_target_pairs={{0,1},{1,0},{2,3},{3,2},{4,5},{5,4},{6,7},{7,6},{8,9},{9,8},{10,11... | collective-permute-start | bytes 2064392 | tf_op jit(solution)/shard_map/ppermute | solution.py:406
  8.0 0.0 collective-permute-done.6
  8.0 0.1 collective-permute-start.7
  8.1 1.7 %collective-permute-done.7 = f32[2,8,128]{2,1,0:T(8,128)S(1)} collective-permute-done((f32[2,8,128]{2,1,0:T(8,128)S(1)}, f32[2,8,128]{2,1,0:T(8,128)S(1)}, u32[]{:S(2)}, u32[]{:S(2)}) %collective-permute-start.7) | collective-permute-done | bytes 8224 | tf_op jit(solution)/shard_map/ppermute | solution.py:415
  9.8 1.5 %collective-permute-start.8 = (f32[4,8,128]{2,1,0:T(8,128)S(1)}, f32[4,8,128]{2,1,0:T(8,128)S(1)}, u32[]{:S(2)}, u32[]{:S(2)}) collective-permute-start(f32[4,8,128]{2,1,0:T(8,128)S(1)} %pad_maximum_fusion), channel_id=1, source_target_pairs={{0,8},{1,9},{2,10},{3,11},{4,12},{5,13},{6,14},{7,15},{8,0},{9,1},... | collective-permute-start | bytes 49160 | tf_op jit(solution)/shard_map/ppermute | solution.py:415
  11.3 2.3 %collective-permute-done.8 = f32[4,8,128]{2,1,0:T(8,128)S(1)} collective-permute-done((f32[4,8,128]{2,1,0:T(8,128)S(1)}, f32[4,8,128]{2,1,0:T(8,128)S(1)}, u32[]{:S(2)}, u32[]{:S(2)}) %collective-permute-start.8) | collective-permute-done | bytes 16416 | tf_op jit(solution)/shard_map/ppermute | solution.py:415
  13.6 0.7 %collective-permute-start.9 = (f32[8,8,128]{2,1,0:T(8,128)S(1)}, f32[8,8,128]{2,1,0:T(8,128)S(1)}, u32[]{:S(2)}, u32[]{:S(2)}) collective-permute-start(f32[8,8,128]{2,1,0:T(8,128)S(1)} %constant_dynamic-update-slice_fusion.traces), channel_id=1, source_target_pairs={{0,4},{1,5},{2,6},{3,7},{4,0},{5,1},{6,2},{7,3},{8,12},{9,13},{10,... | collective-permute-start | bytes 98312 | tf_op jit(solution)/shard_map/ppermute | solution.py:415
  14.2 0.3 shots.1
  14.6 1.8 %collective-permute-done.9.received = f32[8,8,128]{2,1,0:T(8,128)S(1)} collective-permute-done((f32[8,8,128]{2,1,0:T(8,128)S(1)}, f32[8,8,128]{2,1,0:T(8,128)S(1)}, u32[]{:S(2)}, u32[]{:S(2)}) %collective-permute-start.9) | collective-permute-done | bytes 32800 | tf_op jit(solution)/shard_map/ppermute | solution.py:415
  16.3 0.6 %receivers.1.planes = f32[8,16,128]{2,1,0:T(8,128)S(1)} custom-call(s32[16,128]{1,0:T(8,128)S(1)} %get-tuple-element.59.cells, f32[8,8,128]{2,1,0:T(8,128)S(1)} %constant_dynamic-update-slice_fusion.traces, f32[8,8,128]{2,1,0:T(8,128)S(1)} %collective-permute-done.9.received), custom_call_target="tpu_custom_call" | custom-call | flops 25165824 | bytes 1000000 | tf_op jit(solution)/shard_map/receivers/pallas_call | solution.py:468
  16.9 0.0 collective-permute-done.far_own.far_s0
  16.9 1.3 %collective-permute-done.1.far_coef = f32[40,16,128]{2,1,0:T(8,128)S(1)} collective-permute-done((f32[40,16,128]{2,1,0:T(8,128)S(1)}, f32[40,16,128]{2,1,0:T(8,128)S(1)}, u32[]{:S(2)}, u32[]{:S(2)}) %collective-permute-start.1) | collective-permute-done | bytes 327712 | tf_op jit(solution)/shard_map/ppermute | solution.py:409
  18.3 0.0 collective-permute-done.2.ev.ev1
  18.3 1.7 %first_s.1 = (f32[16,16,128]{2,1,0:T(8,128)S(1)}, f32[24,16,128]{2,1,0:T(8,128)S(1)}, f32[24,16,128]{2,1,0:T(8,128)S(1)}, f32[24,16,128]{2,1,0:T(8,128)S(1)}, f3...) custom-call(f32[16,16,128]{2,1,0:T(8,128)S(1)} %get-tuple-element.36, ...), custom_call_target="tpu_custom_call" | custom-call | flops 13762560 | bytes 6000000 | tf_op jit(solution)/shard_map/first_s/pallas_call | solution.py:483
  20.0 2.6 %collective-permute-start.3 = (f32[24,16,128]{2,1,0:T(8,128)S(1)}, f32[24,16,128]{2,1,0:T(8,128)S(1)}, u32[]{:S(2)}, u32[]{:S(2)}) collective-permute-start(f32[24,16,128]{2,1,0:T(8,128)S(1)} %get-tuple-element.50), channel_id=1, source_target_pairs={{1,2},{3,4},{5,6},{7,8},{9,10},{11,12},{13,14},{17,18},{19,20},{21... | collective-permute-start | bytes 589832 | tf_op jit(solution)/shard_map/ppermute | solution.py:409
  22.6 3.0 %collective-permute-start.4 = (f32[24,16,128]{2,1,0:T(8,128)S(1)}, f32[24,16,128]{2,1,0:T(8,128)S(1)}, u32[]{:S(2)}, u32[]{:S(2)}) collective-permute-start(f32[24,16,128]{2,1,0:T(8,128)S(1)} %get-tuple-element.51), channel_id=1, source_target_pairs={{0,1},{1,0},{2,3},{3,2},{4,5},{5,4},{6,7},{7,6},{8,9},{9,8},{10,11... | collective-permute-start | bytes 589832 | tf_op jit(solution)/shard_map/ppermute | solution.py:406
  25.6 0.0 collective-permute-done.5.od.far_r
  25.6 1.3 %first_r.1 = (f32[16,16,128]{2,1,0:T(8,128)S(1)}, f32[24,16,128]{2,1,0:T(8,128)S(1)}, f32[24,16,128]{2,1,0:T(8,128)S(1)}, f32[24,16,128]{2,1,0:T(8,128)S(1)}) custom-call(f32[16,16,128]{2,1,0:T(8,128)S(1)} %get-tuple-element.56.own.r0, f32[16,16,128]{2,1,0:T(8,128)S(1)} %get-tuple-element.57.prior, f32[28,16,128]{2,1,0:T(8,128)S(1)} %collective-permute-done.5.od.far_r, ...), custom_call_target="tpu_custom_call" | custom-call | flops 13762560 | bytes 6000000 | tf_op jit(solution)/shard_map/first_r/pallas_call | solution.py:496
  26.8 1.5 %collective-permute-start.10 = (f32[24,16,128]{2,1,0:T(8,128)S(1)}, f32[24,16,128]{2,1,0:T(8,128)S(1)}, u32[]{:S(2)}, u32[]{:S(2)}) collective-permute-start(f32[24,16,128]{2,1,0:T(8,128)S(1)} %get-tuple-element.63), channel_id=1, source_target_pairs={{1,2},{3,4},{5,6},{7,8},{9,10},{11,12},{13,14},{17,18},{19,20},{21... | collective-permute-start | bytes 589832 | tf_op jit(solution)/shard_map/ppermute | solution.py:409
  28.3 0.0 collective-permute-start.11
  28.4 0.0 collective-permute-done.3.od.ods
  28.4 0.0 collective-permute-done.4.ev.evs
  28.4 1.3 %shard_map.109.s8 = f32[16,16,128]{2,1,0:T(8,128)S(1)} custom-call(f32[16,16,128]{2,1,0:T(8,128)S(1)} %get-tuple-element.48.own.s4, f32[24,16,128]{2,1,0:T(8,128)S(1)} %get-tuple-element.49.prior, f32[24,16,128]{2,1,0:T(8,128)S(1)} %collective-permute-done.3.od.ods, f32[24,16,128]{2,1,0:T(8,128)S(1)} %collective-permute-done.4.ev.evs, ...), custom_call_target="tpu_custom_call" | custom-call | flops 13762560 | bytes 6000000 | tf_op jit(solution)/shard_map/pallas_call | solution.py:520
  29.7 1.5 %collective-permute-start.13 = (f32[16,16,128]{2,1,0:T(8,128)S(1)}, f32[16,16,128]{2,1,0:T(8,128)S(1)}, u32[]{:S(2)}, u32[]{:S(2)}) collective-permute-start(f32[16,16,128]{2,1,0:T(8,128)S(1)} %shard_map.109.s8), channel_id=1, source_target_pairs={{0,1},{1,0},{2,3},{3,2},{4,5},{5,4},{6,7},{7,6},{8,9},{9,8},{10,11... | collective-permute-start | bytes 393224 | tf_op jit(solution)/shard_map/ppermute | solution.py:406
  31.1 0.6 %collective-permute-start.12 = (f32[16,16,128]{2,1,0:T(8,128)S(1)}, f32[16,16,128]{2,1,0:T(8,128)S(1)}, u32[]{:S(2)}, u32[]{:S(2)}) collective-permute-start(f32[16,16,128]{2,1,0:T(8,128)S(1)} %shard_map.109.s8), channel_id=1, source_target_pairs={{1,2},{3,4},{5,6},{7,8},{9,10},{11,12},{13,14},{17,18},{19,20},{21... | collective-permute-start | bytes 393224 | tf_op jit(solution)/shard_map/ppermute | solution.py:409
  31.7 1.3 %collective-permute-done.10.od.odr = f32[24,16,128]{2,1,0:T(8,128)S(1)} collective-permute-done((f32[24,16,128]{2,1,0:T(8,128)S(1)}, f32[24,16,128]{2,1,0:T(8,128)S(1)}, u32[]{:S(2)}, u32[]{:S(2)}) %collective-permute-start.10) | collective-permute-done | bytes 196640 | tf_op jit(solution)/shard_map/ppermute | solution.py:409
  33.1 0.0 collective-permute-done.11.ev.evr
  33.1 1.3 %shard_map.110.r8 = f32[16,16,128]{2,1,0:T(8,128)S(1)} custom-call(f32[16,16,128]{2,1,0:T(8,128)S(1)} %get-tuple-element.61.own.r4, f32[24,16,128]{2,1,0:T(8,128)S(1)} %get-tuple-element.62.prior, f32[24,16,128]{2,1,0:T(8,128)S(1)} %collective-permute-done.10.od.odr, f32[24,16,128]{2,1,0:T(8,128)S(1)} %collective-permute-done.11.ev.evr, ...), custom_call_target="tpu_custom_call" | custom-call | flops 13762560 | bytes 6000000 | tf_op jit(solution)/shard_map/pallas_call | solution.py:523
  34.4 0.1 collective-permute-start.14
  34.4 2.5 %collective-permute-start.15 = (f32[16,16,128]{2,1,0:T(8,128)S(1)}, f32[16,16,128]{2,1,0:T(8,128)S(1)}, u32[]{:S(2)}, u32[]{:S(2)}) collective-permute-start(f32[16,16,128]{2,1,0:T(8,128)S(1)} %shard_map.110.r8), channel_id=1, source_target_pairs={{1,2},{3,4},{5,6},{7,8},{9,10},{11,12},{13,14},{17,18},{19,20},{21... | collective-permute-start | bytes 393224 | tf_op jit(solution)/shard_map/ppermute | solution.py:409
  37.0 0.6 %shard_map.111.before = f32[32,16,16,128]{3,2,1,0:T(8,128)S(1)} custom-call(f32[16,16,128]{2,1,0:T(8,128)S(1)} %get-tuple-element.36.own.s0, f32[16,16,128]{2,1,0:T(8,128)S(1)} %get-tuple-element.56.own.r0, f32[16,16,128]{2,1,0:T(8,128)S(1)} %collective-permute-done.far_own.far_s0, f32[84,16,128]{2,1,0:T(8,128)S(1)} %collective-permute-done.2.ev.ev1), custom_call_target="tpu_custom_call" | custom-call | flops 3244032 | bytes 1000000 | tf_op jit(solution)/shard_map/pallas_call | solution.py:531
  37.5 0.4 rest.1
  37.9 0.7 %shard_map.112.early = f32[32,16,16,128]{3,2,1,0:T(8,128)S(1)} custom-call(f32[16,16,128]{2,1,0:T(8,128)S(1)} %get-tuple-element.48.own.s4, f32[16,16,128]{2,1,0:T(8,128)S(1)} %get-tuple-element.61.own.r4, f32[24,16,128]{2,1,0:T(8,128)S(1)} %collective-permute-done.3.od.ods, f32[24,16,128]{2,1,0:T(8,128)S(1)} %collective-permute-done.4.ev.evs, ...), custom_call_target="tpu_custom_call" | custom-call | flops 3244032 | bytes 1000000 | tf_op jit(solution)/shard_map/pallas_call | solution.py:531
  38.6 0.0 collective-permute-done.13.evs8
  38.6 0.0 collective-permute-done.12.ods8
  38.6 0.0 collective-permute-done.14.evr8
  38.7 2.0 %image.1 = (f32[33,16,16,128]{3,2,1,0:T(8,128)}, f32[48,16,128]{2,1,0:T(8,128)S(1)}) custom-call(f32[16,16,128]{2,1,0:T(8,128)S(1)} %shard_map.109.s8, f32[16,16,128]{2,1,0:T(8,128)S(1)} %shard_map.110.r8, f32[16,16,128]{2,1,0:T(8,128)S(1)} %collective-permute-done.12.ods8, f32[16,16,128]{2,1,0:T(8,128)S(1)} %collective-permute-done.13.evs8, ...), custom_call_target="tpu_custom_call" | custom-call | flops 4325376 | bytes 4400000 | tf_op jit(solution)/shard_map/image/pallas_call | solution.py:553
  40.7 0.0 collective-permute-done.15.odr8
  40.7 1.1 %last_image.1 = f32[33,16,16,128]{3,2,1,0:T(8,128)} custom-call(f32[48,16,128]{2,1,0:T(8,128)S(1)} %get-tuple-element.65.wide_s, f32[16,16,128]{2,1,0:T(8,128)S(1)} %collective-permute-done.15.odr8, f32[136,16,128]{2,1,0:T(8,128)S(1)} %rest.1, f32[33,16,16,128]{3,2,1,0:T(8,128)} %get-tuple-element.66.before), custom_call_target="tpu_custom_call", output_to_operand_aliasing={{}: (3, {})} | custom-call | flops 1048576 | bytes 2200000 | tf_op jit(solution)/shard_map/last_image/pallas_call | solution.py:563
  (6 shorter events, 0.0 us)
Async XLA Ops:
  0.0 8.0 %collective-permute-start.6 = (f32[1,8,128]{2,1,0:T(8,128)}, f32[1,8,128]{2,1,0:T(8,128)S(1)}, u32[]{:S(2)}, u32[]{:S(2)}) collective-permute-start(f32[1,8,128]{2,1,0:T(8,128)} %bitcast.7), channel_id=1, source_target_pairs={{0,2},{1,3},{2,0},{3,1},{4,6},{5,7},{6,4},{7,5},{8,10},{9,11},{10,... | collective-permute-start | bytes 12296 | tf_op jit(solution)/shard_map/ppermute | solution.py:415
  2.1 14.9 %collective-permute-start = (f32[16,16,128]{2,1,0:T(8,128)}, f32[16,16,128]{2,1,0:T(8,128)S(1)}, u32[]{:S(2)}, u32[]{:S(2)}) collective-permute-start(f32[16,16,128]{2,1,0:T(8,128)} %refs_0_.1), channel_id=1, source_target_pairs={{1,2},{3,4},{5,6},{7,8},{9,10},{11,12},{13,14},{17,18},{19,20},{21... | collective-permute-start | bytes 393224 | tf_op jit(solution)/shard_map/ppermute | solution.py:409
  4.0 21.6 %collective-permute-start.5 = (f32[28,16,128]{2,1,0:T(8,128)S(1)}, f32[28,16,128]{2,1,0:T(8,128)S(1)}, u32[]{:S(2)}, u32[]{:S(2)}) collective-permute-start(f32[28,16,128]{2,1,0:T(8,128)S(1)} %get-tuple-element.58), channel_id=1, source_target_pairs={{1,2},{3,4},{5,6},{7,8},{9,10},{11,12},{13,14},{17,18},{19,20},{21... | collective-permute-start | bytes 688136 | tf_op jit(solution)/shard_map/ppermute | solution.py:409
  5.3 13.0 %collective-permute-start.1 = (f32[40,16,128]{2,1,0:T(8,128)S(1)}, f32[40,16,128]{2,1,0:T(8,128)S(1)}, u32[]{:S(2)}, u32[]{:S(2)}) collective-permute-start(f32[40,16,128]{2,1,0:T(8,128)S(1)} %get-tuple-element.40), channel_id=1, source_target_pairs={{1,2},{3,4},{5,6},{7,8},{9,10},{11,12},{13,14},{17,18},{19,20},{21... | collective-permute-start | bytes 983048 | tf_op jit(solution)/shard_map/ppermute | solution.py:409
  5.8 12.4 %collective-permute-start.2 = (f32[84,16,128]{2,1,0:T(8,128)S(1)}, f32[84,16,128]{2,1,0:T(8,128)S(1)}, u32[]{:S(2)}, u32[]{:S(2)}) collective-permute-start(f32[84,16,128]{2,1,0:T(8,128)S(1)} %get-tuple-element.41), channel_id=1, source_target_pairs={{0,1},{1,0},{2,3},{3,2},{4,5},{5,4},{6,7},{7,6},{8,9},{9,8},{10,11... | collective-permute-start | bytes 2064392 | tf_op jit(solution)/shard_map/ppermute | solution.py:406
  8.0 1.8 %collective-permute-start.7 = (f32[2,8,128]{2,1,0:T(8,128)S(1)}, f32[2,8,128]{2,1,0:T(8,128)S(1)}, u32[]{:S(2)}, u32[]{:S(2)}) collective-permute-start(f32[2,8,128]{2,1,0:T(8,128)S(1)} %pad_maximum_fusion.1), channel_id=1, source_target_pairs={{0,1},{1,0},{2,3},{3,2},{4,5},{5,4},{6,7},{7,6},{8,9},{9,8},{10,11... | collective-permute-start | bytes 24584 | tf_op jit(solution)/shard_map/ppermute | solution.py:415
  9.8 3.8 %collective-permute-start.8 = (f32[4,8,128]{2,1,0:T(8,128)S(1)}, f32[4,8,128]{2,1,0:T(8,128)S(1)}, u32[]{:S(2)}, u32[]{:S(2)}) collective-permute-start(f32[4,8,128]{2,1,0:T(8,128)S(1)} %pad_maximum_fusion), channel_id=1, source_target_pairs={{0,8},{1,9},{2,10},{3,11},{4,12},{5,13},{6,14},{7,15},{8,0},{9,1},... | collective-permute-start | bytes 49160 | tf_op jit(solution)/shard_map/ppermute | solution.py:415
  13.6 2.8 %collective-permute-start.9 = (f32[8,8,128]{2,1,0:T(8,128)S(1)}, f32[8,8,128]{2,1,0:T(8,128)S(1)}, u32[]{:S(2)}, u32[]{:S(2)}) collective-permute-start(f32[8,8,128]{2,1,0:T(8,128)S(1)} %constant_dynamic-update-slice_fusion.traces), channel_id=1, source_target_pairs={{0,4},{1,5},{2,6},{3,7},{4,0},{5,1},{6,2},{7,3},{8,12},{9,13},{10,... | collective-permute-start | bytes 98312 | tf_op jit(solution)/shard_map/ppermute | solution.py:415
  20.0 8.4 %collective-permute-start.3 = (f32[24,16,128]{2,1,0:T(8,128)S(1)}, f32[24,16,128]{2,1,0:T(8,128)S(1)}, u32[]{:S(2)}, u32[]{:S(2)}) collective-permute-start(f32[24,16,128]{2,1,0:T(8,128)S(1)} %get-tuple-element.50), channel_id=1, source_target_pairs={{1,2},{3,4},{5,6},{7,8},{9,10},{11,12},{13,14},{17,18},{19,20},{21... | collective-permute-start | bytes 589832 | tf_op jit(solution)/shard_map/ppermute | solution.py:409
  22.6 5.8 %collective-permute-start.4 = (f32[24,16,128]{2,1,0:T(8,128)S(1)}, f32[24,16,128]{2,1,0:T(8,128)S(1)}, u32[]{:S(2)}, u32[]{:S(2)}) collective-permute-start(f32[24,16,128]{2,1,0:T(8,128)S(1)} %get-tuple-element.51), channel_id=1, source_target_pairs={{0,1},{1,0},{2,3},{3,2},{4,5},{5,4},{6,7},{7,6},{8,9},{9,8},{10,11... | collective-permute-start | bytes 589832 | tf_op jit(solution)/shard_map/ppermute | solution.py:406
  26.8 6.2 %collective-permute-start.10 = (f32[24,16,128]{2,1,0:T(8,128)S(1)}, f32[24,16,128]{2,1,0:T(8,128)S(1)}, u32[]{:S(2)}, u32[]{:S(2)}) collective-permute-start(f32[24,16,128]{2,1,0:T(8,128)S(1)} %get-tuple-element.63), channel_id=1, source_target_pairs={{1,2},{3,4},{5,6},{7,8},{9,10},{11,12},{13,14},{17,18},{19,20},{21... | collective-permute-start | bytes 589832 | tf_op jit(solution)/shard_map/ppermute | solution.py:409
  28.3 4.7 %collective-permute-start.11 = (f32[24,16,128]{2,1,0:T(8,128)S(1)}, f32[24,16,128]{2,1,0:T(8,128)S(1)}, u32[]{:S(2)}, u32[]{:S(2)}) collective-permute-start(f32[24,16,128]{2,1,0:T(8,128)S(1)} %get-tuple-element.64), channel_id=1, source_target_pairs={{0,1},{1,0},{2,3},{3,2},{4,5},{5,4},{6,7},{7,6},{8,9},{9,8},{10,11... | collective-permute-start | bytes 589832 | tf_op jit(solution)/shard_map/ppermute | solution.py:406
  29.7 9.0 %collective-permute-start.13 = (f32[16,16,128]{2,1,0:T(8,128)S(1)}, f32[16,16,128]{2,1,0:T(8,128)S(1)}, u32[]{:S(2)}, u32[]{:S(2)}) collective-permute-start(f32[16,16,128]{2,1,0:T(8,128)S(1)} %shard_map.109.s8), channel_id=1, source_target_pairs={{0,1},{1,0},{2,3},{3,2},{4,5},{5,4},{6,7},{7,6},{8,9},{9,8},{10,11... | collective-permute-start | bytes 393224 | tf_op jit(solution)/shard_map/ppermute | solution.py:406
  31.1 7.5 %collective-permute-start.12 = (f32[16,16,128]{2,1,0:T(8,128)S(1)}, f32[16,16,128]{2,1,0:T(8,128)S(1)}, u32[]{:S(2)}, u32[]{:S(2)}) collective-permute-start(f32[16,16,128]{2,1,0:T(8,128)S(1)} %shard_map.109.s8), channel_id=1, source_target_pairs={{1,2},{3,4},{5,6},{7,8},{9,10},{11,12},{13,14},{17,18},{19,20},{21... | collective-permute-start | bytes 393224 | tf_op jit(solution)/shard_map/ppermute | solution.py:409
  34.4 4.3 %collective-permute-start.14 = (f32[16,16,128]{2,1,0:T(8,128)S(1)}, f32[16,16,128]{2,1,0:T(8,128)S(1)}, u32[]{:S(2)}, u32[]{:S(2)}) collective-permute-start(f32[16,16,128]{2,1,0:T(8,128)S(1)} %shard_map.110.r8), channel_id=1, source_target_pairs={{0,1},{1,0},{2,3},{3,2},{4,5},{5,4},{6,7},{7,6},{8,9},{9,8},{10,11... | collective-permute-start | bytes 393224 | tf_op jit(solution)/shard_map/ppermute | solution.py:406
  34.4 6.2 %collective-permute-start.15 = (f32[16,16,128]{2,1,0:T(8,128)S(1)}, f32[16,16,128]{2,1,0:T(8,128)S(1)}, u32[]{:S(2)}, u32[]{:S(2)}) collective-permute-start(f32[16,16,128]{2,1,0:T(8,128)S(1)} %shard_map.110.r8), channel_id=1, source_target_pairs={{1,2},{3,4},{5,6},{7,8},{9,10},{11,12},{13,14},{17,18},{19,20},{21... | collective-permute-start | bytes 393224 | tf_op jit(solution)/shard_map/ppermute | solution.py:409
